TPU v7x, 32 devices: a whole 2x2x4 slice. The times are simulated.
32 devices in a mesh: dp: 8 (over y, x, core), mp: 4 (over z).
Axes of the slice: x: 2, y: 2, z: 4, core: 2. Of those that a mesh axis runs over, the one named last changes fastest.
Arguments:
- mel_pair: bfloat16 [16384, 200], P('dp'), may hold values from -6 to 6
- text_ids: int32 [16384], P('dp'), may hold values from 0 to 2545
- clip_lengths: int32 [8, 4], P('dp'), may hold values from 1 to 1024, 2048 in all within a row
- t_index: int32 [8, 4], P('dp'), may hold values from 0 to 999
- txt_table: bfloat16 [2546, 512], replicated, may hold values from -6 to 6
- txt_conv: float32 [2, 7, 512], replicated, may hold values from -2 to 2
- txt_vec: float32 [2, 3, 512], replicated, may hold values from -1.75 to 1.75
- txt_gain: float32 [2, 512], replicated, may hold values from 0.5 to 1.5
- txt_up: bfloat16 [2, 512, 1024], replicated, may hold values from -0.25 to 0.25
- txt_hid: float32 [2, 3, 1024], replicated, may hold values from -1.75 to 1.75
- txt_down: bfloat16 [2, 1024, 512], replicated, may hold values from -0.1875 to 0.1875
- emb_mel: bfloat16 [200, 1024], replicated, may hold values from -0.21875 to 0.21875
- emb_text: bfloat16 [512, 1024], replicated, may hold values from -0.21875 to 0.21875
- emb_bias: float32 [1024], replicated, may hold values from -1.75 to 1.75
- pos_conv: bfloat16 [2, 31, 64, 1024], P(None, None, None, 'mp'), may hold values from -0.125 to 0.125
- pos_bias: float32 [2, 1024], P(None, 'mp'), may hold values from -1.75 to 1.75
- time_w1: bfloat16 [256, 1024], replicated, may hold values from -0.375 to 0.375
- time_bias: float32 [2, 1024], replicated, may hold values from -1.75 to 1.75
- time_w2: bfloat16 [1024, 1024], replicated, may hold values from -0.1875 to 0.1875
- ada_w: bfloat16 [1024, 6144], replicated, may hold values from -0.1875 to 0.1875
- ada_b: float32 [6144], replicated, may hold values from -1.75 to 1.75
- qkv_w: bfloat16 [3, 1024, 1024], P(None, None, 'mp'), may hold values from -0.1875 to 0.1875
- qkv_b: float32 [3, 1024], P(None, 'mp'), may hold values from -1.75 to 1.75
- out_w: bfloat16 [1024, 1024], P('mp'), may hold values from -0.75 to 0.75
- out_b: float32 [1024], replicated, may hold values from -1.75 to 1.75
- ff_w1: bfloat16 [1024, 2048], P(None, 'mp'), may hold values from -0.1875 to 0.1875
- ff_b1: float32 [2048], P('mp'), may hold values from -1.75 to 1.75
- ff_w2: bfloat16 [2048, 1024], P('mp'), may hold values from -0.125 to 0.125
- ff_b2: float32 [1024], replicated, may hold values from -1.75 to 1.75
- out_grad: bfloat16 [16384, 1024], P('dp'), may hold values from -6 to 6
Outputs:
- out: float32 [16384, 1024], P('dp')
- mel_grad: float32 [16384, 200], P('dp')
- grad_txt_table: float32 [2546, 512], P(None, ('dp', 'mp'))
- grad_txt_conv: float32 [2, 7, 512], P(None, None, ('dp', 'mp'))
- grad_txt_vec: float32 [2, 3, 512], P(None, None, ('dp', 'mp'))
- grad_txt_gain: float32 [2, 512], P(None, ('dp', 'mp'))
- grad_txt_up: float32 [2, 512, 1024], P(None, None, ('dp', 'mp'))
- grad_txt_hid: float32 [2, 3, 1024], P(None, None, ('dp', 'mp'))
- grad_txt_down: float32 [2, 1024, 512], P(None, None, ('dp', 'mp'))
- grad_emb_mel: float32 [200, 1024], P(None, 'dp')
- grad_emb_text: float32 [512, 1024], P(None, 'dp')
- grad_emb_bias: float32 [1024], P('dp')
- grad_pos_conv: float32 [2, 31, 64, 1024], P(None, None, None, ('mp', 'dp'))
- grad_pos_bias: float32 [2, 1024], P(None, ('mp', 'dp'))
- grad_time_w1: float32 [256, 1024], P(None, 'dp')
- grad_time_bias: float32 [2, 1024], P(None, 'dp')
- grad_time_w2: float32 [1024, 1024], P(None, 'dp')
- grad_ada_w: float32 [1024, 6144], P(None, 'dp')
- grad_ada_b: float32 [6144], P('dp')
- grad_qkv_w: float32 [3, 1024, 1024], P(None, 'dp', 'mp')
- grad_qkv_b: float32 [3, 1024], P(None, ('mp', 'dp'))
- grad_out_w: float32 [1024, 1024], P('mp', 'dp')
- grad_out_b: float32 [1024], P('dp')
- grad_ff_w1: float32 [1024, 2048], P('dp', 'mp')
- grad_ff_b1: float32 [2048], P(('mp', 'dp'))
- grad_ff_w2: float32 [2048, 1024], P('mp', 'dp')
- grad_ff_b2: float32 [1024], P('dp')
Inputs may be any that keep to these rules, and one draw needn't show every extreme that they name: `clip_lengths`: A group's 4 clips fill its 2048 frames; one clip of every group has exactly 1024 frames.
All inputs are finite; a program needn't handle non-finite values.
Results may differ from a plain program's by a relative error of at most 0.02.
Values may be sent and summed in bfloat16 or wider, within the bound.
A program may use at most 768 MiB of HBM per device.

v0:
```python
from functools import partial
import math

import jax
import jax.numpy as jnp
from jax import lax
from jax.sharding import PartitionSpec as P

HEAD_DIM = 64


highest = lax.Precision.HIGHEST


def for_sending(shard):
    return jax.tree.map(lambda a: a.astype(jnp.bfloat16) if a.dtype == jnp.float32 else a, shard)


def to_brain(values):
    return lax.optimization_barrier(values.astype(jnp.bfloat16)).astype(jnp.float32)


def build_rounders():

    def keep_value(values):
        return values

    value_rounder = jax.custom_vjp(to_brain)
    grad_rounder = jax.custom_vjp(keep_value)

    def value_ahead(values):
        return (to_brain(values), None)

    def value_behind(saved_state, grad_in):
        return (grad_in,)

    def grad_ahead(values):
        return (values, None)

    def grad_behind(saved_state, grad_in):
        return (to_brain(grad_in),)

    value_rounder.defvjp(value_ahead, value_behind)
    grad_rounder.defvjp(grad_ahead, grad_behind)
    return (value_rounder, grad_rounder)


def round_value(values):
    return build_rounders()[0](values)


def round_grad(values):
    return build_rounders()[1](values)


def matmul(left, right):
    return jnp.dot(left, right, preferred_element_type=jnp.float32)


def precise(left, right):
    return jnp.dot(left, right, precision=highest)


def silu_slope(values):
    sigmoid_val = jax.nn.sigmoid(values)
    return sigmoid_val * (1.0 + values * (1.0 - sigmoid_val))


def layer_norm(values):
    centred = values - jnp.mean(values, axis=-1, keepdims=True)
    variance = jnp.mean(centred * centred, axis=-1, keepdims=True)
    return centred * lax.rsqrt(variance + 1e-06)


def clip_layout(lengths, row_count):
    clip_ends = jnp.cumsum(lengths)
    starts = clip_ends - lengths
    frames = jnp.arange(row_count, dtype=jnp.int32)
    member = (frames[:, None] >= starts[None, :]) & (frames[:, None] < clip_ends[None, :])
    member_int = member.astype(jnp.int32)
    clip_index = jnp.arange(lengths.shape[0], dtype=jnp.int32)
    segment = jnp.sum(member_int * clip_index[None, :], axis=1)
    position = frames - jnp.sum(member_int * starts[None, :], axis=1)
    return (member.astype(jnp.float32), segment, position, starts)


def neighbour(values, segment, offset):
    row_count = values.shape[0]
    reach_rows = abs(offset)
    padded = jnp.pad(values, ((reach_rows, reach_rows), (0, 0)))
    seg_padded = jnp.pad(segment, (reach_rows, reach_rows), constant_values=-1)
    moved_rows = lax.slice_in_dim(
        padded, reach_rows + offset, reach_rows + offset + row_count, axis=0
    )
    moved_seg = lax.slice_in_dim(
        seg_padded, reach_rows + offset, reach_rows + offset + row_count, axis=0
    )
    keep_row = (moved_seg == segment) & (segment >= 0)
    return jnp.where(keep_row[:, None], moved_rows, 0.0)


def mish_act(values):
    softplus = jnp.maximum(values, 0.0) + jnp.log1p(jnp.exp(-jnp.abs(values)))
    return values * jnp.tanh(softplus)


def text_block(
    hidden, segment, onehot, conv_kernel, vec_small, scale_vec, up_weight, vec_big, down_weight
):
    tap_count = conv_kernel.shape[0]
    mixture = vec_small[0] + jnp.zeros_like(hidden)
    for tap_index in range(tap_count):
        mixture = mixture + conv_kernel[tap_index] * neighbour(
            hidden, segment, tap_index - tap_count // 2
        )
    normed = layer_norm(mixture) * scale_vec + vec_small[1]
    upper_pre = round_grad(matmul(round_value(normed), up_weight)) + vec_big[0]
    active = jax.nn.gelu(upper_pre, approximate=False)
    squares = precise(onehot.T, active * active)
    col_norms = jnp.sqrt(jnp.maximum(squares, 1.0))
    norm_ratio = col_norms / (jnp.mean(col_norms, axis=-1, keepdims=True) + 1e-06)
    grn_out = vec_big[1] * (active * precise(onehot, norm_ratio)) + vec_big[2] + active
    return hidden + round_grad(matmul(round_value(grn_out), down_weight)) + vec_small[2]


def refine_text(weights, token_ids, segment, onehot):
    hidden = jnp.take(weights["txt_table"], token_ids, axis=0)
    for block_index in range(weights["txt_conv"].shape[0]):
        hidden = text_block(
            hidden,
            segment,
            onehot,
            weights["txt_conv"][block_index],
            weights["txt_vec"][block_index],
            weights["txt_gain"][block_index],
            weights["txt_up"][block_index],
            weights["txt_hid"][block_index],
            weights["txt_down"][block_index],
        )
    return round_value(hidden)


def position_conv(source, segment, kernel):
    row_count, feature_width = source.shape
    tap_count, group_width = (kernel.shape[0], kernel.shape[1])
    group_count = feature_width // group_width
    stacked = jnp.stack(
        [neighbour(source, segment, tap_index - tap_count // 2) for tap_index in range(tap_count)],
        axis=1,
    )
    stacked = stacked.reshape(row_count, tap_count, group_count, group_width)
    kernel_view = kernel.reshape(tap_count, group_width, group_count, group_width)
    return jnp.einsum("tkgi,kigo->tgo", stacked, kernel_view).reshape(row_count, feature_width)


def position_embed(weights, source, segment):
    conv_entry = round_grad(round_value(source))
    first_out = round_value(
        mish_act(
            round_grad(position_conv(conv_entry, segment, weights["pos_conv"][0]))
            + weights["pos_bias"][0]
        )
    )
    return round_value(
        mish_act(
            round_grad(position_conv(first_out, segment, weights["pos_conv"][1]))
            + weights["pos_bias"][1]
        )
    )


def time_sinusoid(time_steps, full_width):
    half_width = full_width // 2
    frequency = jnp.exp(
        jnp.arange(half_width, dtype=jnp.float32) * (-math.log(10000.0) / (half_width - 1))
    )
    angles = time_steps.astype(jnp.float32)[:, None] * frequency[None, :]
    return jnp.concatenate([jnp.sin(angles), jnp.cos(angles)], axis=-1)


def rotary(position, head_dim):
    inverse = jnp.exp(
        jnp.arange(0, head_dim, 2, dtype=jnp.float32) * (-math.log(10000.0) / head_dim)
    )
    angles = position.astype(jnp.float32)[:, None] * inverse[None, :]
    return (jnp.cos(angles), jnp.sin(angles))


def rotate(values, cosine, sine_table):
    row_count, head_count, head_width = values.shape
    pair_view = values.reshape(row_count, head_count, head_width // 2, 2)
    first_half = pair_view[..., 0]
    second_half = pair_view[..., 1]
    cos_rows = cosine[:, None, :]
    sin_rows = sine_table[:, None, :]
    turned = jnp.stack(
        [
            first_half * cos_rows - second_half * sin_rows,
            second_half * cos_rows + first_half * sin_rows,
        ],
        axis=-1,
    )
    return turned.reshape(row_count, head_count, head_width)


def attend_block(queries, seg_block, key_rows, value_rows, segment):
    score_scale = queries.shape[-1] ** (-0.5)
    scores = round_grad(jnp.einsum("qhd,khd->hqk", queries, key_rows)) * score_scale
    allowed = (seg_block[:, None] == segment[None, :])[None]
    scores = jnp.where(allowed, scores, -1e30)
    row_top = jnp.max(scores, axis=-1, keepdims=True)
    exponent = jnp.exp(scores - row_top)
    attn_probs = round_value(exponent / jnp.sum(exponent, axis=-1, keepdims=True))
    return round_value(round_grad(jnp.einsum("hqk,khd->qhd", attn_probs, value_rows)))


def attention(qkv_weight, qkv_bias, out_weight, normed, segment, position, head_dim):
    row_count = normed.shape[0]
    feature_width = qkv_weight.shape[2]
    head_count = feature_width // head_dim
    cosine, sine_table = rotary(position, head_dim)

    def project(which_part):
        return (round_grad(matmul(normed, qkv_weight[which_part])) + qkv_bias[which_part]).reshape(
            row_count, head_count, head_dim
        )

    queries = round_value(rotate(project(0), cosine, sine_table))
    key_rows = round_value(rotate(project(1), cosine, sine_table))
    value_rows = round_value(project(2))
    block_rows = min(512, row_count)
    block_count = row_count // block_rows
    step_fn = jax.checkpoint(
        partial(attend_block, key_rows=key_rows, value_rows=value_rows, segment=segment)
    )
    attended = lax.map(
        lambda pieces: step_fn(pieces[0], pieces[1]),
        (
            queries.reshape(block_count, block_rows, head_count, head_dim),
            segment.reshape(block_count, block_rows),
        ),
    )
    return matmul(attended.reshape(row_count, feature_width), out_weight)


def expand(onehot, modulation, which_part, feature_width):
    return precise(
        onehot, modulation[:, which_part * feature_width : (which_part + 1) * feature_width]
    )


def modulate(state, onehot, modulation, shift_part, scale_part):
    feature_width = state.shape[1]
    return round_value(
        layer_norm(state) * (1.0 + expand(onehot, modulation, scale_part, feature_width))
        + expand(onehot, modulation, shift_part, feature_width)
    )


def feed_forward(weights_in, normed):
    ff_inner = round_value(
        jax.nn.gelu(
            round_grad(matmul(normed, weights_in["ff_w1"])) + weights_in["ff_b1"], approximate=True
        )
    )
    return matmul(ff_inner, weights_in["ff_w2"])


def local(
    mel_pair,
    text_ids,
    clip_lengths,
    t_index,
    txt_table,
    txt_conv,
    txt_vec,
    txt_gain,
    txt_up,
    txt_hid,
    txt_down,
    emb_mel,
    emb_text,
    emb_bias,
    pos_conv,
    pos_bias,
    time_w1,
    time_bias,
    time_w2,
    ada_w,
    ada_b,
    qkv_w,
    qkv_b,
    out_w,
    out_b,
    ff_w1,
    ff_b1,
    ff_w2,
    ff_b2,
    out_grad,
):
    row_count = mel_pair.shape[0]
    feature_width = emb_mel.shape[1]
    lengths = clip_lengths[0]
    onehot, segment, position, starts = clip_layout(lengths, row_count)
    mp_index = lax.axis_index("mp")
    mp_size = lax.axis_size("mp")
    mel_in = mel_pair.astype(jnp.float32)
    text_weights = {
        "txt_table": txt_table.astype(jnp.float32),
        "txt_conv": txt_conv,
        "txt_vec": txt_vec,
        "txt_gain": txt_gain,
        "txt_up": txt_up.astype(jnp.float32),
        "txt_hid": txt_hid,
        "txt_down": txt_down.astype(jnp.float32),
    }
    text_rows, text_pull = jax.vjp(
        lambda weights_in: refine_text(weights_in, text_ids, segment, onehot), text_weights
    )
    emb_weights = {
        "emb_mel": emb_mel.astype(jnp.float32),
        "emb_text": emb_text.astype(jnp.float32),
        "emb_bias": emb_bias,
    }

    def embed(weights_in, mel_value, text_value):
        return (
            round_grad(
                matmul(round_value(mel_value), weights_in["emb_mel"])
                + matmul(text_value, weights_in["emb_text"])
            )
            + weights_in["emb_bias"]
        )

    start_embed, embed_pull = jax.vjp(embed, emb_weights, mel_in, text_rows)
    local_width = pos_conv.shape[3]
    pos_weights = {"pos_conv": pos_conv.astype(jnp.float32), "pos_bias": pos_bias}
    local_in = lax.dynamic_slice_in_dim(start_embed, mp_index * local_width, local_width, axis=1)
    local_out, pos_pull = jax.vjp(
        lambda weights_in, source: position_embed(weights_in, source, segment),
        pos_weights,
        local_in,
    )
    conv_full = lax.all_gather(local_out.astype(jnp.bfloat16), "mp", axis=1, tiled=True).astype(
        jnp.float32
    )
    state_one = start_embed + conv_full
    sinusoid = time_sinusoid(t_index[0], time_w1.shape[0])
    time_first = time_w1.astype(jnp.float32)
    time_second = time_w2.astype(jnp.float32)
    ada_full = ada_w.astype(jnp.float32)
    pre_one = precise(sinusoid, time_first) + time_bias[0]
    act_one = jax.nn.silu(pre_one)
    time_vec = precise(act_one, time_second) + time_bias[1]
    act_two = jax.nn.silu(time_vec)
    modulation = precise(act_two, ada_full) + ada_b
    normed_one, pre_one_pull = jax.vjp(
        lambda state, mod_in: modulate(state, onehot, mod_in, 0, 1), state_one, modulation
    )
    attn_weights = {
        "qkv_w": qkv_w.astype(jnp.float32),
        "qkv_b": qkv_b,
        "out_w": out_w.astype(jnp.float32),
    }
    attn_part, attn_pull = jax.vjp(
        lambda weights_in, normed: attention(
            weights_in["qkv_w"],
            weights_in["qkv_b"],
            weights_in["out_w"],
            normed,
            segment,
            position,
            HEAD_DIM,
        ),
        attn_weights,
        normed_one,
    )
    ff_weights = {
        "ff_w1": ff_w1.astype(jnp.float32),
        "ff_b1": ff_b1,
        "ff_w2": ff_w2.astype(jnp.float32),
    }
    attn_total = jax.tree.map(
        lambda part: part.astype(jnp.float32), lax.psum(for_sending(attn_part), "mp")
    )

    def attn_residual(state, mod_in, summed, bias_in):
        return state + expand(onehot, mod_in, 2, feature_width) * (round_grad(summed) + bias_in)

    state_two, post_one_pull = jax.vjp(attn_residual, state_one, modulation, attn_total, out_b)
    normed_two, pre_two_pull = jax.vjp(
        lambda state, mod_in: modulate(state, onehot, mod_in, 3, 4), state_two, modulation
    )
    ff_part, ff_pull = jax.vjp(feed_forward, ff_weights, normed_two)
    ff_total = jax.tree.map(
        lambda part: part.astype(jnp.float32), lax.psum(for_sending(ff_part), "mp")
    )

    def ff_residual(state, mod_in, summed, bias_in):
        return state + expand(onehot, mod_in, 5, feature_width) * (round_grad(summed) + bias_in)

    result, post_two_pull = jax.vjp(ff_residual, state_two, modulation, ff_total, ff_b2)
    cotangent = out_grad.astype(jnp.float32)
    grad_state_two, grad_mod_first, grad_ff_total, grad_ff_bias = post_two_pull(cotangent)
    grad_ff, grad_normed_two = ff_pull(grad_ff_total)
    normed_two_grad = jax.tree.map(
        lambda part: part.astype(jnp.float32), lax.psum(for_sending(grad_normed_two), "mp")
    )
    extra_two, grad_mod_second = pre_two_pull(normed_two_grad)
    grad_state_two = grad_state_two + extra_two
    grad_state_one, grad_mod_third, grad_attn_total, grad_out_bias = post_one_pull(grad_state_two)
    grad_attn, grad_normed_one = attn_pull(grad_attn_total)
    normed_one_grad = jax.tree.map(
        lambda part: part.astype(jnp.float32), lax.psum(for_sending(grad_normed_one), "mp")
    )
    extra_one, grad_mod_fourth = pre_one_pull(normed_one_grad)
    grad_state_one = grad_state_one + extra_one
    grad_modulation = grad_mod_first + grad_mod_second + grad_mod_third + grad_mod_fourth
    local_grad = lax.dynamic_slice_in_dim(
        grad_state_one, mp_index * local_width, local_width, axis=1
    )
    grad_pos, grad_local_in = pos_pull(local_grad)
    conv_back = lax.all_gather(grad_local_in.astype(jnp.bfloat16), "mp", axis=1, tiled=True).astype(
        jnp.float32
    )
    grad_emb, mel_grad, text_grad = embed_pull(grad_state_one + conv_back)
    (text_grads,) = text_pull(text_grad)
    text_grads = jax.tree.map(lambda g: g / mp_size, text_grads)
    text_out = (
        lax.psum_scatter(text_grads["txt_table"], ("dp", "mp"), scatter_dimension=1, tiled=True),
        lax.psum_scatter(text_grads["txt_conv"], ("dp", "mp"), scatter_dimension=2, tiled=True),
        lax.psum_scatter(text_grads["txt_vec"], ("dp", "mp"), scatter_dimension=2, tiled=True),
        lax.psum_scatter(text_grads["txt_gain"], ("dp", "mp"), scatter_dimension=1, tiled=True),
        lax.psum_scatter(text_grads["txt_up"], ("dp", "mp"), scatter_dimension=2, tiled=True),
        lax.psum_scatter(text_grads["txt_hid"], ("dp", "mp"), scatter_dimension=2, tiled=True),
        lax.psum_scatter(text_grads["txt_down"], ("dp", "mp"), scatter_dimension=2, tiled=True),
    )
    grad_act_two = precise(grad_modulation, ada_full.T)
    grad_time_vec = grad_act_two * silu_slope(time_vec)
    grad_act_one = precise(grad_time_vec, time_second.T)
    grad_pre_one = grad_act_one * silu_slope(pre_one)
    full_time_one = precise(sinusoid.T, grad_pre_one)
    full_time_bias = jnp.stack([jnp.sum(grad_pre_one, axis=0), jnp.sum(grad_time_vec, axis=0)])
    full_time_two = precise(act_one.T, grad_time_vec)
    full_ada = precise(act_two.T, grad_modulation)
    full_ada_bias = jnp.sum(grad_modulation, axis=0)
    (
        g_emb_mel,
        g_emb_text,
        g_emb_bias,
        g_pos_conv,
        g_pos_bias,
        g_time_one,
        g_time_bias,
        g_time_two,
        g_ada,
        g_ada_bias,
        g_qkv_w,
        g_qkv_b,
        g_out_w,
        g_out_b,
        g_ff_w1,
        g_ff_b1,
        g_ff_w2,
        g_ff_b2,
    ) = (
        lax.psum_scatter(
            grad_emb["emb_mel"].astype(jnp.bfloat16), "dp", scatter_dimension=1, tiled=True
        ).astype(jnp.float32),
        lax.psum_scatter(
            grad_emb["emb_text"].astype(jnp.bfloat16), "dp", scatter_dimension=1, tiled=True
        ).astype(jnp.float32),
        lax.psum_scatter(
            grad_emb["emb_bias"].astype(jnp.bfloat16), "dp", scatter_dimension=0, tiled=True
        ).astype(jnp.float32),
        lax.psum_scatter(
            grad_pos["pos_conv"].astype(jnp.bfloat16), "dp", scatter_dimension=3, tiled=True
        ).astype(jnp.float32),
        lax.psum_scatter(
            grad_pos["pos_bias"].astype(jnp.bfloat16), "dp", scatter_dimension=1, tiled=True
        ).astype(jnp.float32),
        lax.psum_scatter(
            full_time_one.astype(jnp.bfloat16), "dp", scatter_dimension=1, tiled=True
        ).astype(jnp.float32),
        lax.psum_scatter(
            full_time_bias.astype(jnp.bfloat16), "dp", scatter_dimension=1, tiled=True
        ).astype(jnp.float32),
        lax.psum_scatter(
            full_time_two.astype(jnp.bfloat16), "dp", scatter_dimension=1, tiled=True
        ).astype(jnp.float32),
        lax.psum_scatter(
            full_ada.astype(jnp.bfloat16), "dp", scatter_dimension=1, tiled=True
        ).astype(jnp.float32),
        lax.psum_scatter(
            full_ada_bias.astype(jnp.bfloat16), "dp", scatter_dimension=0, tiled=True
        ).astype(jnp.float32),
        lax.psum_scatter(
            grad_attn["qkv_w"].astype(jnp.bfloat16), "dp", scatter_dimension=1, tiled=True
        ).astype(jnp.float32),
        lax.psum_scatter(
            grad_attn["qkv_b"].astype(jnp.bfloat16), "dp", scatter_dimension=1, tiled=True
        ).astype(jnp.float32),
        lax.psum_scatter(
            grad_attn["out_w"].astype(jnp.bfloat16), "dp", scatter_dimension=1, tiled=True
        ).astype(jnp.float32),
        lax.psum_scatter(
            grad_out_bias.astype(jnp.bfloat16), "dp", scatter_dimension=0, tiled=True
        ).astype(jnp.float32),
        lax.psum_scatter(
            grad_ff["ff_w1"].astype(jnp.bfloat16), "dp", scatter_dimension=0, tiled=True
        ).astype(jnp.float32),
        lax.psum_scatter(
            grad_ff["ff_b1"].astype(jnp.bfloat16), "dp", scatter_dimension=0, tiled=True
        ).astype(jnp.float32),
        lax.psum_scatter(
            grad_ff["ff_w2"].astype(jnp.bfloat16), "dp", scatter_dimension=1, tiled=True
        ).astype(jnp.float32),
        lax.psum_scatter(
            grad_ff_bias.astype(jnp.bfloat16), "dp", scatter_dimension=0, tiled=True
        ).astype(jnp.float32),
    )
    return (
        result,
        mel_grad,
        text_out[0],
        text_out[1],
        text_out[2],
        text_out[3],
        text_out[4],
        text_out[5],
        text_out[6],
        g_emb_mel,
        g_emb_text,
        g_emb_bias,
        g_pos_conv,
        g_pos_bias,
        g_time_one,
        g_time_bias,
        g_time_two,
        g_ada,
        g_ada_bias,
        g_qkv_w,
        g_qkv_b,
        g_out_w,
        g_out_b,
        g_ff_w1,
        g_ff_b1,
        g_ff_w2,
        g_ff_b2,
    )


def solution(mesh):
    placed = (
        P("dp", None),
        P("dp"),
        P("dp", None),
        P("dp", None),
        P(),
        P(),
        P(),
        P(),
        P(),
        P(),
        P(),
        P(),
        P(),
        P(),
        P(None, None, None, "mp"),
        P(None, "mp"),
        P(),
        P(),
        P(),
        P(),
        P(),
        P(None, None, "mp"),
        P(None, "mp"),
        P("mp", None),
        P(),
        P(None, "mp"),
        P("mp"),
        P("mp", None),
        P(),
        P("dp", None),
    )
    return jax.shard_map(
        local,
        mesh=mesh,
        in_specs=placed,
        out_specs=(
            P("dp", None),
            P("dp", None),
            P(None, ("dp", "mp")),
            P(None, None, ("dp", "mp")),
            P(None, None, ("dp", "mp")),
            P(None, ("dp", "mp")),
            P(None, None, ("dp", "mp")),
            P(None, None, ("dp", "mp")),
            P(None, None, ("dp", "mp")),
            P(None, "dp"),
            P(None, "dp"),
            P("dp"),
            P(None, None, None, ("mp", "dp")),
            P(None, ("mp", "dp")),
            P(None, "dp"),
            P(None, "dp"),
            P(None, "dp"),
            P(None, "dp"),
            P("dp"),
            P(None, "dp", "mp"),
            P(None, ("mp", "dp")),
            P("mp", "dp"),
            P("dp"),
            P("dp", "mp"),
            P(("mp", "dp")),
            P("mp", "dp"),
            P("dp"),
        ),
        check_vma=False,
    )
```

profile of v0, /device:TPU:0, one launch (start us, length us, event | category | flops | bytes accessed | tf_op | source)
XLA Modules:
  0.0 3505.0 jit_solution(12191968649427753349)
XLA Ops:
  53.6 24.2 multiply_multiply_fusion.11
  82.6 19.5 add_convert_fusion.4
  114.6 25.0 multiply_multiply_fusion.10
  320.7 64.9 %all-gather.3.cloned.1.call-done = bf16[2048,1024]{0,1:T(8,128)(2,1)} async-done(((bf16[2048,256]{0,1:T(8,128)(2,1)}), bf16[2048,1024]{0,1:T(8,128)(2,1)}) %all-gather.3.cloned.1.call-update) | async-done | bytes 4194320 | tf_op jit(solution)/shard_map/all_gather | solution.py:344
  437.4 135.0 %while.30 = (s32[]{:T(128)}, bf16[4,512,4,64]{1,0,3,2:T(4,128)(2,1)}, s32[4,512]{1,0:T(4,128)S(1)}, s32[1,2048]{1,0:T(1,128)S(1)}, bf16[4,512,4,64]{1,3,2,0:T(8,...) while((s32[]{:T(128)}, ...), condition=%wide.region_14.15_spmd, body=%wide.region_11.14_spmd.sunk | while | flops 1099958272 | bytes 60323980 | solution.py:236
  600.7 132.3 %all-reduce.198.cloned.1.call-done = bf16[2048,1024]{0,1:T(8,128)(2,1)} async-done(((bf16[2048,1024]{0,1:T(8,128)(2,1)}), bf16[2048,1024]{0,1:T(8,128)(2,1)}) %all-reduce.198.cloned.1.call-update) | async-done | bytes 4194320 | tf_op jit(solution)/shard_map/psum | solution.py:384
  777.5 147.9 %all-reduce.200.cloned.1.call-done = bf16[2048,1024]{0,1:T(8,128)(2,1)} async-done(((bf16[2048,1024]{0,1:T(8,128)(2,1)}), bf16[2048,1024]{0,1:T(8,128)(2,1)}) %all-reduce.200.cloned.1.call-update) | async-done | bytes 4194320 | tf_op jit(solution)/shard_map/psum | solution.py:407
  962.3 345.0 %while.31 = (s32[]{:T(128)}, f32[2048,4,64]{0,2,1:T(8,128)}, f32[2048,4,64]{0,2,1:T(8,128)}, f32[4,512,4,64]{1,0,3,2:T(4,128)}, bf16[4,512,4,64]{1,3,2,0:T(8,128...) while((s32[]{:T(128)}, f32[2048,4,64]{0,2,1:T(8,128)}, ...), condition=%wide.region_28.29_spmd.clone, body=%wide.region_22.28_spmd.clone.sunk | while | flops 2838495232 | bytes 381876704 | solution.py:236
  1352.5 285.2 %all-reduce.206.cloned.1.call-done = (bf16[2048,1024]{0,1:T(8,128)(2,1)}, bf16[2048,1024]{0,1:T(8,128)(2,1)}) async-done(((bf16[2048,1024]{0,1:T(8,128)(2,1)}, bf16[2048,1024]{0,1:T(8,128)(2,1)}), (bf16[2048,1024]{0,1:T(8,128)(2,1)}, bf16[2048,1024]{0,1:T(8,128)(2,1)})) %all-reduce.206.cloned.1.call-update) | async-done | bytes 8388624 | tf_op jit(solution)/shard_map/psum | solution.py:396
  1672.7 23.5 fusion.527
  1696.2 42.7 %copy.467 = f32[2048,31,4,64]{0,3,2,1:T(8,128)} copy(f32[2048,31,4,64]{0,3,1,2:T(8,128)} %bitcast.909) | data formatting | bytes 130023424 | tf_op jit(solution)/shard_map/transpose(jvp(tkgi,kigo->tgo))/transpose | solution.py:153
  1784.1 24.6 fusion.488
  1808.7 24.0 fusion.528
  1832.7 42.7 %copy.469 = f32[2048,31,4,64]{0,3,2,1:T(8,128)} copy(f32[2048,31,4,64]{0,3,1,2:T(8,128)} %bitcast.910) | data formatting | bytes 130023424 | tf_op jit(solution)/shard_map/transpose(jvp(tkgi,kigo->tgo))/transpose | solution.py:153
  1918.1 22.9 fusion.223
  2024.4 20.8 convolution_bitcast_fusion.4
  2050.2 20.2 convolution_bitcast_fusion.3
  2150.5 20.4 fusion.507
  2230.3 20.0 fusion.508
  2283.6 23.4 multiply_reduce_fusion.15
  2356.0 22.2 convolution_convert_fusion.1
  2387.4 22.6 scatter_custom_fusion
  2463.3 25.7 all-reduce.190
  2496.4 92.9 %reduce-scatter.58.cloned.1.call-done = f32[16,2]{1,0:T(8,128)} async-done(((f32[512,2]{1,0:T(8,128)}), f32[16,2]{1,0:T(8,128)}) %reduce-scatter.58.cloned.1.call-update) | async-done | bytes 144
  2590.6 130.9 %reduce-scatter.56.cloned.1.call-done = f32[16,6]{1,0:T(8,128)} async-done(((f32[512,6]{1,0:T(8,128)}), f32[16,6]{1,0:T(8,128)}) %reduce-scatter.56.cloned.1.call-update) | async-done | bytes 400
  2723.0 131.8 %reduce-scatter.60.cloned.1.call-done = f32[32,6]{1,0:T(8,128)} async-done(((f32[1024,6]{1,0:T(8,128)}), f32[32,6]{1,0:T(8,128)}) %reduce-scatter.60.cloned.1.call-update) | async-done | bytes 784
  2856.3 130.9 %reduce-scatter.54.cloned.1.call-done = f32[16,14]{1,0:T(8,128)} async-done(((f32[512,14]{1,0:T(8,128)}), f32[16,14]{1,0:T(8,128)}) %reduce-scatter.54.cloned.1.call-update) | async-done | bytes 912
  2988.7 32.7 reduce-scatter.62.cloned.1.call-done
  3023.0 37.6 %reduce-scatter.64.cloned.1.call-done = bf16[128,512]{1,0:T(8,128)(2,1)} async-done(((bf16[1024,512]{1,0:T(8,128)(2,1)}), bf16[128,512]{1,0:T(8,128)(2,1)}) %reduce-scatter.64.cloned.1.call-update) | async-done | bytes 131088
  3062.3 183.1 %all-reduce.204.cloned.1.call-done = (f32[2,512,1024]{1,0,2:T(2,128)}, f32[2,1024,512]{1,0,2:T(2,128)}) async-done(((f32[2,512,1024]{1,0,2:T(2,128)}, f32[2,1024,512]{1,0,2:T(2,128)}), (f32[2,512,1024]{1,0,2:T(2,128)}, f32[2,1024,512]{1,0,2:T(2,128)})) %all-reduce.204.cloned.1.call-update) | async-done | bytes 8388624
  3248.7 92.8 %reduce-scatter.46.cloned.1.call-done = bf16[1024,768]{1,0:T(8,128)(2,1)} async-done(((bf16[1024,6144]{1,0:T(8,128)(2,1)}), bf16[1024,768]{1,0:T(8,128)(2,1)}) %reduce-scatter.46.cloned.1.call-update) | async-done | bytes 1572880 | tf_op jit(solution)/shard_map/reduce_scatter | solution.py:491
  3344.8 153.2 %reduce-scatter.52.cloned.1.call-done = f32[16,2546]{1,0:T(8,128)} async-done(((f32[512,2546]{1,0:T(8,128)}), f32[16,2546]{1,0:T(8,128)}) %reduce-scatter.52.cloned.1.call-update) | async-done | bytes 162960
  (1200 shorter events, 1441.6 us)
Async XLA Ops:
  7.2 297.3 %copy-start = (bf16[1024,1024]{1,0:T(8,128)(2,1)S(1)}, bf16[1024,1024]{1,0:T(8,128)(2,1)}, u32[]{:S(2)}) copy-start(bf16[1024,1024]{1,0:T(8,128)(2,1)} %param.52) | copy-start | bytes 6291460
  7.2 378.3 %all-gather.3.cloned.1.call-start = ((), (), s32[]{:S(2)}) async-start(), calls=%async_computation.17 | async-start | bytes 5242880 | tf_op jit(solution)/shard_map/all_gather | solution.py:344
  10.2 733.5 %copy-start.139 = (s32[4,1]{0,1:T(1,128)}, s32[4,1]{0,1:T(1,128)S(1)}, u32[]{:S(2)}) copy-start(s32[4,1]{0,1:T(1,128)S(1)} %reduce-window.4) | copy-start | bytes 52
  10.9 732.9 %copy-start.141 = (s32[4]{0:T(128)}, s32[4]{0:T(128)S(1)}, u32[]{:S(2)}) copy-start(s32[4]{0:T(128)S(1)} %fusion.441) | copy-start | bytes 52
  12.3 227.3 %copy-start.133 = (pred[2048]{0:T(1024)(128)(4,1)}, pred[2048]{0:T(1024)(128)(4,1)S(1)}, u32[]{:S(2)}) copy-start(pred[2048]{0:T(1024)(128)(4,1)S(1)} %get-tuple-element.843) | copy-start | bytes 6148
  12.3 227.3 %copy-start.136 = (pred[2048]{0:T(1024)(128)(4,1)}, pred[2048]{0:T(1024)(128)(4,1)S(1)}, u32[]{:S(2)}) copy-start(pred[2048]{0:T(1024)(128)(4,1)S(1)} %get-tuple-element.845) | copy-start | bytes 6148
  12.3 227.3 %copy-start.146 = (pred[2048]{0:T(1024)(128)(4,1)}, pred[2048]{0:T(1024)(128)(4,1)S(1)}, u32[]{:S(2)}) copy-start(pred[2048]{0:T(1024)(128)(4,1)S(1)} %get-tuple-element.840) | copy-start | bytes 6148
  12.3 227.3 %copy-start.149 = (pred[2048]{0:T(1024)(128)(4,1)}, pred[2048]{0:T(1024)(128)(4,1)S(1)}, u32[]{:S(2)}) copy-start(pred[2048]{0:T(1024)(128)(4,1)S(1)} %get-tuple-element.842) | copy-start | bytes 6148
  301.9 431.1 %all-reduce.198.cloned.1.call-start = ((), (), s32[]{:S(2)}) async-start(), calls=%async_computation.18 | async-start | bytes 8388608 | tf_op jit(solution)/shard_map/psum | solution.py:384
  579.4 346.0 %all-reduce.200.cloned.1.call-start = ((), (), s32[]{:S(2)}) async-start(), calls=%async_computation.19 | async-start | bytes 8388608 | tf_op jit(solution)/shard_map/psum | solution.py:407
  771.2 866.5 %all-reduce.206.cloned.1.call-start = ((), (), s32[]{:S(2)}) async-start(), calls=%async_computation.40 | async-start | bytes 16777216 | tf_op jit(solution)/shard_map/psum | solution.py:396
  1347.0 290.7 %copy-start.100 = (f32[2048]{0:T(1024)S(1)}, f32[2048]{0:T(1024)}, u32[]{:S(2)}) copy-start(f32[2048]{0:T(1024)} %copy-done.99) | copy-start | bytes 24580
  1347.0 767.4 %all-gather.5.cloned.1.call-start = ((), (), s32[]{:S(2)}) async-start(), calls=%async_computation.20 | async-start | bytes 5242880 | tf_op jit(solution)/shard_map/all_gather | solution.py:423
  1941.0 484.3 %reduce-scatter.78.cloned.1.call-start = ((), (), s32[]{:S(2)}) async-start(), calls=%async_computation.37 | async-start | bytes 1179648
  1949.7 477.4 %reduce-scatter.50.cloned.1.call-start = ((), (), s32[]{:S(2)}) async-start(), calls=%async_computation.23 | async-start | bytes 1179648 | tf_op jit(solution)/shard_map/reduce_scatter | solution.py:509
  1956.0 472.7 %reduce-scatter.74.cloned.1.call-start = ((), (), s32[]{:S(2)}) async-start(), calls=%async_computation.35 | async-start | bytes 73728
  1961.9 468.2 %reduce-scatter.76.cloned.1.call-start = ((), (), s32[]{:S(2)}) async-start(), calls=%async_computation.36 | async-start | bytes 589824
  1968.8 462.9 %reduce-scatter.48.cloned.1.call-start = ((), (), s32[]{:S(2)}) async-start(), calls=%async_computation.22 | async-start | bytes 1769472 | tf_op jit(solution)/shard_map/reduce_scatter | solution.py:497
  1975.7 478.7 %reduce-scatter.66.cloned.1.call-start = ((), (), s32[]{:S(2)}) async-start(), calls=%async_computation.31 | async-start | bytes 73728
  2045.2 410.6 %reduce-scatter.70.cloned.1.call-start = ((), (), s32[]{:S(2)}) async-start(), calls=%async_computation.33 | async-start | bytes 294912
  2046.2 411.1 %reduce-scatter.68.cloned.1.call-start = ((), (), s32[]{:S(2)}) async-start(), calls=%async_computation.32 | async-start | bytes 589824
  2050.1 408.7 %all-reduce.202.cloned.1.call-start = ((), (), s32[]{:S(2)}) async-start(), calls=%async_computation.38 | async-start | bytes 8126464
  2104.9 356.4 %reduce-scatter.72.cloned.1.call-start = ((), (), s32[]{:S(2)}) async-start(), calls=%async_computation.34 | async-start | bytes 2359296
  2113.8 475.4 %reduce-scatter.58.cloned.1.call-start = ((), (), s32[]{:S(2)}) async-start(), calls=%async_computation.27 | async-start | bytes 270336
  2283.5 438.0 %reduce-scatter.56.cloned.1.call-start = ((), (), s32[]{:S(2)}) async-start(), calls=%async_computation.26 | async-start | bytes 270336
  2308.4 546.4 %reduce-scatter.60.cloned.1.call-start = ((), (), s32[]{:S(2)}) async-start(), calls=%async_computation.28 | async-start | bytes 540672
  2310.5 676.7 %reduce-scatter.54.cloned.1.call-start = ((), (), s32[]{:S(2)}) async-start(), calls=%async_computation.25 | async-start | bytes 270336
  2311.9 709.4 %reduce-scatter.62.cloned.1.call-start = ((), (), s32[]{:S(2)}) async-start(), calls=%async_computation.29 | async-start | bytes 589824
  2318.3 742.2 %reduce-scatter.64.cloned.1.call-start = ((), (), s32[]{:S(2)}) async-start(), calls=%async_computation.30 | async-start | bytes 1179648
  2324.9 920.6 %all-reduce.204.cloned.1.call-start = ((), (), s32[]{:S(2)}) async-start(), calls=%async_computation.39 | async-start | bytes 16777216
  2355.2 986.2 %reduce-scatter.46.cloned.1.call-start = ((), (), s32[]{:S(2)}) async-start(), calls=%async_computation.21 | async-start | bytes 14155776 | tf_op jit(solution)/shard_map/reduce_scatter | solution.py:491
  2378.3 1119.6 %reduce-scatter.52.cloned.1.call-start = ((), (), s32[]{:S(2)}) async-start(), calls=%async_computation.24 | async-start | bytes 5406720
  (346 other events, 5090.3 us)
Sparse Core Ops, SparseCore 0:
  302.0 83.4 all-gather.2
  579.5 153.4 all-reduce.197
  771.3 153.9 all-reduce.199
  1347.1 290.5 all-reduce.205
  1941.1 79.7 all-gather.4
  2024.0 34.6 reduce-scatter.77
  2061.8 36.0 reduce-scatter.49
  2101.5 33.1 reduce-scatter.73
  2138.1 34.1 reduce-scatter.75
  2176.0 38.4 reduce-scatter.47
  2218.1 33.1 reduce-scatter.65
  2254.5 33.5 reduce-scatter.69
  2291.7 34.1 reduce-scatter.67
  2329.5 79.5 all-reduce.201
  2412.3 41.3 reduce-scatter.71
  2455.8 133.4 reduce-scatter.57
  2591.3 130.1 reduce-scatter.55
  2723.7 131.0 reduce-scatter.59
  2857.6 129.5 reduce-scatter.53
  2990.4 30.8 reduce-scatter.61
  3024.5 36.0 reduce-scatter.63
  3066.5 178.9 all-reduce.203
  3249.0 92.4 reduce-scatter.45
  3344.2 153.7 reduce-scatter.51
where the time goes:
time: 3520 us; the launch traced here: 3500 us
  waiting for transfers between devices  1620 us (46%)
  matrix products  702 us (20%)
  other arithmetic  646 us (18%)
  local copies, waits for them, and re-layouts  490 us (14%)
    unnamed x40, waiting for transfers between devices  894 us
    psum x1, waiting for transfers between devices, local(): lax.psum(for_sending(ff_part), 'mp')  285 us
    dot_general x28, matrix products, precise(): return jnp.dot(left, right, precision=highest)  223 us
    dot_general x36, matrix products, matmul(): return jnp.dot(left, right, preferred_element_type=jnp.float32)  199 us
    unnamed x714, local copies, waits for them, and re-layouts  159 us
    psum x1, waiting for transfers between devices, local(): lax.psum(for_sending(grad_normed_two), 'mp')  148 us
    psum x1, waiting for transfers between devices, local(): lax.psum(for_sending(attn_part), 'mp')  132 us
    select_n x18, other arithmetic, neighbour(): return jnp.where(keep_row[:, None], moved_rows, 0.0)  131 us
  transfers between devices with their start and end apart: 24, of which 13 were waited for; matrix products, arithmetic and copies ran while one was open for 17% of the time, Pallas kernels for 0%

commit v1 on v0

v1 whole, which is shorter than its diff:
```python
from functools import partial
import math

import jax
import jax.numpy as jnp
from jax import lax
from jax.experimental import pallas as pl
from jax.experimental.pallas import tpu as pltpu
from jax.sharding import PartitionSpec as P

HEAD_DIM = 64
GAP = 16
HALO = 8
BF = jnp.bfloat16
F32 = jnp.float32
highest = lax.Precision.HIGHEST
NN = (((1,), (0,)), ((), ()))
NT = (((1,), (1,)), ((), ()))
TN = (((0,), (0,)), ((), ()))


def dot(left, right, dims=NN):
    return lax.dot_general(left.astype(BF), right.astype(BF), dims, preferred_element_type=F32)


def precise(left, right, dims=NN):
    one = lax.reduce_precision(left, 8, 7)
    two = lax.reduce_precision(left - one, 8, 7)
    three = left - one - two
    rows = left.shape[0]
    stacked = jnp.concatenate([one, two, three], axis=0).astype(BF)
    product = lax.dot_general(stacked, right, dims, preferred_element_type=F32)
    return product[:rows] + product[rows : 2 * rows] + product[2 * rows :]


@jax.custom_vjp
def expand(onehot, parts):
    return sum(onehot[:, c : c + 1] * parts[c : c + 1] for c in range(parts.shape[0]))


def expand_ahead(onehot, parts):
    return expand(onehot, parts), onehot


def expand_behind(onehot, grad):
    return None, jnp.dot(onehot.T, grad, precision=highest)


expand.defvjp(expand_ahead, expand_behind)


def silu_slope(values):
    sigmoid_val = jax.nn.sigmoid(values)
    return sigmoid_val * (1.0 + values * (1.0 - sigmoid_val))


def layer_norm(values):
    centred = values - jnp.mean(values, axis=-1, keepdims=True)
    variance = jnp.mean(centred * centred, axis=-1, keepdims=True)
    return centred * lax.rsqrt(variance + 1e-06)


def mish(values):
    grown = jnp.exp(jnp.minimum(values, 20.0))
    wide = grown * (grown + 2.0)
    return values * (wide / (wide + 2.0))


def mish_slope(values):
    grown = jnp.exp(jnp.minimum(values, 20.0))
    wide = grown * (grown + 2.0)
    under = 1.0 / (wide + 2.0)
    return wide * under + values * (4.0 * grown * (1.0 + grown) * under * under)


def conv_norm(hidden, segment, conv, vec, gain):
    taps = conv.shape[0]
    reach = taps // 2
    rows = hidden.shape[0]
    padded = jnp.pad(hidden, ((reach, reach), (0, 0)))
    seg_padded = jnp.pad(segment, (reach, reach), constant_values=-1)
    mixture = vec[0]
    for tap in range(taps):
        keep = (seg_padded[tap : tap + rows] == segment) & (segment >= 0)
        mixture = mixture + conv[tap] * jnp.where(keep[:, None], padded[tap : tap + rows], 0.0)
    return layer_norm(mixture) * gain + vec[1]


def activate(pre, bias):
    return jax.nn.gelu(pre + bias, approximate=False)


def clip_squares(own, active):
    return jnp.dot(own.T, active * active, precision=highest)


def respond(active, squares, onehot, scale, shift):
    norms = jnp.sqrt(jnp.maximum(squares, 1.0))
    ratio = norms / (jnp.mean(norms, axis=-1, keepdims=True) + 1e-06)
    return scale * (active * expand(onehot, ratio)) + shift + active


def text_ahead(hidden, segment, onehot, own, conv, vec, gain, up, hid, down, axis):
    normed, norm_pull = jax.vjp(
        lambda h, c, v, g: conv_norm(h, segment, c, v, g), hidden, conv, vec, gain
    )
    normed = normed.astype(BF)
    active, act_pull = jax.vjp(activate, dot(normed, up), hid[0])
    squares, square_pull = jax.vjp(lambda a: clip_squares(own, a), active)
    squares = lax.psum(squares, axis)
    grown, respond_pull = jax.vjp(
        lambda a, s, g, b: respond(a, s, onehot, g, b), active, squares, hid[1], hid[2]
    )
    grown = grown.astype(BF)
    result = hidden + dot(grown, down) + vec[2]
    return result, (norm_pull, normed, act_pull, square_pull, respond_pull, grown)


def text_behind(kept, grad, up, down, axis):
    norm_pull, normed, act_pull, square_pull, respond_pull, grown = kept
    grad_low = grad.astype(BF)
    g_out = jnp.sum(grad, axis=0)
    g_down = dot(grad_low, grown, TN)
    grad_active, grad_squares, g_scale, g_shift = respond_pull(dot(grad_low, down, NT))
    grad_squares = lax.psum(grad_squares, axis)
    grad_active = grad_active + square_pull(grad_squares)[0]
    grad_pre, g_bias = act_pull(grad_active)
    pre_low = grad_pre.astype(BF)
    g_up = dot(pre_low, normed, TN)
    grad_hidden, g_conv, g_vec, g_gain = norm_pull(dot(pre_low, up, NT))
    g_vec = g_vec.at[2].add(g_out)
    return (
        grad + grad_hidden,
        (g_conv, g_vec, g_gain, g_up, jnp.stack([g_bias, g_scale, g_shift]), g_down),
    )


def spread(values, starts, ends):
    rows = values.shape[0]
    clips = starts.shape[0]
    at = jnp.arange(rows, dtype=jnp.int32)
    total = rows + GAP * clips + 2 * GAP
    out = None
    for c in range(clips):
        keep = (at >= starts[c]) & (at < ends[c])
        part = jnp.where(keep[:, None], values, 0)
        lead = GAP + GAP * c
        part = jnp.pad(part, ((lead, total - lead - rows), (0, 0)))
        out = part if out is None else out + part
    return out


def gather_back(values, starts, ends):
    clips = starts.shape[0]
    rows = values.shape[0] - GAP * clips
    at = jnp.arange(rows, dtype=jnp.int32)
    out = None
    for c in range(clips):
        keep = (at >= starts[c]) & (at < ends[c])
        part = jnp.where(keep[:, None], values[GAP * c : GAP * c + rows], 0)
        out = part if out is None else out + part
    return out


def conv_kernel(taps, x_ref, w_ref, o_ref):
    rows = o_ref.shape[0]
    first = GAP - taps // 2
    columns = [x_ref[first + k : first + k + rows, :].astype(BF) for k in range(taps)]
    o_ref[...] = jnp.dot(
        jnp.concatenate(columns, axis=1), w_ref[...], preferred_element_type=F32
    )


def conv_chunk(rows):
    for size in (528, 352, 256, 128, 64, 32, 16):
        if rows % size == 0:
            return size
    return rows


def apply_conv(spread_rows, weight, taps):
    rows = spread_rows.shape[0] - 2 * GAP
    width = spread_rows.shape[1]
    chunk = conv_chunk(rows)
    return pl.pallas_call(
        partial(conv_kernel, taps),
        out_shape=jax.ShapeDtypeStruct((rows, width), F32),
        grid=(rows // chunk,),
        in_specs=[
            pl.BlockSpec((pl.Element(chunk + 2 * GAP), pl.Element(width)), lambda i: (i * chunk, 0)),
            pl.BlockSpec(weight.shape, lambda i: (0, 0), pipeline_mode=pl.Buffered(1)),
        ],
        out_specs=pl.BlockSpec((chunk, width), lambda i: (i, 0)),
        compiler_params=pltpu.CompilerParams(vmem_limit_bytes=48 << 20),
        cost_estimate=pl.CostEstimate(
            flops=2 * rows * taps * width * width, bytes_accessed=8 << 20, transcendentals=0
        ),
    )(spread_rows, weight)


def conv_grad_kernel(taps, group, x_ref, g_ref, o_ref):
    rows, width = g_ref.shape
    first = GAP - taps // 2
    turned = g_ref[...].T.astype(BF)

    @pl.when(pl.program_id(0) == 0)
    def _():
        o_ref[...] = jnp.zeros_like(o_ref)

    for k in range(taps):
        window = x_ref[first + k : first + k + rows, :].astype(BF)
        product = jnp.dot(turned, window, preferred_element_type=F32)
        for g in range(width // group):
            own = slice(g * group, (g + 1) * group)
            o_ref[own, k * group : (k + 1) * group] += product[own, own]


def conv_grad(spread_rows, grads, taps, group):
    rows, width = grads.shape
    chunk = conv_chunk(rows)
    return pl.pallas_call(
        partial(conv_grad_kernel, taps, group),
        out_shape=jax.ShapeDtypeStruct((width, taps * group), F32),
        grid=(rows // chunk,),
        in_specs=[
            pl.BlockSpec((pl.Element(chunk + 2 * GAP), pl.Element(width)), lambda i: (i * chunk, 0)),
            pl.BlockSpec((chunk, width), lambda i: (i, 0)),
        ],
        out_specs=pl.BlockSpec((width, taps * group), lambda i: (0, 0)),
        compiler_params=pltpu.CompilerParams(vmem_limit_bytes=48 << 20),
        cost_estimate=pl.CostEstimate(
            flops=2 * rows * taps * width * width, bytes_accessed=8 << 20, transcendentals=0
        ),
    )(spread_rows, grads)


def block_diagonal(weight, turned):
    taps, group, width = weight.shape
    groups = width // group
    parts = weight.reshape(taps, group, groups, group)
    if turned:
        parts = parts[::-1].transpose(0, 3, 2, 1)
    eye = jnp.eye(groups, dtype=weight.dtype)
    full = parts[:, None] * eye[None, :, None, :, None]
    return full.reshape(taps * groups * group, groups * group)


def pair_split(columns):
    lead = columns.shape[:-1]
    pairs = columns.reshape(*lead, columns.shape[-1] // 2, 2)
    return jnp.concatenate([pairs[..., 0], pairs[..., 1]], axis=-1)


def pair_merge(columns):
    half = columns.shape[-1] // 2
    return jnp.stack([columns[..., :half], columns[..., half:]], axis=-1).reshape(columns.shape)


def head_masks(width):
    heads = width // HEAD_DIM
    lane = lax.broadcasted_iota(jnp.int32, (1, width), 1)
    half = HEAD_DIM // 2
    paired = [((lane % (width // 2)) // half) == h for h in range(heads)]
    plain = [(lane // HEAD_DIM) == h for h in range(heads)]
    return heads, paired, plain


def attend_kernel(bounds, q_ref, k_ref, v_ref, sq_ref, sk_ref, o_ref, full_ref, lse_ref):
    i = pl.program_id(0)
    q = q_ref[...]
    rows, width = q.shape
    heads, paired, plain = head_masks(width)
    scale = HEAD_DIM**-0.5
    q_heads = [jnp.where(paired[h], q, jnp.zeros_like(q)) for h in range(heads)]
    sq = sq_ref[...]

    def step(kb, carry):
        tops, sums, acc = carry
        k, v = k_ref[kb], v_ref[kb]
        same = sq == sk_ref[kb]
        new_tops, new_sums = [], []
        decay, extra = None, None
        for h in range(heads):
            scores = lax.dot_general(q_heads[h], k, NT, preferred_element_type=F32) * scale
            scores = jnp.where(same, scores, -1e30)
            top = jnp.maximum(tops[h], jnp.max(scores, axis=-1, keepdims=True))
            fade = jnp.exp(tops[h] - top)
            weight = jnp.exp(scores - top)
            new_tops.append(top)
            new_sums.append(fade * sums[h] + jnp.sum(weight, axis=-1, keepdims=True))
            v_head = jnp.where(plain[h], v, jnp.zeros_like(v))
            part = jnp.dot(weight.astype(BF), v_head, preferred_element_type=F32)
            extra = part if extra is None else extra + part
            decay = fade * jnp.ones((1, width), F32) if h == 0 else jnp.where(plain[h], fade, decay)
        return tuple(new_tops), tuple(new_sums), acc * decay + extra

    start = (
        tuple(jnp.full((rows, 1), -1e30, F32) for _ in range(heads)),
        tuple(jnp.zeros((rows, 1), F32) for _ in range(heads)),
        jnp.zeros((rows, width), F32),
    )
    tops, sums, acc = lax.fori_loop(bounds[i, 0], bounds[i, 1], step, start)
    lane = lax.broadcasted_iota(jnp.int32, (1, lse_ref.shape[1]), 1)
    share = jnp.ones((rows, width), F32)
    logs = jnp.zeros((rows, lse_ref.shape[1]), F32)
    for h in range(heads):
        share = jnp.where(plain[h], 1.0 / sums[h], share)
        logs = jnp.where(lane == h, tops[h] + jnp.log(sums[h]), logs)
    full = acc * share
    full_ref[...] = full
    o_ref[...] = full.astype(BF)
    lse_ref[...] = logs


def attend(qkv, seg_rows, seg_blocks, bounds, block):
    shards, _, rows, width = qkv.shape
    total = shards * rows
    per = rows // block
    grid_spec = pltpu.PrefetchScalarGridSpec(
        num_scalar_prefetch=1,
        grid=(total // block,),
        in_specs=[
            pl.BlockSpec((None, None, block, width), lambda i, b: (i // per, 0, i % per, 0)),
            pl.BlockSpec((shards, None, rows, width), lambda i, b: (0, 1, 0, 0)),
            pl.BlockSpec((shards, None, rows, width), lambda i, b: (0, 2, 0, 0)),
            pl.BlockSpec((block, 1), lambda i, b: (i, 0)),
            pl.BlockSpec((shards, 1, rows), lambda i, b: (0, 0, 0)),
        ],
        out_specs=[
            pl.BlockSpec((block, width), lambda i, b: (i, 0)),
            pl.BlockSpec((block, width), lambda i, b: (i, 0)),
            pl.BlockSpec((block, 128), lambda i, b: (i, 0)),
        ],
    )
    return pl.pallas_call(
        attend_kernel,
        out_shape=[
            jax.ShapeDtypeStruct((total, width), BF),
            jax.ShapeDtypeStruct((total, width), F32),
            jax.ShapeDtypeStruct((total, 128), F32),
        ],
        grid_spec=grid_spec,
        compiler_params=pltpu.CompilerParams(vmem_limit_bytes=48 << 20),
        cost_estimate=pl.CostEstimate(
            flops=8 * total * total * width, bytes_accessed=8 << 20, transcendentals=0
        ),
    )(bounds, qkv, qkv, qkv, seg_rows, seg_blocks)


def unrotate(values, cos, sin):
    half = values.shape[1] // 2
    even, odd = values[:, :half], values[:, half:]
    return jnp.concatenate([even * cos + odd * sin, odd * cos - even * sin], axis=1)


def attend_back_kernel(
    bounds, q_ref, k_ref, v_ref, full_ref, lse_ref, do_ref, sq_ref, sk_ref, cos_ref, sin_ref,
    out_ref, dk_ref, dv_ref,
):
    i = pl.program_id(0)
    q, do = q_ref[...], do_ref[...]
    rows, width = q.shape
    shards, _, shard_rows, _ = out_ref.shape
    per = shard_rows // rows
    heads, paired, plain = head_masks(width)
    scale = HEAD_DIM**-0.5

    @pl.when(i == 0)
    def _():
        dk_ref[...] = jnp.zeros_like(dk_ref)
        dv_ref[...] = jnp.zeros_like(dv_ref)

    zero = jnp.zeros_like(q)
    q_heads = [jnp.where(paired[h], q, zero) for h in range(heads)]
    do_heads = [jnp.where(plain[h], do, zero) for h in range(heads)]
    product = do.astype(F32) * full_ref[...]
    deltas = [jnp.sum(jnp.where(plain[h], product, 0.0), axis=-1, keepdims=True) for h in range(heads)]
    logs = [lse_ref[:, h : h + 1] for h in range(heads)]
    sq = sq_ref[...]

    def step(kb, dq):
        k, v = k_ref[kb], v_ref[kb]
        same = sq == sk_ref[kb]
        dk, dv = dk_ref[kb], dv_ref[kb]
        for h in range(heads):
            scores = lax.dot_general(q_heads[h], k, NT, preferred_element_type=F32) * scale
            weight = jnp.where(same, jnp.exp(scores - logs[h]), 0.0)
            dp = lax.dot_general(do_heads[h], v, NT, preferred_element_type=F32)
            ds = (weight * (dp - deltas[h]) * scale).astype(BF)
            dv = dv + lax.dot_general(weight.astype(BF), do_heads[h], TN, preferred_element_type=F32)
            dk = dk + lax.dot_general(ds, q_heads[h], TN, preferred_element_type=F32)
            k_head = jnp.where(paired[h], k, jnp.zeros_like(k))
            dq = dq + jnp.dot(ds, k_head, preferred_element_type=F32)
        dk_ref[kb] = dk
        dv_ref[kb] = dv
        return dq

    dq = lax.fori_loop(bounds[i, 0], bounds[i, 1], step, jnp.zeros((rows, width), F32))
    here = pl.ds(pl.multiple_of(i * rows, rows), rows)
    inside = pl.ds(pl.multiple_of((i % per) * rows, rows), rows)
    out_ref[i // per, 0, inside, :] = unrotate(dq, cos_ref[here, :], sin_ref[here, :]).astype(BF)

    @pl.when(i == pl.num_programs(0) - 1)
    def _():
        for s in range(shards):
            own = slice(s * shard_rows, (s + 1) * shard_rows)
            out_ref[s, 1] = unrotate(dk_ref[s], cos_ref[own, :], sin_ref[own, :]).astype(BF)
            out_ref[s, 2] = dv_ref[s].astype(BF)


def attend_back(qkv, full, logs, grads, seg_rows, seg_blocks, cos, sin, bounds, block):
    shards, _, rows, width = qkv.shape
    total = shards * rows
    per = rows // block
    grid_spec = pltpu.PrefetchScalarGridSpec(
        num_scalar_prefetch=1,
        grid=(total // block,),
        in_specs=[
            pl.BlockSpec((None, None, block, width), lambda i, b: (i // per, 0, i % per, 0)),
            pl.BlockSpec((shards, None, rows, width), lambda i, b: (0, 1, 0, 0)),
            pl.BlockSpec((shards, None, rows, width), lambda i, b: (0, 2, 0, 0)),
            pl.BlockSpec((block, width), lambda i, b: (i, 0)),
            pl.BlockSpec((block, 128), lambda i, b: (i, 0)),
            pl.BlockSpec((block, width), lambda i, b: (i, 0)),
            pl.BlockSpec((block, 1), lambda i, b: (i, 0)),
            pl.BlockSpec((shards, 1, rows), lambda i, b: (0, 0, 0)),
            pl.BlockSpec((total, width // 2), lambda i, b: (0, 0)),
            pl.BlockSpec((total, width // 2), lambda i, b: (0, 0)),
        ],
        out_specs=pl.BlockSpec((shards, 3, rows, width), lambda i, b: (0, 0, 0, 0)),
        scratch_shapes=[
            pltpu.VMEM((shards, rows, width), F32),
            pltpu.VMEM((shards, rows, width), F32),
        ],
    )
    return pl.pallas_call(
        attend_back_kernel,
        out_shape=jax.ShapeDtypeStruct((shards, 3, rows, width), BF),
        grid_spec=grid_spec,
        compiler_params=pltpu.CompilerParams(vmem_limit_bytes=48 << 20),
        cost_estimate=pl.CostEstimate(
            flops=20 * total * total * width, bytes_accessed=16 << 20, transcendentals=0
        ),
    )(bounds, qkv, qkv, qkv, full, logs, grads, seg_rows, seg_blocks, cos, sin)


def exchange(values, axis):
    return lax.all_to_all(values, axis, 0, 0)


def local(
    mel_pair, text_ids, clip_lengths, t_index,
    txt_table, txt_conv, txt_vec, txt_gain, txt_up, txt_hid, txt_down,
    emb_mel, emb_text, emb_bias, pos_conv, pos_bias,
    time_w1, time_bias, time_w2, ada_w, ada_b,
    qkv_w, qkv_b, out_w, out_b, ff_w1, ff_b1, ff_w2, ff_b2, out_grad,
):
    total = mel_pair.shape[0]
    width = emb_mel.shape[1]
    shards, groups = lax.axis_size("mp"), lax.axis_size("dp")
    rank, place = lax.axis_index("mp"), lax.axis_index("dp")
    rows = total // shards
    cols = width // shards
    clips = clip_lengths.shape[1]
    first = rank * rows
    taps = pos_conv.shape[1]
    group = pos_conv.shape[2]

    def spread_slice(weight, axis):
        piece = weight.shape[axis] // groups
        return lax.dynamic_slice_in_dim(weight, place * piece, piece, axis)

    def gather(piece, axis):
        return lax.all_gather(lax.all_gather(piece, "mp"), "dp", axis=axis, tiled=True)

    qkv_piece = spread_slice(qkv_w, 1)
    qkv_piece = jnp.concatenate([pair_split(qkv_piece[:2]), qkv_piece[2:]], axis=0)
    qkv_full = gather(qkv_piece, 2)
    out_full = gather(spread_slice(out_w, 0), 1).reshape(width, width)
    w1_full = lax.all_gather(
        lax.all_gather(spread_slice(ff_w1, 0), "mp", axis=1, tiled=True), "dp", axis=0, tiled=True
    )
    w2_full = gather(spread_slice(ff_w2, 0), 1).reshape(-1, width)
    small = jnp.concatenate([pair_split(qkv_b[:2]), qkv_b[2:]], axis=0)
    qkv_bias = lax.all_gather(small, "mp")
    b1_full = lax.all_gather(ff_b1, "mp", tiled=True)
    all_steps = lax.all_gather(t_index, "dp", tiled=True).reshape(-1)

    lengths = clip_lengths[0]
    clip_index = jnp.arange(clips, dtype=jnp.int32)
    ends = jnp.sum(jnp.where(clip_index[:, None] >= clip_index[None, :], lengths[None, :], 0), axis=1)
    starts = ends - lengths
    frames = jnp.arange(total, dtype=jnp.int32)
    member = (frames[:, None] >= starts[None, :]) & (frames[:, None] < ends[None, :])
    segment = jnp.sum(member * clip_index[None, :], axis=1).astype(jnp.int32)
    position = frames - jnp.sum(member * starts[None, :], axis=1)
    ext = rows + 2 * HALO
    ids = lax.dynamic_slice_in_dim(jnp.pad(text_ids, (HALO, HALO)), first, ext)
    seg_ext = lax.dynamic_slice_in_dim(jnp.pad(segment, (HALO, HALO), constant_values=-1), first, ext)
    hot_ext = (seg_ext[:, None] == clip_index[None, :]).astype(F32)
    ext_index = jnp.arange(ext, dtype=jnp.int32)
    inside = (ext_index >= HALO) & (ext_index < HALO + rows)
    own_ext = jnp.where(inside[:, None], hot_ext, 0.0)
    hot = hot_ext[HALO : HALO + rows]

    def time_path(steps):
        half = time_w1.shape[0] // 2
        frequency = jnp.exp(jnp.arange(half, dtype=F32) * (-math.log(10000.0) / (half - 1)))
        angles = steps.astype(F32)[:, None] * frequency[None, :]
        sinusoid = jnp.concatenate([jnp.sin(angles), jnp.cos(angles)], axis=-1)
        pre_one = precise(sinusoid, time_w1) + time_bias[0]
        act_one = jax.nn.silu(pre_one)
        time_vec = precise(act_one, time_w2) + time_bias[1]
        return sinusoid, pre_one, act_one, time_vec, jax.nn.silu(time_vec)

    mod = precise(time_path(t_index[0])[4], ada_w) + ada_b

    hidden = jnp.take(txt_table, ids, axis=0).astype(F32)
    kept = []
    blocks = txt_conv.shape[0]
    for b in range(blocks):
        hidden, saved = text_ahead(
            hidden, seg_ext, hot_ext, own_ext, txt_conv[b], txt_vec[b], txt_gain[b],
            txt_up[b], txt_hid[b], txt_down[b], "mp",
        )
        kept.append(saved)
    text = hidden[HALO : HALO + rows].astype(BF)

    mel = lax.dynamic_slice_in_dim(mel_pair, first, rows)
    x0 = dot(mel, emb_mel) + dot(text, emb_text) + emb_bias

    def to_channels(values):
        blocks_of = values.reshape(rows, shards, cols).transpose(1, 0, 2)
        return exchange(blocks_of, "mp").reshape(total, cols)

    def to_rows(values):
        return exchange(values.reshape(shards, rows, cols), "mp").transpose(1, 0, 2).reshape(rows, width)

    spread_in = spread(to_channels(x0.astype(BF)).astype(F32), starts, ends)
    real = spread(jnp.ones((total, 1), F32), starts, ends)
    pre_a = apply_conv(spread_in, block_diagonal(pos_conv[0], False), taps) + pos_bias[0]
    y_a = jnp.pad(
        jnp.where(real[GAP:-GAP] > 0, mish(pre_a), 0.0).astype(BF).astype(F32), ((GAP, GAP), (0, 0))
    )
    pre_b = apply_conv(y_a, block_diagonal(pos_conv[1], False), taps) + pos_bias[1]
    c_pos = to_rows(gather_back(mish(pre_b).astype(BF), starts, ends))
    x1 = x0 + c_pos.astype(F32)

    def modulate(state, mod_in, shift_part, scale_part):
        scale = expand(hot, mod_in[:, scale_part * width : (scale_part + 1) * width])
        shift = expand(hot, mod_in[:, shift_part * width : (shift_part + 1) * width])
        return layer_norm(state) * (1.0 + scale) + shift

    n1, n1_pull = jax.vjp(lambda s, m: modulate(s, m, 0, 1), x1, mod)
    n1 = n1.astype(BF)
    half = HEAD_DIM // 2
    inverse = jnp.exp(jnp.arange(0, HEAD_DIM, 2, dtype=F32) * (-math.log(10000.0) / HEAD_DIM))
    angles = position.astype(F32)[:, None] * jnp.tile(inverse, cols // HEAD_DIM)[None, :]
    cos, sin = jnp.cos(angles), jnp.sin(angles)
    cos_own = lax.dynamic_slice_in_dim(cos, first, rows)
    sin_own = lax.dynamic_slice_in_dim(sin, first, rows)
    projected = []
    for s in range(shards):
        for p in range(3):
            value = dot(n1, qkv_full[s, p]) + qkv_bias[s, p]
            if p < 2:
                even, odd = value[:, : cols // 2], value[:, cols // 2 :]
                value = jnp.concatenate(
                    [even * cos_own - odd * sin_own, odd * cos_own + even * sin_own], axis=1
                )
            projected.append(value.astype(BF))
    qkv = jnp.stack(projected).reshape(shards, 3, rows, cols)
    qkv = exchange(qkv, "mp")
    block = 256
    heads_of = segment[::block]
    tails_of = segment[block - 1 :: block]
    low_key = jnp.sum(jnp.where(heads_of[:, None] == clip_index, starts[None, :], 0), axis=1)
    high_key = jnp.sum(jnp.where(tails_of[:, None] == clip_index, ends[None, :], 0), axis=1)
    bounds = jnp.stack([low_key // rows, (high_key + rows - 1) // rows], axis=1).astype(jnp.int32)
    seg_rows = segment[:, None]
    seg_blocks = segment.reshape(shards, 1, rows)
    o, o_full, logs = attend(qkv, seg_rows, seg_blocks, bounds, block)
    o_rows = to_rows(o)

    def residual(state, mod_in, summed, bias, part):
        return state + expand(hot, mod_in[:, part * width : (part + 1) * width]) * (summed + bias)

    x2, att_pull = jax.vjp(
        lambda s, m, a, b: residual(s, m, a, b, 2), x1, mod, dot(o_rows, out_full), out_b
    )

    n2, n2_pull = jax.vjp(lambda s, m: modulate(s, m, 3, 4), x2, mod)
    n2 = n2.astype(BF)
    r, r_pull = jax.vjp(
        lambda v, b: jax.nn.gelu(v + b, approximate=True), dot(n2, w1_full), b1_full
    )
    r = r.astype(BF)
    out, ff_pull = jax.vjp(lambda s, m, a, b: residual(s, m, a, b, 5), x2, mod, dot(r, w2_full), ff_b2)
    result = lax.all_gather(out.astype(BF), "mp", tiled=True).astype(F32)

    grad = lax.dynamic_slice_in_dim(out_grad, first, rows).astype(F32)
    dx2, dmod_a, df, g_ff_b2 = ff_pull(grad)
    df = df.astype(BF)
    g_ff_w2 = dot(df, r, TN)
    dh, g_ff_b1 = r_pull(dot(df, w2_full, NT))
    g_ff_b1 = jnp.sum(dh.astype(BF).astype(F32), axis=0)
    dh = dh.astype(BF)
    g_ff_w1 = dot(n2, dh, TN)
    more, dmod_b = n2_pull(dot(dh, w1_full, NT))
    dx2 = dx2 + more

    def by_rank(matrix):
        return matrix.reshape(matrix.shape[0], shards, -1)

    def scatter(matrix):
        part = lax.psum_scatter(matrix.astype(BF), "dp", scatter_dimension=0, tiled=True)
        return lax.psum_scatter(part, "mp", scatter_dimension=1, tiled=True).astype(F32)

    ff_pair = jnp.concatenate([by_rank(g_ff_w1), by_rank(g_ff_w2)], axis=2)
    ff_pair = scatter(ff_pair.reshape(width, -1))
    ff_cols = ff_w1.shape[1]
    o_ff_w1, o_ff_w2 = ff_pair[:, :ff_cols], ff_pair[:, ff_cols:].T

    dx1, dmod_c, da, g_out_b = att_pull(dx2)
    da = da.astype(BF)
    g_out_w = dot(da, o_rows, TN)
    do = to_channels(dot(da, out_full, NT).astype(BF))
    dqkv = attend_back(qkv, o_full, logs, do, seg_rows, seg_blocks, cos, sin, bounds, block)
    dqkv = exchange(dqkv, "mp").transpose(2, 0, 1, 3).reshape(rows, 3 * width)
    g_qkv_w = dot(n1, dqkv, TN)
    g_qkv_b = jnp.sum(dqkv.astype(F32), axis=0).reshape(shards, 3, cols)
    w_all = qkv_full.transpose(2, 0, 1, 3).reshape(width, 3 * width)
    more, dmod_d = n1_pull(dot(dqkv, w_all, NT))
    dx1 = dx1 + more
    at_pair = jnp.concatenate([by_rank(g_qkv_w), by_rank(g_out_w)], axis=2)
    at_pair = scatter(at_pair.reshape(width, -1))
    g_qkv = at_pair[:, : 3 * cols].reshape(-1, 3, cols).transpose(1, 0, 2)
    o_qkv_w = jnp.concatenate([pair_merge(g_qkv[:2]), g_qkv[2:]], axis=0)
    o_out_w = at_pair[:, 3 * cols :].T

    dmod = dmod_a + dmod_b + dmod_c + dmod_d
    dmod_all = jnp.sum(
        lax.all_gather(lax.all_gather(dmod, "mp"), "dp"), axis=1
    ).reshape(groups * clips, -1)

    slope_b = gather_back(mish_slope(pre_b), starts, ends)
    dy_b = to_channels(dx1.astype(BF)).astype(F32) * slope_b
    g_pos_b = jnp.sum(dy_b, axis=0)
    dy_b = spread(dy_b.astype(BF).astype(F32), starts, ends)
    dy_a = apply_conv(dy_b, block_diagonal(pos_conv[1], True), taps) * mish_slope(pre_a)
    dy_a = jnp.where(real[GAP:-GAP] > 0, dy_a, 0.0)
    g_pos_a = jnp.sum(dy_a, axis=0)
    dy_a = jnp.pad(dy_a.astype(BF).astype(F32), ((GAP, GAP), (0, 0)))
    dc = gather_back(
        apply_conv(dy_a, block_diagonal(pos_conv[0], True), taps).astype(BF), starts, ends
    )
    dx0_full = dx1 + to_rows(dc).astype(F32)
    g_conv = jnp.concatenate(
        [conv_grad(spread_in, dy_a[GAP:-GAP], taps, group), conv_grad(y_a, dy_b[GAP:-GAP], taps, group)],
        axis=1,
    )
    g_conv = lax.psum_scatter(g_conv.astype(BF), "dp", scatter_dimension=0, tiled=True)
    o_pos_conv = g_conv.astype(F32).T.reshape(2, taps, group, -1)

    g_emb_bias = jnp.sum(dx0_full, axis=0)
    dx0 = dx0_full.astype(BF)
    mel_grad = lax.all_gather(dot(dx0, emb_mel, NT).astype(BF), "mp", tiled=True).astype(F32)
    g_emb = jnp.concatenate([dot(dx0, text, TN), dot(dx0, mel, TN)], axis=1)
    g_emb = lax.psum_scatter(g_emb.astype(BF), "dp", scatter_dimension=0, tiled=True)
    g_emb = lax.psum(g_emb, "mp").astype(F32)
    text_width = text.shape[1]
    o_emb_text, o_emb_mel = g_emb[:, :text_width].T, g_emb[:, text_width:].T

    dtext = jnp.pad(dot(dx0, emb_text, NT), ((HALO, HALO), (0, 0)))
    text_grads = [None] * blocks
    for b in reversed(range(blocks)):
        dtext, text_grads[b] = text_behind(kept[b], dtext, txt_up[b], txt_down[b], "mp")
    vocab = txt_table.shape[0]
    chosen = (ids[:, None] == jnp.arange(vocab, dtype=jnp.int32)[None, :]).astype(BF)
    g_table = dot(dtext, chosen, TN)

    def scatter_rows(matrix):
        part = lax.psum_scatter(matrix.astype(BF), "dp", scatter_dimension=0, tiled=True)
        return lax.psum_scatter(part, "mp", scatter_dimension=0, tiled=True).astype(F32)

    ups = scatter_rows(jnp.concatenate([text_grads[b][3] for b in range(blocks)], axis=1))
    downs = scatter_rows(
        jnp.concatenate([text_grads[b][5] for b in range(blocks)] + [g_table], axis=1)
    )
    hidden_width = txt_up.shape[2]
    o_up = ups.T.reshape(blocks, text_width, -1)
    o_down = downs[:, : blocks * hidden_width].T.reshape(blocks, hidden_width, -1)
    o_table = downs[:, blocks * hidden_width :].T

    def placed(values):
        full = jnp.zeros((shards,) + values.shape, F32)
        return lax.dynamic_update_slice_in_dim(full, values[None], rank, 0)

    g_pos_bias = placed(jnp.stack([g_pos_a, g_pos_b])).transpose(1, 0, 2).reshape(2, width)
    g_qkv_b = jnp.concatenate([pair_merge(g_qkv_b[:, :2]), g_qkv_b[:, 2:]], axis=1)
    g_qkv_b = g_qkv_b.transpose(1, 0, 2).reshape(3, width)
    small = [
        jnp.stack([g[0] for g in text_grads]), jnp.stack([g[1] for g in text_grads]),
        jnp.stack([g[2] for g in text_grads]), jnp.stack([g[4] for g in text_grads]),
        g_emb_bias, g_pos_bias, g_qkv_b, g_out_b, g_ff_b1, g_ff_b2,
    ]
    packed = lax.psum(jnp.concatenate([s.reshape(-1) for s in small]), ("dp", "mp"))
    unpacked, at = [], 0
    for s in small:
        unpacked.append(packed[at : at + s.size].reshape(s.shape))
        at += s.size
    both, crossed = place * shards + rank, rank * groups + place
    everyone = groups * shards

    def own(values, index, parts):
        piece = values.shape[-1] // parts
        return lax.dynamic_slice_in_dim(values, index * piece, piece, values.ndim - 1)

    sinusoid, pre_one, act_one, time_vec, act_two = time_path(all_steps)
    de = precise(dmod_all, ada_w, NT) * silu_slope(time_vec)
    dpre = precise(de, time_w2, NT) * silu_slope(pre_one)

    def outer(left, right):
        return lax.dot_general(left, own(right, place, groups), TN, precision=highest)

    return (
        result,
        mel_grad,
        o_table,
        own(unpacked[0], both, everyone),
        own(unpacked[1], both, everyone),
        own(unpacked[2], both, everyone),
        o_up,
        own(unpacked[3], both, everyone),
        o_down,
        o_emb_mel,
        o_emb_text,
        own(unpacked[4], place, groups),
        o_pos_conv,
        own(unpacked[5], crossed, everyone),
        outer(sinusoid, dpre),
        own(jnp.stack([jnp.sum(dpre, axis=0), jnp.sum(de, axis=0)]), place, groups),
        outer(act_one, de),
        outer(act_two, dmod_all),
        own(jnp.sum(dmod_all, axis=0), place, groups),
        o_qkv_w,
        own(unpacked[6], crossed, everyone),
        o_out_w,
        own(unpacked[7], place, groups),
        o_ff_w1,
        own(unpacked[8], crossed, everyone),
        o_ff_w2,
        own(unpacked[9], place, groups),
    )


def solution(mesh):
    both, crossed = ("dp", "mp"), ("mp", "dp")
    placed = (
        P("dp", None), P("dp"), P("dp", None), P("dp", None),
        P(), P(), P(), P(), P(), P(), P(), P(), P(), P(),
        P(None, None, None, "mp"), P(None, "mp"),
        P(), P(), P(), P(), P(),
        P(None, None, "mp"), P(None, "mp"), P("mp", None), P(),
        P(None, "mp"), P("mp"), P("mp", None), P(),
        P("dp", None),
    )
    given = (
        P("dp", None), P("dp", None),
        P(None, both), P(None, None, both), P(None, None, both), P(None, both),
        P(None, None, both), P(None, None, both), P(None, None, both),
        P(None, "dp"), P(None, "dp"), P("dp"),
        P(None, None, None, crossed), P(None, crossed),
        P(None, "dp"), P(None, "dp"), P(None, "dp"), P(None, "dp"), P("dp"),
        P(None, "dp", "mp"), P(None, crossed), P("mp", "dp"), P("dp"),
        P("dp", "mp"), P(crossed), P("mp", "dp"), P("dp"),
    )
    return jax.shard_map(local, mesh=mesh, in_specs=placed, out_specs=given, check_vma=False)
```

time: 3520 us -> 1540 us (0.44)
  waiting for transfers between devices: 1620 us -> 353 us
  matrix products: 702 us -> 180 us
  other arithmetic: 646 us -> 142 us
  blocking collectives: 25.7 us -> 407 us
  local copies, waits for them, and re-layouts: 490 us -> 237 us
  Pallas kernels: 0 us -> 150 us
    unnamed x40 -> x25, waiting for transfers between devices: 894 us -> 181 us
    psum x3 -> x2, waiting for transfers between devices: 565 us -> 28.2 us  [the longest x1 28.2 us: local(): g_emb = lax.psum(g_emb, 'mp').astype(F32)]
    dot_general x92 -> x64, matrix products: 612 us -> 180 us  [the longest x42 124 us: dot(): lax.dot_general(left.astype(BF), right.astype(BF), dims, preferred_elemen...]
    all_gather x0 -> x9, blocking collectives: none -> 242 us  [the longest x3 104 us: gather(): lax.all_gather(piece, 'mp')]
    reduce_sum x24 -> x18, other arithmetic: 214 us -> 26.1 us  [the longest x2 5.44 us: conv_norm(): conv[tap] * jnp.where(keep[:, None], padded[tap:tap + rows], 0.0)]
    pallas_call x0 -> x8, Pallas kernels: none -> 150 us  [the longest x4 48.1 us: apply_conv(): pl.pallas_call(partial(conv_kernel, taps), out_shape=jax.ShapeDtypeStruct...]
    convert_element_type x39 -> x19, other arithmetic: 156 us -> 23.9 us  [the longest x1 7.4 us: local(): result = lax.all_gather(out.astype(BF), 'mp', tiled=True).astype(F32)]
    select_n x20 -> x9, other arithmetic: 135 us -> 9.6 us  [the longest x5 7.98 us: spread(): part = jnp.where(keep[:, None], values, 0)]
  transfers between devices with their start and end apart: 24 -> 24, of which waited for: 13 -> 12; matrix products, arithmetic and copies ran while one was open for 17% -> 32% of each run, Pallas kernels for 0% -> 6%
where the time goes in v1:
time: 1540 us; the launch traced here: 1510 us
  blocking collectives  407 us (26%)
  waiting for transfers between devices  353 us (23%)
  local copies, waits for them, and re-layouts  237 us (15%)
  matrix products  180 us (12%)
  Pallas kernels  150 us (10%)
  other arithmetic  142 us (9%)
  starting transfers between devices  27.5 us (2%)
  between operations  18.7 us (1%)
    unnamed x25, waiting for transfers between devices  181 us
    dot_general x42, matrix products, dot(): lax.dot_general(left.astype(BF), right.astype(BF), dims, preferred_elemen...  124 us
    all_gather x3, blocking collectives, gather(): lax.all_gather(piece, 'mp')  104 us
    all_to_all x2, blocking collectives, exchange(): return lax.all_to_all(values, axis, 0, 0)  95.5 us
    unnamed x552, local copies, waits for them, and re-layouts  85 us
    mul x6, local copies, waits for them, and re-layouts, block_diagonal(): full = parts[:, None] * eye[None, :, None, :, None]  57.1 us
    pallas_call x4, Pallas kernels, apply_conv(): pl.pallas_call(partial(conv_kernel, taps), out_shape=jax.ShapeDtypeStruct...  48.1 us
    reduce_scatter x2, waiting for transfers between devices, scatter(): lax.psum_scatter(part, 'mp', scatter_dimension=1, tiled=True).astype(F32)  45.1 us
  transfers between devices with their start and end apart: 24, of which 12 were waited for; matrix products, arithmetic and copies ran while one was open for 32% of the time, Pallas kernels for 6%

profile of v1, /device:TPU:0, one launch (start us, length us, event | category | flops | bytes accessed | tf_op | source)
XLA Modules:
  0.0 1514.0 jit_solution(15219299576572654579)
XLA Ops:
  9.9 21.7 %all-gather = bf16[12,128,256]{2,1,0:T(8,128)(2,1)} all-gather(bf16[3,128,256]{2,1,0:T(8,128)(2,1)S(1)} %pad_maximum_fusion.8), channel_id=2, replica_groups=mesh['dp'=8,'mp'=4] {'mp'}, dimensions={0}, use_global_device_ids=true | all-gather | bytes 983040 | tf_op jit(solution)/shard_map/all_gather | solution.py:474
  32.5 14.8 all-gather.2
  66.8 17.9 %psum.42 = f32[4,1024]{1,0:T(4,128)S(1)} all-reduce(f32[4,1024]{1,0:T(4,128)S(1)} %fusion.37), channel_id=1, replica_groups=mesh['dp'=8,'mp'=4] {'mp'}, use_global_device_ids=true, to_apply=%region_4.5 | all-reduce | flops 4096 | bytes 32768 | tf_op jit(solution)/shard_map/psum | solution.py:110
  100.3 15.5 %psum.43 = f32[4,1024]{1,0:T(4,128)S(1)} all-reduce(f32[4,1024]{1,0:T(4,128)S(1)} %fusion.29), channel_id=1, replica_groups=mesh['dp'=8,'mp'=4] {'mp'}, use_global_device_ids=true, to_apply=%region_8.9 | all-reduce | flops 4096 | bytes 32768 | tf_op jit(solution)/shard_map/psum | solution.py:110
  130.3 25.8 %all_gather.71 = bf16[128,2048]{1,0:T(8,128)(2,1)} all-gather(bf16[128,512]{1,0:T(8,128)(2,1)S(1)} %constant_dynamic-slice_fusion.8), channel_id=1, replica_groups=mesh['dp'=8,'mp'=4] {'mp'}, dimensions={1}, use_global_device_ids=true | all-gather | bytes 655360 | tf_op jit(solution)/shard_map/all_gather | solution.py:481
  170.2 13.3 all-gather.6
  211.2 17.5 %broadcast_multiply_fusion = (bf16[31,4,64,4,64]{4,3,2,1,0:T(4,128)(2,1)}, bf16[31,4,64,4,64]{4,3,2,1,0:T(4,128)(2,1)}, bf16[31,4,64,4,64]{4,3,2,1,0:T(4,128)(2,1)}, bf16[31,4,64,4,64]{4,3,2,1,0:T(4,128)(2,1)}) fusion(bf16[31,64,4,64]{3,2,1,0:T(4,128)(2,1)} %copy.293, bf16[4,4]{1,0:T(4,128)(2,1)S(1)} %fusion.266, bf16[31,64,4,64]{3,2,1,0:T(4,128)(2,1)S(1)} %mul.1639, ...), kind=kLoop, calls=%fused_computation.21 | loop fusion | flops 8126464 | bytes 20316192 | tf_op jit(solution)/shard_map/mul | solution.py:244
  342.2 67.6 %all-gather.3 = bf16[256,1024]{1,0:T(8,128)(2,1)} all-gather(bf16[64,1024]{1,0:T(8,128)(2,1)S(1)} %constant_dynamic-slice_fusion.7), channel_id=5, replica_groups=mesh['dp'=8,'mp'=4] {'mp'}, dimensions={0}, use_global_device_ids=true | all-gather | bytes 655360 | tf_op jit(solution)/shard_map/all_gather | solution.py:474
  410.6 31.1 %shard_map.495 = (bf16[2048,256]{1,0:T(8,128)(2,1)S(1)}, f32[2048,256]{1,0:T(8,128)S(1)}, f32[2048,128]{1,0:T(8,128)S(1)}) custom-call(s32[8,2]{1,0:T(8,128)S(1)} %copy.286.bounds, bf16[4,3,512,256]{3,2,1,0:T(8,128)(2,1)} %all-to-all-done.2.q_ref.k_ref.v_ref, bf16[4,3,512,256]{3,2,1,0:T(8,128)(2,1)} %all-to-all-done.2.q_ref.k_ref.v_ref, ...), custom_call_target="tpu_custom_call" | custom-call | flops 8589934592 | bytes 8388608 | tf_op jit(solution)/shard_map/pallas_call | solution.py:335
  449.3 22.5 %all-gather.7 = f32[4,1,512]{2,1,0:T(1,128)S(1)} all-gather(f32[1,1,512]{2,1,0:T(1,128)S(1)} %bitcast.760), channel_id=1, replica_groups=mesh['dp'=8,'mp'=4] {'mp'}, dimensions={0}, use_global_device_ids=true | all-gather | bytes 10240 | tf_op jit(solution)/shard_map/all_gather | solution.py:486
  511.6 23.3 %all_to_all.40 = bf16[4,512,256]{2,1,0:T(8,128)(2,1)S(1)} all-to-all(bf16[4,512,256]{2,1,0:T(8,128)(2,1)S(1)} %bitcast.518), channel_id=1, replica_groups=mesh['dp'=8,'mp'=4] {'mp'}, dimensions={0} | all-to-all | bytes 2097152 | tf_op jit(solution)/shard_map/all_to_all | solution.py:448
  534.9 39.0 %shard_map.496 = bf16[4,3,512,256]{3,2,1,0:T(8,128)(2,1)} custom-call(s32[8,2]{1,0:T(8,128)S(1)} %copy.286.bounds, bf16[4,3,512,256]{3,2,1,0:T(8,128)(2,1)} %all-to-all-done.2.q_ref.k_ref.v_ref, bf16[4,3,512,256]{3,2,1,0:T(8,128)(2,1)} %all-to-all-done.2.q_ref.k_ref.v_ref, bf16[4,3,512,256]{3,2,1,0:T(8,128)(2,1)} %all-to-all-done.2.q_ref.k_ref.v_ref, ...), custom_call_target="tpu_custom_call" | custom-call | flops 21474836480 | bytes 16777216 | tf_op jit(solution)/shard_map/pallas_call | solution.py:436
  574.0 72.2 %all_to_all.41 = bf16[4,3,512,256]{3,2,1,0:T(8,128)(2,1)S(1)} all-to-all(bf16[4,3,512,256]{3,2,1,0:T(8,128)(2,1)} %shard_map.496), channel_id=1, replica_groups=mesh['dp'=8,'mp'=4] {'mp'}, dimensions={0} | all-to-all | bytes 6291456 | tf_op jit(solution)/shard_map/all_to_all | solution.py:448
  733.5 16.2 %all-to-all-done.7 = bf16[4,512,256]{2,1,0:T(8,128)(2,1)} async-done(((bf16[4,512,256]{2,1,0:T(8,128)(2,1)}), bf16[4,512,256]{2,1,0:T(8,128)(2,1)}, u32[]{:S(2)}, u32[]{:S(2)}) %all-to-all-start.7) | async-done | bytes 1048608 | tf_op jit(solution)/shard_map/all_to_all | solution.py:448
  759.7 17.5 %psum.44 = f32[4,1024]{1,0:T(4,128)S(1)} all-reduce(f32[4,1024]{1,0:T(4,128)S(1)} %fusion.206), channel_id=1, replica_groups=mesh['dp'=8,'mp'=4] {'mp'}, use_global_device_ids=true, to_apply=%region_22.23 | all-reduce | flops 4096 | bytes 32768 | tf_op jit(solution)/shard_map/psum | solution.py:125
  798.3 18.6 %psum.45 = f32[4,1024]{1,0:T(4,128)S(1)} all-reduce(f32[4,1024]{1,0:T(4,128)S(1)} %fusion.207), channel_id=1, replica_groups=mesh['dp'=8,'mp'=4] {'mp'}, use_global_device_ids=true, to_apply=%region_26.27 | all-reduce | flops 4096 | bytes 32768 | tf_op jit(solution)/shard_map/psum | solution.py:125
  894.9 13.8 copy.303
  921.1 15.7 %shard_map.500 = f32[256,1984]{1,0:T(8,128)S(1)} custom-call(f32[2144,256]{1,0:T(8,128)} %copy-done.5, f32[2112,256]{1,0:T(8,128)S(1)} %slice.1239.g_ref), custom_call_target="tpu_custom_call" | custom-call | flops 8581545984 | bytes 8388608 | tf_op jit(solution)/shard_map/pallas_call | solution.py:221
  937.0 15.7 %shard_map.499 = f32[256,1984]{1,0:T(8,128)S(1)} custom-call(f32[2144,256]{1,0:T(8,128)} %copy-done.4, f32[2112,256]{1,0:T(8,128)S(1)} %convert_element_type.559.g_ref), custom_call_target="tpu_custom_call" | custom-call | flops 8581545984 | bytes 8388608 | tf_op jit(solution)/shard_map/pallas_call | solution.py:221
  966.4 15.0 all-gather.9
  1040.8 42.5 %all-gather.8 = s32[8,1,4]{2,1,0:T(1,128)S(1)} all-gather(s32[1,1,4]{2,1,0:T(1,128)S(1)} %bitcast.778), channel_id=1, replica_groups=mesh['dp'=8,'mp'=4] {'dp'}, dimensions={0}, use_global_device_ids=true | all-gather | bytes 144 | tf_op jit(solution)/shard_map/all_gather | solution.py:487
  1093.1 18.3 %all_gather.78 = bf16[2048,200]{0,1:T(8,128)(2,1)S(1)} all-gather(bf16[512,200]{0,1:T(8,128)(2,1)S(1)} %convolution_convert_fusion.11), channel_id=1, replica_groups=mesh['dp'=8,'mp'=4] {'mp'}, dimensions={0}, use_global_device_ids=true | all-gather | bytes 1024000 | tf_op jit(solution)/shard_map/all_gather | solution.py:667
  1124.7 31.1 %reduce-scatter.43.cloned.1.call-done = bf16[128,4096]{1,0:T(8,128)(2,1)} async-done(((bf16[1024,4096]{1,0:T(8,128)(2,1)}), bf16[128,4096]{1,0:T(8,128)(2,1)}) %reduce-scatter.43.cloned.1.call-update) | async-done | bytes 1048592
  1158.1 41.9 %reduce-scatter.25.cloned.1.call-done = bf16[32,3968]{1,0:T(8,128)(2,1)} async-done(((bf16[256,3968]{1,0:T(8,128)(2,1)}), bf16[32,3968]{1,0:T(8,128)(2,1)}) %reduce-scatter.25.cloned.1.call-update) | async-done | bytes 253968 | tf_op jit(solution)/shard_map/reduce_scatter | solution.py:662
  1204.9 29.3 %all-gather.27.cloned.1.call-done = f32[32,4,6144]{2,1,0:T(4,128)} async-done(((f32[4,4,6144]{2,1,0:T(4,128)}), f32[32,4,6144]{2,1,0:T(4,128)}) %all-gather.27.cloned.1.call-update) | async-done | bytes 3145744 | tf_op jit(solution)/shard_map/all_gather | solution.py:643
  1240.2 51.2 %reduce-scatter.31.cloned.1.call-done = bf16[64,4594]{1,0:T(8,128)(2,1)} async-done(((bf16[512,4594]{1,0:T(8,128)(2,1)}), bf16[64,4594]{1,0:T(8,128)(2,1)}) %reduce-scatter.31.cloned.1.call-update) | async-done | bytes 588048
  1308.2 58.5 %reduce-scatter.41.cloned.1.call-done = bf16[128,4096]{1,0:T(8,128)(2,1)} async-done(((bf16[1024,4096]{1,0:T(8,128)(2,1)}), bf16[128,4096]{1,0:T(8,128)(2,1)}) %reduce-scatter.41.cloned.1.call-update) | async-done | bytes 1048592
  1375.7 28.2 %all-reduce.63.cloned.1.call-done = bf16[128,712]{0,1:T(8,128)(2,1)} async-done(((bf16[128,712]{0,1:T(8,128)(2,1)}), bf16[128,712]{0,1:T(8,128)(2,1)}) %all-reduce.63.cloned.1.call-update) | async-done | bytes 182288 | tf_op jit(solution)/shard_map/psum | solution.py:670
  1406.2 19.5 %reduce-scatter.37.cloned.1.call-done = bf16[32,1024]{1,0:T(8,128)(2,1)} async-done(((bf16[128,1024]{1,0:T(8,128)(2,1)}), bf16[32,1024]{1,0:T(8,128)(2,1)}) %reduce-scatter.37.cloned.1.call-update) | async-done | bytes 65552
  1427.6 25.8 %reduce-scatter.29.cloned.1.call-done = bf16[128,1024]{0,1:T(8,128)(2,1)} async-done(((bf16[128,4096]{0,1:T(8,128)(2,1)}), bf16[128,1024]{0,1:T(8,128)(2,1)}) %reduce-scatter.29.cloned.1.call-update) | async-done | bytes 262160 | tf_op jit(solution)/shard_map/reduce_scatter | solution.py:617
  1456.9 19.4 %reduce-scatter.33.cloned.1.call-done = bf16[16,4594]{1,0:T(8,128)(2,1)} async-done(((bf16[64,4594]{1,0:T(8,128)(2,1)}), bf16[16,4594]{1,0:T(8,128)(2,1)}) %reduce-scatter.33.cloned.1.call-update) | async-done | bytes 147024
  1484.7 19.3 %reduce-scatter.27.cloned.1.call-done = bf16[128,1024]{0,1:T(8,128)(2,1)} async-done(((bf16[128,4096]{0,1:T(8,128)(2,1)}), bf16[128,1024]{0,1:T(8,128)(2,1)}) %reduce-scatter.27.cloned.1.call-update) | async-done | bytes 262160 | tf_op jit(solution)/shard_map/reduce_scatter | solution.py:617
  (941 shorter events, 615.7 us)
Async XLA Ops:
  7.2 317.3 %all-gather.17.cloned.1.call-start = ((), (), s32[]{:S(2)}) async-start(), calls=%async_computation.18 | async-start | bytes 7077888 | tf_op jit(solution)/shard_map/all_gather | solution.py:474
  31.6 440.2 %all-gather.19.cloned.1.call-start = ((), (), s32[]{:S(2)}) async-start(), calls=%async_computation.19 | async-start | bytes 2359296 | tf_op jit(solution)/shard_map/all_gather | solution.py:474
  125.6 134.3 %all-to-all-start = ((bf16[4,512,256]{2,1,0:T(8,128)(2,1)}), bf16[4,512,256]{2,1,0:T(8,128)(2,1)S(1)}, u32[]{:S(2)}, u32[]{:S(2)}) async-start(bf16[4,512,256]{2,1,0:T(8,128)(2,1)} %bitcast.505), calls=%async_computation | async-start | bytes 2097152 | tf_op jit(solution)/shard_map/all_to_all | solution.py:448
  129.3 349.7 %all-gather.21.cloned.1.call-start = ((), (), s32[]{:S(2)}) async-start(), calls=%async_computation.20 | async-start | bytes 4718592 | tf_op jit(solution)/shard_map/all_gather | solution.py:480
  295.2 19.6 %all-to-all-start.1 = ((bf16[4,512,256]{2,1,0:T(8,128)(2,1)}), bf16[4,512,256]{2,1,0:T(8,128)(2,1)S(1)}, u32[]{:S(2)}, u32[]{:S(2)}) async-start(bf16[4,512,256]{2,1,0:T(8,128)(2,1)} %bitcast.56), calls=%async_computation.1 | async-start | bytes 2097152 | tf_op jit(solution)/shard_map/all_to_all | solution.py:448
  299.2 206.4 %copy-start.168 = (f32[1,1024]{1,0:T(1,128)}, f32[1,1024]{1,0:T(1,128)S(1)}, u32[]{:S(2)}) copy-start(f32[1,1024]{1,0:T(1,128)S(1)} %get-tuple-element.388) | copy-start | bytes 12292
  299.2 206.4 %copy-start.170 = (f32[1,1024]{1,0:T(1,128)}, f32[1,1024]{1,0:T(1,128)S(1)}, u32[]{:S(2)}) copy-start(f32[1,1024]{1,0:T(1,128)S(1)} %get-tuple-element.389) | copy-start | bytes 12292
  299.2 208.3 %copy-start.199 = (f32[1,1024]{1,0:T(1,128)}, f32[1,1024]{1,0:T(1,128)S(1)}, u32[]{:S(2)}) copy-start(f32[1,1024]{1,0:T(1,128)S(1)} %get-tuple-element.383) | copy-start | bytes 12292
  299.2 208.3 %copy-start.201 = (f32[1,1024]{1,0:T(1,128)}, f32[1,1024]{1,0:T(1,128)S(1)}, u32[]{:S(2)}) copy-start(f32[1,1024]{1,0:T(1,128)S(1)} %get-tuple-element.392) | copy-start | bytes 12292
  299.3 208.3 %copy-start.203 = (f32[1,1024]{1,0:T(1,128)}, f32[1,1024]{1,0:T(1,128)S(1)}, u32[]{:S(2)}) copy-start(f32[1,1024]{1,0:T(1,128)S(1)} %get-tuple-element.393) | copy-start | bytes 12292
  299.3 208.3 %copy-start.205 = (f32[1,1024]{1,0:T(1,128)}, f32[1,1024]{1,0:T(1,128)S(1)}, u32[]{:S(2)}) copy-start(f32[1,1024]{1,0:T(1,128)S(1)} %get-tuple-element.394) | copy-start | bytes 12292
  316.9 337.1 %copy-start.89 = (f32[512]{0:T(512)}, f32[512]{0:T(512)S(1)}, u32[]{:S(2)}) copy-start(f32[512]{0:T(512)S(1)} %broadcast_multiply_fusion.7) | copy-start | bytes 6148
  317.3 336.7 %copy-start.129 = (f32[512]{0:T(512)}, f32[512]{0:T(512)S(1)}, u32[]{:S(2)}) copy-start(f32[512]{0:T(512)S(1)} %fusion.269) | copy-start | bytes 6148
  336.6 74.1 %all-to-all-start.2 = ((bf16[4,3,512,256]{3,2,1,0:T(8,128)(2,1)}), bf16[4,3,512,256]{3,2,1,0:T(8,128)(2,1)}, u32[]{:S(2)}, u32[]{:S(2)}) async-start(bf16[4,3,512,256]{3,2,1,0:T(8,128)(2,1)} %bitcast.521), calls=%async_computation.2 | async-start | bytes 6291456 | tf_op jit(solution)/shard_map/all_to_all | solution.py:448
  341.2 146.2 %all-gather.23.cloned.1.call-start = ((), (), s32[]{:S(2)}) async-start(), calls=%async_computation.21 | async-start | bytes 4718592 | tf_op jit(solution)/shard_map/all_gather | solution.py:474
  445.0 26.8 %all-to-all-start.3 = ((bf16[4,512,256]{2,1,0:T(8,128)(2,1)}), bf16[4,512,256]{2,1,0:T(8,128)(2,1)}, u32[]{:S(2)}, u32[]{:S(2)}) async-start(bf16[4,512,256]{2,1,0:T(8,128)(2,1)} %bitcast.506), calls=%async_computation.3 | async-start | bytes 2097152 | tf_op jit(solution)/shard_map/all_to_all | solution.py:448
  658.6 28.8 %all-to-all-start.6 = ((bf16[4,512,256]{2,1,0:T(8,128)(2,1)}), bf16[4,512,256]{2,1,0:T(8,128)(2,1)S(1)}, u32[]{:S(2)}, u32[]{:S(2)}) async-start(bf16[4,512,256]{2,1,0:T(8,128)(2,1)} %bitcast.501), calls=%async_computation.6 | async-start | bytes 2097152 | tf_op jit(solution)/shard_map/all_to_all | solution.py:448
  721.0 28.7 %all-to-all-start.7 = ((bf16[4,512,256]{2,1,0:T(8,128)(2,1)}), bf16[4,512,256]{2,1,0:T(8,128)(2,1)}, u32[]{:S(2)}, u32[]{:S(2)}) async-start(bf16[4,512,256]{2,1,0:T(8,128)(2,1)} %bitcast.516), calls=%async_computation.7 | async-start | bytes 2097152 | tf_op jit(solution)/shard_map/all_to_all | solution.py:448
  726.1 359.1 %all-gather.25.cloned.1.call-start = ((), (), s32[]{:S(2)}) async-start(), calls=%async_computation.22 | async-start | bytes 5242880 | tf_op jit(solution)/shard_map/all_gather | solution.py:599
  726.7 386.1 %all-reduce.61.cloned.1.call-start = ((), (), s32[]{:S(2)}) async-start(), calls=%async_computation.23 | async-start | bytes 221184 | tf_op jit(solution)/shard_map/psum | solution.py:707
  839.7 277.7 %reduce-scatter.39.cloned.1.call-start = ((), (), s32[]{:S(2)}) async-start(), calls=%async_computation.33 | async-start | bytes 1769472
  845.0 275.7 %reduce-scatter.35.cloned.1.call-start = ((), (), s32[]{:S(2)}) async-start(), calls=%async_computation.31 | async-start | bytes 2359296
  854.6 301.1 %reduce-scatter.43.cloned.1.call-start = ((), (), s32[]{:S(2)}) async-start(), calls=%async_computation.35 | async-start | bytes 9437184
  920.5 279.5 %reduce-scatter.25.cloned.1.call-start = ((), (), s32[]{:S(2)}) async-start(), calls=%async_computation.25 | async-start | bytes 2285568 | tf_op jit(solution)/shard_map/reduce_scatter | solution.py:662
  954.6 279.6 %all-gather.27.cloned.1.call-start = ((), (), s32[]{:S(2)}) async-start(), calls=%async_computation.28 | async-start | bytes 3538944 | tf_op jit(solution)/shard_map/all_gather | solution.py:643
  981.4 310.0 %reduce-scatter.31.cloned.1.call-start = ((), (), s32[]{:S(2)}) async-start(), calls=%async_computation.29 | async-start | bytes 5308416
  1003.2 363.4 %reduce-scatter.41.cloned.1.call-start = ((), (), s32[]{:S(2)}) async-start(), calls=%async_computation.34 | async-start | bytes 9437184
  1040.2 363.7 %all-reduce.63.cloned.1.call-start = ((), (), s32[]{:S(2)}) async-start(), calls=%async_computation.24 | async-start | bytes 364544 | tf_op jit(solution)/shard_map/psum | solution.py:670
  1119.2 306.5 %reduce-scatter.37.cloned.1.call-start = ((), (), s32[]{:S(2)}) async-start(), calls=%async_computation.32 | async-start | bytes 327680
  1120.8 332.6 %reduce-scatter.29.cloned.1.call-start = ((), (), s32[]{:S(2)}) async-start(), calls=%async_computation.27 | async-start | bytes 1310720 | tf_op jit(solution)/shard_map/reduce_scatter | solution.py:617
  1158.1 318.2 %reduce-scatter.33.cloned.1.call-start = ((), (), s32[]{:S(2)}) async-start(), calls=%async_computation.30 | async-start | bytes 737280
  1291.5 212.6 %reduce-scatter.27.cloned.1.call-start = ((), (), s32[]{:S(2)}) async-start(), calls=%async_computation.26 | async-start | bytes 1310720 | tf_op jit(solution)/shard_map/reduce_scatter | solution.py:617
  (253 other events, 4269.0 us)
Sparse Core Ops, SparseCore 0:
  31.7 45.1 all-gather.16
  78.9 27.8 all-gather.18
  156.2 36.3 all-gather.20
  409.9 37.0 all-gather.22
  728.2 101.7 all-gather.24
  839.9 153.4 all-reduce.60
  996.7 39.3 reduce-scatter.38
  1039.3 41.2 reduce-scatter.34
  1084.5 71.2 reduce-scatter.42
  1159.0 40.9 reduce-scatter.24
  1201.9 32.2 all-gather.26
  1237.5 53.8 reduce-scatter.30
  1295.3 71.2 reduce-scatter.40
  1369.4 34.4 all-reduce.62
  1406.1 19.5 reduce-scatter.36
  1427.9 25.4 reduce-scatter.28
  1455.6 20.5 reduce-scatter.32
  1478.5 25.4 reduce-scatter.26

commit v2 on v1

--- a/solution.py
+++ b/solution.py
@@ -71,6 +71,61 @@
     wide = grown * (grown + 2.0)
     under = 1.0 / (wide + 2.0)
     return wide * under + values * (4.0 * grown * (1.0 + grown) * under * under)
+
+
+def sum_kernel(axis, size, x_ref, o_ref, slots, send_sems, recv_sems):
+    me = lax.axis_index(axis)
+    barrier = pltpu.get_barrier_semaphore()
+    peers = [lax.rem(me + step, size) for step in range(1, size)]
+    for peer in peers:
+        pl.semaphore_signal(
+            barrier, inc=1, device_id={axis: peer}, device_id_type=pl.DeviceIdType.MESH
+        )
+    pl.semaphore_wait(barrier, size - 1)
+    for step, peer in enumerate(peers):
+        pltpu.make_async_remote_copy(
+            src_ref=x_ref,
+            dst_ref=slots.at[me],
+            send_sem=send_sems.at[step],
+            recv_sem=recv_sems.at[me],
+            device_id={axis: peer},
+            device_id_type=pl.DeviceIdType.MESH,
+        ).start()
+    slots[me] = x_ref[...]
+    for step, peer in enumerate(peers):
+        copy = pltpu.make_async_remote_copy(
+            src_ref=x_ref,
+            dst_ref=slots.at[peer],
+            send_sem=send_sems.at[step],
+            recv_sem=recv_sems.at[peer],
+            device_id={axis: peer},
+            device_id_type=pl.DeviceIdType.MESH,
+        )
+        copy.wait_send()
+        copy.wait_recv()
+    total = slots[0]
+    for device in range(1, size):
+        total = total + slots[device]
+    o_ref[...] = total
+
+
+def small_sum(values, axis, name):
+    size = lax.axis_size(axis)
+    whole = pl.BlockSpec(memory_space=pltpu.VMEM)
+    return pl.pallas_call(
+        partial(sum_kernel, axis, size),
+        out_shape=jax.ShapeDtypeStruct(values.shape, F32),
+        in_specs=[whole],
+        out_specs=whole,
+        scratch_shapes=[
+            pltpu.VMEM((size,) + values.shape, F32),
+            pltpu.SemaphoreType.DMA((size - 1,)),
+            pltpu.SemaphoreType.DMA((size,)),
+        ],
+        compiler_params=pltpu.CompilerParams(
+            collective_id=name, has_side_effects=True, vmem_limit_bytes=16 << 20
+        ),
+    )(values)
 
 
 def conv_norm(hidden, segment, conv, vec, gain):
@@ -100,14 +155,14 @@
     return scale * (active * expand(onehot, ratio)) + shift + active
 
 
-def text_ahead(hidden, segment, onehot, own, conv, vec, gain, up, hid, down, axis):
+def text_ahead(hidden, segment, onehot, own, conv, vec, gain, up, hid, down):
     normed, norm_pull = jax.vjp(
         lambda h, c, v, g: conv_norm(h, segment, c, v, g), hidden, conv, vec, gain
     )
     normed = normed.astype(BF)
     active, act_pull = jax.vjp(activate, dot(normed, up), hid[0])
     squares, square_pull = jax.vjp(lambda a: clip_squares(own, a), active)
-    squares = lax.psum(squares, axis)
+    squares = small_sum(squares, "mp", 1)
     grown, respond_pull = jax.vjp(
         lambda a, s, g, b: respond(a, s, onehot, g, b), active, squares, hid[1], hid[2]
     )
@@ -116,13 +171,17 @@
     return result, (norm_pull, normed, act_pull, square_pull, respond_pull, grown)
 
 
-def text_behind(kept, grad, up, down, axis):
+def text_behind(kept, grad, up, down, extra):
     norm_pull, normed, act_pull, square_pull, respond_pull, grown = kept
     grad_low = grad.astype(BF)
     g_out = jnp.sum(grad, axis=0)
     g_down = dot(grad_low, grown, TN)
     grad_active, grad_squares, g_scale, g_shift = respond_pull(dot(grad_low, down, NT))
-    grad_squares = lax.psum(grad_squares, axis)
+    if extra is None:
+        grad_squares = small_sum(grad_squares, "mp", 1)
+    else:
+        joined = small_sum(jnp.concatenate([grad_squares, extra], axis=1), "mp", 2)
+        grad_squares, extra = joined[:, : grad_squares.shape[1]], joined[:, grad_squares.shape[1] :]
     grad_active = grad_active + square_pull(grad_squares)[0]
     grad_pre, g_bias = act_pull(grad_active)
     pre_low = grad_pre.astype(BF)
@@ -132,6 +191,7 @@
     return (
         grad + grad_hidden,
         (g_conv, g_vec, g_gain, g_up, jnp.stack([g_bias, g_scale, g_shift]), g_down),
+        extra,
     )
 
 
@@ -162,12 +222,29 @@
     return out
 
 
-def conv_kernel(taps, x_ref, w_ref, o_ref):
-    rows = o_ref.shape[0]
+def conv_kernel(taps, turned, x_ref, w_ref, o_ref, full_ref):
+    rows, width = o_ref.shape
+    group = w_ref.shape[1]
     first = GAP - taps // 2
+
+    @pl.when(pl.program_id(0) == 0)
+    def _():
+        lane = lax.broadcasted_iota(jnp.int32, (group, width), 1) // group
+        for k in range(taps):
+            tap = w_ref[taps - 1 - k if turned else k]
+            for g in range(width // group):
+                piece = jnp.where(lane == g, tap, jnp.zeros_like(tap))
+                if turned:
+                    full_ref[g * group : (g + 1) * group, k * width : (k + 1) * width] = piece
+                else:
+                    full_ref[k * width + g * group : k * width + (g + 1) * group, :] = piece
+
     columns = [x_ref[first + k : first + k + rows, :].astype(BF) for k in range(taps)]
-    o_ref[...] = jnp.dot(
-        jnp.concatenate(columns, axis=1), w_ref[...], preferred_element_type=F32
+    o_ref[...] = lax.dot_general(
+        jnp.concatenate(columns, axis=1),
+        full_ref[...],
+        NT if turned else NN,
+        preferred_element_type=F32,
     )
 
 
@@ -178,19 +255,23 @@
     return rows
 
 
-def apply_conv(spread_rows, weight, taps):
+def apply_conv(spread_rows, weight, turned):
     rows = spread_rows.shape[0] - 2 * GAP
     width = spread_rows.shape[1]
+    taps, group = weight.shape[:2]
     chunk = conv_chunk(rows)
     return pl.pallas_call(
-        partial(conv_kernel, taps),
+        partial(conv_kernel, taps, turned),
         out_shape=jax.ShapeDtypeStruct((rows, width), F32),
         grid=(rows // chunk,),
         in_specs=[
             pl.BlockSpec((pl.Element(chunk + 2 * GAP), pl.Element(width)), lambda i: (i * chunk, 0)),
-            pl.BlockSpec(weight.shape, lambda i: (0, 0), pipeline_mode=pl.Buffered(1)),
+            pl.BlockSpec(weight.shape, lambda i: (0, 0, 0), pipeline_mode=pl.Buffered(1)),
         ],
         out_specs=pl.BlockSpec((chunk, width), lambda i: (i, 0)),
+        scratch_shapes=[
+            pltpu.VMEM((width, taps * width) if turned else (taps * width, width), BF)
+        ],
         compiler_params=pltpu.CompilerParams(vmem_limit_bytes=48 << 20),
         cost_estimate=pl.CostEstimate(
             flops=2 * rows * taps * width * width, bytes_accessed=8 << 20, transcendentals=0
@@ -232,17 +313,6 @@
             flops=2 * rows * taps * width * width, bytes_accessed=8 << 20, transcendentals=0
         ),
     )(spread_rows, grads)
-
-
-def block_diagonal(weight, turned):
-    taps, group, width = weight.shape
-    groups = width // group
-    parts = weight.reshape(taps, group, groups, group)
-    if turned:
-        parts = parts[::-1].transpose(0, 3, 2, 1)
-    eye = jnp.eye(groups, dtype=weight.dtype)
-    full = parts[:, None] * eye[None, :, None, :, None]
-    return full.reshape(taps * groups * group, groups * group)
 
 
 def pair_split(columns):
@@ -470,20 +540,25 @@
         piece = weight.shape[axis] // groups
         return lax.dynamic_slice_in_dim(weight, place * piece, piece, axis)
 
+    def to_all(piece, axis_name="mp"):
+        size = lax.axis_size(axis_name)
+        return lax.all_to_all(jnp.broadcast_to(piece[None], (size,) + piece.shape), axis_name, 0, 0)
+
     def gather(piece, axis):
-        return lax.all_gather(lax.all_gather(piece, "mp"), "dp", axis=axis, tiled=True)
+        return lax.all_gather(to_all(piece), "dp", axis=axis, tiled=True)
 
     qkv_piece = spread_slice(qkv_w, 1)
     qkv_piece = jnp.concatenate([pair_split(qkv_piece[:2]), qkv_piece[2:]], axis=0)
     qkv_full = gather(qkv_piece, 2)
     out_full = gather(spread_slice(out_w, 0), 1).reshape(width, width)
-    w1_full = lax.all_gather(
-        lax.all_gather(spread_slice(ff_w1, 0), "mp", axis=1, tiled=True), "dp", axis=0, tiled=True
-    )
+    w1_piece = to_all(spread_slice(ff_w1, 0)).transpose(1, 0, 2)
+    w1_full = lax.all_gather(w1_piece.reshape(w1_piece.shape[0], -1), "dp", axis=0, tiled=True)
     w2_full = gather(spread_slice(ff_w2, 0), 1).reshape(-1, width)
     small = jnp.concatenate([pair_split(qkv_b[:2]), qkv_b[2:]], axis=0)
-    qkv_bias = lax.all_gather(small, "mp")
-    b1_full = lax.all_gather(ff_b1, "mp", tiled=True)
+    small = jnp.concatenate([small, ff_b1.reshape(-1, cols)], axis=0)
+    small = to_all(small)
+    qkv_bias = small[:, :3]
+    b1_full = small[:, 3:].reshape(-1)
     all_steps = lax.all_gather(t_index, "dp", tiled=True).reshape(-1)
 
     lengths = clip_lengths[0]
@@ -521,7 +596,7 @@
     for b in range(blocks):
         hidden, saved = text_ahead(
             hidden, seg_ext, hot_ext, own_ext, txt_conv[b], txt_vec[b], txt_gain[b],
-            txt_up[b], txt_hid[b], txt_down[b], "mp",
+            txt_up[b], txt_hid[b], txt_down[b],
         )
         kept.append(saved)
     text = hidden[HALO : HALO + rows].astype(BF)
@@ -538,11 +613,11 @@
 
     spread_in = spread(to_channels(x0.astype(BF)).astype(F32), starts, ends)
     real = spread(jnp.ones((total, 1), F32), starts, ends)
-    pre_a = apply_conv(spread_in, block_diagonal(pos_conv[0], False), taps) + pos_bias[0]
+    pre_a = apply_conv(spread_in, pos_conv[0], False) + pos_bias[0]
     y_a = jnp.pad(
         jnp.where(real[GAP:-GAP] > 0, mish(pre_a), 0.0).astype(BF).astype(F32), ((GAP, GAP), (0, 0))
     )
-    pre_b = apply_conv(y_a, block_diagonal(pos_conv[1], False), taps) + pos_bias[1]
+    pre_b = apply_conv(y_a, pos_conv[1], False) + pos_bias[1]
     c_pos = to_rows(gather_back(mish(pre_b).astype(BF), starts, ends))
     x1 = x0 + c_pos.astype(F32)
 
@@ -596,7 +671,7 @@
     )
     r = r.astype(BF)
     out, ff_pull = jax.vjp(lambda s, m, a, b: residual(s, m, a, b, 5), x2, mod, dot(r, w2_full), ff_b2)
-    result = lax.all_gather(out.astype(BF), "mp", tiled=True).astype(F32)
+    result = to_all(out.astype(BF)).reshape(total, width).astype(F32)
 
     grad = lax.dynamic_slice_in_dim(out_grad, first, rows).astype(F32)
     dx2, dmod_a, df, g_ff_b2 = ff_pull(grad)
@@ -609,17 +684,20 @@
     more, dmod_b = n2_pull(dot(dh, w1_full, NT))
     dx2 = dx2 + more
 
+    def send_dp(matrix):
+        parts = matrix.astype(BF).reshape(groups, matrix.shape[0] // groups, matrix.shape[1])
+        return lax.all_to_all(parts, "dp", 0, 0)
+
+    def total_of(received):
+        return jnp.sum(received.astype(F32), axis=0)
+
     def by_rank(matrix):
-        return matrix.reshape(matrix.shape[0], shards, -1)
-
-    def scatter(matrix):
-        part = lax.psum_scatter(matrix.astype(BF), "dp", scatter_dimension=0, tiled=True)
-        return lax.psum_scatter(part, "mp", scatter_dimension=1, tiled=True).astype(F32)
-
-    ff_pair = jnp.concatenate([by_rank(g_ff_w1), by_rank(g_ff_w2)], axis=2)
-    ff_pair = scatter(ff_pair.reshape(width, -1))
-    ff_cols = ff_w1.shape[1]
-    o_ff_w1, o_ff_w2 = ff_pair[:, :ff_cols], ff_pair[:, ff_cols:].T
+        return matrix.reshape(matrix.shape[0], shards, -1).transpose(1, 0, 2)
+
+    def send_mp(parts):
+        return lax.all_to_all(parts.astype(BF), "mp", 0, 0)
+
+    sent_w1, sent_w2 = send_dp(g_ff_w1), send_dp(g_ff_w2)
 
     dx1, dmod_c, da, g_out_b = att_pull(dx2)
     da = da.astype(BF)
@@ -632,65 +710,84 @@
     w_all = qkv_full.transpose(2, 0, 1, 3).reshape(width, 3 * width)
     more, dmod_d = n1_pull(dot(dqkv, w_all, NT))
     dx1 = dx1 + more
-    at_pair = jnp.concatenate([by_rank(g_qkv_w), by_rank(g_out_w)], axis=2)
-    at_pair = scatter(at_pair.reshape(width, -1))
-    g_qkv = at_pair[:, : 3 * cols].reshape(-1, 3, cols).transpose(1, 0, 2)
-    o_qkv_w = jnp.concatenate([pair_merge(g_qkv[:2]), g_qkv[2:]], axis=0)
-    o_out_w = at_pair[:, 3 * cols :].T
+    sent_w1, sent_w2, dx1 = lax.optimization_barrier((sent_w1, sent_w2, dx1))
+    ff_pair = jnp.concatenate([by_rank(total_of(sent_w1)), by_rank(total_of(sent_w2))], axis=2)
+    ff_pair = send_mp(ff_pair)
+    sent_qkv, sent_out = send_dp(g_qkv_w), send_dp(g_out_w)
 
     dmod = dmod_a + dmod_b + dmod_c + dmod_d
-    dmod_all = jnp.sum(
-        lax.all_gather(lax.all_gather(dmod, "mp"), "dp"), axis=1
-    ).reshape(groups * clips, -1)
 
     slope_b = gather_back(mish_slope(pre_b), starts, ends)
     dy_b = to_channels(dx1.astype(BF)).astype(F32) * slope_b
     g_pos_b = jnp.sum(dy_b, axis=0)
     dy_b = spread(dy_b.astype(BF).astype(F32), starts, ends)
-    dy_a = apply_conv(dy_b, block_diagonal(pos_conv[1], True), taps) * mish_slope(pre_a)
+    dy_a = apply_conv(dy_b, pos_conv[1], True) * mish_slope(pre_a)
     dy_a = jnp.where(real[GAP:-GAP] > 0, dy_a, 0.0)
     g_pos_a = jnp.sum(dy_a, axis=0)
     dy_a = jnp.pad(dy_a.astype(BF).astype(F32), ((GAP, GAP), (0, 0)))
     dc = gather_back(
-        apply_conv(dy_a, block_diagonal(pos_conv[0], True), taps).astype(BF), starts, ends
+        apply_conv(dy_a, pos_conv[0], True).astype(BF), starts, ends
     )
     dx0_full = dx1 + to_rows(dc).astype(F32)
     g_conv = jnp.concatenate(
         [conv_grad(spread_in, dy_a[GAP:-GAP], taps, group), conv_grad(y_a, dy_b[GAP:-GAP], taps, group)],
         axis=1,
     )
-    g_conv = lax.psum_scatter(g_conv.astype(BF), "dp", scatter_dimension=0, tiled=True)
-    o_pos_conv = g_conv.astype(F32).T.reshape(2, taps, group, -1)
+    sent_qkv, sent_out, ff_pair, dx0_full = lax.optimization_barrier(
+        (sent_qkv, sent_out, ff_pair, dx0_full)
+    )
+    ff_pair = total_of(ff_pair)
+    ff_cols = ff_w1.shape[1]
+    o_ff_w1, o_ff_w2 = ff_pair[:, :ff_cols], ff_pair[:, ff_cols:].T
+    at_pair = jnp.concatenate([by_rank(total_of(sent_qkv)), by_rank(total_of(sent_out))], axis=2)
+    at_pair = send_mp(at_pair)
+    sent_conv = send_dp(g_conv)
 
     g_emb_bias = jnp.sum(dx0_full, axis=0)
     dx0 = dx0_full.astype(BF)
-    mel_grad = lax.all_gather(dot(dx0, emb_mel, NT).astype(BF), "mp", tiled=True).astype(F32)
+    mel_grad = to_all(dot(dx0, emb_mel, NT).astype(BF)).reshape(total, -1).astype(F32)
     g_emb = jnp.concatenate([dot(dx0, text, TN), dot(dx0, mel, TN)], axis=1)
-    g_emb = lax.psum_scatter(g_emb.astype(BF), "dp", scatter_dimension=0, tiled=True)
-    g_emb = lax.psum(g_emb, "mp").astype(F32)
+    sent_emb = send_dp(g_emb)
     text_width = text.shape[1]
-    o_emb_text, o_emb_mel = g_emb[:, :text_width].T, g_emb[:, text_width:].T
 
     dtext = jnp.pad(dot(dx0, emb_text, NT), ((HALO, HALO), (0, 0)))
     text_grads = [None] * blocks
+    extra = dmod
+    sent_up, sent_down = [None] * blocks, [None] * blocks
     for b in reversed(range(blocks)):
-        dtext, text_grads[b] = text_behind(kept[b], dtext, txt_up[b], txt_down[b], "mp")
+        dtext, text_grads[b], summed = text_behind(kept[b], dtext, txt_up[b], txt_down[b], extra)
+        if extra is not None:
+            dmod_all = lax.all_gather(summed, "dp", tiled=True)
+        extra = None
+        sent_up[b], sent_down[b] = send_dp(text_grads[b][3]), send_dp(text_grads[b][5])
+        if b == blocks - 1:
+            at_pair, sent_conv, sent_emb, dtext = lax.optimization_barrier(
+                (at_pair, sent_conv, sent_emb, dtext)
+            )
+            at_pair = total_of(at_pair)
+            g_emb = total_of(to_all(total_of(sent_emb).astype(BF)))
+    g_qkv = at_pair[:, : 3 * cols].reshape(-1, 3, cols).transpose(1, 0, 2)
+    o_qkv_w = jnp.concatenate([pair_merge(g_qkv[:2]), g_qkv[2:]], axis=0)
+    o_out_w = at_pair[:, 3 * cols :].T
+    o_pos_conv = total_of(sent_conv).T.reshape(2, taps, group, -1)
+    o_emb_text, o_emb_mel = g_emb[:, :text_width].T, g_emb[:, text_width:].T
     vocab = txt_table.shape[0]
-    chosen = (ids[:, None] == jnp.arange(vocab, dtype=jnp.int32)[None, :]).astype(BF)
-    g_table = dot(dtext, chosen, TN)
-
-    def scatter_rows(matrix):
-        part = lax.psum_scatter(matrix.astype(BF), "dp", scatter_dimension=0, tiled=True)
-        return lax.psum_scatter(part, "mp", scatter_dimension=0, tiled=True).astype(F32)
-
-    ups = scatter_rows(jnp.concatenate([text_grads[b][3] for b in range(blocks)], axis=1))
-    downs = scatter_rows(
-        jnp.concatenate([text_grads[b][5] for b in range(blocks)] + [g_table], axis=1)
+    wide = -(-vocab // 128) * 128
+    chosen = (ids[:, None] == jnp.arange(wide, dtype=jnp.int32)[None, :]).astype(BF)
+    sent_table = send_dp(dot(dtext, chosen, TN))
+
+    def rows_by_rank(matrix):
+        return matrix.reshape(shards, matrix.shape[0] // shards, -1)
+
+    ups = send_mp(rows_by_rank(jnp.concatenate([total_of(v) for v in sent_up], axis=1)))
+    downs = send_mp(
+        rows_by_rank(jnp.concatenate([total_of(v) for v in sent_down + [sent_table]], axis=1))
     )
     hidden_width = txt_up.shape[2]
-    o_up = ups.T.reshape(blocks, text_width, -1)
+    downs = total_of(downs)
+    o_up = total_of(ups).T.reshape(blocks, text_width, -1)
     o_down = downs[:, : blocks * hidden_width].T.reshape(blocks, hidden_width, -1)
-    o_table = downs[:, blocks * hidden_width :].T
+    o_table = downs[:, blocks * hidden_width :].T[:vocab]
 
     def placed(values):
         full = jnp.zeros((shards,) + values.shape, F32)
@@ -704,7 +801,8 @@
         jnp.stack([g[2] for g in text_grads]), jnp.stack([g[4] for g in text_grads]),
         g_emb_bias, g_pos_bias, g_qkv_b, g_out_b, g_ff_b1, g_ff_b2,
     ]
-    packed = lax.psum(jnp.concatenate([s.reshape(-1) for s in small]), ("dp", "mp"))
+    packed = jnp.concatenate([s.reshape(-1) for s in small]).reshape(8, -1)
+    packed = small_sum(small_sum(packed, "mp", 3), "dp", 4).reshape(-1)
     unpacked, at = [], 0
     for s in small:
         unpacked.append(packed[at : at + s.size].reshape(s.shape))

time: 1540 us -> 1320 us (0.86)
  blocking collectives: 407 us -> 49.3 us
  local copies, waits for them, and re-layouts: 237 us -> 96.4 us
  starting transfers between devices: 27.5 us -> 137 us
  Pallas kernels: 150 us -> 239 us
  waiting for transfers between devices: 353 us -> 429 us
    all_to_all x0 -> x23, waiting for transfers between devices: none -> 211 us  [the longest x11 100 us: send_dp(): return lax.all_to_all(parts, 'dp', 0, 0)]
    all_to_all x6 -> x7, waiting for transfers between devices: 28.1 us -> 217 us  [exchange(): return lax.all_to_all(values, axis, 0, 0)]
    all_gather x8 -> x1, blocking collectives: 199 us -> 10.9 us  [local(): dmod_all = lax.all_gather(summed, 'dp', tiled=True)]
    unnamed x25 -> x4, waiting for transfers between devices: 181 us -> 1.12 us
    all_to_all x0 -> x23, starting transfers between devices: none -> 106 us  [the longest x11 52.8 us: send_dp(): return lax.all_to_all(parts, 'dp', 0, 0)]
    reduce_scatter x3 -> x0, waiting for transfers between devices: 87 us -> none  [the longest x2 45.1 us: scatter(): lax.psum_scatter(part, 'mp', scatter_dimension=1, tiled=True).astype(F32)]
    psum x4 -> x0, blocking collectives: 69.5 us -> none  [the longest x2 36.1 us: text_behind(): grad_squares = lax.psum(grad_squares, axis)]
    all_to_all x2 -> x1, blocking collectives: 95.5 us -> 27.4 us  [exchange(): return lax.all_to_all(values, axis, 0, 0)]
  transfers between devices with their start and end apart: 24 -> 34, of which waited for: 12 -> 22; matrix products, arithmetic and copies ran while one was open for 32% -> 27% of each run, Pallas kernels for 6% -> 18%
where the time goes in v2:
time: 1320 us; the launch traced here: 1300 us
  waiting for transfers between devices  429 us (32%)
  Pallas kernels  239 us (18%)
  matrix products  184 us (14%)
  other arithmetic  149 us (11%)
  starting transfers between devices  137 us (10%)
  local copies, waits for them, and re-layouts  96.4 us (7%)
  blocking collectives  49.3 us (4%)
  between operations  18.8 us (1%)
    all_to_all x7, waiting for transfers between devices, exchange(): return lax.all_to_all(values, axis, 0, 0)  217 us
    dot_general x42, matrix products, dot(): lax.dot_general(left.astype(BF), right.astype(BF), dims, preferred_elemen...  128 us
    all_to_all x11, waiting for transfers between devices, send_dp(): return lax.all_to_all(parts, 'dp', 0, 0)  100 us
    all_to_all x8, waiting for transfers between devices, to_all(): lax.all_to_all(jnp.broadcast_to(piece[None], (size,) + piece.shape), axis...  82.3 us
    pallas_call x6, Pallas kernels, small_sum(): pl.pallas_call(partial(sum_kernel, axis, size), out_shape=jax.ShapeDtypeS...  69.3 us
    pallas_call x1, Pallas kernels, attend_back(): pl.pallas_call(attend_back_kernel, out_shape=jax.ShapeDtypeStruct((shards...  54.3 us
    all_to_all x11, starting transfers between devices, send_dp(): return lax.all_to_all(parts, 'dp', 0, 0)  52.8 us
    pallas_call x1, Pallas kernels, attend(): pl.pallas_call(attend_kernel, out_shape=[jax.ShapeDtypeStruct((total, wid...  44 us
  transfers between devices with their start and end apart: 34, of which 22 were waited for; matrix products, arithmetic and copies ran while one was open for 27% of the time, Pallas kernels for 18%

profile of v2, /device:TPU:0, one launch (start us, length us, event | category | flops | bytes accessed | tf_op | source)
XLA Modules:
  0.0 1302.0 jit_solution(17678828722907023262)
XLA Ops:
  111.6 21.1 %all-to-all-done = bf16[4,512,256]{2,1,0:T(8,128)(2,1)S(1)} async-done(((bf16[4,512,256]{2,1,0:T(8,128)(2,1)}), bf16[4,512,256]{2,1,0:T(8,128)(2,1)S(1)}, u32[]{:S(2)}, u32[]{:S(2)}) %all-to-all-start) | async-done | bytes 1048608 | tf_op jit(solution)/shard_map/all_to_all | solution.py:518
  139.4 9.8 shard_map.495
  152.1 9.8 shard_map.496
  189.9 18.8 %all-to-all-done.1 = bf16[4,512,256]{2,1,0:T(8,128)(2,1)} async-done(((bf16[4,512,256]{2,1,0:T(8,128)(2,1)}), bf16[4,512,256]{2,1,0:T(8,128)(2,1)}, u32[]{:S(2)}, u32[]{:S(2)}) %all-to-all-start.1) | async-done | bytes 1048608 | tf_op jit(solution)/shard_map/all_to_all | solution.py:518
  253.0 66.7 %all-to-all-done.4.q_ref.k_ref.v_ref = bf16[4,3,512,256]{3,2,1,0:T(8,128)(2,1)} async-done(((bf16[4,3,512,256]{3,2,1,0:T(8,128)(2,1)}), bf16[4,3,512,256]{3,2,1,0:T(8,128)(2,1)}, u32[]{:S(2)}, u32[]{:S(2)}) %all-to-all-start.4) | async-done | bytes 3145760 | tf_op jit(solution)/shard_map/all_to_all | solution.py:518
  320.9 44.0 %shard_map.497 = (bf16[2048,256]{1,0:T(8,128)(2,1)S(1)}, f32[2048,256]{1,0:T(8,128)S(1)}, f32[2048,128]{1,0:T(8,128)S(1)}) custom-call(s32[8,2]{1,0:T(8,128)S(1)} %copy.404.bounds, bf16[4,3,512,256]{3,2,1,0:T(8,128)(2,1)} %all-to-all-done.4.q_ref.k_ref.v_ref, bf16[4,3,512,256]{3,2,1,0:T(8,128)(2,1)} %all-to-all-done.4.q_ref.k_ref.v_ref, ...), custom_call_target="tpu_custom_call" | custom-call | flops 8589934592 | bytes 8388608 | tf_op jit(solution)/shard_map/pallas_call | solution.py:405
  371.4 23.5 %all-to-all-done.5 = bf16[4,512,256]{2,1,0:T(8,128)(2,1)} async-done(((bf16[4,512,256]{2,1,0:T(8,128)(2,1)}), bf16[4,512,256]{2,1,0:T(8,128)(2,1)}, u32[]{:S(2)}, u32[]{:S(2)}) %all-to-all-start.5) | async-done | bytes 1048608 | tf_op jit(solution)/shard_map/all_to_all | solution.py:518
  402.0 8.3 fusion.307
  446.3 17.6 %all-to-all-done.10 = bf16[4,512,256]{2,1,0:T(8,128)(2,1)S(1)} async-done(((bf16[4,512,256]{2,1,0:T(8,128)(2,1)}), bf16[4,512,256]{2,1,0:T(8,128)(2,1)S(1)}, u32[]{:S(2)}, u32[]{:S(2)}) %all-to-all-start.10) | async-done | bytes 1048608 | tf_op jit(solution)/shard_map/all_to_all | solution.py:518
  477.3 41.3 %all-to-all-done.14 = bf16[8,128,2048]{2,1,0:T(8,128)(2,1)} async-done(((bf16[8,128,2048]{2,1,0:T(8,128)(2,1)}), bf16[8,128,2048]{2,1,0:T(8,128)(2,1)}, u32[]{:S(2)}, u32[]{:S(2)}) %all-to-all-start.14) | async-done | bytes 4194336 | tf_op jit(solution)/shard_map/all_to_all | solution.py:689
  527.4 54.3 %shard_map.498 = bf16[4,3,512,256]{3,2,1,0:T(8,128)(2,1)} custom-call(s32[8,2]{1,0:T(8,128)S(1)} %copy.404.bounds, bf16[4,3,512,256]{3,2,1,0:T(8,128)(2,1)} %all-to-all-done.4.q_ref.k_ref.v_ref, bf16[4,3,512,256]{3,2,1,0:T(8,128)(2,1)} %all-to-all-done.4.q_ref.k_ref.v_ref, bf16[4,3,512,256]{3,2,1,0:T(8,128)(2,1)} %all-to-all-done.4.q_ref.k_ref.v_ref, ...), custom_call_target="tpu_custom_call" | custom-call | flops 21474836480 | bytes 16777216 | tf_op jit(solution)/shard_map/pallas_call | solution.py:506
  590.6 65.3 %all-to-all-done.11 = bf16[4,3,512,256]{3,2,1,0:T(8,128)(2,1)} async-done(((bf16[4,3,512,256]{3,2,1,0:T(8,128)(2,1)}), bf16[4,3,512,256]{3,2,1,0:T(8,128)(2,1)}, u32[]{:S(2)}, u32[]{:S(2)}) %all-to-all-start.11) | async-done | bytes 3145760 | tf_op jit(solution)/shard_map/all_to_all | solution.py:518
  673.7 13.2 %all-to-all-done.13 = bf16[8,128,1024]{2,1,0:T(8,128)(2,1)} async-done(((bf16[8,128,1024]{2,1,0:T(8,128)(2,1)}), bf16[8,128,1024]{2,1,0:T(8,128)(2,1)}, u32[]{:S(2)}, u32[]{:S(2)}) %all-to-all-start.13) | async-done | bytes 2097184 | tf_op jit(solution)/shard_map/all_to_all | solution.py:689
  687.0 27.4 %all_to_all.155 = bf16[4,512,256]{2,1,0:T(8,128)(2,1)} all-to-all(bf16[4,512,256]{2,1,0:T(8,128)(2,1)} %bitcast.531), channel_id=1, replica_groups=mesh['dp'=8,'mp'=4] {'mp'}, dimensions={0} | all-to-all | bytes 2097152 | tf_op jit(solution)/shard_map/all_to_all | solution.py:518
  723.4 11.1 all-gather
  754.9 9.8 shard_map.499
  766.1 48.8 %all-to-all-done.9 = bf16[4,512,1024]{2,1,0:T(8,128)(2,1)} async-done(((bf16[4,512,1024]{2,1,0:T(8,128)(2,1)}), bf16[4,512,1024]{2,1,0:T(8,128)(2,1)}, u32[]{:S(2)}, u32[]{:S(2)}) %all-to-all-start.9) | async-done | bytes 4194336 | tf_op jit(solution)/shard_map/all_to_all | solution.py:545
  824.3 10.0 shard_map.500
  861.9 8.3 convolution_convert_fusion
  898.7 15.8 %shard_map.501 = f32[256,1984]{1,0:T(8,128)S(1)} custom-call(f32[2144,256]{1,0:T(8,128)} %copy-done.7, f32[2112,256]{1,0:T(8,128)S(1)} %convert_element_type.647.g_ref), custom_call_target="tpu_custom_call" | custom-call | flops 8581545984 | bytes 8388608 | tf_op jit(solution)/shard_map/pallas_call | solution.py:302
  915.6 15.9 %shard_map.502 = f32[256,1984]{1,0:T(8,128)S(1)} custom-call(f32[2144,256]{1,0:T(8,128)} %copy-done.8, f32[2112,256]{1,0:T(8,128)S(1)} %slice.1229.g_ref), custom_call_target="tpu_custom_call" | custom-call | flops 8581545984 | bytes 8388608 | tf_op jit(solution)/shard_map/pallas_call | solution.py:302
  941.4 11.1 all-to-all-done.12
  963.3 12.0 shard_map.503
  1018.3 10.9 all-gather.1
  1039.7 11.2 all-to-all-done.24
  1057.4 16.9 %all-to-all-done.19 = bf16[4,512,200]{1,2,0:T(8,128)(2,1)} async-done(((bf16[4,512,200]{1,2,0:T(8,128)(2,1)}), bf16[4,512,200]{1,2,0:T(8,128)(2,1)}, u32[]{:S(2)}, u32[]{:S(2)}) %all-to-all-start.19) | async-done | bytes 819232 | tf_op jit(solution)/shard_map/all_to_all | solution.py:545
  1083.3 8.9 fusion.74
  1178.5 9.1 all-to-all-done.23
  1192.6 11.7 shard_map.505.x_ref
  1204.3 27.0 %shard_map.506 = f32[8,3456]{1,0:T(8,128)S(1)} custom-call(f32[8,3456]{1,0:T(8,128)S(1)} %shard_map.505.x_ref), custom_call_target="tpu_custom_call" | custom-call | tf_op jit(solution)/shard_map/pallas_call | solution.py:115
  1248.0 11.2 all-to-all-done.30
  1263.5 9.0 all-to-all-done.29
  (1027 shorter events, 603.7 us)
Async XLA Ops:
  10.8 38.0 %all-to-all-start.2 = ((bf16[4,3,128,256]{3,2,1,0:T(8,128)(2,1)}), bf16[4,3,128,256]{3,2,1,0:T(8,128)(2,1)}, u32[]{:S(2)}, u32[]{:S(2)}) async-start(bf16[4,3,128,256]{3,2,1,0:T(8,128)(2,1)} %broadcast_in_dim.486), calls=%async_computation.2 | async-start | bytes 1572864 | tf_op jit(solution)/shard_map/all_to_all | solution.py:545
  49.6 56.1 %all-to-all-start.6 = ((bf16[4,32,1024]{2,1,0:T(8,128)(2,1)}), bf16[4,32,1024]{2,1,0:T(8,128)(2,1)S(1)}, u32[]{:S(2)}, u32[]{:S(2)}) async-start(bf16[4,32,1024]{2,1,0:T(8,128)(2,1)} %broadcast_in_dim.489), calls=%async_computation.6 | async-start | bytes 524288 | tf_op jit(solution)/shard_map/all_to_all | solution.py:545
  54.1 170.8 %all-gather.7.cloned.1.call-start = ((), (), s32[]{:S(2)}) async-start(), calls=%async_computation.31 | async-start | bytes 7077888 | tf_op jit(solution)/shard_map/all_gather | solution.py:548
  105.6 27.1 %all-to-all-start = ((bf16[4,512,256]{2,1,0:T(8,128)(2,1)}), bf16[4,512,256]{2,1,0:T(8,128)(2,1)S(1)}, u32[]{:S(2)}, u32[]{:S(2)}) async-start(bf16[4,512,256]{2,1,0:T(8,128)(2,1)} %bitcast.512), calls=%async_computation | async-start | bytes 2097152 | tf_op jit(solution)/shard_map/all_to_all | solution.py:518
  110.3 261.0 %all-gather.9.cloned.1.call-start = ((), (), s32[]{:S(2)}) async-start(), calls=%async_computation.32 | async-start | bytes 2359296 | tf_op jit(solution)/shard_map/all_gather | solution.py:548
  133.3 29.9 %all-to-all-start.3 = ((f32[4,5,256]{2,1,0:T(8,128)}), f32[4,5,256]{2,1,0:T(8,128)S(1)}, u32[]{:S(2)}, u32[]{:S(2)}) async-start(f32[4,5,256]{2,1,0:T(8,128)} %broadcast_in_dim.487), calls=%async_computation.3 | async-start | bytes 65536 | tf_op jit(solution)/shard_map/all_to_all | solution.py:545
  181.6 27.1 %all-to-all-start.1 = ((bf16[4,512,256]{2,1,0:T(8,128)(2,1)}), bf16[4,512,256]{2,1,0:T(8,128)(2,1)}, u32[]{:S(2)}, u32[]{:S(2)}) async-start(bf16[4,512,256]{2,1,0:T(8,128)(2,1)} %bitcast.58), calls=%async_computation.1 | async-start | bytes 2097152 | tf_op jit(solution)/shard_map/all_to_all | solution.py:518
  185.9 216.2 %all-gather.11.cloned.1.call-start = ((), (), s32[]{:S(2)}) async-start(), calls=%async_computation.33 | async-start | bytes 4718592 | tf_op jit(solution)/shard_map/all_gather | solution.py:555
  209.5 35.3 %all-to-all-start.8 = ((bf16[4,64,1024]{2,1,0:T(8,128)(2,1)}), bf16[4,64,1024]{2,1,0:T(8,128)(2,1)S(1)}, u32[]{:S(2)}, u32[]{:S(2)}) async-start(bf16[4,64,1024]{2,1,0:T(8,128)(2,1)} %broadcast_in_dim.491), calls=%async_computation.8 | async-start | bytes 1048576 | tf_op jit(solution)/shard_map/all_to_all | solution.py:545
  245.6 74.1 %all-to-all-start.4 = ((bf16[4,3,512,256]{3,2,1,0:T(8,128)(2,1)}), bf16[4,3,512,256]{3,2,1,0:T(8,128)(2,1)}, u32[]{:S(2)}, u32[]{:S(2)}) async-start(bf16[4,3,512,256]{3,2,1,0:T(8,128)(2,1)} %bitcast.128), calls=%async_computation.4 | async-start | bytes 6291456 | tf_op jit(solution)/shard_map/all_to_all | solution.py:518
  250.6 159.7 %all-gather.13.cloned.1.call-start = ((), (), s32[]{:S(2)}) async-start(), calls=%async_computation.34 | async-start | bytes 4718592 | tf_op jit(solution)/shard_map/all_gather | solution.py:548
  366.9 28.0 %all-to-all-start.5 = ((bf16[4,512,256]{2,1,0:T(8,128)(2,1)}), bf16[4,512,256]{2,1,0:T(8,128)(2,1)}, u32[]{:S(2)}, u32[]{:S(2)}) async-start(bf16[4,512,256]{2,1,0:T(8,128)(2,1)} %bitcast.518), calls=%async_computation.5 | async-start | bytes 2097152 | tf_op jit(solution)/shard_map/all_to_all | solution.py:518
  435.2 28.7 %all-to-all-start.10 = ((bf16[4,512,256]{2,1,0:T(8,128)(2,1)}), bf16[4,512,256]{2,1,0:T(8,128)(2,1)S(1)}, u32[]{:S(2)}, u32[]{:S(2)}) async-start(bf16[4,512,256]{2,1,0:T(8,128)(2,1)} %bitcast.510), calls=%async_computation.10 | async-start | bytes 2097152 | tf_op jit(solution)/shard_map/all_to_all | solution.py:518
  464.9 53.7 %all-to-all-start.14 = ((bf16[8,128,2048]{2,1,0:T(8,128)(2,1)}), bf16[8,128,2048]{2,1,0:T(8,128)(2,1)}, u32[]{:S(2)}, u32[]{:S(2)}) async-start(bf16[8,128,2048]{2,1,0:T(8,128)(2,1)} %bitcast.528), calls=%async_computation.14 | async-start | bytes 8388608 | tf_op jit(solution)/shard_map/all_to_all | solution.py:689
  518.6 63.1 %all-to-all-start.15 = ((bf16[8,128,2048]{2,1,0:T(8,128)(2,1)}), bf16[8,128,2048]{2,1,0:T(8,128)(2,1)}, u32[]{:S(2)}, u32[]{:S(2)}) async-start(bf16[8,128,2048]{2,1,0:T(8,128)(2,1)} %bitcast.527), calls=%async_computation.15 | async-start | bytes 8388608 | tf_op jit(solution)/shard_map/all_to_all | solution.py:689
  581.7 74.2 %all-to-all-start.11 = ((bf16[4,3,512,256]{3,2,1,0:T(8,128)(2,1)}), bf16[4,3,512,256]{3,2,1,0:T(8,128)(2,1)}, u32[]{:S(2)}, u32[]{:S(2)}) async-start(bf16[4,3,512,256]{3,2,1,0:T(8,128)(2,1)} %shard_map.498), calls=%async_computation.11 | async-start | bytes 6291456 | tf_op jit(solution)/shard_map/all_to_all | solution.py:518
  655.8 31.1 %all-to-all-start.13 = ((bf16[8,128,1024]{2,1,0:T(8,128)(2,1)}), bf16[8,128,1024]{2,1,0:T(8,128)(2,1)}, u32[]{:S(2)}, u32[]{:S(2)}) async-start(bf16[8,128,1024]{2,1,0:T(8,128)(2,1)} %bitcast.536), calls=%async_computation.13 | async-start | bytes 4194304 | tf_op jit(solution)/shard_map/all_to_all | solution.py:689
  718.2 96.7 %all-to-all-start.9 = ((bf16[4,512,1024]{2,1,0:T(8,128)(2,1)}), bf16[4,512,1024]{2,1,0:T(8,128)(2,1)}, u32[]{:S(2)}, u32[]{:S(2)}) async-start(bf16[4,512,1024]{2,1,0:T(8,128)(2,1)} %broadcast_in_dim.492), calls=%async_computation.9 | async-start | bytes 8388608 | tf_op jit(solution)/shard_map/all_to_all | solution.py:545
  814.9 29.5 %all-to-all-start.16 = ((bf16[4,128,1024]{2,1,0:T(8,128)(2,1)}), bf16[4,128,1024]{2,1,0:T(8,128)(2,1)}, u32[]{:S(2)}, u32[]{:S(2)}) async-start(bf16[4,128,1024]{2,1,0:T(8,128)(2,1)} %copy.414), calls=%async_computation.16 | async-start | bytes 2097152 | tf_op jit(solution)/shard_map/all_to_all | solution.py:698
  844.5 29.8 %all-to-all-start.18 = ((bf16[4,512,256]{2,1,0:T(8,128)(2,1)}), bf16[4,512,256]{2,1,0:T(8,128)(2,1)}, u32[]{:S(2)}, u32[]{:S(2)}) async-start(bf16[4,512,256]{2,1,0:T(8,128)(2,1)} %bitcast.525), calls=%async_computation.18 | async-start | bytes 2097152 | tf_op jit(solution)/shard_map/all_to_all | solution.py:518
  874.2 78.3 %all-to-all-start.12 = ((bf16[8,128,3072]{2,1,0:T(8,128)(2,1)}), bf16[8,128,3072]{2,1,0:T(8,128)(2,1)}, u32[]{:S(2)}, u32[]{:S(2)}) async-start(bf16[8,128,3072]{2,1,0:T(8,128)(2,1)} %bitcast.524), calls=%async_computation.12 | async-start | bytes 12582912 | tf_op jit(solution)/shard_map/all_to_all | solution.py:689
  952.6 41.0 %all-to-all-start.21 = ((bf16[8,32,3968]{2,1,0:T(8,128)(2,1)}), bf16[8,32,3968]{2,1,0:T(8,128)(2,1)}, u32[]{:S(2)}, u32[]{:S(2)}) async-start(bf16[8,32,3968]{2,1,0:T(8,128)(2,1)} %pad_maximum_fusion), calls=%async_computation.21 | async-start | bytes 4063232 | tf_op jit(solution)/shard_map/all_to_all | solution.py:689
  993.6 37.6 %all-to-all-start.28 = ((bf16[8,128,512]{2,1,0:T(8,128)(2,1)}), bf16[8,128,512]{2,1,0:T(8,128)(2,1)}, u32[]{:S(2)}, u32[]{:S(2)}) async-start(bf16[8,128,512]{2,1,0:T(8,128)(2,1)} %bitcast.547), calls=%async_computation.28 | async-start | bytes 2097152 | tf_op jit(solution)/shard_map/all_to_all | solution.py:689
  1031.2 19.7 %all-to-all-start.24 = ((bf16[8,64,1024]{2,1,0:T(8,128)(2,1)}), bf16[8,64,1024]{2,1,0:T(8,128)(2,1)}, u32[]{:S(2)}, u32[]{:S(2)}) async-start(bf16[8,64,1024]{2,1,0:T(8,128)(2,1)} %bitcast.550), calls=%async_computation.24 | async-start | bytes 2097152 | tf_op jit(solution)/shard_map/all_to_all | solution.py:689
  1051.8 22.5 %all-to-all-start.19 = ((bf16[4,512,200]{1,2,0:T(8,128)(2,1)}), bf16[4,512,200]{1,2,0:T(8,128)(2,1)}, u32[]{:S(2)}, u32[]{:S(2)}) async-start(bf16[4,512,200]{1,2,0:T(8,128)(2,1)} %broadcast_in_dim.497), calls=%async_computation.19 | async-start | bytes 1638400 | tf_op jit(solution)/shard_map/all_to_all | solution.py:545
  1074.3 24.9 %all-to-all-start.22 = ((bf16[8,128,712]{1,2,0:T(8,128)(2,1)}), bf16[8,128,712]{1,2,0:T(8,128)(2,1)}, u32[]{:S(2)}, u32[]{:S(2)}) async-start(bf16[8,128,712]{1,2,0:T(8,128)(2,1)} %pad_maximum_fusion.1), calls=%async_computation.22 | async-start | bytes 2916352 | tf_op jit(solution)/shard_map/all_to_all | solution.py:689
  1099.2 27.4 %all-to-all-start.20 = ((bf16[4,128,1024]{2,1,0:T(8,128)(2,1)}), bf16[4,128,1024]{2,1,0:T(8,128)(2,1)}, u32[]{:S(2)}, u32[]{:S(2)}) async-start(bf16[4,128,1024]{2,1,0:T(8,128)(2,1)} %copy.420), calls=%async_computation.20 | async-start | bytes 2097152 | tf_op jit(solution)/shard_map/all_to_all | solution.py:698
  1147.4 20.6 %all-to-all-start.27 = ((bf16[8,128,512]{2,1,0:T(8,128)(2,1)}), bf16[8,128,512]{2,1,0:T(8,128)(2,1)}, u32[]{:S(2)}, u32[]{:S(2)}) async-start(bf16[8,128,512]{2,1,0:T(8,128)(2,1)} %bitcast.548), calls=%async_computation.27 | async-start | bytes 2097152 | tf_op jit(solution)/shard_map/all_to_all | solution.py:689
  1168.0 19.7 %all-to-all-start.23 = ((bf16[8,64,1024]{2,1,0:T(8,128)(2,1)}), bf16[8,64,1024]{2,1,0:T(8,128)(2,1)}, u32[]{:S(2)}, u32[]{:S(2)}) async-start(bf16[8,64,1024]{2,1,0:T(8,128)(2,1)} %bitcast.549), calls=%async_computation.23 | async-start | bytes 2097152 | tf_op jit(solution)/shard_map/all_to_all | solution.py:689
  1187.7 47.5 %all-to-all-start.25 = ((bf16[8,64,2560]{2,1,0:T(8,128)(2,1)}), bf16[8,64,2560]{2,1,0:T(8,128)(2,1)}, u32[]{:S(2)}, u32[]{:S(2)}) async-start(bf16[8,64,2560]{2,1,0:T(8,128)(2,1)} %bitcast.535), calls=%async_computation.25 | async-start | bytes 5242880 | tf_op jit(solution)/shard_map/all_to_all | solution.py:689
  1236.2 23.0 %all-to-all-start.30 = ((bf16[4,128,712]{1,2,0:T(8,128)(2,1)}), bf16[4,128,712]{1,2,0:T(8,128)(2,1)S(1)}, u32[]{:S(2)}, u32[]{:S(2)}) async-start(bf16[4,128,712]{1,2,0:T(8,128)(2,1)} %broadcast_in_dim.506), calls=%async_computation.30 | async-start | bytes 1458176 | tf_op jit(solution)/shard_map/all_to_all | solution.py:545
  1272.5 20.3 %all-to-all-start.26 = ((bf16[4,16,4608]{2,1,0:T(8,128)(2,1)}), bf16[4,16,4608]{2,1,0:T(8,128)(2,1)}, u32[]{:S(2)}, u32[]{:S(2)}) async-start(bf16[4,16,4608]{2,1,0:T(8,128)(2,1)} %bitcast.182), calls=%async_computation.26 | async-start | bytes 1179648 | tf_op jit(solution)/shard_map/all_to_all | solution.py:698
  (300 other events, 2734.1 us)
Sparse Core Ops, SparseCore 0:
  56.8 46.9 all-gather.6
  113.6 29.3 all-gather.8
  190.0 38.6 all-gather.10
  253.6 38.1 all-gather.12

commit v3 on v2

--- a/solution.py
+++ b/solution.py
@@ -128,6 +128,136 @@
     )(values)
 
 
+def last_kernel(dp, mp, n_all, n_mp, n_both, *refs):
+    n_in = n_all + n_mp + n_both
+    ins, outs, rest = refs[:n_in], refs[n_in : 2 * n_in], refs[2 * n_in :]
+    first, second = rest[:n_in], rest[n_in : n_in + n_all]
+    middle = rest[n_in + n_all : n_in + 2 * n_all]
+    send_one, recv_one, send_two, recv_two, own_sems = rest[n_in + 2 * n_all :]
+    me = {"dp": lax.axis_index("dp"), "mp": lax.axis_index("mp")}
+    sizes = {"dp": dp, "mp": mp}
+    peers = {
+        axis: [lax.rem(me[axis] + step, sizes[axis]) for step in range(1, sizes[axis])]
+        for axis in sizes
+    }
+    mesh_id = pl.DeviceIdType.MESH
+    barrier = pltpu.get_barrier_semaphore()
+    for axis in sizes:
+        for peer in peers[axis]:
+            pl.semaphore_signal(barrier, inc=1, device_id={axis: peer}, device_id_type=mesh_id)
+    pl.semaphore_wait(barrier, dp + mp - 2)
+
+    def send(source, slots, send_sem, recv_sems, index, axis, peer, step, mine):
+        return pltpu.make_async_remote_copy(
+            src_ref=source,
+            dst_ref=slots.at[mine],
+            send_sem=send_sem.at[index, step],
+            recv_sem=recv_sems.at[index, mine],
+            device_id={axis: peer},
+            device_id_type=mesh_id,
+        )
+
+    def source_of(t, axis, device):
+        return ins[t] if t >= n_all + n_mp else ins[t].at[device]
+
+    axes = ["dp"] * n_all + ["mp"] * (n_mp + n_both)
+    local = []
+    for t in range(n_in):
+        axis = axes[t]
+        for step, peer in enumerate(peers[axis]):
+            send(
+                source_of(t, axis, peer), first[t], send_one, recv_one, t, axis, peer, step, me[axis]
+            ).start()
+        copy = pltpu.make_async_copy(
+            source_of(t, axis, me[axis]), first[t].at[me[axis]], own_sems.at[t]
+        )
+        copy.start()
+        local.append(copy)
+
+    def arrived(slots, send_sem, recv_sems, index, axis):
+        for step, peer in enumerate(peers[axis]):
+            copy = send(slots.at[peer], slots, send_sem, recv_sems, index, axis, peer, step, peer)
+            copy.wait_send()
+            copy.wait_recv()
+
+    def total(slots, size):
+        value = slots[0].astype(F32)
+        for device in range(1, size):
+            value = value + slots[device].astype(F32)
+        return value
+
+    for t in range(n_all):
+        local[t].wait()
+        arrived(first[t], send_one, recv_one, t, "dp")
+        value = total(first[t], dp)
+        if t < n_all - 1:
+            rows = value.shape[0] // mp
+            for z in range(mp):
+                middle[t][z] = value[z * rows : (z + 1) * rows].astype(middle[t].dtype)
+        else:
+            middle[t][...] = value
+        for step, peer in enumerate(peers["mp"]):
+            source = middle[t].at[peer] if t < n_all - 1 else middle[t]
+            send(source, second[t], send_two, recv_two, t, "mp", peer, step, me["mp"]).start()
+        if t < n_all - 1:
+            second[t][me["mp"]] = middle[t][me["mp"]]
+        else:
+            second[t][me["mp"]] = value
+    for t in range(n_all, n_in):
+        local[t].wait()
+        arrived(first[t], send_one, recv_one, t, "mp")
+        outs[t][...] = total(first[t], mp)
+    for t in range(n_all):
+        arrived(second[t], send_two, recv_two, t, "mp")
+        outs[t][...] = total(second[t], mp)
+
+
+def last_sums(over_all, small, over_mp, both):
+    dp, mp = lax.axis_size("dp"), lax.axis_size("mp")
+    ins = list(over_all) + [small] + list(over_mp) + list(both)
+    n_all, n_mp, n_both = len(over_all) + 1, len(over_mp), len(both)
+    outs, first, second, middle = [], [], [], []
+    for t, value in enumerate(ins):
+        if t < n_all - 1:
+            rows, columns = value.shape[1] // mp, value.shape[2]
+            outs.append((rows, columns))
+            first.append(pltpu.VMEM(value.shape, value.dtype))
+            second.append(pltpu.VMEM((mp, rows, columns), value.dtype))
+            middle.append(pltpu.VMEM((mp, rows, columns), value.dtype))
+        elif t == n_all - 1:
+            outs.append(value.shape[1:])
+            first.append(pltpu.VMEM(value.shape, value.dtype))
+            second.append(pltpu.VMEM((mp,) + value.shape[1:], value.dtype))
+            middle.append(pltpu.VMEM(value.shape[1:], value.dtype))
+        elif t < n_all + n_mp:
+            outs.append(value.shape[1:])
+            first.append(pltpu.VMEM(value.shape, value.dtype))
+        else:
+            outs.append(value.shape)
+            first.append(pltpu.VMEM((mp,) + value.shape, value.dtype))
+    most = max(dp, mp)
+    dma = pltpu.SemaphoreType.DMA
+    return pl.pallas_call(
+        partial(last_kernel, dp, mp, n_all, n_mp, n_both),
+        out_shape=[jax.ShapeDtypeStruct(shape, F32) for shape in outs],
+        in_specs=[pl.BlockSpec(memory_space=pl.ANY)] * len(ins),
+        out_specs=[pl.BlockSpec(memory_space=pltpu.VMEM)] * len(ins),
+        scratch_shapes=first
+        + second
+        + middle
+        + [
+            dma((len(ins), most)),
+            dma((len(ins), most)),
+            dma((n_all, mp)),
+            dma((n_all, mp)),
+            dma((len(ins),)),
+        ],
+        compiler_params=pltpu.CompilerParams(
+            collective_id=3, has_side_effects=True, vmem_limit_bytes=48 << 20
+        ),
+    )(*ins)
+
+
 def conv_norm(hidden, segment, conv, vec, gain):
     taps = conv.shape[0]
     reach = taps // 2
@@ -684,20 +814,16 @@
     more, dmod_b = n2_pull(dot(dh, w1_full, NT))
     dx2 = dx2 + more
 
-    def send_dp(matrix):
-        parts = matrix.astype(BF).reshape(groups, matrix.shape[0] // groups, matrix.shape[1])
-        return lax.all_to_all(parts, "dp", 0, 0)
-
-    def total_of(received):
-        return jnp.sum(received.astype(F32), axis=0)
+    def for_dp(matrix):
+        return matrix.astype(BF).reshape(groups, matrix.shape[0] // groups, matrix.shape[1])
 
     def by_rank(matrix):
         return matrix.reshape(matrix.shape[0], shards, -1).transpose(1, 0, 2)
 
-    def send_mp(parts):
-        return lax.all_to_all(parts.astype(BF), "mp", 0, 0)
-
-    sent_w1, sent_w2 = send_dp(g_ff_w1), send_dp(g_ff_w2)
+    def scatter_dp(matrix):
+        return lax.psum_scatter(matrix.astype(BF), "dp", scatter_dimension=0, tiled=True)
+
+    sent_w1, sent_w2 = scatter_dp(g_ff_w1), scatter_dp(g_ff_w2)
 
     dx1, dmod_c, da, g_out_b = att_pull(dx2)
     da = da.astype(BF)
@@ -705,15 +831,14 @@
     do = to_channels(dot(da, out_full, NT).astype(BF))
     dqkv = attend_back(qkv, o_full, logs, do, seg_rows, seg_blocks, cos, sin, bounds, block)
     dqkv = exchange(dqkv, "mp").transpose(2, 0, 1, 3).reshape(rows, 3 * width)
+    sent_w1, sent_w2, dqkv = lax.optimization_barrier((sent_w1, sent_w2, dqkv))
     g_qkv_w = dot(n1, dqkv, TN)
     g_qkv_b = jnp.sum(dqkv.astype(F32), axis=0).reshape(shards, 3, cols)
     w_all = qkv_full.transpose(2, 0, 1, 3).reshape(width, 3 * width)
     more, dmod_d = n1_pull(dot(dqkv, w_all, NT))
     dx1 = dx1 + more
-    sent_w1, sent_w2, dx1 = lax.optimization_barrier((sent_w1, sent_w2, dx1))
-    ff_pair = jnp.concatenate([by_rank(total_of(sent_w1)), by_rank(total_of(sent_w2))], axis=2)
-    ff_pair = send_mp(ff_pair)
-    sent_qkv, sent_out = send_dp(g_qkv_w), send_dp(g_out_w)
+    ff_pair = jnp.concatenate([by_rank(sent_w1), by_rank(sent_w2)], axis=2)
+    sent_qkv, sent_out = scatter_dp(g_qkv_w), scatter_dp(g_out_w)
 
     dmod = dmod_a + dmod_b + dmod_c + dmod_d
 
@@ -733,61 +858,32 @@
         [conv_grad(spread_in, dy_a[GAP:-GAP], taps, group), conv_grad(y_a, dy_b[GAP:-GAP], taps, group)],
         axis=1,
     )
-    sent_qkv, sent_out, ff_pair, dx0_full = lax.optimization_barrier(
-        (sent_qkv, sent_out, ff_pair, dx0_full)
-    )
-    ff_pair = total_of(ff_pair)
-    ff_cols = ff_w1.shape[1]
-    o_ff_w1, o_ff_w2 = ff_pair[:, :ff_cols], ff_pair[:, ff_cols:].T
-    at_pair = jnp.concatenate([by_rank(total_of(sent_qkv)), by_rank(total_of(sent_out))], axis=2)
-    at_pair = send_mp(at_pair)
-    sent_conv = send_dp(g_conv)
+    sent_qkv, sent_out, dx0_full = lax.optimization_barrier((sent_qkv, sent_out, dx0_full))
+    at_pair = jnp.concatenate([by_rank(sent_qkv), by_rank(sent_out)], axis=2)
+    sent_conv = scatter_dp(g_conv)
 
     g_emb_bias = jnp.sum(dx0_full, axis=0)
     dx0 = dx0_full.astype(BF)
     mel_grad = to_all(dot(dx0, emb_mel, NT).astype(BF)).reshape(total, -1).astype(F32)
     g_emb = jnp.concatenate([dot(dx0, text, TN), dot(dx0, mel, TN)], axis=1)
-    sent_emb = send_dp(g_emb)
+    sent_emb = scatter_dp(g_emb)
     text_width = text.shape[1]
 
     dtext = jnp.pad(dot(dx0, emb_text, NT), ((HALO, HALO), (0, 0)))
     text_grads = [None] * blocks
     extra = dmod
-    sent_up, sent_down = [None] * blocks, [None] * blocks
     for b in reversed(range(blocks)):
         dtext, text_grads[b], summed = text_behind(kept[b], dtext, txt_up[b], txt_down[b], extra)
         if extra is not None:
             dmod_all = lax.all_gather(summed, "dp", tiled=True)
+            sent_conv, dtext = lax.optimization_barrier((sent_conv, dtext))
         extra = None
-        sent_up[b], sent_down[b] = send_dp(text_grads[b][3]), send_dp(text_grads[b][5])
-        if b == blocks - 1:
-            at_pair, sent_conv, sent_emb, dtext = lax.optimization_barrier(
-                (at_pair, sent_conv, sent_emb, dtext)
-            )
-            at_pair = total_of(at_pair)
-            g_emb = total_of(to_all(total_of(sent_emb).astype(BF)))
-    g_qkv = at_pair[:, : 3 * cols].reshape(-1, 3, cols).transpose(1, 0, 2)
-    o_qkv_w = jnp.concatenate([pair_merge(g_qkv[:2]), g_qkv[2:]], axis=0)
-    o_out_w = at_pair[:, 3 * cols :].T
-    o_pos_conv = total_of(sent_conv).T.reshape(2, taps, group, -1)
-    o_emb_text, o_emb_mel = g_emb[:, :text_width].T, g_emb[:, text_width:].T
+    sent_emb, dtext = lax.optimization_barrier((sent_emb, dtext))
     vocab = txt_table.shape[0]
     wide = -(-vocab // 128) * 128
     chosen = (ids[:, None] == jnp.arange(wide, dtype=jnp.int32)[None, :]).astype(BF)
-    sent_table = send_dp(dot(dtext, chosen, TN))
-
-    def rows_by_rank(matrix):
-        return matrix.reshape(shards, matrix.shape[0] // shards, -1)
-
-    ups = send_mp(rows_by_rank(jnp.concatenate([total_of(v) for v in sent_up], axis=1)))
-    downs = send_mp(
-        rows_by_rank(jnp.concatenate([total_of(v) for v in sent_down + [sent_table]], axis=1))
-    )
+    g_table = dot(dtext, chosen, TN)
     hidden_width = txt_up.shape[2]
-    downs = total_of(downs)
-    o_up = total_of(ups).T.reshape(blocks, text_width, -1)
-    o_down = downs[:, : blocks * hidden_width].T.reshape(blocks, hidden_width, -1)
-    o_table = downs[:, blocks * hidden_width :].T[:vocab]
 
     def placed(values):
         full = jnp.zeros((shards,) + values.shape, F32)
@@ -797,18 +893,58 @@
     g_qkv_b = jnp.concatenate([pair_merge(g_qkv_b[:, :2]), g_qkv_b[:, 2:]], axis=1)
     g_qkv_b = g_qkv_b.transpose(1, 0, 2).reshape(3, width)
     small = [
-        jnp.stack([g[0] for g in text_grads]), jnp.stack([g[1] for g in text_grads]),
-        jnp.stack([g[2] for g in text_grads]), jnp.stack([g[4] for g in text_grads]),
-        g_emb_bias, g_pos_bias, g_qkv_b, g_out_b, g_ff_b1, g_ff_b2,
+        (jnp.stack([g[0] for g in text_grads]), "both"),
+        (jnp.stack([g[1] for g in text_grads]), "both"),
+        (jnp.stack([g[2] for g in text_grads]), "both"),
+        (jnp.stack([g[4] for g in text_grads]), "both"),
+        (g_emb_bias, "dp"),
+        (g_pos_bias, "crossed"),
+        (g_qkv_b, "crossed"),
+        (g_out_b, "dp"),
+        (g_ff_b1, "crossed"),
+        (g_ff_b2, "dp"),
     ]
-    packed = jnp.concatenate([s.reshape(-1) for s in small]).reshape(8, -1)
-    packed = small_sum(small_sum(packed, "mp", 3), "dp", 4).reshape(-1)
+    packed = []
+    for value, kind in small:
+        lead = value.size // value.shape[-1]
+        if kind == "crossed":
+            value = value.reshape(lead, shards, groups, -1).transpose(2, 0, 1, 3)
+        else:
+            value = value.reshape(lead, groups, -1).transpose(1, 0, 2)
+        packed.append(value.reshape(groups, -1))
+    packed = jnp.concatenate(packed, axis=1)
+    length = packed.shape[1]
+    packed = jnp.pad(packed, ((0, 0), (0, -length % 1024))).reshape(groups, -1, 128)
+    table_sum, up0, up1, down0, down1, packed, ff_pair, at_pair, g_emb = last_sums(
+        [for_dp(g_table)]
+        + [for_dp(text_grads[b][3]) for b in range(blocks)]
+        + [for_dp(text_grads[b][5]) for b in range(blocks)],
+        packed,
+        [ff_pair, at_pair],
+        [sent_emb],
+    )
+    packed = packed.reshape(-1)
     unpacked, at = [], 0
-    for s in small:
-        unpacked.append(packed[at : at + s.size].reshape(s.shape))
-        at += s.size
-    both, crossed = place * shards + rank, rank * groups + place
-    everyone = groups * shards
+    for value, kind in small:
+        size = value.size // groups
+        piece = packed[at : at + size]
+        at += size
+        if kind == "dp":
+            unpacked.append(piece.reshape(value.shape[:-1] + (-1,)))
+        else:
+            piece = piece.reshape(value.size // value.shape[-1], shards, -1)
+            piece = lax.dynamic_slice_in_dim(piece, rank, 1, 1)
+            unpacked.append(piece.reshape(value.shape[:-1] + (-1,)))
+    o_table = table_sum[:, :vocab].T
+    o_up = jnp.stack([up0.T, up1.T])
+    o_down = jnp.stack([down0.T, down1.T])
+    ff_cols = ff_w1.shape[1]
+    o_ff_w1, o_ff_w2 = ff_pair[:, :ff_cols], ff_pair[:, ff_cols:].T
+    g_qkv = at_pair[:, : 3 * cols].reshape(-1, 3, cols).transpose(1, 0, 2)
+    o_qkv_w = jnp.concatenate([pair_merge(g_qkv[:2]), g_qkv[2:]], axis=0)
+    o_out_w = at_pair[:, 3 * cols :].T
+    o_pos_conv = sent_conv.astype(F32).T.reshape(2, taps, group, -1)
+    o_emb_text, o_emb_mel = g_emb[:, :text_width].T, g_emb[:, text_width:].T
 
     def own(values, index, parts):
         piece = values.shape[-1] // parts
@@ -825,30 +961,30 @@
         result,
         mel_grad,
         o_table,
-        own(unpacked[0], both, everyone),
-        own(unpacked[1], both, everyone),
-        own(unpacked[2], both, everyone),
+        unpacked[0],
+        unpacked[1],
+        unpacked[2],
         o_up,
-        own(unpacked[3], both, everyone),
+        unpacked[3],
         o_down,
         o_emb_mel,
         o_emb_text,
-        own(unpacked[4], place, groups),
+        unpacked[4],
         o_pos_conv,
-        own(unpacked[5], crossed, everyone),
+        unpacked[5],
         outer(sinusoid, dpre),
         own(jnp.stack([jnp.sum(dpre, axis=0), jnp.sum(de, axis=0)]), place, groups),
         outer(act_one, de),
         outer(act_two, dmod_all),
         own(jnp.sum(dmod_all, axis=0), place, groups),
         o_qkv_w,
-        own(unpacked[6], crossed, everyone),
+        unpacked[6],
         o_out_w,
-        own(unpacked[7], place, groups),
+        unpacked[7],
         o_ff_w1,
-        own(unpacked[8], crossed, everyone),
+        unpacked[8],
         o_ff_w2,
-        own(unpacked[9], place, groups),
+        unpacked[9],
     )
 
 

time: 1320 us -> 1070 us (0.81)
  waiting for transfers between devices: 429 us -> 232 us
  starting transfers between devices: 137 us -> 66.7 us
  Pallas kernels: 239 us -> 262 us
  other arithmetic: 149 us -> 131 us
  blocking collectives: 49.3 us -> 63.3 us
    all_to_all x15 -> x0, waiting for transfers between devices: 128 us -> none  [the longest x11 100 us: send_dp(): return lax.all_to_all(parts, 'dp', 0, 0)]
    pallas_call x0 -> x1, Pallas kernels: none -> 89 us  [last_sums(): pl.pallas_call(partial(last_kernel, dp, mp, n_all, n_mp, n_both), out_sha...]
    all_to_all x15 -> x0, starting transfers between devices: 69.4 us -> none  [the longest x11 52.8 us: send_dp(): return lax.all_to_all(parts, 'dp', 0, 0)]
    all_to_all x7, waiting for transfers between devices: 217 us -> 163 us  [exchange(): return lax.all_to_all(values, axis, 0, 0)]
    pallas_call x6 -> x4, Pallas kernels: 69.3 us -> 30 us  [small_sum(): pl.pallas_call(partial(sum_kernel, axis, size), out_shape=jax.ShapeDtypeS...]
    all_to_all x8 -> x7, waiting for transfers between devices: 82.3 us -> 48.5 us  [to_all(): lax.all_to_all(jnp.broadcast_to(piece[None], (size,) + piece.shape), axis...]
    reduce_sum x17 -> x0, other arithmetic: 30.8 us -> none  [the longest x16 28.2 us: total_of(): return jnp.sum(received.astype(F32), axis=0)]
    reduce_scatter x0 -> x6, waiting for transfers between devices: none -> 19.1 us  [scatter_dp(): lax.psum_scatter(matrix.astype(BF), 'dp', scatter_dimension=0, tiled=True)]
  transfers between devices with their start and end apart: 34 -> 24, of which waited for: 22 -> 10; matrix products, arithmetic and copies ran while one was open for 27% -> 27% of each run, Pallas kernels for 18% -> 16%
where the time goes in v3:
time: 1070 us; the launch traced here: 1060 us
  Pallas kernels  262 us (24%)
  waiting for transfers between devices  232 us (22%)
  matrix products  188 us (18%)
  other arithmetic  131 us (12%)
  local copies, waits for them, and re-layouts  104 us (10%)
  starting transfers between devices  66.7 us (6%)
  blocking collectives  63.3 us (6%)
  between operations  18.7 us (2%)
    all_to_all x7, waiting for transfers between devices, exchange(): return lax.all_to_all(values, axis, 0, 0)  163 us
    dot_general x42, matrix products, dot(): lax.dot_general(left.astype(BF), right.astype(BF), dims, preferred_elemen...  134 us
    pallas_call x1, Pallas kernels, last_sums(): pl.pallas_call(partial(last_kernel, dp, mp, n_all, n_mp, n_both), out_sha...  89 us
    all_to_all x7, waiting for transfers between devices, to_all(): lax.all_to_all(jnp.broadcast_to(piece[None], (size,) + piece.shape), axis...  48.5 us
    unnamed x612, local copies, waits for them, and re-layouts  47.4 us
    pallas_call x4, Pallas kernels, apply_conv(): pl.pallas_call(partial(conv_kernel, taps, turned), out_shape=jax.ShapeDty...  39.6 us
    pallas_call x1, Pallas kernels, attend_back(): pl.pallas_call(attend_back_kernel, out_shape=jax.ShapeDtypeStruct((shards...  39.3 us
    all_to_all x7, starting transfers between devices, to_all(): lax.all_to_all(jnp.broadcast_to(piece[None], (size,) + piece.shape), axis...  33 us
  transfers between devices with their start and end apart: 24, of which 10 were waited for; matrix products, arithmetic and copies ran while one was open for 27% of the time, Pallas kernels for 16%

profile of v3, /device:TPU:0, one launch (start us, length us, event | category | flops | bytes accessed | tf_op | source)
XLA Modules:
  0.0 1064.7 jit_solution(12584607819244985282)
XLA Ops:
  55.1 8.1 multiply_multiply_fusion.14
  111.2 21.1 %all-to-all-done = bf16[4,512,256]{2,1,0:T(8,128)(2,1)S(1)} async-done(((bf16[4,512,256]{2,1,0:T(8,128)(2,1)}), bf16[4,512,256]{2,1,0:T(8,128)(2,1)S(1)}, u32[]{:S(2)}, u32[]{:S(2)}) %all-to-all-start) | async-done | bytes 1048608 | tf_op jit(solution)/shard_map/all_to_all | solution.py:648
  140.9 9.9 shard_map.495
  153.6 9.9 shard_map.496
  176.3 7.0 all-to-all-done.7
  191.5 18.8 %all-to-all-done.1 = bf16[4,512,256]{2,1,0:T(8,128)(2,1)} async-done(((bf16[4,512,256]{2,1,0:T(8,128)(2,1)}), bf16[4,512,256]{2,1,0:T(8,128)(2,1)}, u32[]{:S(2)}, u32[]{:S(2)}) %all-to-all-start.1) | async-done | bytes 1048608 | tf_op jit(solution)/shard_map/all_to_all | solution.py:648
  219.7 6.8 add_convert_fusion.4
  254.9 66.7 %all-to-all-done.4.q_ref.k_ref.v_ref = bf16[4,3,512,256]{3,2,1,0:T(8,128)(2,1)} async-done(((bf16[4,3,512,256]{3,2,1,0:T(8,128)(2,1)}), bf16[4,3,512,256]{3,2,1,0:T(8,128)(2,1)}, u32[]{:S(2)}, u32[]{:S(2)}) %all-to-all-start.4) | async-done | bytes 3145760 | tf_op jit(solution)/shard_map/all_to_all | solution.py:648
  322.8 32.1 %shard_map.497 = (bf16[2048,256]{1,0:T(8,128)(2,1)S(1)}, f32[2048,256]{1,0:T(8,128)S(1)}, f32[2048,128]{1,0:T(8,128)S(1)}) custom-call(s32[8,2]{1,0:T(8,128)S(1)} %copy.414.bounds, bf16[4,3,512,256]{3,2,1,0:T(8,128)(2,1)} %all-to-all-done.4.q_ref.k_ref.v_ref, bf16[4,3,512,256]{3,2,1,0:T(8,128)(2,1)} %all-to-all-done.4.q_ref.k_ref.v_ref, ...), custom_call_target="tpu_custom_call" | custom-call | flops 8589934592 | bytes 8388608 | tf_op jit(solution)/shard_map/pallas_call | solution.py:535
  363.2 23.1 %all-to-all-done.5 = bf16[4,512,256]{2,1,0:T(8,128)(2,1)} async-done(((bf16[4,512,256]{2,1,0:T(8,128)(2,1)}), bf16[4,512,256]{2,1,0:T(8,128)(2,1)}, u32[]{:S(2)}, u32[]{:S(2)}) %all-to-all-start.5) | async-done | bytes 1048608 | tf_op jit(solution)/shard_map/all_to_all | solution.py:648
  393.4 8.3 fusion.309
  401.7 7.8 fusion.299
  423.7 8.9 fusion.62
  438.0 28.6 %all_to_all.75 = bf16[4,512,256]{2,1,0:T(8,128)(2,1)} all-to-all(bf16[4,512,256]{2,1,0:T(8,128)(2,1)S(1)} %bitcast.534), channel_id=1, replica_groups=mesh['dp'=8,'mp'=4] {'mp'}, dimensions={0} | all-to-all | bytes 2097152 | tf_op jit(solution)/shard_map/all_to_all | solution.py:648
  474.1 7.6 convolution_convert_fusion.1
  485.4 39.3 %shard_map.498 = bf16[4,3,512,256]{3,2,1,0:T(8,128)(2,1)} custom-call(s32[8,2]{1,0:T(8,128)S(1)} %copy.414.bounds, bf16[4,3,512,256]{3,2,1,0:T(8,128)(2,1)} %all-to-all-done.4.q_ref.k_ref.v_ref, bf16[4,3,512,256]{3,2,1,0:T(8,128)(2,1)} %all-to-all-done.4.q_ref.k_ref.v_ref, bf16[4,3,512,256]{3,2,1,0:T(8,128)(2,1)} %all-to-all-done.4.q_ref.k_ref.v_ref, ...), custom_call_target="tpu_custom_call" | custom-call | flops 21474836480 | bytes 16777216 | tf_op jit(solution)/shard_map/pallas_call | solution.py:636
  524.8 41.5 %all-to-all-done.9 = bf16[4,512,1024]{2,1,0:T(8,128)(2,1)} async-done(((bf16[4,512,1024]{2,1,0:T(8,128)(2,1)}), bf16[4,512,1024]{2,1,0:T(8,128)(2,1)}, u32[]{:S(2)}, u32[]{:S(2)}) %all-to-all-start.9) | async-done | bytes 4194336 | tf_op jit(solution)/shard_map/all_to_all | solution.py:675
  571.0 23.7 %all-gather = s32[8,1,4]{2,1,0:T(1,128)S(1)} all-gather(s32[1,1,4]{2,1,0:T(1,128)S(1)} %bitcast.812), channel_id=1, replica_groups=mesh['dp'=8,'mp'=4] {'dp'}, dimensions={0}, use_global_device_ids=true | all-gather | bytes 144 | tf_op jit(solution)/shard_map/all_gather | solution.py:692
  613.8 6.9 bitcast_convert_fusion
  620.6 20.5 %all-to-all-done.11 = bf16[4,3,512,256]{3,2,1,0:T(8,128)(2,1)} async-done(((bf16[4,3,512,256]{3,2,1,0:T(8,128)(2,1)}), bf16[4,3,512,256]{3,2,1,0:T(8,128)(2,1)}, u32[]{:S(2)}, u32[]{:S(2)}) %all-to-all-start.11) | async-done | bytes 3145760 | tf_op jit(solution)/shard_map/all_to_all | solution.py:648
  646.0 9.4 fusion.85
  684.7 13.3 %all-to-all-done.12 = bf16[4,512,256]{2,1,0:T(8,128)(2,1)} async-done(((bf16[4,512,256]{2,1,0:T(8,128)(2,1)}), bf16[4,512,256]{2,1,0:T(8,128)(2,1)}, u32[]{:S(2)}, u32[]{:S(2)}) %all-to-all-start.12) | async-done | bytes 1048608 | tf_op jit(solution)/shard_map/all_to_all | solution.py:648
  698.0 7.0 fusion.318
  707.7 9.8 shard_map.499
  722.3 10.0 shard_map.500
  741.5 15.8 %shard_map.501 = f32[256,1984]{1,0:T(8,128)S(1)} custom-call(f32[2144,256]{1,0:T(8,128)} %copy-done.4, f32[2112,256]{1,0:T(8,128)S(1)} %copy-done.6), custom_call_target="tpu_custom_call" | custom-call | flops 8581545984 | bytes 8388608 | tf_op jit(solution)/shard_map/pallas_call | solution.py:432
  761.5 15.8 %shard_map.502 = f32[256,1984]{1,0:T(8,128)S(1)} custom-call(f32[2144,256]{1,0:T(8,128)} %copy-done.5, f32[2112,256]{1,0:T(8,128)S(1)} %copy-done.7), custom_call_target="tpu_custom_call" | custom-call | flops 8581545984 | bytes 8388608 | tf_op jit(solution)/shard_map/pallas_call | solution.py:432
  793.7 11.0 %shard_map.503 = f32[4,7168]{1,0:T(4,128)S(1)} custom-call(f32[4,7168]{1,0:T(4,128)S(1)} %pad_maximum_fusion.9.x_ref), custom_call_target="tpu_custom_call" | custom-call | tf_op jit(solution)/shard_map/pallas_call | solution.py:115
  820.2 16.4 %reduce-scatter.17.cloned.1.call-done = bf16[32,3968]{1,0:T(8,128)(2,1)} async-done(((bf16[256,3968]{1,0:T(8,128)(2,1)}), bf16[32,3968]{1,0:T(8,128)(2,1)}) %reduce-scatter.17.cloned.1.call-update) | async-done | bytes 253968 | tf_op jit(solution)/shard_map/reduce_scatter | solution.py:824
  872.1 11.1 %all-gather.1 = f32[8,4,6144]{2,1,0:T(4,128)S(1)} all-gather(f32[1,4,6144]{2,1,0:T(4,128)S(1)} %slice_bitcast_fusion.33), channel_id=1, replica_groups=mesh['dp'=8,'mp'=4] {'dp'}, dimensions={0}, use_global_device_ids=true | all-gather | bytes 884736 | tf_op jit(solution)/shard_map/all_gather | solution.py:878
  883.7 8.7 fusion.71
  947.6 89.0 %shard_map.505 = (f32[16,2560]{1,0:T(8,128)S(1)}, f32[32,512]{1,0:T(8,128)S(1)}, f32[32,512]{1,0:T(8,128)S(1)}, f32[16,1024]{1,0:T(8,128)S(1)}, f32[16,1024]{1,0...) custom-call(bf16[8,64,2560]{2,1,0:T(8,128)(2,1)} %bitcast.538, ...), custom_call_target="tpu_custom_call" | custom-call | tf_op jit(solution)/shard_map/pallas_call | solution.py:240
  (1004 shorter events, 432.2 us)
Async XLA Ops:
  11.0 38.0 %all-to-all-start.2 = ((bf16[4,3,128,256]{2,3,1,0:T(8,128)(2,1)}), bf16[4,3,128,256]{2,3,1,0:T(8,128)(2,1)}, u32[]{:S(2)}, u32[]{:S(2)}) async-start(bf16[4,3,128,256]{2,3,1,0:T(8,128)(2,1)} %broadcast_in_dim.480), calls=%async_computation.2 | async-start | bytes 1572864 | tf_op jit(solution)/shard_map/all_to_all | solution.py:675
  18.0 65.3 %copy-start.189 = (s32[4]{0:T(128)}, s32[4]{0:T(128)S(1)}, u32[]{:S(2)}) copy-start(s32[4]{0:T(128)S(1)} %select_reduce_fusion.4) | copy-start | bytes 52
  49.8 55.4 %all-to-all-start.6 = ((bf16[4,32,1024]{2,1,0:T(8,128)(2,1)}), bf16[4,32,1024]{2,1,0:T(8,128)(2,1)S(1)}, u32[]{:S(2)}, u32[]{:S(2)}) async-start(bf16[4,32,1024]{2,1,0:T(8,128)(2,1)} %broadcast_in_dim.483), calls=%async_computation.6 | async-start | bytes 524288 | tf_op jit(solution)/shard_map/all_to_all | solution.py:675
  54.3 172.1 %all-gather.7.cloned.1.call-start = ((), (), s32[]{:S(2)}) async-start(), calls=%async_computation.21 | async-start | bytes 7077888 | tf_op jit(solution)/shard_map/all_gather | solution.py:678
  92.0 81.4 %copy-start.120 = (pred[2048]{0:T(1024)(128)(4,1)}, pred[2048]{0:T(1024)(128)(4,1)S(1)}, u32[]{:S(2)}) copy-start(pred[2048]{0:T(1024)(128)(4,1)S(1)} %get-tuple-element.587) | copy-start | bytes 6148
  92.0 81.4 %copy-start.122 = (pred[2048]{0:T(1024)(128)(4,1)}, pred[2048]{0:T(1024)(128)(4,1)S(1)}, u32[]{:S(2)}) copy-start(pred[2048]{0:T(1024)(128)(4,1)S(1)} %get-tuple-element.588) | copy-start | bytes 6148
  103.8 69.7 %copy-start.124 = (pred[2048]{0:T(1024)(128)(4,1)}, pred[2048]{0:T(1024)(128)(4,1)S(1)}, u32[]{:S(2)}) copy-start(pred[2048]{0:T(1024)(128)(4,1)S(1)} %get-tuple-element.589) | copy-start | bytes 6148
  103.8 69.7 %copy-start.126 = (pred[2048]{0:T(1024)(128)(4,1)}, pred[2048]{0:T(1024)(128)(4,1)S(1)}, u32[]{:S(2)}) copy-start(pred[2048]{0:T(1024)(128)(4,1)S(1)} %get-tuple-element.590) | copy-start | bytes 6148
  105.2 27.1 %all-to-all-start = ((bf16[4,512,256]{2,1,0:T(8,128)(2,1)}), bf16[4,512,256]{2,1,0:T(8,128)(2,1)S(1)}, u32[]{:S(2)}, u32[]{:S(2)}) async-start(bf16[4,512,256]{2,1,0:T(8,128)(2,1)} %bitcast.510), calls=%async_computation | async-start | bytes 2097152 | tf_op jit(solution)/shard_map/all_to_all | solution.py:648
  110.0 253.2 %all-gather.9.cloned.1.call-start = ((), (), s32[]{:S(2)}) async-start(), calls=%async_computation.22 | async-start | bytes 2359296 | tf_op jit(solution)/shard_map/all_gather | solution.py:678
  133.0 31.8 %all-to-all-start.3 = ((f32[4,5,256]{2,1,0:T(8,128)}), f32[4,5,256]{2,1,0:T(8,128)S(1)}, u32[]{:S(2)}, u32[]{:S(2)}) async-start(f32[4,5,256]{2,1,0:T(8,128)} %broadcast_in_dim.481), calls=%async_computation.3 | async-start | bytes 65536 | tf_op jit(solution)/shard_map/all_to_all | solution.py:675
  165.7 17.6 %all-to-all-start.7 = ((bf16[4,128,512]{1,2,0:T(8,128)(2,1)}), bf16[4,128,512]{1,2,0:T(8,128)(2,1)S(1)}, u32[]{:S(2)}, u32[]{:S(2)}) async-start(bf16[4,128,512]{1,2,0:T(8,128)(2,1)} %broadcast_in_dim.484), calls=%async_computation.7 | async-start | bytes 1048576 | tf_op jit(solution)/shard_map/all_to_all | solution.py:675
  183.3 27.1 %all-to-all-start.1 = ((bf16[4,512,256]{2,1,0:T(8,128)(2,1)}), bf16[4,512,256]{2,1,0:T(8,128)(2,1)}, u32[]{:S(2)}, u32[]{:S(2)}) async-start(bf16[4,512,256]{2,1,0:T(8,128)(2,1)} %bitcast.58), calls=%async_computation.1 | async-start | bytes 2097152 | tf_op jit(solution)/shard_map/all_to_all | solution.py:648
  187.5 205.9 %all-gather.11.cloned.1.call-start = ((), (), s32[]{:S(2)}) async-start(), calls=%async_computation.23 | async-start | bytes 4718592 | tf_op jit(solution)/shard_map/all_gather | solution.py:685
  211.2 35.5 %all-to-all-start.8 = ((bf16[4,64,1024]{2,1,0:T(8,128)(2,1)}), bf16[4,64,1024]{2,1,0:T(8,128)(2,1)S(1)}, u32[]{:S(2)}, u32[]{:S(2)}) async-start(bf16[4,64,1024]{2,1,0:T(8,128)(2,1)} %broadcast_in_dim.485), calls=%async_computation.8 | async-start | bytes 1048576 | tf_op jit(solution)/shard_map/all_to_all | solution.py:675
  247.5 74.1 %all-to-all-start.4 = ((bf16[4,3,512,256]{3,2,1,0:T(8,128)(2,1)}), bf16[4,3,512,256]{3,2,1,0:T(8,128)(2,1)}, u32[]{:S(2)}, u32[]{:S(2)}) async-start(bf16[4,3,512,256]{3,2,1,0:T(8,128)(2,1)} %bitcast.128), calls=%async_computation.4 | async-start | bytes 6291456 | tf_op jit(solution)/shard_map/all_to_all | solution.py:648
  252.6 149.2 %all-gather.13.cloned.1.call-start = ((), (), s32[]{:S(2)}) async-start(), calls=%async_computation.24 | async-start | bytes 4718592 | tf_op jit(solution)/shard_map/all_gather | solution.py:678
  358.3 28.0 %all-to-all-start.5 = ((bf16[4,512,256]{2,1,0:T(8,128)(2,1)}), bf16[4,512,256]{2,1,0:T(8,128)(2,1)}, u32[]{:S(2)}, u32[]{:S(2)}) async-start(bf16[4,512,256]{2,1,0:T(8,128)(2,1)} %bitcast.517), calls=%async_computation.5 | async-start | bytes 2097152 | tf_op jit(solution)/shard_map/all_to_all | solution.py:648
  362.7 283.3 %reduce-scatter.7.cloned.1.call-start = ((), (), s32[]{:S(2)}) async-start(), calls=%async_computation.25 | async-start | bytes 4718592 | tf_op jit(solution)/shard_map/reduce_scatter | solution.py:824
  469.1 97.2 %all-to-all-start.9 = ((bf16[4,512,1024]{2,1,0:T(8,128)(2,1)}), bf16[4,512,1024]{2,1,0:T(8,128)(2,1)}, u32[]{:S(2)}, u32[]{:S(2)}) async-start(bf16[4,512,1024]{2,1,0:T(8,128)(2,1)} %broadcast_in_dim.486), calls=%async_computation.9 | async-start | bytes 8388608 | tf_op jit(solution)/shard_map/all_to_all | solution.py:675
  474.0 172.0 %reduce-scatter.9.cloned.1.call-start = ((), (), s32[]{:S(2)}) async-start(), calls=%async_computation.26 | async-start | bytes 4718592 | tf_op jit(solution)/shard_map/reduce_scatter | solution.py:824
  524.8 70.0 %copy-start.259 = (f32[128]{0:T(128)S(1)}, f32[128]{0:T(128)}, u32[]{:S(2)}) copy-start(f32[128]{0:T(128)} %copy-done.258) | copy-start | bytes 1540
  524.8 70.2 %copy-start.85 = (bf16[256,1024]{1,0:T(8,128)(2,1)S(1)}, bf16[256,1024]{1,0:T(8,128)(2,1)}, u32[]{:S(2)}) copy-start(bf16[256,1024]{1,0:T(8,128)(2,1)} %param.50) | copy-start | bytes 1572868
  524.8 70.4 %copy-start.155 = (f32[1,1024]{1,0:T(1,128)S(1)}, f32[1,1024]{1,0:T(1,128)}, u32[]{:S(2)}) copy-start(f32[1,1024]{1,0:T(1,128)} %copy-done.154) | copy-start | bytes 12292
  566.3 74.9 %all-to-all-start.11 = ((bf16[4,3,512,256]{3,2,1,0:T(8,128)(2,1)}), bf16[4,3,512,256]{3,2,1,0:T(8,128)(2,1)}, u32[]{:S(2)}, u32[]{:S(2)}) async-start(bf16[4,3,512,256]{3,2,1,0:T(8,128)(2,1)} %shard_map.498), calls=%async_computation.13 | async-start | bytes 6291456 | tf_op jit(solution)/shard_map/all_to_all | solution.py:648
  571.0 214.2 %reduce-scatter.13.cloned.1.call-start = ((), (), s32[]{:S(2)}) async-start(), calls=%async_computation.28 | async-start | bytes 2359296 | tf_op jit(solution)/shard_map/reduce_scatter | solution.py:824
  605.0 180.1 %reduce-scatter.11.cloned.1.call-start = ((), (), s32[]{:S(2)}) async-start(), calls=%async_computation.27 | async-start | bytes 7077888 | tf_op jit(solution)/shard_map/reduce_scatter | solution.py:824
  668.3 29.7 %all-to-all-start.12 = ((bf16[4,512,256]{2,1,0:T(8,128)(2,1)}), bf16[4,512,256]{2,1,0:T(8,128)(2,1)}, u32[]{:S(2)}, u32[]{:S(2)}) async-start(bf16[4,512,256]{2,1,0:T(8,128)(2,1)} %bitcast.533), calls=%async_computation.16 | async-start | bytes 2097152 | tf_op jit(solution)/shard_map/all_to_all | solution.py:648
  735.5 44.2 %all-to-all-start.13 = ((bf16[4,512,256]{2,1,0:T(8,128)(2,1)}), bf16[4,512,256]{2,1,0:T(8,128)(2,1)}, u32[]{:S(2)}, u32[]{:S(2)}) async-start(bf16[4,512,256]{2,1,0:T(8,128)(2,1)} %bitcast.531), calls=%async_computation.17 | async-start | bytes 2097152 | tf_op jit(solution)/shard_map/all_to_all | solution.py:648
  739.8 96.8 %reduce-scatter.17.cloned.1.call-start = ((), (), s32[]{:S(2)}) async-start(), calls=%async_computation.30 | async-start | bytes 2285568 | tf_op jit(solution)/shard_map/reduce_scatter | solution.py:824
  779.3 164.4 %reduce-scatter.15.cloned.1.call-start = ((), (), s32[]{:S(2)}) async-start(), calls=%async_computation.29 | async-start | bytes 1769472 | tf_op jit(solution)/shard_map/reduce_scatter | solution.py:824
  908.8 29.4 %all-to-all-start.14 = ((bf16[4,512,200]{1,2,0:T(8,128)(2,1)}), bf16[4,512,200]{1,2,0:T(8,128)(2,1)}, u32[]{:S(2)}, u32[]{:S(2)}) async-start(bf16[4,512,200]{1,2,0:T(8,128)(2,1)} %broadcast_in_dim.491), calls=%async_computation.18 | async-start | bytes 1638400 | tf_op jit(solution)/shard_map/all_to_all | solution.py:675
  (286 other events, 2284.0 us)
Sparse Core Ops, SparseCore 0:
  57.0 48.1 all-gather.6
  113.3 29.3 all-gather.8
  191.7 38.8 all-gather.10
  255.6 38.2 all-gather.12
  423.2 64.2 reduce-scatter.6
  491.1 58.4 reduce-scatter.8
  605.2 42.2 reduce-scatter.12
  664.9 76.2 reduce-scatter.10
  779.4 57.1 reduce-scatter.16
  905.2 38.4 reduce-scatter.14

commit v4 on v3

--- a/solution.py
+++ b/solution.py
@@ -128,132 +128,172 @@
     )(values)
 
 
-def last_kernel(dp, mp, n_all, n_mp, n_both, *refs):
-    n_in = n_all + n_mp + n_both
-    ins, outs, rest = refs[:n_in], refs[n_in : 2 * n_in], refs[2 * n_in :]
-    first, second = rest[:n_in], rest[n_in : n_in + n_all]
-    middle = rest[n_in + n_all : n_in + 2 * n_all]
-    send_one, recv_one, send_two, recv_two, own_sems = rest[n_in + 2 * n_all :]
-    me = {"dp": lax.axis_index("dp"), "mp": lax.axis_index("mp")}
-    sizes = {"dp": dp, "mp": mp}
-    peers = {
-        axis: [lax.rem(me[axis] + step, sizes[axis]) for step in range(1, sizes[axis])]
-        for axis in sizes
-    }
+def last_kernel(dp, mp, n_all, n_mp, n_both, n_gather, *refs):
+    n_in = n_all + n_mp + n_both + n_gather
+    ins, outs, rest = refs[:n_in], refs[n_in : 2 * n_in], list(refs[2 * n_in :])
+
+    def take(count):
+        return [rest.pop(0) for _ in range(count)]
+
+    own, pair, joint, chip_slots, middle, slots = (
+        take(n_all), take(n_all), take(n_all), take(n_all), take(n_all), take(n_in)
+    )
+    pair_send, pair_recv, chip_send, chip_recv, mp_send, mp_recv, own_sems = rest
+    me, z = lax.axis_index("dp"), lax.axis_index("mp")
+    chips = dp // 2
+    core, chip = lax.rem(me, 2), me // 2
+    partner = me + 1 - 2 * core
+    other_chips = [lax.rem(chip + step, chips) for step in range(1, chips)]
+    other_z = [lax.rem(z + step, mp) for step in range(1, mp)]
     mesh_id = pl.DeviceIdType.MESH
     barrier = pltpu.get_barrier_semaphore()
-    for axis in sizes:
-        for peer in peers[axis]:
-            pl.semaphore_signal(barrier, inc=1, device_id={axis: peer}, device_id_type=mesh_id)
-    pl.semaphore_wait(barrier, dp + mp - 2)
-
-    def send(source, slots, send_sem, recv_sems, index, axis, peer, step, mine):
+    greeted = (
+        [{"dp": partner}]
+        + [{"dp": 2 * q + core} for q in other_chips]
+        + [{"mp": peer} for peer in other_z]
+    )
+    for device in greeted:
+        pl.semaphore_signal(barrier, inc=1, device_id=device, device_id_type=mesh_id)
+    pl.semaphore_wait(barrier, chips + mp - 1)
+
+    def to_partner(t):
+        return pltpu.make_async_remote_copy(
+            src_ref=ins[t].at[:, 1 - core],
+            dst_ref=pair[t],
+            send_sem=pair_send.at[t],
+            recv_sem=pair_recv.at[t],
+            device_id={"dp": partner},
+            device_id_type=mesh_id,
+        )
+
+    def to_chip(t, step, mine):
+        q = other_chips[step]
+        return pltpu.make_async_remote_copy(
+            src_ref=joint[t].at[q],
+            dst_ref=chip_slots[t].at[mine],
+            send_sem=chip_send.at[t, step],
+            recv_sem=chip_recv.at[t, mine],
+            device_id={"dp": 2 * q + core},
+            device_id_type=mesh_id,
+        )
+
+    def to_z(t, step, mine):
+        peer = other_z[step]
+        if t < n_all - 1:
+            source = middle[t].at[peer]
+        elif t == n_all - 1:
+            source = middle[t]
+        else:
+            source = ins[t].at[peer] if t < n_all + n_mp else ins[t]
         return pltpu.make_async_remote_copy(
             src_ref=source,
-            dst_ref=slots.at[mine],
-            send_sem=send_sem.at[index, step],
-            recv_sem=recv_sems.at[index, mine],
-            device_id={axis: peer},
+            dst_ref=slots[t].at[mine],
+            send_sem=mp_send.at[t, step],
+            recv_sem=mp_recv.at[t, mine],
+            device_id={"mp": peer},
             device_id_type=mesh_id,
         )
 
-    def source_of(t, axis, device):
-        return ins[t] if t >= n_all + n_mp else ins[t].at[device]
-
-    axes = ["dp"] * n_all + ["mp"] * (n_mp + n_both)
     local = []
-    for t in range(n_in):
-        axis = axes[t]
-        for step, peer in enumerate(peers[axis]):
-            send(
-                source_of(t, axis, peer), first[t], send_one, recv_one, t, axis, peer, step, me[axis]
-            ).start()
-        copy = pltpu.make_async_copy(
-            source_of(t, axis, me[axis]), first[t].at[me[axis]], own_sems.at[t]
-        )
+    for t in range(n_all):
+        to_partner(t).start()
+        copy = pltpu.make_async_copy(ins[t].at[:, core], own[t], own_sems.at[t])
         copy.start()
         local.append(copy)
-
-    def arrived(slots, send_sem, recv_sems, index, axis):
-        for step, peer in enumerate(peers[axis]):
-            copy = send(slots.at[peer], slots, send_sem, recv_sems, index, axis, peer, step, peer)
+    for t in range(n_all, n_in):
+        for step in range(mp - 1):
+            to_z(t, step, z).start()
+        source = ins[t].at[z] if t < n_all + n_mp else ins[t]
+        copy = pltpu.make_async_copy(source, slots[t].at[z], own_sems.at[t])
+        copy.start()
+        local.append(copy)
+
+    def total(ref, size):
+        value = ref[0].astype(F32)
+        for device in range(1, size):
+            value = value + ref[device].astype(F32)
+        return value
+
+    for t in range(n_all):
+        local[t].wait()
+        copy = to_partner(t)
+        copy.wait_send()
+        copy.wait_recv()
+        for q in range(chips):
+            value = own[t][q].astype(F32) + pair[t][q].astype(F32)
+            joint[t][q] = value.astype(joint[t].dtype)
+        for step in range(chips - 1):
+            to_chip(t, step, chip).start()
+        chip_slots[t][chip] = joint[t][chip]
+    for t in range(n_all):
+        for step in range(chips - 1):
+            copy = to_chip(t, step, other_chips[step])
             copy.wait_send()
             copy.wait_recv()
-
-    def total(slots, size):
-        value = slots[0].astype(F32)
-        for device in range(1, size):
-            value = value + slots[device].astype(F32)
-        return value
-
-    for t in range(n_all):
-        local[t].wait()
-        arrived(first[t], send_one, recv_one, t, "dp")
-        value = total(first[t], dp)
+        value = total(chip_slots[t], chips)
         if t < n_all - 1:
             rows = value.shape[0] // mp
-            for z in range(mp):
-                middle[t][z] = value[z * rows : (z + 1) * rows].astype(middle[t].dtype)
+            for device in range(mp):
+                part = value[device * rows : (device + 1) * rows]
+                middle[t][device] = part.astype(middle[t].dtype)
+            slots[t][z] = middle[t][z]
         else:
             middle[t][...] = value
-        for step, peer in enumerate(peers["mp"]):
-            source = middle[t].at[peer] if t < n_all - 1 else middle[t]
-            send(source, second[t], send_two, recv_two, t, "mp", peer, step, me["mp"]).start()
-        if t < n_all - 1:
-            second[t][me["mp"]] = middle[t][me["mp"]]
+            slots[t][z] = value
+        for step in range(mp - 1):
+            to_z(t, step, z).start()
+    for t in list(range(n_all, n_in)) + list(range(n_all)):
+        if t >= n_all:
+            local[t].wait()
+        for step in range(mp - 1):
+            copy = to_z(t, step, other_z[step])
+            copy.wait_send()
+            copy.wait_recv()
+        if t < n_in - n_gather:
+            outs[t][...] = total(slots[t], mp)
         else:
-            second[t][me["mp"]] = value
-    for t in range(n_all, n_in):
-        local[t].wait()
-        arrived(first[t], send_one, recv_one, t, "mp")
-        outs[t][...] = total(first[t], mp)
-    for t in range(n_all):
-        arrived(second[t], send_two, recv_two, t, "mp")
-        outs[t][...] = total(second[t], mp)
-
-
-def last_sums(over_all, small, over_mp, both):
+            outs[t][...] = slots[t][...].astype(F32)
+
+
+def last_sums(over_all, small, over_mp, both, gathered):
     dp, mp = lax.axis_size("dp"), lax.axis_size("mp")
-    ins = list(over_all) + [small] + list(over_mp) + list(both)
-    n_all, n_mp, n_both = len(over_all) + 1, len(over_mp), len(both)
-    outs, first, second, middle = [], [], [], []
+    chips = dp // 2
+    everywhere = [v.reshape((chips, 2) + v.shape[1:]) for v in list(over_all) + [small]]
+    ins = everywhere + list(over_mp) + list(both) + list(gathered)
+    n_all, n_mp, n_both, n_gather = len(everywhere), len(over_mp), len(both), len(gathered)
+    halves = [pltpu.VMEM((chips,) + v.shape[2:], v.dtype) for v in everywhere]
+    outs, middle, slots = [], [], []
     for t, value in enumerate(ins):
         if t < n_all - 1:
-            rows, columns = value.shape[1] // mp, value.shape[2]
-            outs.append((rows, columns))
-            first.append(pltpu.VMEM(value.shape, value.dtype))
-            second.append(pltpu.VMEM((mp, rows, columns), value.dtype))
-            middle.append(pltpu.VMEM((mp, rows, columns), value.dtype))
+            shape = (value.shape[2] // mp, value.shape[3])
+            middle.append(pltpu.VMEM((mp,) + shape, value.dtype))
         elif t == n_all - 1:
-            outs.append(value.shape[1:])
-            first.append(pltpu.VMEM(value.shape, value.dtype))
-            second.append(pltpu.VMEM((mp,) + value.shape[1:], value.dtype))
-            middle.append(pltpu.VMEM(value.shape[1:], value.dtype))
-        elif t < n_all + n_mp:
-            outs.append(value.shape[1:])
-            first.append(pltpu.VMEM(value.shape, value.dtype))
+            shape = value.shape[2:]
+            middle.append(pltpu.VMEM(shape, value.dtype))
         else:
-            outs.append(value.shape)
-            first.append(pltpu.VMEM((mp,) + value.shape, value.dtype))
-    most = max(dp, mp)
+            shape = value.shape[1:] if t < n_all + n_mp else value.shape
+        slots.append(pltpu.VMEM((mp,) + shape, value.dtype))
+        outs.append((mp,) + shape if t >= len(ins) - n_gather else shape)
     dma = pltpu.SemaphoreType.DMA
     return pl.pallas_call(
-        partial(last_kernel, dp, mp, n_all, n_mp, n_both),
+        partial(last_kernel, dp, mp, n_all, n_mp, n_both, n_gather),
         out_shape=[jax.ShapeDtypeStruct(shape, F32) for shape in outs],
         in_specs=[pl.BlockSpec(memory_space=pl.ANY)] * len(ins),
         out_specs=[pl.BlockSpec(memory_space=pltpu.VMEM)] * len(ins),
-        scratch_shapes=first
-        + second
+        scratch_shapes=halves * 4
         + middle
+        + slots
         + [
-            dma((len(ins), most)),
-            dma((len(ins), most)),
-            dma((n_all, mp)),
-            dma((n_all, mp)),
+            dma((n_all,)),
+            dma((n_all,)),
+            dma((n_all, chips)),
+            dma((n_all, chips)),
+            dma((len(ins), mp)),
+            dma((len(ins), mp)),
             dma((len(ins),)),
         ],
         compiler_params=pltpu.CompilerParams(
-            collective_id=3, has_side_effects=True, vmem_limit_bytes=48 << 20
+            collective_id=3, has_side_effects=True, vmem_limit_bytes=56 << 20
         ),
     )(*ins)
 
@@ -445,15 +485,51 @@
     )(spread_rows, grads)
 
 
+LANES = 128
+
+
 def pair_split(columns):
-    lead = columns.shape[:-1]
-    pairs = columns.reshape(*lead, columns.shape[-1] // 2, 2)
-    return jnp.concatenate([pairs[..., 0], pairs[..., 1]], axis=-1)
+    pairs = columns.reshape(*columns.shape[:-1], -1, LANES // 2, 2)
+    return jnp.swapaxes(pairs, -1, -2).reshape(columns.shape)
 
 
 def pair_merge(columns):
-    half = columns.shape[-1] // 2
-    return jnp.stack([columns[..., :half], columns[..., half:]], axis=-1).reshape(columns.shape)
+    pairs = columns.reshape(*columns.shape[:-1], -1, 2, LANES // 2)
+    return jnp.swapaxes(pairs, -1, -2).reshape(columns.shape)
+
+
+def project_kernel(x_ref, w_ref, b_ref, cos_ref, sin_ref, *out_refs):
+    cos, sin = cos_ref[...], sin_ref[...]
+    for p in range(3):
+        value = jnp.dot(x_ref[...], w_ref[p], preferred_element_type=F32) + b_ref[p : p + 1, :]
+        for at, out_ref in enumerate(out_refs):
+            piece = value[:, at * LANES : (at + 1) * LANES]
+            if p < 2:
+                piece = piece * cos + pltpu.roll(piece, LANES // 2, 1) * sin
+            out_ref[p] = piece.astype(BF)
+
+
+def project(normed, weight, bias, cos, sin):
+    rows = normed.shape[0]
+    shards, _, width, cols = weight.shape
+    parts = cols // LANES
+    return pl.pallas_call(
+        project_kernel,
+        out_shape=[jax.ShapeDtypeStruct((shards, 3, rows, LANES), BF)] * parts,
+        grid=(shards,),
+        in_specs=[
+            pl.BlockSpec((rows, width), lambda i: (0, 0)),
+            pl.BlockSpec((None, 3, width, cols), lambda i: (i, 0, 0, 0)),
+            pl.BlockSpec((None, 3, cols), lambda i: (i, 0, 0)),
+            pl.BlockSpec((rows, LANES), lambda i: (0, 0)),
+            pl.BlockSpec((rows, LANES), lambda i: (0, 0)),
+        ],
+        out_specs=[pl.BlockSpec((None, 3, rows, LANES), lambda i: (i, 0, 0, 0))] * parts,
+        compiler_params=pltpu.CompilerParams(vmem_limit_bytes=32 << 20),
+        cost_estimate=pl.CostEstimate(
+            flops=6 * rows * width * width, bytes_accessed=10 << 20, transcendentals=0
+        ),
+    )(normed, weight, bias, cos, sin)
 
 
 def head_masks(width):
@@ -542,15 +618,13 @@
         grid_spec=grid_spec,
         compiler_params=pltpu.CompilerParams(vmem_limit_bytes=48 << 20),
         cost_estimate=pl.CostEstimate(
-            flops=8 * total * total * width, bytes_accessed=8 << 20, transcendentals=0
+            flops=4 * total * total * width, bytes_accessed=8 << 20, transcendentals=0
         ),
     )(bounds, qkv, qkv, qkv, seg_rows, seg_blocks)
 
 
 def unrotate(values, cos, sin):
-    half = values.shape[1] // 2
-    even, odd = values[:, :half], values[:, half:]
-    return jnp.concatenate([even * cos + odd * sin, odd * cos - even * sin], axis=1)
+    return values * cos - pltpu.roll(values, LANES // 2, 1) * sin
 
 
 def attend_back_kernel(
@@ -624,8 +698,8 @@
             pl.BlockSpec((block, width), lambda i, b: (i, 0)),
             pl.BlockSpec((block, 1), lambda i, b: (i, 0)),
             pl.BlockSpec((shards, 1, rows), lambda i, b: (0, 0, 0)),
-            pl.BlockSpec((total, width // 2), lambda i, b: (0, 0)),
-            pl.BlockSpec((total, width // 2), lambda i, b: (0, 0)),
+            pl.BlockSpec((total, width), lambda i, b: (0, 0)),
+            pl.BlockSpec((total, width), lambda i, b: (0, 0)),
         ],
         out_specs=pl.BlockSpec((shards, 3, rows, width), lambda i, b: (0, 0, 0, 0)),
         scratch_shapes=[
@@ -639,7 +713,7 @@
         grid_spec=grid_spec,
         compiler_params=pltpu.CompilerParams(vmem_limit_bytes=48 << 20),
         cost_estimate=pl.CostEstimate(
-            flops=20 * total * total * width, bytes_accessed=16 << 20, transcendentals=0
+            flops=10 * total * total * width, bytes_accessed=16 << 20, transcendentals=0
         ),
     )(bounds, qkv, qkv, qkv, full, logs, grads, seg_rows, seg_blocks, cos, sin)
 
@@ -675,20 +749,36 @@
         return lax.all_to_all(jnp.broadcast_to(piece[None], (size,) + piece.shape), axis_name, 0, 0)
 
     def gather(piece, axis):
-        return lax.all_gather(to_all(piece), "dp", axis=axis, tiled=True)
+        return lax.all_gather(piece, "dp", axis=axis, tiled=True)
+
+    def three(values):
+        one = lax.reduce_precision(values, 8, 7)
+        two = lax.reduce_precision(values - one, 8, 7)
+        return jnp.concatenate([one, two, values - one - two], axis=0).astype(BF)
 
     qkv_piece = spread_slice(qkv_w, 1)
     qkv_piece = jnp.concatenate([pair_split(qkv_piece[:2]), qkv_piece[2:]], axis=0)
-    qkv_full = gather(qkv_piece, 2)
-    out_full = gather(spread_slice(out_w, 0), 1).reshape(width, width)
-    w1_piece = to_all(spread_slice(ff_w1, 0)).transpose(1, 0, 2)
-    w1_full = lax.all_gather(w1_piece.reshape(w1_piece.shape[0], -1), "dp", axis=0, tiled=True)
-    w2_full = gather(spread_slice(ff_w2, 0), 1).reshape(-1, width)
-    small = jnp.concatenate([pair_split(qkv_b[:2]), qkv_b[2:]], axis=0)
-    small = jnp.concatenate([small, ff_b1.reshape(-1, cols)], axis=0)
-    small = to_all(small)
-    qkv_bias = small[:, :3]
-    b1_full = small[:, 3:].reshape(-1)
+    in_rows = qkv_piece.shape[1]
+    biases = jnp.concatenate(
+        [pair_split(qkv_b[:2]), qkv_b[2:], ff_b1.reshape(-1, cols)], axis=0
+    )
+    bias_rows = biases.shape[0]
+    biases = three(biases)
+    biases = jnp.pad(biases, ((0, -biases.shape[0] % 16), (0, 0)))
+    received = to_all(jnp.concatenate([qkv_piece.reshape(3 * in_rows, cols), biases], axis=0))
+    qkv_full = gather(received[:, : 3 * in_rows].reshape(shards, 3, in_rows, cols), 2)
+    biases = received[:, 3 * in_rows :].astype(F32)
+    biases = sum(biases[:, i * bias_rows : (i + 1) * bias_rows] for i in range(3))
+    qkv_bias = biases[:, :3]
+    b1_full = biases[:, 3:].reshape(-1)
+    out_piece, w2_piece, w1_piece = spread_slice(out_w, 0), spread_slice(ff_w2, 0), spread_slice(ff_w1, 0)
+    w1_shape = w1_piece.shape
+    cut = [out_piece.shape[0], out_piece.shape[0] + w2_piece.shape[0]]
+    received = to_all(jnp.concatenate([out_piece, w2_piece, w1_piece.reshape(-1, width)], axis=0))
+    out_full = gather(received[:, : cut[0]], 1).reshape(width, width)
+    w1_piece = received[:, cut[1] :].reshape((shards,) + w1_shape).transpose(1, 0, 2)
+    w1_full = gather(w1_piece.reshape(w1_shape[0], -1), 0)
+    w2_full = gather(received[:, cut[0] : cut[1]], 1).reshape(-1, width)
     all_steps = lax.all_gather(t_index, "dp", tiled=True).reshape(-1)
 
     lengths = clip_lengths[0]
@@ -758,24 +848,14 @@
 
     n1, n1_pull = jax.vjp(lambda s, m: modulate(s, m, 0, 1), x1, mod)
     n1 = n1.astype(BF)
-    half = HEAD_DIM // 2
     inverse = jnp.exp(jnp.arange(0, HEAD_DIM, 2, dtype=F32) * (-math.log(10000.0) / HEAD_DIM))
-    angles = position.astype(F32)[:, None] * jnp.tile(inverse, cols // HEAD_DIM)[None, :]
-    cos, sin = jnp.cos(angles), jnp.sin(angles)
+    angles = position.astype(F32)[:, None] * jnp.tile(inverse, LANES // inverse.shape[0])[None, :]
+    cos = jnp.cos(angles)
+    sin = jnp.sin(angles) * jnp.where(jnp.arange(LANES) < LANES // 2, -1.0, 1.0)
     cos_own = lax.dynamic_slice_in_dim(cos, first, rows)
     sin_own = lax.dynamic_slice_in_dim(sin, first, rows)
-    projected = []
-    for s in range(shards):
-        for p in range(3):
-            value = dot(n1, qkv_full[s, p]) + qkv_bias[s, p]
-            if p < 2:
-                even, odd = value[:, : cols // 2], value[:, cols // 2 :]
-                value = jnp.concatenate(
-                    [even * cos_own - odd * sin_own, odd * cos_own + even * sin_own], axis=1
-                )
-            projected.append(value.astype(BF))
-    qkv = jnp.stack(projected).reshape(shards, 3, rows, cols)
-    qkv = exchange(qkv, "mp")
+    parts = range(cols // LANES)
+    qkv = [exchange(v, "mp") for v in project(n1, qkv_full, qkv_bias, cos_own, sin_own)]
     block = 256
     heads_of = segment[::block]
     tails_of = segment[block - 1 :: block]
@@ -784,8 +864,9 @@
     bounds = jnp.stack([low_key // rows, (high_key + rows - 1) // rows], axis=1).astype(jnp.int32)
     seg_rows = segment[:, None]
     seg_blocks = segment.reshape(shards, 1, rows)
-    o, o_full, logs = attend(qkv, seg_rows, seg_blocks, bounds, block)
-    o_rows = to_rows(o)
+    attended = [attend(qkv[h], seg_rows, seg_blocks, bounds, block) for h in parts]
+    o_rows = jnp.stack([exchange(a[0].reshape(shards, rows, LANES), "mp") for a in attended])
+    o_rows = o_rows.transpose(2, 1, 0, 3).reshape(rows, width)
 
     def residual(state, mod_in, summed, bias, part):
         return state + expand(hot, mod_in[:, part * width : (part + 1) * width]) * (summed + bias)
@@ -801,7 +882,6 @@
     )
     r = r.astype(BF)
     out, ff_pull = jax.vjp(lambda s, m, a, b: residual(s, m, a, b, 5), x2, mod, dot(r, w2_full), ff_b2)
-    result = to_all(out.astype(BF)).reshape(total, width).astype(F32)
 
     grad = lax.dynamic_slice_in_dim(out_grad, first, rows).astype(F32)
     dx2, dmod_a, df, g_ff_b2 = ff_pull(grad)
@@ -828,15 +908,24 @@
     dx1, dmod_c, da, g_out_b = att_pull(dx2)
     da = da.astype(BF)
     g_out_w = dot(da, o_rows, TN)
-    do = to_channels(dot(da, out_full, NT).astype(BF))
-    dqkv = attend_back(qkv, o_full, logs, do, seg_rows, seg_blocks, cos, sin, bounds, block)
-    dqkv = exchange(dqkv, "mp").transpose(2, 0, 1, 3).reshape(rows, 3 * width)
-    sent_w1, sent_w2, dqkv = lax.optimization_barrier((sent_w1, sent_w2, dqkv))
+    do = dot(da, out_full, NT).astype(BF).reshape(rows, shards, -1, LANES)
+    dqkv = []
+    for h in parts:
+        do_part = exchange(do[:, :, h].transpose(1, 0, 2), "mp").reshape(total, LANES)
+        d_part = attend_back(
+            qkv[h], attended[h][1], attended[h][2], do_part, seg_rows, seg_blocks, cos, sin, bounds, block
+        )
+        dqkv.append(exchange(d_part, "mp"))
+    result = lax.all_gather(out.astype(BF), "mp", tiled=True)
+    result, dqkv = lax.optimization_barrier((result, dqkv))
+    result = result.astype(F32)
+    dqkv = jnp.stack(dqkv).transpose(3, 1, 2, 0, 4).reshape(rows, 3 * width)
     g_qkv_w = dot(n1, dqkv, TN)
     g_qkv_b = jnp.sum(dqkv.astype(F32), axis=0).reshape(shards, 3, cols)
     w_all = qkv_full.transpose(2, 0, 1, 3).reshape(width, 3 * width)
     more, dmod_d = n1_pull(dot(dqkv, w_all, NT))
     dx1 = dx1 + more
+    sent_w1, sent_w2, dx1 = lax.optimization_barrier((sent_w1, sent_w2, dx1))
     ff_pair = jnp.concatenate([by_rank(sent_w1), by_rank(sent_w2)], axis=2)
     sent_qkv, sent_out = scatter_dp(g_qkv_w), scatter_dp(g_out_w)
 
@@ -853,6 +942,7 @@
     dc = gather_back(
         apply_conv(dy_a, pos_conv[0], True).astype(BF), starts, ends
     )
+    ff_got, dc = lax.optimization_barrier((exchange(ff_pair, "mp"), dc))
     dx0_full = dx1 + to_rows(dc).astype(F32)
     g_conv = jnp.concatenate(
         [conv_grad(spread_in, dy_a[GAP:-GAP], taps, group), conv_grad(y_a, dy_b[GAP:-GAP], taps, group)],
@@ -864,7 +954,7 @@
 
     g_emb_bias = jnp.sum(dx0_full, axis=0)
     dx0 = dx0_full.astype(BF)
-    mel_grad = to_all(dot(dx0, emb_mel, NT).astype(BF)).reshape(total, -1).astype(F32)
+    mel_grad = dot(dx0, emb_mel, NT).astype(BF)
     g_emb = jnp.concatenate([dot(dx0, text, TN), dot(dx0, mel, TN)], axis=1)
     sent_emb = scatter_dp(g_emb)
     text_width = text.shape[1]
@@ -872,6 +962,7 @@
     dtext = jnp.pad(dot(dx0, emb_text, NT), ((HALO, HALO), (0, 0)))
     text_grads = [None] * blocks
     extra = dmod
+    at_got, dtext = lax.optimization_barrier((exchange(at_pair, "mp"), dtext))
     for b in reversed(range(blocks)):
         dtext, text_grads[b], summed = text_behind(kept[b], dtext, txt_up[b], txt_down[b], extra)
         if extra is not None:
@@ -915,14 +1006,16 @@
     packed = jnp.concatenate(packed, axis=1)
     length = packed.shape[1]
     packed = jnp.pad(packed, ((0, 0), (0, -length % 1024))).reshape(groups, -1, 128)
-    table_sum, up0, up1, down0, down1, packed, ff_pair, at_pair, g_emb = last_sums(
+    table_sum, up0, up1, down0, down1, packed, g_emb, mel_grad = last_sums(
         [for_dp(g_table)]
         + [for_dp(text_grads[b][3]) for b in range(blocks)]
         + [for_dp(text_grads[b][5]) for b in range(blocks)],
         packed,
-        [ff_pair, at_pair],
+        [],
         [sent_emb],
-    )
+        [mel_grad],
+    )
+    mel_grad = mel_grad.reshape(total, -1)
     packed = packed.reshape(-1)
     unpacked, at = [], 0
     for value, kind in small:
@@ -938,6 +1031,7 @@
     o_table = table_sum[:, :vocab].T
     o_up = jnp.stack([up0.T, up1.T])
     o_down = jnp.stack([down0.T, down1.T])
+    ff_pair, at_pair = (jnp.sum(v.astype(F32), axis=0) for v in (ff_got, at_got))
     ff_cols = ff_w1.shape[1]
     o_ff_w1, o_ff_w2 = ff_pair[:, :ff_cols], ff_pair[:, ff_cols:].T
     g_qkv = at_pair[:, : 3 * cols].reshape(-1, 3, cols).transpose(1, 0, 2)

time: 1070 us -> 1020 us (0.953); the launches traced: 1060 us -> 1000 us
  waiting for transfers between devices: 232 us -> 187 us
  blocking collectives: 63.3 us -> 29.2 us
  local copies, waits for them, and re-layouts: 104 us -> 135 us
  matrix products: 188 us -> 172 us
    all_to_all x7 -> x2, waiting for transfers between devices: 48.5 us -> 0.01 us  [to_all(): lax.all_to_all(jnp.broadcast_to(piece[None], (size,) + piece.shape), axis...]
    all_to_all x7 -> x14, starting transfers between devices: 31.7 us -> 60.8 us  [exchange(): return lax.all_to_all(values, axis, 0, 0)]
    all_to_all x1 -> x0, blocking collectives: 28.6 us -> none  [exchange(): return lax.all_to_all(values, axis, 0, 0)]
    all_to_all x7 -> x2, starting transfers between devices: 33 us -> 11 us  [to_all(): lax.all_to_all(jnp.broadcast_to(piece[None], (size,) + piece.shape), axis...]
    pallas_call x1 -> x2, Pallas kernels: 89 us -> 69.5 us  [the longest x1 65.2 us: last_sums(): pl.pallas_call(partial(last_kernel, dp, mp, n_all, n_mp, n_both, n_gather...]
    all_to_all x7 -> x14, waiting for transfers between devices: 163 us -> 180 us  [exchange(): return lax.all_to_all(values, axis, 0, 0)]
    dot_general x42 -> x30, matrix products: 134 us -> 118 us  [dot(): lax.dot_general(left.astype(BF), right.astype(BF), dims, preferred_elemen...]
    unnamed x612 -> x544, local copies, waits for them, and re-layouts: 47.4 us -> 60.7 us
  transfers between devices with their start and end apart: 24 -> 27, of which waited for: 10 -> 11; matrix products, arithmetic and copies ran while one was open for 27% -> 35% of each run, Pallas kernels for 16% -> 19%
where the time goes in v4:
time: 1020 us; the launch traced here: 1000 us
  Pallas kernels  257 us (25%)
  waiting for transfers between devices  187 us (18%)
  matrix products  172 us (17%)
  local copies, waits for them, and re-layouts  135 us (13%)
  other arithmetic  129 us (13%)
  starting transfers between devices  73.4 us (7%)
  blocking collectives  29.2 us (3%)
  between operations  18.3 us (2%)
    all_to_all x14, waiting for transfers between devices, exchange(): return lax.all_to_all(values, axis, 0, 0)  180 us
    dot_general x30, matrix products, dot(): lax.dot_general(left.astype(BF), right.astype(BF), dims, preferred_elemen...  118 us
    pallas_call x1, Pallas kernels, last_sums(): pl.pallas_call(partial(last_kernel, dp, mp, n_all, n_mp, n_both, n_gather...  65.2 us
    all_to_all x14, starting transfers between devices, exchange(): return lax.all_to_all(values, axis, 0, 0)  60.8 us
    unnamed x544, local copies, waits for them, and re-layouts  60.7 us
    pallas_call x2, Pallas kernels, attend_back(): pl.pallas_call(attend_back_kernel, out_shape=jax.ShapeDtypeStruct((shards...  48.2 us
    pallas_call x4, Pallas kernels, apply_conv(): pl.pallas_call(partial(conv_kernel, taps, turned), out_shape=jax.ShapeDty...  39.5 us
    pallas_call x4, Pallas kernels, small_sum(): pl.pallas_call(partial(sum_kernel, axis, size), out_shape=jax.ShapeDtypeS...  37.5 us
  transfers between devices with their start and end apart: 27, of which 11 were waited for; matrix products, arithmetic and copies ran while one was open for 35% of the time, Pallas kernels for 19%

profile of v4, /device:TPU:0, one launch (start us, length us, event | category | flops | bytes accessed | tf_op | source)
XLA Modules:
  0.0 1001.1 jit_solution(15958851757439108234)
XLA Ops:
  65.2 7.9 multiply_multiply_fusion.14
  75.4 14.1 %shard_map.494 = f32[4,1024]{1,0:T(4,128)S(1)} custom-call(f32[4,1024]{1,0:T(4,128)S(1)} %fusion.27.x_ref), custom_call_target="tpu_custom_call" | custom-call | tf_op jit(solution)/shard_map/pallas_call | solution.py:115
  123.5 16.9 %all-to-all-done = bf16[4,512,256]{2,1,0:T(8,128)(2,1)S(1)} async-done(((bf16[4,512,256]{2,1,0:T(8,128)(2,1)}), bf16[4,512,256]{2,1,0:T(8,128)(2,1)S(1)}, u32[]{:S(2)}, u32[]{:S(2)}) %all-to-all-start) | async-done | bytes 1048608 | tf_op jit(solution)/shard_map/all_to_all | solution.py:722
  145.9 9.9 shard_map.495
  166.0 9.8 shard_map.496
  190.4 20.5 %all-to-all-done.1 = bf16[4,512,256]{2,1,0:T(8,128)(2,1)} async-done(((bf16[4,512,256]{2,1,0:T(8,128)(2,1)}), bf16[4,512,256]{2,1,0:T(8,128)(2,1)}, u32[]{:S(2)}, u32[]{:S(2)}) %all-to-all-start.1) | async-done | bytes 1048608 | tf_op jit(solution)/shard_map/all_to_all | solution.py:722
  214.6 6.8 add_convert_fusion.4.x_ref
  236.2 35.8 %all-to-all-done.5.q_ref.k_ref.v_ref = bf16[4,3,512,128]{3,2,1,0:T(8,128)(2,1)S(1)} async-done(((bf16[4,3,512,128]{3,2,1,0:T(8,128)(2,1)}), bf16[4,3,512,128]{3,2,1,0:T(8,128)(2,1)S(1)}, u32[]{:S(2)}, u32[]{:S(2)}) %all-to-all-start.5) | async-done | bytes 1572896 | tf_op jit(solution)/shard_map/all_to_all | solution.py:722
  279.4 14.7 %shard_map.499 = (bf16[2048,128]{1,0:T(8,128)(2,1)S(1)}, f32[2048,128]{1,0:T(8,128)S(1)}, f32[2048,128]{1,0:T(8,128)S(1)}) custom-call(s32[8,2]{1,0:T(8,128)S(1)} %copy.366.bounds, bf16[4,3,512,128]{3,2,1,0:T(8,128)(2,1)S(1)} %all-to-all-done.5.q_ref.k_ref.v_ref, bf16[4,3,512,128]{3,2,1,0:T(8,128)(2,1)S(1)} %all-to-all-done.5.q_ref.k_ref.v_ref, ...), custom_call_target="tpu_custom_call" | custom-call | flops 2147483648 | bytes 8388608 | tf_op jit(solution)/shard_map/pallas_call | solution.py:611
  297.1 15.8 %all-to-all-done.3.q_ref.k_ref.v_ref = bf16[4,3,512,128]{3,2,1,0:T(8,128)(2,1)} async-done(((bf16[4,3,512,128]{3,2,1,0:T(8,128)(2,1)}), bf16[4,3,512,128]{3,2,1,0:T(8,128)(2,1)}, u32[]{:S(2)}, u32[]{:S(2)}) %all-to-all-start.3) | async-done | bytes 1572896 | tf_op jit(solution)/shard_map/all_to_all | solution.py:722
  317.6 16.1 %shard_map.498 = (bf16[2048,128]{1,0:T(8,128)(2,1)S(1)}, f32[2048,128]{1,0:T(8,128)S(1)}, f32[2048,128]{1,0:T(8,128)S(1)}) custom-call(s32[8,2]{1,0:T(8,128)S(1)} %copy.366.bounds, bf16[4,3,512,128]{3,2,1,0:T(8,128)(2,1)} %all-to-all-done.3.q_ref.k_ref.v_ref, bf16[4,3,512,128]{3,2,1,0:T(8,128)(2,1)} %all-to-all-done.3.q_ref.k_ref.v_ref, ...), custom_call_target="tpu_custom_call" | custom-call | flops 2147483648 | bytes 8388608 | tf_op jit(solution)/shard_map/pallas_call | solution.py:611
  342.1 13.3 %all-to-all-done.4 = bf16[4,512,128]{1,2,0:T(8,128)(2,1)} async-done(((bf16[4,512,128]{1,2,0:T(8,128)(2,1)}), bf16[4,512,128]{1,2,0:T(8,128)(2,1)}, u32[]{:S(2)}, u32[]{:S(2)}) %all-to-all-start.4) | async-done | bytes 524320 | tf_op jit(solution)/shard_map/all_to_all | solution.py:722
  364.2 8.3 fusion.283
  379.0 7.1 convert_reduce_fusion.1
  391.6 7.8 convolution_convert_fusion.1
  424.8 27.0 %all-to-all-done.10 = bf16[4,512,128]{2,1,0:T(8,128)(2,1)S(1)} async-done(((bf16[4,512,128]{2,1,0:T(8,128)(2,1)}), bf16[4,512,128]{2,1,0:T(8,128)(2,1)S(1)}, u32[]{:S(2)}, u32[]{:S(2)}) %all-to-all-start.10) | async-done | bytes 524320 | tf_op jit(solution)/shard_map/all_to_all | solution.py:722
  461.4 24.1 %shard_map.501 = bf16[4,3,512,128]{3,2,1,0:T(8,128)(2,1)} custom-call(s32[8,2]{1,0:T(8,128)S(1)} %copy.366.bounds, bf16[4,3,512,128]{3,2,1,0:T(8,128)(2,1)} %copy-done.13, bf16[4,3,512,128]{3,2,1,0:T(8,128)(2,1)} %copy-done.13, bf16[4,3,512,128]{3,2,1,0:T(8,128)(2,1)} %copy-done.13, f32[2048,128]{1,0:T(8,128)S(1)} %copy-done.36, f32[2048,128]{1,0:T(8,128)S(1)} %copy-done.38, ...), custom_call_target="tpu_custom_call" | custom-call | flops 5368709120 | bytes 16777216 | tf_op jit(solution)/shard_map/pallas_call | solution.py:710
  490.7 17.1 %all-gather = s32[8,1,4]{2,1,0:T(1,128)S(1)} all-gather(s32[1,1,4]{2,1,0:T(1,128)S(1)} %bitcast.715), channel_id=1, replica_groups=mesh['dp'=8,'mp'=4] {'dp'}, dimensions={0}, use_global_device_ids=true | all-gather | bytes 144 | tf_op jit(solution)/shard_map/all_gather | solution.py:782
  511.5 24.1 %shard_map.500 = bf16[4,3,512,128]{3,2,1,0:T(8,128)(2,1)} custom-call(s32[8,2]{1,0:T(8,128)S(1)} %copy.366.bounds, bf16[4,3,512,128]{3,2,1,0:T(8,128)(2,1)} %all-to-all-done.3.q_ref.k_ref.v_ref, bf16[4,3,512,128]{3,2,1,0:T(8,128)(2,1)} %all-to-all-done.3.q_ref.k_ref.v_ref, bf16[4,3,512,128]{3,2,1,0:T(8,128)(2,1)} %all-to-all-done.3.q_ref.k_ref.v_ref, ...), custom_call_target="tpu_custom_call" | custom-call | flops 5368709120 | bytes 16777216 | tf_op jit(solution)/shard_map/pallas_call | solution.py:710
  547.9 8.7 copy.380
  562.8 15.3 %all-to-all-done.9 = bf16[4,3,512,128]{3,2,1,0:T(8,128)(2,1)} async-done(((bf16[4,3,512,128]{3,2,1,0:T(8,128)(2,1)}), bf16[4,3,512,128]{3,2,1,0:T(8,128)(2,1)}, u32[]{:S(2)}, u32[]{:S(2)}) %all-to-all-start.9) | async-done | bytes 1572896 | tf_op jit(solution)/shard_map/all_to_all | solution.py:722
  586.8 10.1 %multiply_reduce_fusion.2 = (f32[512]{0:T(512)S(1)}, f32[512,1024]{1,0:T(8,128)}) fusion(f32[512,1024]{1,0:T(8,128)} %copy-done.39, f32[512]{0:T(512)S(1)} %broadcast_multiply_fusion.3, f32[1024]{0:T(1024)S(1)} %bitcast.535, f32[512]{0:T(512)S(1)} %bitcast.527, f32[1024]{0:T(1024)S(1)} %bitcast.538, f32[512]{0:T(512)S(1)} %bitcast.505, ...), kind=kOutput, calls=%fused_computation.127 | convolution fusion | flops 3227516416 | bytes 13660160 | tf_op jit(solution)/shard_map/dot_general | solution.py:23
  663.7 10.0 shard_map.502
  675.9 15.8 %shard_map.505 = f32[256,1984]{1,0:T(8,128)S(1)} custom-call(f32[2144,256]{1,0:T(8,128)} %copy-done.6, f32[2112,256]{1,0:T(8,128)S(1)} %slice.1039.g_ref), custom_call_target="tpu_custom_call" | custom-call | flops 8581545984 | bytes 8388608 | tf_op jit(solution)/shard_map/pallas_call | solution.py:472
  691.8 15.9 %shard_map.504 = f32[256,1984]{1,0:T(8,128)S(1)} custom-call(f32[2144,256]{1,0:T(8,128)} %copy-done.5, f32[2112,256]{1,0:T(8,128)S(1)} %convert_element_type.472.g_ref), custom_call_target="tpu_custom_call" | custom-call | flops 8581545984 | bytes 8388608 | tf_op jit(solution)/shard_map/pallas_call | solution.py:472
  711.1 9.8 shard_map.503
  736.1 17.7 %all-to-all-done.14 = bf16[4,512,256]{2,1,0:T(8,128)(2,1)S(1)} async-done(((bf16[4,512,256]{2,1,0:T(8,128)(2,1)}), bf16[4,512,256]{2,1,0:T(8,128)(2,1)S(1)}, u32[]{:S(2)}, u32[]{:S(2)}) %all-to-all-start.14) | async-done | bytes 1048608 | tf_op jit(solution)/shard_map/all_to_all | solution.py:722
  775.6 14.7 %all-to-all-done.15 = bf16[4,128,1024]{2,1,0:T(8,128)(2,1)} async-done(((bf16[4,128,1024]{2,1,0:T(8,128)(2,1)}), bf16[4,128,1024]{2,1,0:T(8,128)(2,1)}, u32[]{:S(2)}, u32[]{:S(2)}) %all-to-all-start.15) | async-done | bytes 1048608 | tf_op jit(solution)/shard_map/all_to_all | solution.py:722
  797.3 11.2 %shard_map.506 = f32[4,7168]{1,0:T(4,128)S(1)} custom-call(f32[4,7168]{1,0:T(4,128)S(1)} %pad_maximum_fusion.11.x_ref), custom_call_target="tpu_custom_call" | custom-call | tf_op jit(solution)/shard_map/pallas_call | solution.py:115
  808.5 12.1 %all-gather.1 = f32[8,4,6144]{2,1,0:T(4,128)S(1)} all-gather(f32[1,4,6144]{2,1,0:T(4,128)S(1)} %slice_bitcast_fusion.7), channel_id=1, replica_groups=mesh['dp'=8,'mp'=4] {'dp'}, dimensions={0}, use_global_device_ids=true | all-gather | bytes 884736 | tf_op jit(solution)/shard_map/all_gather | solution.py:969
  823.9 8.7 fusion.68
  911.7 65.2 %shard_map.508 = (f32[16,2560]{1,0:T(8,128)}, f32[32,512]{1,0:T(8,128)}, f32[32,512]{1,0:T(8,128)}, f32[16,1024]{1,0:T(8,128)}, f32[16,1024]{1,0:T(8,128)}, /*in...) custom-call(bf16[4,2,64,2560]{3,2,1,0:T(8,128)(2,1)} %bitcast.448, bf16[4,2,128,512]{3,2,1,0:T(8,128)(2,1)} %bitcast.460, ...), custom_call_target="tpu_custom_call" | custom-call | tf_op jit(solution)/shard_map/pallas_call | solution.py:278
  (930 shorter events, 470.6 us)
Async XLA Ops:
  13.1 39.5 %all-to-all-start.2 = ((bf16[4,400,256]{2,1,0:T(8,128)(2,1)}), bf16[4,400,256]{2,1,0:T(8,128)(2,1)}, u32[]{:S(2)}, u32[]{:S(2)}) async-start(bf16[4,400,256]{2,1,0:T(8,128)(2,1)} %broadcast_in_dim.459), calls=%async_computation.2 | async-start | bytes 1638400 | tf_op jit(solution)/shard_map/all_to_all | solution.py:749
  22.8 78.6 %copy-start.122 = (f32[528]{0:T(1024)}, f32[528]{0:T(1024)S(1)}, u32[]{:S(2)}) copy-start(f32[528]{0:T(1024)S(1)} %get-tuple-element.336) | copy-start | bytes 6340
  22.8 78.6 %copy-start.124 = (f32[528]{0:T(1024)}, f32[528]{0:T(1024)S(1)}, u32[]{:S(2)}) copy-start(f32[528]{0:T(1024)S(1)} %get-tuple-element.337) | copy-start | bytes 6340
  22.8 78.6 %copy-start.126 = (f32[528]{0:T(1024)}, f32[528]{0:T(1024)S(1)}, u32[]{:S(2)}) copy-start(f32[528]{0:T(1024)S(1)} %get-tuple-element.338) | copy-start | bytes 6340
  22.8 78.6 %copy-start.128 = (f32[528]{0:T(1024)}, f32[528]{0:T(1024)S(1)}, u32[]{:S(2)}) copy-start(f32[528]{0:T(1024)S(1)} %get-tuple-element.339) | copy-start | bytes 6340
  23.4 78.0 %copy-start.138 = (f32[1,1,1024]{2,0,1:T(1,128)}, f32[1,1,1024]{2,0,1:T(1,128)S(1)}, u32[]{:S(2)}) copy-start(f32[1,1,1024]{2,0,1:T(1,128)S(1)} %get-tuple-element.472) | copy-start | bytes 12292
  53.9 57.8 %all-to-all-start.7 = ((bf16[4,160,1024]{2,1,0:T(8,128)(2,1)}), bf16[4,160,1024]{2,1,0:T(8,128)(2,1)}, u32[]{:S(2)}, u32[]{:S(2)}) async-start(bf16[4,160,1024]{2,1,0:T(8,128)(2,1)} %broadcast_in_dim.463), calls=%async_computation.7 | async-start | bytes 2621440 | tf_op jit(solution)/shard_map/all_to_all | solution.py:749
  58.6 162.9 %all-gather.8.cloned.1.call-start = ((), (), s32[]{:S(2)}) async-start(), calls=%async_computation.22 | async-start | bytes 7077888 | tf_op jit(solution)/shard_map/all_gather | solution.py:752
  111.7 28.8 %all-to-all-start = ((bf16[4,512,256]{2,1,0:T(8,128)(2,1)}), bf16[4,512,256]{2,1,0:T(8,128)(2,1)S(1)}, u32[]{:S(2)}, u32[]{:S(2)}) async-start(bf16[4,512,256]{2,1,0:T(8,128)(2,1)} %bitcast.413), calls=%async_computation | async-start | bytes 2097152 | tf_op jit(solution)/shard_map/all_to_all | solution.py:722
  115.3 242.2 %all-gather.10.cloned.1.call-start = ((), (), s32[]{:S(2)}) async-start(), calls=%async_computation.23 | async-start | bytes 2359296 | tf_op jit(solution)/shard_map/all_gather | solution.py:752
  117.6 246.6 %all-gather.12.cloned.1.call-start = ((), (), s32[]{:S(2)}) async-start(), calls=%async_computation.24 | async-start | bytes 4718592 | tf_op jit(solution)/shard_map/all_gather | solution.py:752
  181.1 29.7 %all-to-all-start.1 = ((bf16[4,512,256]{2,1,0:T(8,128)(2,1)}), bf16[4,512,256]{2,1,0:T(8,128)(2,1)}, u32[]{:S(2)}, u32[]{:S(2)}) async-start(bf16[4,512,256]{2,1,0:T(8,128)(2,1)} %bitcast.58), calls=%async_computation.1 | async-start | bytes 2097152 | tf_op jit(solution)/shard_map/all_to_all | solution.py:722
  232.0 40.0 %all-to-all-start.5 = ((bf16[4,3,512,128]{3,2,1,0:T(8,128)(2,1)}), bf16[4,3,512,128]{3,2,1,0:T(8,128)(2,1)S(1)}, u32[]{:S(2)}, u32[]{:S(2)}) async-start(bf16[4,3,512,128]{3,2,1,0:T(8,128)(2,1)} %copy-done.15), calls=%async_computation.5 | async-start | bytes 3145728 | tf_op jit(solution)/shard_map/all_to_all | solution.py:722
  235.6 136.9 %all-gather.14.cloned.1.call-start = ((), (), s32[]{:S(2)}) async-start(), calls=%async_computation.25 | async-start | bytes 4718592 | tf_op jit(solution)/shard_map/all_gather | solution.py:752
  272.0 40.9 %all-to-all-start.3 = ((bf16[4,3,512,128]{3,2,1,0:T(8,128)(2,1)}), bf16[4,3,512,128]{3,2,1,0:T(8,128)(2,1)}, u32[]{:S(2)}, u32[]{:S(2)}) async-start(bf16[4,3,512,128]{3,2,1,0:T(8,128)(2,1)} %copy-done.14), calls=%async_computation.3 | async-start | bytes 3145728 | tf_op jit(solution)/shard_map/all_to_all | solution.py:722
  312.9 23.8 %all-to-all-start.6 = ((bf16[4,512,128]{1,2,0:T(8,128)(2,1)}), bf16[4,512,128]{1,2,0:T(8,128)(2,1)S(1)}, u32[]{:S(2)}, u32[]{:S(2)}) async-start(bf16[4,512,128]{1,2,0:T(8,128)(2,1)} %copy.371), calls=%async_computation.6 | async-start | bytes 1048576 | tf_op jit(solution)/shard_map/all_to_all | solution.py:722
  336.7 18.7 %all-to-all-start.4 = ((bf16[4,512,128]{1,2,0:T(8,128)(2,1)}), bf16[4,512,128]{1,2,0:T(8,128)(2,1)}, u32[]{:S(2)}, u32[]{:S(2)}) async-start(bf16[4,512,128]{1,2,0:T(8,128)(2,1)} %copy.368), calls=%async_computation.4 | async-start | bytes 1048576 | tf_op jit(solution)/shard_map/all_to_all | solution.py:722
  341.9 236.3 %all-gather.16.cloned.1.call-start = ((), (), s32[]{:S(2)}) async-start(), calls=%async_computation.26 | async-start | bytes 5242880 | tf_op jit(solution)/shard_map/all_gather | solution.py:919
  391.1 219.2 %reduce-scatter.13.cloned.1.call-start = ((), (), s32[]{:S(2)}) async-start(), calls=%async_computation.30 | async-start | bytes 4718592 | tf_op jit(solution)/shard_map/reduce_scatter | solution.py:904
  399.4 217.0 %reduce-scatter.11.cloned.1.call-start = ((), (), s32[]{:S(2)}) async-start(), calls=%async_computation.29 | async-start | bytes 4718592 | tf_op jit(solution)/shard_map/reduce_scatter | solution.py:904
  419.0 32.8 %all-to-all-start.10 = ((bf16[4,512,128]{2,1,0:T(8,128)(2,1)}), bf16[4,512,128]{2,1,0:T(8,128)(2,1)S(1)}, u32[]{:S(2)}, u32[]{:S(2)}) async-start(bf16[4,512,128]{2,1,0:T(8,128)(2,1)} %bitcast.420), calls=%async_computation.10 | async-start | bytes 1048576 | tf_op jit(solution)/shard_map/all_to_all | solution.py:722
  451.8 33.7 %all-to-all-start.8 = ((bf16[4,512,128]{2,1,0:T(8,128)(2,1)}), bf16[4,512,128]{2,1,0:T(8,128)(2,1)S(1)}, u32[]{:S(2)}, u32[]{:S(2)}) async-start(bf16[4,512,128]{2,1,0:T(8,128)(2,1)} %bitcast.421), calls=%async_computation.8 | async-start | bytes 1048576 | tf_op jit(solution)/shard_map/all_to_all | solution.py:722
  485.5 50.1 %all-to-all-start.11 = ((bf16[4,3,512,128]{3,2,1,0:T(8,128)(2,1)}), bf16[4,3,512,128]{3,2,1,0:T(8,128)(2,1)}, u32[]{:S(2)}, u32[]{:S(2)}) async-start(bf16[4,3,512,128]{3,2,1,0:T(8,128)(2,1)} %shard_map.501), calls=%async_computation.11 | async-start | bytes 3145728 | tf_op jit(solution)/shard_map/all_to_all | solution.py:722
  535.6 42.5 %all-to-all-start.9 = ((bf16[4,3,512,128]{3,2,1,0:T(8,128)(2,1)}), bf16[4,3,512,128]{3,2,1,0:T(8,128)(2,1)}, u32[]{:S(2)}, u32[]{:S(2)}) async-start(bf16[4,3,512,128]{3,2,1,0:T(8,128)(2,1)} %shard_map.500), calls=%async_computation.9 | async-start | bytes 3145728 | tf_op jit(solution)/shard_map/all_to_all | solution.py:722
  540.5 217.0 %reduce-scatter.9.cloned.1.call-start = ((), (), s32[]{:S(2)}) async-start(), calls=%async_computation.28 | async-start | bytes 2359296 | tf_op jit(solution)/shard_map/reduce_scatter | solution.py:904
  545.1 212.5 %reduce-scatter.7.cloned.1.call-start = ((), (), s32[]{:S(2)}) async-start(), calls=%async_computation.27 | async-start | bytes 7077888 | tf_op jit(solution)/shard_map/reduce_scatter | solution.py:904
  619.2 30.8 %all-to-all-start.13 = ((bf16[4,512,256]{2,1,0:T(8,128)(2,1)}), bf16[4,512,256]{2,1,0:T(8,128)(2,1)}, u32[]{:S(2)}, u32[]{:S(2)}) async-start(bf16[4,512,256]{2,1,0:T(8,128)(2,1)} %bitcast.442), calls=%async_computation.17 | async-start | bytes 2097152 | tf_op jit(solution)/shard_map/all_to_all | solution.py:722
  650.0 74.0 %all-to-all-start.12 = ((bf16[4,128,1024]{2,1,0:T(8,128)(2,1)}), bf16[4,128,1024]{2,1,0:T(8,128)(2,1)}, u32[]{:S(2)}, u32[]{:S(2)}) async-start(bf16[4,128,1024]{2,1,0:T(8,128)(2,1)} %pad_maximum_fusion.3), calls=%async_computation.16 | async-start | bytes 2097152 | tf_op jit(solution)/shard_map/all_to_all | solution.py:722
  724.0 29.9 %all-to-all-start.14 = ((bf16[4,512,256]{2,1,0:T(8,128)(2,1)}), bf16[4,512,256]{2,1,0:T(8,128)(2,1)S(1)}, u32[]{:S(2)}, u32[]{:S(2)}) async-start(bf16[4,512,256]{2,1,0:T(8,128)(2,1)} %bitcast.128), calls=%async_computation.18 | async-start | bytes 2097152 | tf_op jit(solution)/shard_map/all_to_all | solution.py:722
  729.2 120.7 %reduce-scatter.17.cloned.1.call-start = ((), (), s32[]{:S(2)}) async-start(), calls=%async_computation.32 | async-start | bytes 2285568 | tf_op jit(solution)/shard_map/reduce_scatter | solution.py:904
  760.9 29.3 %all-to-all-start.15 = ((bf16[4,128,1024]{2,1,0:T(8,128)(2,1)}), bf16[4,128,1024]{2,1,0:T(8,128)(2,1)}, u32[]{:S(2)}, u32[]{:S(2)}) async-start(bf16[4,128,1024]{2,1,0:T(8,128)(2,1)} %pad_maximum_fusion.4), calls=%async_computation.21 | async-start | bytes 2097152 | tf_op jit(solution)/shard_map/all_to_all | solution.py:722
  765.2 142.6 %reduce-scatter.15.cloned.1.call-start = ((), (), s32[]{:S(2)}) async-start(), calls=%async_computation.31 | async-start | bytes 1769472 | tf_op jit(solution)/shard_map/reduce_scatter | solution.py:904
  (252 other events, 2078.3 us)
Sparse Core Ops, SparseCore 0:
  61.3 46.9 all-gather.7
  118.7 29.3 all-gather.9
  162.7 36.5 all-gather.11
  238.0 38.0 all-gather.13
  391.2 117.8 all-gather.15
  512.3 48.9 reduce-scatter.12
  565.1 51.2 reduce-scatter.10
  619.7 41.1 reduce-scatter.8
  664.7 61.7 reduce-scatter.6
  733.0 41.4 reduce-scatter.16
  778.4 39.7 reduce-scatter.14

commit v5 on v4

--- a/solution.py
+++ b/solution.py
@@ -368,27 +368,33 @@
 def spread(values, starts, ends):
     rows = values.shape[0]
     clips = starts.shape[0]
-    at = jnp.arange(rows, dtype=jnp.int32)
+    at = lax.broadcasted_iota(jnp.int32, values.shape, 0)
     total = rows + GAP * clips + 2 * GAP
     out = None
     for c in range(clips):
-        keep = (at >= starts[c]) & (at < ends[c])
-        part = jnp.where(keep[:, None], values, 0)
+        part = jnp.where((at >= starts[c]) & (at < ends[c]), values, 0)
         lead = GAP + GAP * c
         part = jnp.pad(part, ((lead, total - lead - rows), (0, 0)))
         out = part if out is None else out + part
     return out
 
 
+def only_clips(values, starts, ends):
+    at = lax.broadcasted_iota(jnp.int32, values.shape, 0)
+    keep = None
+    for c in range(starts.shape[0]):
+        inside = (at >= starts[c] + GAP * c) & (at < ends[c] + GAP * c)
+        keep = inside if keep is None else keep | inside
+    return jnp.where(keep, values, 0.0)
+
+
 def gather_back(values, starts, ends):
     clips = starts.shape[0]
     rows = values.shape[0] - GAP * clips
-    at = jnp.arange(rows, dtype=jnp.int32)
-    out = None
-    for c in range(clips):
-        keep = (at >= starts[c]) & (at < ends[c])
-        part = jnp.where(keep[:, None], values[GAP * c : GAP * c + rows], 0)
-        out = part if out is None else out + part
+    at = lax.broadcasted_iota(jnp.int32, (rows, values.shape[1]), 0)
+    out = values[:rows]
+    for c in range(1, clips):
+        out = jnp.where(at >= starts[c], values[GAP * c : GAP * c + rows], out)
     return out
 
 
@@ -532,6 +538,57 @@
     )(normed, weight, bias, cos, sin)
 
 
+def unproject_kernel(parts, *refs):
+    d_refs, (x_ref, w_ref, dx_ref, gw_ref, gb_ref, turned) = refs[:parts], refs[parts:]
+    s = pl.program_id(0)
+    cols = w_ref.shape[2]
+
+    @pl.when(s == 0)
+    def _():
+        turned[...] = x_ref[...].T
+        dx_ref[...] = jnp.zeros_like(dx_ref)
+
+    total = None
+    for p in range(3):
+        grad = jnp.concatenate([d_ref[p] for d_ref in d_refs], axis=1)
+        product = lax.dot_general(grad, w_ref[p], NT, preferred_element_type=F32)
+        total = product if total is None else total + product
+        weight = jnp.dot(turned[...], grad, preferred_element_type=F32)
+        gw_ref[:, p * cols : (p + 1) * cols] = weight.astype(BF)
+        gb_ref[p : p + 1, :] = jnp.sum(grad.astype(F32), axis=0, keepdims=True)
+    dx_ref[...] += total
+
+
+def unproject(grads, normed, weight):
+    rows = normed.shape[0]
+    shards, _, width, cols = weight.shape
+    parts = len(grads)
+    return pl.pallas_call(
+        partial(unproject_kernel, parts),
+        out_shape=[
+            jax.ShapeDtypeStruct((rows, width), F32),
+            jax.ShapeDtypeStruct((width, shards * 3 * cols), BF),
+            jax.ShapeDtypeStruct((shards, 3, cols), F32),
+        ],
+        grid=(shards,),
+        in_specs=[pl.BlockSpec((None, 3, rows, LANES), lambda i: (i, 0, 0, 0))] * parts
+        + [
+            pl.BlockSpec((rows, width), lambda i: (0, 0)),
+            pl.BlockSpec((None, 3, width, cols), lambda i: (i, 0, 0, 0)),
+        ],
+        out_specs=[
+            pl.BlockSpec((rows, width), lambda i: (0, 0)),
+            pl.BlockSpec((width, 3 * cols), lambda i: (0, i)),
+            pl.BlockSpec((None, 3, cols), lambda i: (i, 0, 0)),
+        ],
+        scratch_shapes=[pltpu.VMEM((width, rows), BF)],
+        compiler_params=pltpu.CompilerParams(vmem_limit_bytes=48 << 20),
+        cost_estimate=pl.CostEstimate(
+            flops=12 * rows * width * width, bytes_accessed=20 << 20, transcendentals=0
+        ),
+    )(*grads, normed, weight)
+
+
 def head_masks(width):
     heads = width // HEAD_DIM
     lane = lax.broadcasted_iota(jnp.int32, (1, width), 1)
@@ -541,54 +598,56 @@
     return heads, paired, plain
 
 
-def attend_kernel(bounds, q_ref, k_ref, v_ref, sq_ref, sk_ref, o_ref, full_ref, lse_ref):
+def masked(values, masks):
+    return [jnp.where(mask, values, jnp.zeros_like(values)) for mask in masks]
+
+
+def attend_kernel(bounds, q_ref, k_ref, v_ref, sq_ref, sk_ref, o_ref, full_ref, lse_ref, vt_ref):
     i = pl.program_id(0)
-    q = q_ref[...]
-    rows, width = q.shape
-    heads, paired, plain = head_masks(width)
-    scale = HEAD_DIM**-0.5
-    q_heads = [jnp.where(paired[h], q, jnp.zeros_like(q)) for h in range(heads)]
+    rows, width = q_ref.shape
+    heads, paired, _ = head_masks(width)
+
+    @pl.when(i == 0)
+    def _():
+        for b in range(v_ref.shape[0]):
+            vt_ref[b] = v_ref[b].T
+
+    q_heads = masked(q_ref[...] * jnp.asarray(HEAD_DIM**-0.5, BF), paired)
     sq = sq_ref[...]
 
     def step(kb, carry):
-        tops, sums, acc = carry
-        k, v = k_ref[kb], v_ref[kb]
-        same = sq == sk_ref[kb]
-        new_tops, new_sums = [], []
-        decay, extra = None, None
+        k = k_ref[kb]
+        same = sk_ref[kb] == sq
+        new = []
         for h in range(heads):
-            scores = lax.dot_general(q_heads[h], k, NT, preferred_element_type=F32) * scale
+            top_was, total, acc = carry[h]
+            scores = lax.dot_general(k, q_heads[h], NT, preferred_element_type=F32)
             scores = jnp.where(same, scores, -1e30)
-            top = jnp.maximum(tops[h], jnp.max(scores, axis=-1, keepdims=True))
-            fade = jnp.exp(tops[h] - top)
+            top = jnp.maximum(top_was, jnp.max(scores, axis=0, keepdims=True))
+            fade = jnp.exp(top_was - top)
             weight = jnp.exp(scores - top)
-            new_tops.append(top)
-            new_sums.append(fade * sums[h] + jnp.sum(weight, axis=-1, keepdims=True))
-            v_head = jnp.where(plain[h], v, jnp.zeros_like(v))
-            part = jnp.dot(weight.astype(BF), v_head, preferred_element_type=F32)
-            extra = part if extra is None else extra + part
-            decay = fade * jnp.ones((1, width), F32) if h == 0 else jnp.where(plain[h], fade, decay)
-        return tuple(new_tops), tuple(new_sums), acc * decay + extra
-
-    start = (
-        tuple(jnp.full((rows, 1), -1e30, F32) for _ in range(heads)),
-        tuple(jnp.zeros((rows, 1), F32) for _ in range(heads)),
-        jnp.zeros((rows, width), F32),
-    )
-    tops, sums, acc = lax.fori_loop(bounds[i, 0], bounds[i, 1], step, start)
-    lane = lax.broadcasted_iota(jnp.int32, (1, lse_ref.shape[1]), 1)
-    share = jnp.ones((rows, width), F32)
-    logs = jnp.zeros((rows, lse_ref.shape[1]), F32)
-    for h in range(heads):
-        share = jnp.where(plain[h], 1.0 / sums[h], share)
-        logs = jnp.where(lane == h, tops[h] + jnp.log(sums[h]), logs)
-    full = acc * share
+            total = fade * total + jnp.sum(weight, axis=0, keepdims=True)
+            v_head = vt_ref[kb, h * HEAD_DIM : (h + 1) * HEAD_DIM, :]
+            acc = acc * fade + jnp.dot(v_head, weight.astype(BF), preferred_element_type=F32)
+            new.append((top, total, acc))
+        return tuple(new)
+
+    start = tuple(
+        (jnp.full((1, rows), -1e30, F32), jnp.zeros((1, rows), F32), jnp.zeros((HEAD_DIM, rows), F32))
+        for _ in range(heads)
+    )
+    done = lax.fori_loop(bounds[i, 0], bounds[i, 1], step, start)
+    full = jnp.concatenate([acc * (1.0 / total) for _, total, acc in done], axis=0)
     full_ref[...] = full
-    o_ref[...] = full.astype(BF)
+    o_ref[...] = full.T.astype(BF)
+    row = lax.broadcasted_iota(jnp.int32, lse_ref.shape, 0)
+    logs = jnp.zeros(lse_ref.shape, F32)
+    for h, (top, total, _) in enumerate(done):
+        logs = jnp.where(row == h, top + jnp.log(total), logs)
     lse_ref[...] = logs
 
 
-def attend(qkv, seg_rows, seg_blocks, bounds, block):
+def attend(qkv, seg_rows, seg_columns, bounds, block):
     shards, _, rows, width = qkv.shape
     total = shards * rows
     per = rows // block
@@ -599,28 +658,29 @@
             pl.BlockSpec((None, None, block, width), lambda i, b: (i // per, 0, i % per, 0)),
             pl.BlockSpec((shards, None, rows, width), lambda i, b: (0, 1, 0, 0)),
             pl.BlockSpec((shards, None, rows, width), lambda i, b: (0, 2, 0, 0)),
-            pl.BlockSpec((block, 1), lambda i, b: (i, 0)),
-            pl.BlockSpec((shards, 1, rows), lambda i, b: (0, 0, 0)),
+            pl.BlockSpec((1, block), lambda i, b: (0, i)),
+            pl.BlockSpec((shards, rows, 1), lambda i, b: (0, 0, 0)),
         ],
         out_specs=[
             pl.BlockSpec((block, width), lambda i, b: (i, 0)),
-            pl.BlockSpec((block, width), lambda i, b: (i, 0)),
-            pl.BlockSpec((block, 128), lambda i, b: (i, 0)),
-        ],
+            pl.BlockSpec((width, block), lambda i, b: (0, i)),
+            pl.BlockSpec((8, block), lambda i, b: (0, i)),
+        ],
+        scratch_shapes=[pltpu.VMEM((shards, width, rows), BF)],
     )
     return pl.pallas_call(
         attend_kernel,
         out_shape=[
             jax.ShapeDtypeStruct((total, width), BF),
-            jax.ShapeDtypeStruct((total, width), F32),
-            jax.ShapeDtypeStruct((total, 128), F32),
+            jax.ShapeDtypeStruct((width, total), F32),
+            jax.ShapeDtypeStruct((8, total), F32),
         ],
         grid_spec=grid_spec,
         compiler_params=pltpu.CompilerParams(vmem_limit_bytes=48 << 20),
         cost_estimate=pl.CostEstimate(
             flops=4 * total * total * width, bytes_accessed=8 << 20, transcendentals=0
         ),
-    )(bounds, qkv, qkv, qkv, seg_rows, seg_blocks)
+    )(bounds, qkv, qkv, qkv, seg_rows, seg_columns)
 
 
 def unrotate(values, cos, sin):
@@ -629,11 +689,10 @@
 
 def attend_back_kernel(
     bounds, q_ref, k_ref, v_ref, full_ref, lse_ref, do_ref, sq_ref, sk_ref, cos_ref, sin_ref,
-    out_ref, dk_ref, dv_ref,
+    out_ref, dk_ref, dv_ref, kt_ref,
 ):
     i = pl.program_id(0)
-    q, do = q_ref[...], do_ref[...]
-    rows, width = q.shape
+    rows, width = q_ref.shape
     shards, _, shard_rows, _ = out_ref.shape
     per = shard_rows // rows
     heads, paired, plain = head_masks(width)
@@ -643,33 +702,39 @@
     def _():
         dk_ref[...] = jnp.zeros_like(dk_ref)
         dv_ref[...] = jnp.zeros_like(dv_ref)
-
-    zero = jnp.zeros_like(q)
-    q_heads = [jnp.where(paired[h], q, zero) for h in range(heads)]
-    do_heads = [jnp.where(plain[h], do, zero) for h in range(heads)]
-    product = do.astype(F32) * full_ref[...]
-    deltas = [jnp.sum(jnp.where(plain[h], product, 0.0), axis=-1, keepdims=True) for h in range(heads)]
-    logs = [lse_ref[:, h : h + 1] for h in range(heads)]
+        for b in range(shards):
+            for h, k_head in enumerate(masked(k_ref[b], paired)):
+                kt_ref[b, h] = k_head.T
+
+    do = do_ref[...]
+    q_heads = masked(q_ref[...] * jnp.asarray(scale, BF), paired)
+    do_heads = masked(do, plain)
+    product = do.astype(F32).T * full_ref[...]
+    deltas = [
+        jnp.sum(product[h * HEAD_DIM : (h + 1) * HEAD_DIM], axis=0, keepdims=True)
+        for h in range(heads)
+    ]
+    logs = [lse_ref[h : h + 1, :] for h in range(heads)]
     sq = sq_ref[...]
 
     def step(kb, dq):
         k, v = k_ref[kb], v_ref[kb]
-        same = sq == sk_ref[kb]
+        same = sk_ref[kb] == sq
         dk, dv = dk_ref[kb], dv_ref[kb]
         for h in range(heads):
-            scores = lax.dot_general(q_heads[h], k, NT, preferred_element_type=F32) * scale
+            scores = lax.dot_general(k, q_heads[h], NT, preferred_element_type=F32)
             weight = jnp.where(same, jnp.exp(scores - logs[h]), 0.0)
-            dp = lax.dot_general(do_heads[h], v, NT, preferred_element_type=F32)
-            ds = (weight * (dp - deltas[h]) * scale).astype(BF)
-            dv = dv + lax.dot_general(weight.astype(BF), do_heads[h], TN, preferred_element_type=F32)
-            dk = dk + lax.dot_general(ds, q_heads[h], TN, preferred_element_type=F32)
-            k_head = jnp.where(paired[h], k, jnp.zeros_like(k))
-            dq = dq + jnp.dot(ds, k_head, preferred_element_type=F32)
+            dp = lax.dot_general(v, do_heads[h], NT, preferred_element_type=F32)
+            ds = (weight * (dp - deltas[h])).astype(BF)
+            dv = dv + jnp.dot(weight.astype(BF), do_heads[h], preferred_element_type=F32)
+            dk = dk + jnp.dot(ds, q_heads[h], preferred_element_type=F32)
+            dq = dq + jnp.dot(kt_ref[kb, h], ds, preferred_element_type=F32)
         dk_ref[kb] = dk
         dv_ref[kb] = dv
         return dq
 
-    dq = lax.fori_loop(bounds[i, 0], bounds[i, 1], step, jnp.zeros((rows, width), F32))
+    dq = lax.fori_loop(bounds[i, 0], bounds[i, 1], step, jnp.zeros((width, rows), F32))
+    dq = dq.T * scale
     here = pl.ds(pl.multiple_of(i * rows, rows), rows)
     inside = pl.ds(pl.multiple_of((i % per) * rows, rows), rows)
     out_ref[i // per, 0, inside, :] = unrotate(dq, cos_ref[here, :], sin_ref[here, :]).astype(BF)
@@ -682,10 +747,11 @@
             out_ref[s, 2] = dv_ref[s].astype(BF)
 
 
-def attend_back(qkv, full, logs, grads, seg_rows, seg_blocks, cos, sin, bounds, block):
+def attend_back(qkv, full, logs, grads, seg_rows, seg_columns, cos, sin, bounds, block):
     shards, _, rows, width = qkv.shape
     total = shards * rows
     per = rows // block
+    heads = width // HEAD_DIM
     grid_spec = pltpu.PrefetchScalarGridSpec(
         num_scalar_prefetch=1,
         grid=(total // block,),
@@ -693,11 +759,11 @@
             pl.BlockSpec((None, None, block, width), lambda i, b: (i // per, 0, i % per, 0)),
             pl.BlockSpec((shards, None, rows, width), lambda i, b: (0, 1, 0, 0)),
             pl.BlockSpec((shards, None, rows, width), lambda i, b: (0, 2, 0, 0)),
+            pl.BlockSpec((width, block), lambda i, b: (0, i)),
+            pl.BlockSpec((8, block), lambda i, b: (0, i)),
             pl.BlockSpec((block, width), lambda i, b: (i, 0)),
-            pl.BlockSpec((block, 128), lambda i, b: (i, 0)),
-            pl.BlockSpec((block, width), lambda i, b: (i, 0)),
-            pl.BlockSpec((block, 1), lambda i, b: (i, 0)),
-            pl.BlockSpec((shards, 1, rows), lambda i, b: (0, 0, 0)),
+            pl.BlockSpec((1, block), lambda i, b: (0, i)),
+            pl.BlockSpec((shards, rows, 1), lambda i, b: (0, 0, 0)),
             pl.BlockSpec((total, width), lambda i, b: (0, 0)),
             pl.BlockSpec((total, width), lambda i, b: (0, 0)),
         ],
@@ -705,6 +771,7 @@
         scratch_shapes=[
             pltpu.VMEM((shards, rows, width), F32),
             pltpu.VMEM((shards, rows, width), F32),
+            pltpu.VMEM((shards, heads, width, rows), BF),
         ],
     )
     return pl.pallas_call(
@@ -715,7 +782,141 @@
         cost_estimate=pl.CostEstimate(
             flops=10 * total * total * width, bytes_accessed=16 << 20, transcendentals=0
         ),
-    )(bounds, qkv, qkv, qkv, full, logs, grads, seg_rows, seg_blocks, cos, sin)
+    )(bounds, qkv, qkv, qkv, full, logs, grads, seg_rows, seg_columns, cos, sin)
+
+
+def middle_kernel(
+    parts, clips, *refs,
+):
+    o_refs, refs = refs[:parts], refs[parts:]
+    (x_ref, g_ref, seg_ref, mod_ref, wo_ref, bo_ref, w1_ref, b1_ref, w2_ref, b2_ref) = refs[:10]
+    (out_ref, n_ref, r_ref, df_ref, dh_ref, da_ref, dx_ref, gb1_ref, gsum_ref) = refs[10:19]
+    do_refs = refs[19:]
+    rows, width = x_ref.shape
+    shards = o_refs[0].shape[0]
+    seg = seg_ref[...]
+
+    @pl.when(pl.program_id(0) == 0)
+    def _():
+        gb1_ref[...] = jnp.zeros_like(gb1_ref)
+        gsum_ref[...] = jnp.zeros_like(gsum_ref)
+
+    def of_clip(part):
+        columns = slice(part * width, (part + 1) * width)
+        value = jnp.broadcast_to(mod_ref[0:1, columns], (rows, width))
+        for c in range(1, clips):
+            value = jnp.where(seg == c, mod_ref[c : c + 1, columns], value)
+        return value
+
+    def clip_sums(at, value):
+        for c in range(clips):
+            part = jnp.sum(jnp.where(seg == c, value, 0.0), axis=0, keepdims=True)
+            gsum_ref[at + c : at + c + 1, :] += part
+
+    def column_sum(at, value):
+        gsum_ref[at : at + 1, :] += jnp.sum(value, axis=0, keepdims=True)
+
+    def mean(value):
+        return jnp.mean(value, axis=-1, keepdims=True)
+
+    heads = [o_refs[p][s] for s in range(shards) for p in range(parts)]
+    att = jnp.dot(jnp.concatenate(heads, axis=1), wo_ref[...], preferred_element_type=F32) + bo_ref[...]
+    gate_a, gate_f, scale = of_clip(2), of_clip(5), 1.0 + of_clip(4)
+    x2 = x_ref[...] + gate_a * att
+    centred = x2 - mean(x2)
+    under = lax.rsqrt(mean(centred * centred) + 1e-06)
+    y = centred * under
+    n2 = (y * scale + of_clip(3)).astype(BF)
+    n_ref[...] = n2
+    h = jnp.dot(n2, w1_ref[...], preferred_element_type=F32) + b1_ref[...]
+    root = math.sqrt(2.0 / math.pi)
+    square = h * h
+    bent = jnp.tanh(root * h * (1.0 + 0.044715 * square))
+    r = (0.5 * h * (1.0 + bent)).astype(BF)
+    r_ref[...] = r
+    slope = 0.5 * (1.0 + bent) + 0.5 * h * (1.0 - bent * bent) * root * (1.0 + 3 * 0.044715 * square)
+    fo = jnp.dot(r, w2_ref[...], preferred_element_type=F32) + b2_ref[...]
+    out_ref[...] = (x2 + gate_f * fo).astype(BF)
+
+    g = g_ref[...].astype(F32)
+    clip_sums(0, g * fo)
+    gated = g * gate_f
+    column_sum(4 * clips, gated)
+    df = gated.astype(BF)
+    df_ref[...] = df
+    dh = (lax.dot_general(df, w2_ref[...], NT, preferred_element_type=F32) * slope).astype(BF)
+    dh_ref[...] = dh
+    gb1_ref[0:1, :] += jnp.sum(dh.astype(F32), axis=0, keepdims=True)
+    dn2 = lax.dot_general(dh, w1_ref[...], NT, preferred_element_type=F32)
+    clip_sums(clips, dn2)
+    clip_sums(2 * clips, dn2 * y)
+    z = dn2 * scale
+    dx2 = g + (z - mean(z) - y * mean(z * y)) * under
+    dx_ref[...] = dx2
+    clip_sums(3 * clips, dx2 * att)
+    gated = dx2 * gate_a
+    column_sum(4 * clips + 1, gated)
+    da = gated.astype(BF)
+    da_ref[...] = da
+    do = lax.dot_general(da, wo_ref[...], NT, preferred_element_type=F32).astype(BF)
+    for s in range(shards):
+        for p in range(parts):
+            at = (s * parts + p) * LANES
+            do_refs[p][s] = do[:, at : at + LANES]
+
+
+def middle(o_parts, x1, grad, seg, mod, out_w, out_b, w1, b1, w2, b2):
+    rows, width = x1.shape
+    hidden = w1.shape[1]
+    shards, parts, clips = o_parts[0].shape[0], len(o_parts), mod.shape[0]
+    block = min(rows, 256)
+
+    def row_block(columns):
+        return pl.BlockSpec((block, columns), lambda i: (i, 0))
+
+    def whole(shape):
+        return pl.BlockSpec(shape, lambda i: (0, 0), pipeline_mode=pl.Buffered(1))
+
+    def kept(shape):
+        return pl.BlockSpec(shape, lambda i: (0, 0))
+
+    by_shard = pl.BlockSpec((shards, block, LANES), lambda i: (0, i, 0))
+    sums = -(-(4 * clips + 2) // 8) * 8
+    shape = jax.ShapeDtypeStruct
+    outs = [
+        (shape((rows, width), BF), row_block(width)),
+        (shape((rows, width), BF), row_block(width)),
+        (shape((rows, hidden), BF), row_block(hidden)),
+        (shape((rows, width), BF), row_block(width)),
+        (shape((rows, hidden), BF), row_block(hidden)),
+        (shape((rows, width), BF), row_block(width)),
+        (shape((rows, width), F32), row_block(width)),
+        (shape((8, hidden), F32), kept((8, hidden))),
+        (shape((sums, width), F32), kept((sums, width))),
+    ] + [(shape((shards, rows, LANES), BF), by_shard)] * parts
+    return pl.pallas_call(
+        partial(middle_kernel, parts, clips),
+        out_shape=[o[0] for o in outs],
+        grid=(rows // block,),
+        in_specs=[by_shard] * parts
+        + [
+            row_block(width),
+            row_block(width),
+            row_block(1),
+            whole(mod.shape),
+            whole(out_w.shape),
+            whole((1, width)),
+            whole(w1.shape),
+            whole((1, hidden)),
+            whole(w2.shape),
+            whole((1, width)),
+        ],
+        out_specs=[o[1] for o in outs],
+        compiler_params=pltpu.CompilerParams(vmem_limit_bytes=56 << 20),
+        cost_estimate=pl.CostEstimate(
+            flops=2 * rows * width * (4 * hidden + 2 * width), bytes_accessed=20 << 20, transcendentals=0
+        ),
+    )(*o_parts, x1, grad, seg, mod, out_w, out_b[None], w1, b1[None], w2, b2[None])
 
 
 def exchange(values, axis):
@@ -774,11 +975,6 @@
     out_piece, w2_piece, w1_piece = spread_slice(out_w, 0), spread_slice(ff_w2, 0), spread_slice(ff_w1, 0)
     w1_shape = w1_piece.shape
     cut = [out_piece.shape[0], out_piece.shape[0] + w2_piece.shape[0]]
-    received = to_all(jnp.concatenate([out_piece, w2_piece, w1_piece.reshape(-1, width)], axis=0))
-    out_full = gather(received[:, : cut[0]], 1).reshape(width, width)
-    w1_piece = received[:, cut[1] :].reshape((shards,) + w1_shape).transpose(1, 0, 2)
-    w1_full = gather(w1_piece.reshape(w1_shape[0], -1), 0)
-    w2_full = gather(received[:, cut[0] : cut[1]], 1).reshape(-1, width)
     all_steps = lax.all_gather(t_index, "dp", tiled=True).reshape(-1)
 
     lengths = clip_lengths[0]
@@ -831,11 +1027,19 @@
     def to_rows(values):
         return exchange(values.reshape(shards, rows, cols), "mp").transpose(1, 0, 2).reshape(rows, width)
 
-    spread_in = spread(to_channels(x0.astype(BF)).astype(F32), starts, ends)
-    real = spread(jnp.ones((total, 1), F32), starts, ends)
+    channels = to_channels(x0.astype(BF))
+    pieces = jnp.concatenate([out_piece, w2_piece, w1_piece.reshape(-1, width)], axis=0)
+    pieces, channels = lax.optimization_barrier((pieces, channels))
+    spread_in = spread(channels.astype(F32), starts, ends)
     pre_a = apply_conv(spread_in, pos_conv[0], False) + pos_bias[0]
+    received = to_all(pieces)
+    received, pre_a = lax.optimization_barrier((received, pre_a))
+    out_full = gather(received[:, : cut[0]], 1).reshape(width, width)
+    w1_piece = received[:, cut[1] :].reshape((shards,) + w1_shape).transpose(1, 0, 2)
+    w1_full = gather(w1_piece.reshape(w1_shape[0], -1), 0)
+    w2_full = gather(received[:, cut[0] : cut[1]], 1).reshape(-1, width)
     y_a = jnp.pad(
-        jnp.where(real[GAP:-GAP] > 0, mish(pre_a), 0.0).astype(BF).astype(F32), ((GAP, GAP), (0, 0))
+        only_clips(mish(pre_a), starts, ends).astype(BF).astype(F32), ((GAP, GAP), (0, 0))
     )
     pre_b = apply_conv(y_a, pos_conv[1], False) + pos_bias[1]
     c_pos = to_rows(gather_back(mish(pre_b).astype(BF), starts, ends))
@@ -856,43 +1060,28 @@
     sin_own = lax.dynamic_slice_in_dim(sin, first, rows)
     parts = range(cols // LANES)
     qkv = [exchange(v, "mp") for v in project(n1, qkv_full, qkv_bias, cos_own, sin_own)]
-    block = 256
+    block = rows
     heads_of = segment[::block]
     tails_of = segment[block - 1 :: block]
     low_key = jnp.sum(jnp.where(heads_of[:, None] == clip_index, starts[None, :], 0), axis=1)
     high_key = jnp.sum(jnp.where(tails_of[:, None] == clip_index, ends[None, :], 0), axis=1)
     bounds = jnp.stack([low_key // rows, (high_key + rows - 1) // rows], axis=1).astype(jnp.int32)
-    seg_rows = segment[:, None]
-    seg_blocks = segment.reshape(shards, 1, rows)
+    seg_rows = segment[None, :]
+    seg_blocks = segment.reshape(shards, rows, 1)
     attended = [attend(qkv[h], seg_rows, seg_blocks, bounds, block) for h in parts]
-    o_rows = jnp.stack([exchange(a[0].reshape(shards, rows, LANES), "mp") for a in attended])
-    o_rows = o_rows.transpose(2, 1, 0, 3).reshape(rows, width)
-
-    def residual(state, mod_in, summed, bias, part):
-        return state + expand(hot, mod_in[:, part * width : (part + 1) * width]) * (summed + bias)
-
-    x2, att_pull = jax.vjp(
-        lambda s, m, a, b: residual(s, m, a, b, 2), x1, mod, dot(o_rows, out_full), out_b
-    )
-
-    n2, n2_pull = jax.vjp(lambda s, m: modulate(s, m, 3, 4), x2, mod)
-    n2 = n2.astype(BF)
-    r, r_pull = jax.vjp(
-        lambda v, b: jax.nn.gelu(v + b, approximate=True), dot(n2, w1_full), b1_full
-    )
-    r = r.astype(BF)
-    out, ff_pull = jax.vjp(lambda s, m, a, b: residual(s, m, a, b, 5), x2, mod, dot(r, w2_full), ff_b2)
-
-    grad = lax.dynamic_slice_in_dim(out_grad, first, rows).astype(F32)
-    dx2, dmod_a, df, g_ff_b2 = ff_pull(grad)
-    df = df.astype(BF)
+    o_parts = [exchange(a[0].reshape(shards, rows, LANES), "mp") for a in attended]
+    grad = lax.dynamic_slice_in_dim(out_grad, first, rows)
+    seg_own = lax.dynamic_slice_in_dim(segment, first, rows)[:, None]
+    out, n2, r, df, dh, da, dx2, g_ff_b1, sums, *do_parts = middle(
+        o_parts, x1, grad, seg_own, mod, out_full, out_b, w1_full, b1_full, w2_full, ff_b2
+    )
+    g_ff_b1, g_ff_b2, g_out_b = g_ff_b1[0], sums[4 * clips], sums[4 * clips + 1]
+    dmod_gate_f, dmod_shift_f, dmod_scale_f, dmod_gate_a = (
+        sums[i * clips : (i + 1) * clips] for i in range(4)
+    )
     g_ff_w2 = dot(df, r, TN)
-    dh, g_ff_b1 = r_pull(dot(df, w2_full, NT))
-    g_ff_b1 = jnp.sum(dh.astype(BF).astype(F32), axis=0)
-    dh = dh.astype(BF)
     g_ff_w1 = dot(n2, dh, TN)
-    more, dmod_b = n2_pull(dot(dh, w1_full, NT))
-    dx2 = dx2 + more
+    o_rows = jnp.stack(o_parts).transpose(2, 1, 0, 3).reshape(rows, width)
 
     def for_dp(matrix):
         return matrix.astype(BF).reshape(groups, matrix.shape[0] // groups, matrix.shape[1])
@@ -905,38 +1094,34 @@
 
     sent_w1, sent_w2 = scatter_dp(g_ff_w1), scatter_dp(g_ff_w2)
 
-    dx1, dmod_c, da, g_out_b = att_pull(dx2)
-    da = da.astype(BF)
     g_out_w = dot(da, o_rows, TN)
-    do = dot(da, out_full, NT).astype(BF).reshape(rows, shards, -1, LANES)
     dqkv = []
     for h in parts:
-        do_part = exchange(do[:, :, h].transpose(1, 0, 2), "mp").reshape(total, LANES)
+        do_part = exchange(do_parts[h], "mp").reshape(total, LANES)
         d_part = attend_back(
             qkv[h], attended[h][1], attended[h][2], do_part, seg_rows, seg_blocks, cos, sin, bounds, block
         )
         dqkv.append(exchange(d_part, "mp"))
-    result = lax.all_gather(out.astype(BF), "mp", tiled=True)
-    result, dqkv = lax.optimization_barrier((result, dqkv))
-    result = result.astype(F32)
-    dqkv = jnp.stack(dqkv).transpose(3, 1, 2, 0, 4).reshape(rows, 3 * width)
-    g_qkv_w = dot(n1, dqkv, TN)
-    g_qkv_b = jnp.sum(dqkv.astype(F32), axis=0).reshape(shards, 3, cols)
-    w_all = qkv_full.transpose(2, 0, 1, 3).reshape(width, 3 * width)
-    more, dmod_d = n1_pull(dot(dqkv, w_all, NT))
-    dx1 = dx1 + more
-    sent_w1, sent_w2, dx1 = lax.optimization_barrier((sent_w1, sent_w2, dx1))
+    dn1, g_qkv_w, g_qkv_b = unproject(dqkv, n1, qkv_full)
+    more, dmod_d = n1_pull(dn1)
+    dx1 = dx2 + more
+    sent_w1, sent_w2, dx1, out = lax.optimization_barrier((sent_w1, sent_w2, dx1, out))
+    result = lax.all_gather(out, "mp", tiled=True)
     ff_pair = jnp.concatenate([by_rank(sent_w1), by_rank(sent_w2)], axis=2)
     sent_qkv, sent_out = scatter_dp(g_qkv_w), scatter_dp(g_out_w)
 
-    dmod = dmod_a + dmod_b + dmod_c + dmod_d
+    dmod = dmod_d + jnp.concatenate(
+        [
+            jnp.zeros((clips, 2 * width), F32), dmod_gate_a, dmod_shift_f, dmod_scale_f, dmod_gate_f,
+        ],
+        axis=1,
+    )
 
     slope_b = gather_back(mish_slope(pre_b), starts, ends)
     dy_b = to_channels(dx1.astype(BF)).astype(F32) * slope_b
     g_pos_b = jnp.sum(dy_b, axis=0)
     dy_b = spread(dy_b.astype(BF).astype(F32), starts, ends)
-    dy_a = apply_conv(dy_b, pos_conv[1], True) * mish_slope(pre_a)
-    dy_a = jnp.where(real[GAP:-GAP] > 0, dy_a, 0.0)
+    dy_a = only_clips(apply_conv(dy_b, pos_conv[1], True) * mish_slope(pre_a), starts, ends)
     g_pos_a = jnp.sum(dy_a, axis=0)
     dy_a = jnp.pad(dy_a.astype(BF).astype(F32), ((GAP, GAP), (0, 0)))
     dc = gather_back(
@@ -962,7 +1147,8 @@
     dtext = jnp.pad(dot(dx0, emb_text, NT), ((HALO, HALO), (0, 0)))
     text_grads = [None] * blocks
     extra = dmod
-    at_got, dtext = lax.optimization_barrier((exchange(at_pair, "mp"), dtext))
+    at_got, result, dtext = lax.optimization_barrier((exchange(at_pair, "mp"), result, dtext))
+    result = result.astype(F32)
     for b in reversed(range(blocks)):
         dtext, text_grads[b], summed = text_behind(kept[b], dtext, txt_up[b], txt_down[b], extra)
         if extra is not None:

time: 1020 us -> 973 us (0.954)
  blocking collectives: 29.2 us -> 117 us
  matrix products: 172 us -> 117 us
  waiting for transfers between devices: 187 us -> 137 us
  Pallas kernels: 257 us -> 287 us
  other arithmetic: 129 us -> 99.8 us
  starting transfers between devices: 73.4 us -> 58.5 us
  local copies, waits for them, and re-layouts: 135 us -> 124 us
    all_to_all x0 -> x3, blocking collectives: none -> 98.2 us  [exchange(): return lax.all_to_all(values, axis, 0, 0)]
    all_to_all x14 -> x11, waiting for transfers between devices: 180 us -> 91 us  [exchange(): return lax.all_to_all(values, axis, 0, 0)]
    dot_general x30 -> x22, matrix products: 118 us -> 66.9 us  [dot(): lax.dot_general(left.astype(BF), right.astype(BF), dims, preferred_elemen...]
    pallas_call x0 -> x2, Pallas kernels: none -> 34.9 us  [the longest x1 23.4 us: middle(): pl.pallas_call(partial(middle_kernel, parts, clips), out_shape=[o[0] for...]
    all_to_all x2, waiting for transfers between devices: 0.01 us -> 18.4 us  [to_all(): lax.all_to_all(jnp.broadcast_to(piece[None], (size,) + piece.shape), axis...]
    all_gather x1, waiting for transfers between devices: 0.01 us -> 16.8 us  [local(): result = lax.all_gather(out, 'mp', tiled=True)]
    all_to_all x14 -> x11, starting transfers between devices: 60.8 us -> 46.4 us  [exchange(): return lax.all_to_all(values, axis, 0, 0)]
    transpose x3 -> x1, local copies, waits for them, and re-layouts: 14.3 us -> 2.36 us  [local(): o_rows = jnp.stack(o_parts).transpose(2, 1, 0, 3).reshape(rows, width)]
  transfers between devices with their start and end apart: 27 -> 24, of which waited for: 11 -> 12; matrix products, arithmetic and copies ran while one was open for 35% -> 28% of each run, Pallas kernels for 19% -> 21%
where the time goes in v5:
time: 973 us; the launch traced here: 963 us
  Pallas kernels  287 us (29%)
  waiting for transfers between devices  137 us (14%)
  local copies, waits for them, and re-layouts  124 us (13%)
  matrix products  117 us (12%)
  blocking collectives  117 us (12%)
  other arithmetic  99.8 us (10%)
  starting transfers between devices  58.5 us (6%)
  between operations  22.8 us (2%)
    all_to_all x3, blocking collectives, exchange(): return lax.all_to_all(values, axis, 0, 0)  98.2 us
    all_to_all x11, waiting for transfers between devices, exchange(): return lax.all_to_all(values, axis, 0, 0)  91 us
    dot_general x22, matrix products, dot(): lax.dot_general(left.astype(BF), right.astype(BF), dims, preferred_elemen...  66.9 us
    pallas_call x1, Pallas kernels, last_sums(): pl.pallas_call(partial(last_kernel, dp, mp, n_all, n_mp, n_both, n_gather...  65.4 us
    unnamed x677, local copies, waits for them, and re-layouts  49.8 us
    pallas_call x2, Pallas kernels, attend_back(): pl.pallas_call(attend_back_kernel, out_shape=jax.ShapeDtypeStruct((shards...  47.5 us
    all_to_all x11, starting transfers between devices, exchange(): return lax.all_to_all(values, axis, 0, 0)  46.4 us
    pallas_call x4, Pallas kernels, apply_conv(): pl.pallas_call(partial(conv_kernel, taps, turned), out_shape=jax.ShapeDty...  39.2 us
  transfers between devices with their start and end apart: 24, of which 12 were waited for; matrix products, arithmetic and copies ran while one was open for 28% of the time, Pallas kernels for 21%

profile of v5, /device:TPU:0, one launch (start us, length us, event | category | flops | bytes accessed | tf_op | source)
XLA Modules:
  0.0 962.8 jit_solution(15656279982239664910)
XLA Ops:
  52.6 7.6 multiply_multiply_fusion.12
  94.8 9.2 all-to-all-done
  111.5 9.8 %shard_map.495 = f32[2112,256]{1,0:T(8,128)S(1)} custom-call(f32[2144,256]{1,0:T(8,128)S(1)} %pad_add_fusion.1.x_ref, bf16[31,64,256]{2,1,0:T(8,128)(2,1)S(1)} %get-tuple-element.418.w_ref), custom_call_target="tpu_custom_call" | custom-call | flops 8581545984 | bytes 8388608 | tf_op jit(solution)/shard_map/pallas_call | solution.py:439
  121.5 18.4 %all-to-all-done.1 = bf16[4,160,1024]{2,1,0:T(8,128)(2,1)} async-done(((bf16[4,160,1024]{2,1,0:T(8,128)(2,1)}), bf16[4,160,1024]{2,1,0:T(8,128)(2,1)}, u32[]{:S(2)}, u32[]{:S(2)}) %all-to-all-start.1) | async-done | bytes 1310752 | tf_op jit(solution)/shard_map/all_to_all | solution.py:950
  163.4 7.2 fusion.139
  173.9 9.8 %shard_map.496 = f32[2112,256]{1,0:T(8,128)S(1)} custom-call(f32[2144,256]{1,0:T(8,128)S(1)} %pad_convert_fusion.x_ref, bf16[31,64,256]{2,1,0:T(8,128)(2,1)S(1)} %copy-done.17), custom_call_target="tpu_custom_call" | custom-call | flops 8581545984 | bytes 8388608 | tf_op jit(solution)/shard_map/pallas_call | solution.py:439
  193.7 24.2 %all-to-all-done.2 = bf16[4,512,256]{2,1,0:T(8,128)(2,1)S(1)} async-done(((bf16[4,512,256]{2,1,0:T(8,128)(2,1)}), bf16[4,512,256]{2,1,0:T(8,128)(2,1)S(1)}, u32[]{:S(2)}, u32[]{:S(2)}) %all-to-all-start.2) | async-done | bytes 1048608 | tf_op jit(solution)/shard_map/all_to_all | solution.py:923
  234.7 39.8 %all_to_all.80.q_ref.k_ref.v_ref = bf16[4,3,512,128]{3,2,1,0:T(8,128)(2,1)} all-to-all(bf16[4,3,512,128]{3,2,1,0:T(8,128)(2,1)S(1)} %get-tuple-element.104), channel_id=1, replica_groups=mesh['dp'=8,'mp'=4] {'mp'}, dimensions={0} | all-to-all | bytes 3145728 | tf_op jit(solution)/shard_map/all_to_all | solution.py:923
  284.1 17.0 %shard_map.498 = (bf16[2048,128]{1,0:T(8,128)(2,1)}, f32[128,2048]{1,0:T(8,128)S(1)}, f32[8,2048]{1,0:T(8,128)S(1)}) custom-call(s32[4,2]{1,0:T(4,128)S(1)} %pad_add_fusion.16.bounds, bf16[4,3,512,128]{3,2,1,0:T(8,128)(2,1)S(1)} %copy-done.8, bf16[4,3,512,128]{3,2,1,0:T(8,128)(2,1)S(1)} %copy-done.8, bf16[4,3,512,128]{3,2,1,0:T(8,128)(2,1)S(1)} %copy-done.8, ...), custom_call_target="tpu_custom_call" | custom-call | flops 2147483648 | bytes 8388608 | tf_op jit(solution)/shard_map/pallas_call | solution.py:671
  302.1 12.1 %all-to-all-done.6.q_ref.k_ref.v_ref = bf16[4,3,512,128]{3,2,1,0:T(8,128)(2,1)S(1)} async-done(((bf16[4,3,512,128]{3,2,1,0:T(8,128)(2,1)}), bf16[4,3,512,128]{3,2,1,0:T(8,128)(2,1)S(1)}, u32[]{:S(2)}, u32[]{:S(2)}) %all-to-all-start.6) | async-done | bytes 1572896 | tf_op jit(solution)/shard_map/all_to_all | solution.py:923
  319.0 17.0 %shard_map.499 = (bf16[2048,128]{1,0:T(8,128)(2,1)}, f32[128,2048]{1,0:T(8,128)S(1)}, f32[8,2048]{1,0:T(8,128)S(1)}) custom-call(s32[4,2]{1,0:T(4,128)S(1)} %pad_add_fusion.16.bounds, bf16[4,3,512,128]{3,2,1,0:T(8,128)(2,1)S(1)} %all-to-all-done.6.q_ref.k_ref.v_ref, bf16[4,3,512,128]{3,2,1,0:T(8,128)(2,1)S(1)} %all-to-all-done.6.q_ref.k_ref.v_ref, ...), custom_call_target="tpu_custom_call" | custom-call | flops 2147483648 | bytes 8388608 | tf_op jit(solution)/shard_map/pallas_call | solution.py:671
  345.8 9.6 all-to-all-done.7.refs_1_
  356.2 23.4 %shard_map.500 = (bf16[512,1024]{1,0:T(8,128)(2,1)}, bf16[512,1024]{1,0:T(8,128)(2,1)}, bf16[512,2048]{1,0:T(8,128)(2,1)}, bf16[512,1024]{1,0:T(8,128)(2,1)}, bf...) custom-call(bf16[4,512,128]{2,1,0:T(8,128)(2,1)} %copy-done.75, ...), custom_call_target="tpu_custom_call" | custom-call | flops 10737418240 | bytes 20971520 | tf_op jit(solution)/shard_map/pallas_call | solution.py:897
  393.2 18.4 %all_to_all.81 = bf16[4,512,128]{2,1,0:T(8,128)(2,1)} all-to-all(bf16[4,512,128]{2,1,0:T(8,128)(2,1)} %get-tuple-element.111), channel_id=1, replica_groups=mesh['dp'=8,'mp'=4] {'mp'}, dimensions={0} | all-to-all | bytes 1048576 | tf_op jit(solution)/shard_map/all_to_all | solution.py:923
  418.1 23.7 %shard_map.501 = bf16[4,3,512,128]{3,2,1,0:T(8,128)(2,1)} custom-call(s32[4,2]{1,0:T(4,128)S(1)} %pad_add_fusion.16.bounds, bf16[4,3,512,128]{3,2,1,0:T(8,128)(2,1)} %all_to_all.80.q_ref.k_ref.v_ref, bf16[4,3,512,128]{3,2,1,0:T(8,128)(2,1)} %all_to_all.80.q_ref.k_ref.v_ref, bf16[4,3,512,128]{3,2,1,0:T(8,128)(2,1)} %all_to_all.80.q_ref.k_ref.v_ref, ...), custom_call_target="tpu_custom_call" | custom-call | flops 5368709120 | bytes 16777216 | tf_op jit(solution)/shard_map/pallas_call | solution.py:777
  457.3 23.8 %shard_map.502 = bf16[4,3,512,128]{3,2,1,0:T(8,128)(2,1)} custom-call(s32[4,2]{1,0:T(4,128)S(1)} %pad_add_fusion.16.bounds, bf16[4,3,512,128]{3,2,1,0:T(8,128)(2,1)} %copy-done.7, bf16[4,3,512,128]{3,2,1,0:T(8,128)(2,1)} %copy-done.7, bf16[4,3,512,128]{3,2,1,0:T(8,128)(2,1)} %copy-done.7, f32[128,2048]{1,0:T(8,128)S(1)} %copy-done.27, ...), custom_call_target="tpu_custom_call" | custom-call | flops 5368709120 | bytes 16777216 | tf_op jit(solution)/shard_map/pallas_call | solution.py:777
  482.4 40.0 %all_to_all.82.refs_1_ = bf16[4,3,512,128]{3,2,1,0:T(8,128)(2,1)S(1)} all-to-all(bf16[4,3,512,128]{3,2,1,0:T(8,128)(2,1)} %shard_map.502), channel_id=1, replica_groups=mesh['dp'=8,'mp'=4] {'mp'}, dimensions={0} | all-to-all | bytes 3145728 | tf_op jit(solution)/shard_map/all_to_all | solution.py:923
  522.4 11.5 %shard_map.503 = (f32[512,1024]{1,0:T(8,128)}, bf16[1024,3072]{1,0:T(8,128)(2,1)}, f32[4,3,256]{2,1,0:T(4,128)S(1)}) custom-call(bf16[4,3,512,128]{3,2,1,0:T(8,128)(2,1)} %all-to-all-done.9.refs_0_, bf16[4,3,512,128]{3,2,1,0:T(8,128)(2,1)S(1)} %all_to_all.82.refs_1_, bf16[512,1024]{1,0:T(8,128)(2,1)S(1)} %copy-done.11, ...), custom_call_target="tpu_custom_call" | custom-call | flops 6442450944 | bytes 20971520 | tf_op jit(solution)/shard_map/pallas_call | solution.py:566
  534.6 8.3 all-gather
  573.8 14.9 %all-to-all-done.13 = bf16[4,512,256]{2,1,0:T(8,128)(2,1)S(1)} async-done(((bf16[4,512,256]{2,1,0:T(8,128)(2,1)}), bf16[4,512,256]{2,1,0:T(8,128)(2,1)S(1)}, u32[]{:S(2)}, u32[]{:S(2)}) %all-to-all-start.13) | async-done | bytes 1048608 | tf_op jit(solution)/shard_map/all_to_all | solution.py:923
  599.4 9.8 %shard_map.504 = f32[2112,256]{1,0:T(8,128)S(1)} custom-call(f32[2144,256]{1,0:T(8,128)S(1)} %pad_add_fusion.x_ref, bf16[31,64,256]{2,1,0:T(8,128)(2,1)S(1)} %copy-done.18), custom_call_target="tpu_custom_call" | custom-call | flops 8581545984 | bytes 8388608 | tf_op jit(solution)/shard_map/pallas_call | solution.py:439
  614.3 9.8 %shard_map.505 = f32[2112,256]{1,0:T(8,128)S(1)} custom-call(f32[2144,256]{1,0:T(8,128)S(1)} %pad.199.x_ref, bf16[31,64,256]{2,1,0:T(8,128)(2,1)S(1)} %copy-done.16), custom_call_target="tpu_custom_call" | custom-call | flops 8581545984 | bytes 8388608 | tf_op jit(solution)/shard_map/pallas_call | solution.py:439
  638.1 15.7 %shard_map.507 = f32[256,1984]{1,0:T(8,128)S(1)} custom-call(f32[2144,256]{1,0:T(8,128)} %copy-done.3, f32[2112,256]{1,0:T(8,128)S(1)} %copy-done.4), custom_call_target="tpu_custom_call" | custom-call | flops 8581545984 | bytes 8388608 | tf_op jit(solution)/shard_map/pallas_call | solution.py:478
  653.9 15.7 %shard_map.506 = f32[256,1984]{1,0:T(8,128)S(1)} custom-call(f32[2144,256]{1,0:T(8,128)} %copy-done.2, f32[2112,256]{1,0:T(8,128)S(1)} %convert_element_type.356.g_ref), custom_call_target="tpu_custom_call" | custom-call | flops 8581545984 | bytes 8388608 | tf_op jit(solution)/shard_map/pallas_call | solution.py:478
  676.1 12.8 %all-to-all-done.14 = bf16[4,512,256]{2,1,0:T(8,128)(2,1)S(1)} async-done(((bf16[4,512,256]{2,1,0:T(8,128)(2,1)}), bf16[4,512,256]{2,1,0:T(8,128)(2,1)S(1)}, u32[]{:S(2)}, u32[]{:S(2)}) %all-to-all-start.14) | async-done | bytes 1048608 | tf_op jit(solution)/shard_map/all_to_all | solution.py:923
  712.3 16.8 %all-gather.16.cloned.1.call-done = bf16[2048,1024]{1,0:T(8,128)(2,1)} async-done(((bf16[512,1024]{1,0:T(8,128)(2,1)}), bf16[2048,1024]{1,0:T(8,128)(2,1)}) %all-gather.16.cloned.1.call-update) | async-done | bytes 4194320 | tf_op jit(solution)/shard_map/all_gather | solution.py:1109
  735.1 11.4 %shard_map.508 = f32[4,7168]{1,0:T(4,128)S(1)} custom-call(f32[4,7168]{1,0:T(4,128)S(1)} %pad_maximum_fusion.10.x_ref), custom_call_target="tpu_custom_call" | custom-call | tf_op jit(solution)/shard_map/pallas_call | solution.py:115
  761.7 10.5 %reduce-scatter.17.cloned.1.call-done = bf16[32,3968]{1,0:T(8,128)(2,1)} async-done(((bf16[256,3968]{1,0:T(8,128)(2,1)}), bf16[32,3968]{1,0:T(8,128)(2,1)}) %reduce-scatter.17.cloned.1.call-update) | async-done | bytes 253968 | tf_op jit(solution)/shard_map/reduce_scatter | solution.py:1093
  778.5 10.7 %all-gather.1 = f32[8,4,6144]{2,1,0:T(4,128)S(1)} all-gather(f32[1,4,6144]{2,1,0:T(4,128)S(1)} %slice_bitcast_fusion.7), channel_id=1, replica_groups=mesh['dp'=8,'mp'=4] {'dp'}, dimensions={0}, use_global_device_ids=true | all-gather | bytes 884736 | tf_op jit(solution)/shard_map/all_gather | solution.py:1155
  791.7 8.6 fusion.47
  810.4 6.8 convert_element_type.241
  873.4 65.4 %shard_map.510 = (f32[16,2560]{1,0:T(8,128)}, f32[32,512]{1,0:T(8,128)}, f32[32,512]{1,0:T(8,128)}, f32[16,1024]{1,0:T(8,128)}, f32[16,1024]{1,0:T(8,128)}, /*in...) custom-call(bf16[4,2,64,2560]{3,2,1,0:T(8,128)(2,1)} %bitcast.368, bf16[4,2,128,512]{3,2,1,0:T(8,128)(2,1)} %bitcast.380, ...), custom_call_target="tpu_custom_call" | custom-call | tf_op jit(solution)/shard_map/pallas_call | solution.py:278
  (1046 shorter events, 400.5 us)
Async XLA Ops:
  13.1 31.7 %all-to-all-start.3 = ((bf16[4,400,256]{2,1,0:T(8,128)(2,1)}), bf16[4,400,256]{2,1,0:T(8,128)(2,1)}, u32[]{:S(2)}, u32[]{:S(2)}) async-start(bf16[4,400,256]{2,1,0:T(8,128)(2,1)} %broadcast_in_dim.310), calls=%async_computation.3 | async-start | bytes 1638400 | tf_op jit(solution)/shard_map/all_to_all | solution.py:950
  19.4 207.8 %all-gather.8.cloned.1.call-start = ((), (), s32[]{:S(2)}) async-start(), calls=%async_computation.22 | async-start | bytes 7077888 | tf_op jit(solution)/shard_map/all_gather | solution.py:953
  22.1 48.0 %copy-start.155 = (f32[1,1,1024]{2,0,1:T(1,128)}, f32[1,1,1024]{2,0,1:T(1,128)S(1)}, u32[]{:S(2)}) copy-start(f32[1,1,1024]{2,0,1:T(1,128)S(1)} %get-tuple-element.481) | copy-start | bytes 12292
  36.8 709.7 %copy-start.100 = (pred[528,4]{0,1:T(4,128)(4,1)}, pred[528,4]{0,1:T(4,128)(4,1)S(1)}, u32[]{:S(2)}) copy-start(pred[528,4]{0,1:T(4,128)(4,1)S(1)} %get-tuple-element.404) | copy-start | bytes 6340
  76.8 27.2 %all-to-all-start = ((bf16[4,512,256]{2,1,0:T(8,128)(2,1)}), bf16[4,512,256]{2,1,0:T(8,128)(2,1)S(1)}, u32[]{:S(2)}, u32[]{:S(2)}) async-start(bf16[4,512,256]{2,1,0:T(8,128)(2,1)} %bitcast.345), calls=%async_computation | async-start | bytes 2097152 | tf_op jit(solution)/shard_map/all_to_all | solution.py:923
  87.6 98.7 %copy-start.182 = (pred[2048]{0:T(1024)(128)(4,1)}, pred[2048]{0:T(1024)(128)(4,1)S(1)}, u32[]{:S(2)}) copy-start(pred[2048]{0:T(1024)(128)(4,1)S(1)} %get-tuple-element.574) | copy-start | bytes 6148
  88.9 97.4 %copy-start.184 = (pred[2048]{0:T(1024)(128)(4,1)}, pred[2048]{0:T(1024)(128)(4,1)S(1)}, u32[]{:S(2)}) copy-start(pred[2048]{0:T(1024)(128)(4,1)S(1)} %get-tuple-element.576) | copy-start | bytes 6148
  90.3 96.1 %copy-start.186 = (pred[2048]{0:T(1024)(128)(4,1)}, pred[2048]{0:T(1024)(128)(4,1)S(1)}, u32[]{:S(2)}) copy-start(pred[2048]{0:T(1024)(128)(4,1)S(1)} %get-tuple-element.578) | copy-start | bytes 6148
  105.3 34.6 %all-to-all-start.1 = ((bf16[4,160,1024]{2,1,0:T(8,128)(2,1)}), bf16[4,160,1024]{2,1,0:T(8,128)(2,1)}, u32[]{:S(2)}, u32[]{:S(2)}) async-start(bf16[4,160,1024]{2,1,0:T(8,128)(2,1)} %broadcast_in_dim.307), calls=%async_computation.1 | async-start | bytes 2621440 | tf_op jit(solution)/shard_map/all_to_all | solution.py:950
  109.6 236.2 %all-gather.10.cloned.1.call-start = ((), (), s32[]{:S(2)}) async-start(), calls=%async_computation.23 | async-start | bytes 2359296 | tf_op jit(solution)/shard_map/all_gather | solution.py:953
  121.5 49.2 %copy-start.39 = (f32[2112,256]{1,0:T(8,128)}, f32[2112,256]{1,0:T(8,128)S(1)}, u32[]{:S(2)}) copy-start(f32[2112,256]{1,0:T(8,128)S(1)} %broadcast_add_fusion) | copy-start | bytes 6488068
  141.5 204.3 %all-gather.12.cloned.1.call-start = ((), (), s32[]{:S(2)}) async-start(), calls=%async_computation.24 | async-start | bytes 4718592 | tf_op jit(solution)/shard_map/all_gather | solution.py:953
  189.1 28.8 %all-to-all-start.2 = ((bf16[4,512,256]{2,1,0:T(8,128)(2,1)}), bf16[4,512,256]{2,1,0:T(8,128)(2,1)S(1)}, u32[]{:S(2)}, u32[]{:S(2)}) async-start(bf16[4,512,256]{2,1,0:T(8,128)(2,1)} %bitcast.59), calls=%async_computation.2 | async-start | bytes 2097152 | tf_op jit(solution)/shard_map/all_to_all | solution.py:923
  192.7 153.1 %all-gather.14.cloned.1.call-start = ((), (), s32[]{:S(2)}) async-start(), calls=%async_computation.25 | async-start | bytes 4718592 | tf_op jit(solution)/shard_map/all_gather | solution.py:953
  234.6 39.8 %copy-start.9 = (bf16[4,3,512,128]{3,2,1,0:T(8,128)(2,1)}, bf16[4,3,512,128]{3,2,1,0:T(8,128)(2,1)S(1)}, u32[]{:S(2)}) copy-start(bf16[4,3,512,128]{3,2,1,0:T(8,128)(2,1)S(1)} %get-tuple-element.108) | copy-start | bytes 4718596
  274.4 39.7 %all-to-all-start.6 = ((bf16[4,3,512,128]{3,2,1,0:T(8,128)(2,1)}), bf16[4,3,512,128]{3,2,1,0:T(8,128)(2,1)S(1)}, u32[]{:S(2)}, u32[]{:S(2)}) async-start(bf16[4,3,512,128]{3,2,1,0:T(8,128)(2,1)} %copy-done.9), calls=%async_computation.6 | async-start | bytes 3145728 | tf_op jit(solution)/shard_map/all_to_all | solution.py:923
  314.1 22.8 %all-to-all-start.5 = ((bf16[4,512,128]{2,1,0:T(8,128)(2,1)}), bf16[4,512,128]{2,1,0:T(8,128)(2,1)S(1)}, u32[]{:S(2)}, u32[]{:S(2)}) async-start(bf16[4,512,128]{2,1,0:T(8,128)(2,1)} %bitcast.83), calls=%async_computation.5 | async-start | bytes 1048576 | tf_op jit(solution)/shard_map/all_to_all | solution.py:923
  337.0 18.5 %all-to-all-start.7 = ((bf16[4,512,128]{2,1,0:T(8,128)(2,1)}), bf16[4,512,128]{2,1,0:T(8,128)(2,1)S(1)}, u32[]{:S(2)}, u32[]{:S(2)}) async-start(bf16[4,512,128]{2,1,0:T(8,128)(2,1)} %bitcast.84), calls=%async_computation.7 | async-start | bytes 1048576 | tf_op jit(solution)/shard_map/all_to_all | solution.py:923
  342.0 213.8 %reduce-scatter.11.cloned.1.call-start = ((), (), s32[]{:S(2)}) async-start(), calls=%async_computation.28 | async-start | bytes 4718592 | tf_op jit(solution)/shard_map/reduce_scatter | solution.py:1093
  386.0 169.8 %reduce-scatter.13.cloned.1.call-start = ((), (), s32[]{:S(2)}) async-start(), calls=%async_computation.29 | async-start | bytes 4718592 | tf_op jit(solution)/shard_map/reduce_scatter | solution.py:1093
  411.6 30.2 %all-to-all-start.10 = ((bf16[4,512,128]{2,1,0:T(8,128)(2,1)}), bf16[4,512,128]{2,1,0:T(8,128)(2,1)}, u32[]{:S(2)}, u32[]{:S(2)}) async-start(bf16[4,512,128]{2,1,0:T(8,128)(2,1)} %get-tuple-element.114), calls=%async_computation.10 | async-start | bytes 1048576 | tf_op jit(solution)/shard_map/all_to_all | solution.py:923
  441.8 40.6 %all-to-all-start.9 = ((bf16[4,3,512,128]{3,2,1,0:T(8,128)(2,1)}), bf16[4,3,512,128]{3,2,1,0:T(8,128)(2,1)}, u32[]{:S(2)}, u32[]{:S(2)}) async-start(bf16[4,3,512,128]{3,2,1,0:T(8,128)(2,1)} %shard_map.501), calls=%async_computation.9 | async-start | bytes 3145728 | tf_op jit(solution)/shard_map/all_to_all | solution.py:923
  446.9 244.2 %reduce-scatter.9.cloned.1.call-start = ((), (), s32[]{:S(2)}) async-start(), calls=%async_computation.27 | async-start | bytes 2359296 | tf_op jit(solution)/shard_map/reduce_scatter | solution.py:1093
  456.0 235.1 %reduce-scatter.7.cloned.1.call-start = ((), (), s32[]{:S(2)}) async-start(), calls=%async_computation.26 | async-start | bytes 7077888 | tf_op jit(solution)/shard_map/reduce_scatter | solution.py:1093
  481.1 41.3 %copy-start.11 = (bf16[512,1024]{1,0:T(8,128)(2,1)S(1)}, bf16[512,1024]{1,0:T(8,128)(2,1)}, u32[]{:S(2)}) copy-start(bf16[512,1024]{1,0:T(8,128)(2,1)} %copy-done.10) | copy-start | bytes 3145732
  558.7 30.1 %all-to-all-start.13 = ((bf16[4,512,256]{2,1,0:T(8,128)(2,1)}), bf16[4,512,256]{2,1,0:T(8,128)(2,1)S(1)}, u32[]{:S(2)}, u32[]{:S(2)}) async-start(bf16[4,512,256]{2,1,0:T(8,128)(2,1)} %bitcast.343), calls=%async_computation.17 | async-start | bytes 2097152 | tf_op jit(solution)/shard_map/all_to_all | solution.py:923
  562.2 166.9 %all-gather.16.cloned.1.call-start = ((), (), s32[]{:S(2)}) async-start(), calls=%async_computation.30 | async-start | bytes 5242880 | tf_op jit(solution)/shard_map/all_gather | solution.py:1109
  589.7 41.5 %all-to-all-start.12 = ((bf16[4,128,1024]{2,1,0:T(8,128)(2,1)}), bf16[4,128,1024]{2,1,0:T(8,128)(2,1)S(1)}, u32[]{:S(2)}, u32[]{:S(2)}) async-start(bf16[4,128,1024]{2,1,0:T(8,128)(2,1)} %pad_maximum_fusion.2), calls=%async_computation.16 | async-start | bytes 2097152 | tf_op jit(solution)/shard_map/all_to_all | solution.py:923
  632.2 56.7 %all-to-all-start.14 = ((bf16[4,512,256]{2,1,0:T(8,128)(2,1)}), bf16[4,512,256]{2,1,0:T(8,128)(2,1)S(1)}, u32[]{:S(2)}, u32[]{:S(2)}) async-start(bf16[4,512,256]{2,1,0:T(8,128)(2,1)} %bitcast.363), calls=%async_computation.18 | async-start | bytes 2097152 | tf_op jit(solution)/shard_map/all_to_all | solution.py:923
  636.1 136.1 %reduce-scatter.17.cloned.1.call-start = ((), (), s32[]{:S(2)}) async-start(), calls=%async_computation.32 | async-start | bytes 2285568 | tf_op jit(solution)/shard_map/reduce_scatter | solution.py:1093
  694.4 37.3 %all-to-all-start.15 = ((bf16[4,128,1024]{2,1,0:T(8,128)(2,1)}), bf16[4,128,1024]{2,1,0:T(8,128)(2,1)}, u32[]{:S(2)}, u32[]{:S(2)}) async-start(bf16[4,128,1024]{2,1,0:T(8,128)(2,1)} %pad_maximum_fusion.3), calls=%async_computation.19 | async-start | bytes 2097152 | tf_op jit(solution)/shard_map/all_to_all | solution.py:923
  700.2 169.3 %reduce-scatter.15.cloned.1.call-start = ((), (), s32[]{:S(2)}) async-start(), calls=%async_computation.31 | async-start | bytes 1769472 | tf_op jit(solution)/shard_map/reduce_scatter | solution.py:1093
  (315 other events, 2477.1 us)
Sparse Core Ops, SparseCore 0:
  47.0 46.4 all-gather.7
  141.7 26.9 all-gather.9
  170.6 36.7 all-gather.11
  209.1 36.7 all-gather.13
  386.2 50.3 reduce-scatter.10
  440.2 51.3 reduce-scatter.12
  494.8 41.1 reduce-scatter.8
  540.4 61.7 reduce-scatter.6
  603.8 125.2 all-gather.15
  732.3 39.7 reduce-scatter.16
  776.0 38.5 reduce-scatter.14

commit v6 on v5

--- a/solution.py
+++ b/solution.py
@@ -341,12 +341,13 @@
     return result, (norm_pull, normed, act_pull, square_pull, respond_pull, grown)
 
 
-def text_behind(kept, grad, up, down, extra):
+def text_behind(kept, grad, up, down, extra, waiting):
     norm_pull, normed, act_pull, square_pull, respond_pull, grown = kept
     grad_low = grad.astype(BF)
     g_out = jnp.sum(grad, axis=0)
     g_down = dot(grad_low, grown, TN)
     grad_active, grad_squares, g_scale, g_shift = respond_pull(dot(grad_low, down, NT))
+    grad_squares, waiting = lax.optimization_barrier((grad_squares, waiting))
     if extra is None:
         grad_squares = small_sum(grad_squares, "mp", 1)
     else:
@@ -362,6 +363,7 @@
         grad + grad_hidden,
         (g_conv, g_vec, g_gain, g_up, jnp.stack([g_bias, g_scale, g_shift]), g_down),
         extra,
+        waiting,
     )
 
 
@@ -975,7 +977,6 @@
     out_piece, w2_piece, w1_piece = spread_slice(out_w, 0), spread_slice(ff_w2, 0), spread_slice(ff_w1, 0)
     w1_shape = w1_piece.shape
     cut = [out_piece.shape[0], out_piece.shape[0] + w2_piece.shape[0]]
-    all_steps = lax.all_gather(t_index, "dp", tiled=True).reshape(-1)
 
     lengths = clip_lengths[0]
     clip_index = jnp.arange(clips, dtype=jnp.int32)
@@ -1032,16 +1033,16 @@
     pieces, channels = lax.optimization_barrier((pieces, channels))
     spread_in = spread(channels.astype(F32), starts, ends)
     pre_a = apply_conv(spread_in, pos_conv[0], False) + pos_bias[0]
+    y_a = jnp.pad(
+        only_clips(mish(pre_a), starts, ends).astype(BF).astype(F32), ((GAP, GAP), (0, 0))
+    )
+    pre_b = apply_conv(y_a, pos_conv[1], False) + pos_bias[1]
     received = to_all(pieces)
-    received, pre_a = lax.optimization_barrier((received, pre_a))
+    received, pre_b = lax.optimization_barrier((received, pre_b))
     out_full = gather(received[:, : cut[0]], 1).reshape(width, width)
     w1_piece = received[:, cut[1] :].reshape((shards,) + w1_shape).transpose(1, 0, 2)
     w1_full = gather(w1_piece.reshape(w1_shape[0], -1), 0)
     w2_full = gather(received[:, cut[0] : cut[1]], 1).reshape(-1, width)
-    y_a = jnp.pad(
-        only_clips(mish(pre_a), starts, ends).astype(BF).astype(F32), ((GAP, GAP), (0, 0))
-    )
-    pre_b = apply_conv(y_a, pos_conv[1], False) + pos_bias[1]
     c_pos = to_rows(gather_back(mish(pre_b).astype(BF), starts, ends))
     x1 = x0 + c_pos.astype(F32)
 
@@ -1106,7 +1107,6 @@
     more, dmod_d = n1_pull(dn1)
     dx1 = dx2 + more
     sent_w1, sent_w2, dx1, out = lax.optimization_barrier((sent_w1, sent_w2, dx1, out))
-    result = lax.all_gather(out, "mp", tiled=True)
     ff_pair = jnp.concatenate([by_rank(sent_w1), by_rank(sent_w2)], axis=2)
     sent_qkv, sent_out = scatter_dp(g_qkv_w), scatter_dp(g_out_w)
 
@@ -1147,15 +1147,25 @@
     dtext = jnp.pad(dot(dx0, emb_text, NT), ((HALO, HALO), (0, 0)))
     text_grads = [None] * blocks
     extra = dmod
-    at_got, result, dtext = lax.optimization_barrier((exchange(at_pair, "mp"), result, dtext))
-    result = result.astype(F32)
+    at_got, out, dtext = lax.optimization_barrier((exchange(at_pair, "mp"), out, dtext))
+    result = [
+        lax.all_gather(half, "mp", tiled=True) for half in (out[:, : width // 2], out[:, width // 2 :])
+    ]
+    waiting = sent_conv
     for b in reversed(range(blocks)):
-        dtext, text_grads[b], summed = text_behind(kept[b], dtext, txt_up[b], txt_down[b], extra)
+        dtext, text_grads[b], summed, waiting = text_behind(
+            kept[b], dtext, txt_up[b], txt_down[b], extra, waiting
+        )
         if extra is not None:
-            dmod_all = lax.all_gather(summed, "dp", tiled=True)
-            sent_conv, dtext = lax.optimization_barrier((sent_conv, dtext))
+            stamps = jnp.broadcast_to(t_index[0].astype(F32)[:, None], (clips, 128))
+            dmod_all = lax.all_gather(jnp.concatenate([summed, stamps], axis=1), "dp", tiled=True)
+            sent_emb, dtext = lax.optimization_barrier((sent_emb, dtext))
+            sent_conv, waiting = waiting, result[0]
+            dmod_all, all_steps = dmod_all[:, : 6 * width], dmod_all[:, 6 * width]
         extra = None
-    sent_emb, dtext = lax.optimization_barrier((sent_emb, dtext))
+    result = [waiting, result[1]]
+    result[1], dtext = lax.optimization_barrier((result[1], dtext))
+    result = jnp.concatenate(result, axis=1).astype(F32)
     vocab = txt_table.shape[0]
     wide = -(-vocab // 128) * 128
     chosen = (ids[:, None] == jnp.arange(wide, dtype=jnp.int32)[None, :]).astype(BF)

time: 973 us -> 945 us (0.971)
  blocking collectives: 117 us -> 69.7 us
  waiting for transfers between devices: 137 us -> 156 us
  Pallas kernels: 287 us -> 269 us
    all_to_all x3 -> x2, blocking collectives: 98.2 us -> 57.7 us  [exchange(): return lax.all_to_all(values, axis, 0, 0)]
    all_to_all x11 -> x12, waiting for transfers between devices: 91 us -> 124 us  [exchange(): return lax.all_to_all(values, axis, 0, 0)]
    all_to_all x2, waiting for transfers between devices: 18.4 us -> 4.31 us  [to_all(): lax.all_to_all(jnp.broadcast_to(piece[None], (size,) + piece.shape), axis...]
    pallas_call x2, Pallas kernels: 47.5 us -> 35.6 us  [attend_back(): pl.pallas_call(attend_back_kernel, out_shape=jax.ShapeDtypeStruct((shards...]
    all_to_all x11 -> x12, starting transfers between devices: 46.4 us -> 53.7 us  [exchange(): return lax.all_to_all(values, axis, 0, 0)]
    unnamed x677 -> x611, local copies, waits for them, and re-layouts: 49.8 us -> 54.3 us
  transfers between devices with their start and end apart: 24 -> 26, of which waited for: 12 -> 11; matrix products, arithmetic and copies ran while one was open for 28% -> 29% of each run, Pallas kernels for 21% -> 19%
where the time goes in v6:
time: 945 us; the launch traced here: 934 us
  Pallas kernels  269 us (28%)
  waiting for transfers between devices  156 us (17%)
  matrix products  124 us (13%)
  local copies, waits for them, and re-layouts  121 us (13%)
  other arithmetic  105 us (11%)
  blocking collectives  69.7 us (7%)
  starting transfers between devices  66.8 us (7%)
  between operations  22.6 us (2%)
    all_to_all x12, waiting for transfers between devices, exchange(): return lax.all_to_all(values, axis, 0, 0)  124 us
    dot_general x22, matrix products, dot(): lax.dot_general(left.astype(BF), right.astype(BF), dims, preferred_elemen...  69 us
    pallas_call x1, Pallas kernels, last_sums(): pl.pallas_call(partial(last_kernel, dp, mp, n_all, n_mp, n_both, n_gather...  65.5 us
    all_to_all x2, blocking collectives, exchange(): return lax.all_to_all(values, axis, 0, 0)  57.7 us
    unnamed x611, local copies, waits for them, and re-layouts  54.3 us
    all_to_all x12, starting transfers between devices, exchange(): return lax.all_to_all(values, axis, 0, 0)  53.7 us
    pallas_call x4, Pallas kernels, apply_conv(): pl.pallas_call(partial(conv_kernel, taps, turned), out_shape=jax.ShapeDty...  39.2 us
    pallas_call x2, Pallas kernels, attend_back(): pl.pallas_call(attend_back_kernel, out_shape=jax.ShapeDtypeStruct((shards...  35.6 us
  transfers between devices with their start and end apart: 26, of which 11 were waited for; matrix products, arithmetic and copies ran while one was open for 29% of the time, Pallas kernels for 19%

profile of v6, /device:TPU:0, one launch (start us, length us, event | category | flops | bytes accessed | tf_op | source)
XLA Modules:
  0.0 934.1 jit_solution(16506394599542709940)
XLA Ops:
  53.9 8.5 multiply_multiply_fusion.12
  115.4 9.8 %shard_map.495 = f32[2112,256]{1,0:T(8,128)S(1)} custom-call(f32[2144,256]{1,0:T(8,128)S(1)} %pad_add_fusion.1.x_ref, bf16[31,64,256]{2,1,0:T(8,128)(2,1)S(1)} %get-tuple-element.426.w_ref), custom_call_target="tpu_custom_call" | custom-call | flops 8581545984 | bytes 8388608 | tf_op jit(solution)/shard_map/pallas_call | solution.py:441
  128.1 9.8 %shard_map.496 = f32[2112,256]{1,0:T(8,128)S(1)} custom-call(f32[2144,256]{1,0:T(8,128)S(1)} %pad_convert_fusion.x_ref, bf16[31,64,256]{2,1,0:T(8,128)(2,1)S(1)} %copy-done.18), custom_call_target="tpu_custom_call" | custom-call | flops 8581545984 | bytes 8388608 | tf_op jit(solution)/shard_map/pallas_call | solution.py:441
  157.6 7.2 fusion.139
  177.4 22.3 %all-to-all-done.2 = bf16[4,512,256]{2,1,0:T(8,128)(2,1)} async-done(((bf16[4,512,256]{2,1,0:T(8,128)(2,1)}), bf16[4,512,256]{2,1,0:T(8,128)(2,1)}, u32[]{:S(2)}, u32[]{:S(2)}) %all-to-all-start.2) | async-done | bytes 1048608 | tf_op jit(solution)/shard_map/all_to_all | solution.py:925
  221.1 39.6 %all_to_all.80.q_ref.k_ref.v_ref = bf16[4,3,512,128]{3,2,1,0:T(8,128)(2,1)} all-to-all(bf16[4,3,512,128]{3,2,1,0:T(8,128)(2,1)S(1)} %get-tuple-element.108), channel_id=1, replica_groups=mesh['dp'=8,'mp'=4] {'mp'}, dimensions={0} | all-to-all | bytes 3145728 | tf_op jit(solution)/shard_map/all_to_all | solution.py:925
  271.2 11.6 %shard_map.498 = (bf16[2048,128]{1,0:T(8,128)(2,1)S(1)}, f32[128,2048]{1,0:T(8,128)S(1)}, f32[8,2048]{1,0:T(8,128)S(1)}) custom-call(s32[4,2]{1,0:T(4,128)S(1)} %pad_add_fusion.16.bounds, bf16[4,3,512,128]{3,2,1,0:T(8,128)(2,1)S(1)} %copy-done.8, bf16[4,3,512,128]{3,2,1,0:T(8,128)(2,1)S(1)} %copy-done.8, bf16[4,3,512,128]{3,2,1,0:T(8,128)(2,1)S(1)} %copy-done.8, ...), custom_call_target="tpu_custom_call" | custom-call | flops 2147483648 | bytes 8388608 | tf_op jit(solution)/shard_map/pallas_call | solution.py:673
  284.6 16.6 %all-to-all-done.6.q_ref.k_ref.v_ref = bf16[4,3,512,128]{3,2,1,0:T(8,128)(2,1)} async-done(((bf16[4,3,512,128]{3,2,1,0:T(8,128)(2,1)}), bf16[4,3,512,128]{3,2,1,0:T(8,128)(2,1)}, u32[]{:S(2)}, u32[]{:S(2)}) %all-to-all-start.6) | async-done | bytes 1572896 | tf_op jit(solution)/shard_map/all_to_all | solution.py:925
  306.6 12.8 %shard_map.499 = (bf16[2048,128]{1,0:T(8,128)(2,1)S(1)}, f32[128,2048]{1,0:T(8,128)S(1)}, f32[8,2048]{1,0:T(8,128)S(1)}) custom-call(s32[4,2]{1,0:T(4,128)S(1)} %pad_add_fusion.16.bounds, bf16[4,3,512,128]{3,2,1,0:T(8,128)(2,1)} %all-to-all-done.6.q_ref.k_ref.v_ref, bf16[4,3,512,128]{3,2,1,0:T(8,128)(2,1)} %all-to-all-done.6.q_ref.k_ref.v_ref, ...), custom_call_target="tpu_custom_call" | custom-call | flops 2147483648 | bytes 8388608 | tf_op jit(solution)/shard_map/pallas_call | solution.py:673
  330.6 9.2 all-to-all-done.7.refs_1_
  339.8 23.4 %shard_map.500 = (bf16[512,1024]{1,0:T(8,128)(2,1)}, bf16[512,1024]{1,0:T(8,128)(2,1)}, bf16[512,2048]{1,0:T(8,128)(2,1)}, bf16[512,1024]{1,0:T(8,128)(2,1)}, bf...) custom-call(bf16[4,512,128]{2,1,0:T(8,128)(2,1)} %all-to-all-done.5., ...), custom_call_target="tpu_custom_call" | custom-call | flops 10737418240 | bytes 20971520 | tf_op jit(solution)/shard_map/pallas_call | solution.py:899
  376.1 18.1 %all_to_all.81 = bf16[4,512,128]{2,1,0:T(8,128)(2,1)} all-to-all(bf16[4,512,128]{2,1,0:T(8,128)(2,1)} %get-tuple-element.115), channel_id=1, replica_groups=mesh['dp'=8,'mp'=4] {'mp'}, dimensions={0} | all-to-all | bytes 1048576 | tf_op jit(solution)/shard_map/all_to_all | solution.py:925
  403.1 17.8 %shard_map.501 = bf16[4,3,512,128]{3,2,1,0:T(8,128)(2,1)} custom-call(s32[4,2]{1,0:T(4,128)S(1)} %pad_add_fusion.16.bounds, bf16[4,3,512,128]{3,2,1,0:T(8,128)(2,1)} %all_to_all.80.q_ref.k_ref.v_ref, bf16[4,3,512,128]{3,2,1,0:T(8,128)(2,1)} %all_to_all.80.q_ref.k_ref.v_ref, bf16[4,3,512,128]{3,2,1,0:T(8,128)(2,1)} %all_to_all.80.q_ref.k_ref.v_ref, ...), custom_call_target="tpu_custom_call" | custom-call | flops 5368709120 | bytes 16777216 | tf_op jit(solution)/shard_map/pallas_call | solution.py:779
  429.6 17.8 %shard_map.502 = bf16[4,3,512,128]{3,2,1,0:T(8,128)(2,1)} custom-call(s32[4,2]{1,0:T(4,128)S(1)} %pad_add_fusion.16.bounds, bf16[4,3,512,128]{3,2,1,0:T(8,128)(2,1)} %all-to-all-done.6.q_ref.k_ref.v_ref, bf16[4,3,512,128]{3,2,1,0:T(8,128)(2,1)} %all-to-all-done.6.q_ref.k_ref.v_ref, bf16[4,3,512,128]{3,2,1,0:T(8,128)(2,1)} %all-to-all-done.6.q_ref.k_ref.v_ref, ...), custom_call_target="tpu_custom_call" | custom-call | flops 5368709120 | bytes 16777216 | tf_op jit(solution)/shard_map/pallas_call | solution.py:779
  447.4 14.2 %all-to-all-done.9.refs_0_ = bf16[4,3,512,128]{3,2,1,0:T(8,128)(2,1)} async-done(((bf16[4,3,512,128]{3,2,1,0:T(8,128)(2,1)}), bf16[4,3,512,128]{3,2,1,0:T(8,128)(2,1)}, u32[]{:S(2)}, u32[]{:S(2)}) %all-to-all-start.9) | async-done | bytes 1572896 | tf_op jit(solution)/shard_map/all_to_all | solution.py:925
  474.8 27.7 %all-to-all-done.11.refs_1_ = bf16[4,3,512,128]{3,2,1,0:T(8,128)(2,1)} async-done(((bf16[4,3,512,128]{3,2,1,0:T(8,128)(2,1)}), bf16[4,3,512,128]{3,2,1,0:T(8,128)(2,1)}, u32[]{:S(2)}, u32[]{:S(2)}) %all-to-all-start.11) | async-done | bytes 1572896 | tf_op jit(solution)/shard_map/all_to_all | solution.py:925
  502.4 11.9 %shard_map.503 = (f32[512,1024]{1,0:T(8,128)}, bf16[1024,3072]{1,0:T(8,128)(2,1)}, f32[4,3,256]{2,1,0:T(4,128)S(1)}) custom-call(bf16[4,3,512,128]{3,2,1,0:T(8,128)(2,1)} %all-to-all-done.9.refs_0_, bf16[4,3,512,128]{3,2,1,0:T(8,128)(2,1)} %all-to-all-done.11.refs_1_, bf16[512,1024]{1,0:T(8,128)(2,1)S(1)} %copy-done.11, ...), custom_call_target="tpu_custom_call" | custom-call | flops 6442450944 | bytes 20971520 | tf_op jit(solution)/shard_map/pallas_call | solution.py:568
  536.2 18.1 %all-to-all-done.13 = bf16[4,512,256]{2,1,0:T(8,128)(2,1)S(1)} async-done(((bf16[4,512,256]{2,1,0:T(8,128)(2,1)}), bf16[4,512,256]{2,1,0:T(8,128)(2,1)S(1)}, u32[]{:S(2)}, u32[]{:S(2)}) %all-to-all-start.13) | async-done | bytes 1048608 | tf_op jit(solution)/shard_map/all_to_all | solution.py:925
  567.4 9.8 %shard_map.504 = f32[2112,256]{1,0:T(8,128)S(1)} custom-call(f32[2144,256]{1,0:T(8,128)S(1)} %pad_add_fusion.x_ref, bf16[31,64,256]{2,1,0:T(8,128)(2,1)S(1)} %copy-done.19), custom_call_target="tpu_custom_call" | custom-call | flops 8581545984 | bytes 8388608 | tf_op jit(solution)/shard_map/pallas_call | solution.py:441
  582.2 9.8 %shard_map.505 = f32[2112,256]{1,0:T(8,128)S(1)} custom-call(f32[2144,256]{1,0:T(8,128)S(1)} %pad.199.x_ref, bf16[31,64,256]{2,1,0:T(8,128)(2,1)S(1)} %copy-done.17), custom_call_target="tpu_custom_call" | custom-call | flops 8581545984 | bytes 8388608 | tf_op jit(solution)/shard_map/pallas_call | solution.py:441
  603.0 15.7 %shard_map.507 = f32[256,1984]{1,0:T(8,128)S(1)} custom-call(f32[2144,256]{1,0:T(8,128)} %copy-done.3, f32[2112,256]{1,0:T(8,128)S(1)} %copy-done.4), custom_call_target="tpu_custom_call" | custom-call | flops 8581545984 | bytes 8388608 | tf_op jit(solution)/shard_map/pallas_call | solution.py:480
  618.9 15.7 %shard_map.506 = f32[256,1984]{1,0:T(8,128)S(1)} custom-call(f32[2144,256]{1,0:T(8,128)} %copy-done.2, f32[2112,256]{1,0:T(8,128)S(1)} %convert_element_type.344.g_ref), custom_call_target="tpu_custom_call" | custom-call | flops 8581545984 | bytes 8388608 | tf_op jit(solution)/shard_map/pallas_call | solution.py:480
  663.4 11.9 %all-to-all-done.15 = bf16[4,128,1024]{2,1,0:T(8,128)(2,1)} async-done(((bf16[4,128,1024]{2,1,0:T(8,128)(2,1)}), bf16[4,128,1024]{2,1,0:T(8,128)(2,1)}, u32[]{:S(2)}, u32[]{:S(2)}) %all-to-all-start.15) | async-done | bytes 1048608 | tf_op jit(solution)/shard_map/all_to_all | solution.py:925
  678.7 10.6 %reduce-scatter.17.cloned.1.call-done = bf16[32,3968]{1,0:T(8,128)(2,1)} async-done(((bf16[256,3968]{1,0:T(8,128)(2,1)}), bf16[32,3968]{1,0:T(8,128)(2,1)}) %reduce-scatter.17.cloned.1.call-update) | async-done | bytes 253968 | tf_op jit(solution)/shard_map/reduce_scatter | solution.py:1094
  689.3 11.9 %shard_map.508 = f32[4,7168]{1,0:T(4,128)S(1)} custom-call(f32[4,7168]{1,0:T(4,128)S(1)} %pad_maximum_fusion.10.x_ref), custom_call_target="tpu_custom_call" | custom-call | tf_op jit(solution)/shard_map/pallas_call | solution.py:115
  701.3 7.1 fusion.290
  712.0 12.0 %all-gather = f32[8,4,6272]{2,1,0:T(4,128)S(1)} all-gather(f32[1,4,6272]{2,1,0:T(4,128)S(1)} %maximum_bitcast_fusion.1), channel_id=1, replica_groups=mesh['dp'=8,'mp'=4] {'dp'}, dimensions={0}, use_global_device_ids=true | all-gather | bytes 903168 | tf_op jit(solution)/shard_map/all_gather | solution.py:1161
  738.5 9.3 fusion.47
  790.3 8.9 shard_map.509
  815.4 16.6 %all-gather.18.cloned.1.call-done = bf16[2048,512]{1,0:T(8,128)(2,1)} async-done(((bf16[512,512]{1,0:T(8,128)(2,1)}), bf16[2048,512]{1,0:T(8,128)(2,1)}) %all-gather.18.cloned.1.call-update) | async-done | bytes 2097168 | tf_op jit(solution)/shard_map/all_gather | solution.py:1152
  837.5 65.5 %shard_map.510 = (f32[16,2560]{1,0:T(8,128)}, f32[32,512]{1,0:T(8,128)}, f32[32,512]{1,0:T(8,128)}, f32[16,1024]{1,0:T(8,128)}, f32[16,1024]{1,0:T(8,128)}, /*in...) custom-call(bf16[4,2,64,2560]{3,2,1,0:T(8,128)(2,1)} %bitcast.372, bf16[4,2,128,512]{3,2,1,0:T(8,128)(2,1)} %bitcast.383, ...), custom_call_target="tpu_custom_call" | custom-call | tf_op jit(solution)/shard_map/pallas_call | solution.py:278
  918.9 6.9 maximum_convert_fusion
  (986 shorter events, 403.4 us)
Async XLA Ops:
  13.1 38.6 %all-to-all-start.3 = ((bf16[4,400,256]{2,1,0:T(8,128)(2,1)}), bf16[4,400,256]{2,1,0:T(8,128)(2,1)}, u32[]{:S(2)}, u32[]{:S(2)}) async-start(bf16[4,400,256]{2,1,0:T(8,128)(2,1)} %broadcast_in_dim.313), calls=%async_computation.3 | async-start | bytes 1638400 | tf_op jit(solution)/shard_map/all_to_all | solution.py:952
  19.4 192.4 %all-gather.8.cloned.1.call-start = ((), (), s32[]{:S(2)}) async-start(), calls=%async_computation.22 | async-start | bytes 7077888 | tf_op jit(solution)/shard_map/all_gather | solution.py:955
  22.7 50.6 %copy-start.132 = (f32[1,1,1024]{2,0,1:T(1,128)}, f32[1,1,1024]{2,0,1:T(1,128)S(1)}, u32[]{:S(2)}) copy-start(f32[1,1,1024]{2,0,1:T(1,128)S(1)} %get-tuple-element.493) | copy-start | bytes 12292
  80.3 27.5 %all-to-all-start = ((bf16[4,512,256]{2,1,0:T(8,128)(2,1)}), bf16[4,512,256]{2,1,0:T(8,128)(2,1)S(1)}, u32[]{:S(2)}, u32[]{:S(2)}) async-start(bf16[4,512,256]{2,1,0:T(8,128)(2,1)} %bitcast.345), calls=%async_computation | async-start | bytes 2097152 | tf_op jit(solution)/shard_map/all_to_all | solution.py:925
  96.4 70.9 %copy-start.159 = (pred[2048]{0:T(1024)(128)(4,1)}, pred[2048]{0:T(1024)(128)(4,1)S(1)}, u32[]{:S(2)}) copy-start(pred[2048]{0:T(1024)(128)(4,1)S(1)} %get-tuple-element.586) | copy-start | bytes 6148
  97.7 69.6 %copy-start.161 = (pred[2048]{0:T(1024)(128)(4,1)}, pred[2048]{0:T(1024)(128)(4,1)S(1)}, u32[]{:S(2)}) copy-start(pred[2048]{0:T(1024)(128)(4,1)S(1)} %get-tuple-element.588) | copy-start | bytes 6148
  99.1 68.3 %copy-start.163 = (pred[2048]{0:T(1024)(128)(4,1)}, pred[2048]{0:T(1024)(128)(4,1)S(1)}, u32[]{:S(2)}) copy-start(pred[2048]{0:T(1024)(128)(4,1)S(1)} %get-tuple-element.590) | copy-start | bytes 6148
  109.0 34.7 %all-to-all-start.1 = ((bf16[4,160,1024]{2,1,0:T(8,128)(2,1)}), bf16[4,160,1024]{2,1,0:T(8,128)(2,1)}, u32[]{:S(2)}, u32[]{:S(2)}) async-start(bf16[4,160,1024]{2,1,0:T(8,128)(2,1)} %broadcast_in_dim.310), calls=%async_computation.1 | async-start | bytes 2621440 | tf_op jit(solution)/shard_map/all_to_all | solution.py:952
  113.3 217.3 %all-gather.10.cloned.1.call-start = ((), (), s32[]{:S(2)}) async-start(), calls=%async_computation.23 | async-start | bytes 2359296 | tf_op jit(solution)/shard_map/all_gather | solution.py:955
  145.4 185.2 %all-gather.12.cloned.1.call-start = ((), (), s32[]{:S(2)}) async-start(), calls=%async_computation.24 | async-start | bytes 4718592 | tf_op jit(solution)/shard_map/all_gather | solution.py:955
  170.0 29.7 %all-to-all-start.2 = ((bf16[4,512,256]{2,1,0:T(8,128)(2,1)}), bf16[4,512,256]{2,1,0:T(8,128)(2,1)}, u32[]{:S(2)}, u32[]{:S(2)}) async-start(bf16[4,512,256]{2,1,0:T(8,128)(2,1)} %bitcast.367), calls=%async_computation.2 | async-start | bytes 2097152 | tf_op jit(solution)/shard_map/all_to_all | solution.py:925
  174.4 156.2 %all-gather.14.cloned.1.call-start = ((), (), s32[]{:S(2)}) async-start(), calls=%async_computation.25 | async-start | bytes 4718592 | tf_op jit(solution)/shard_map/all_gather | solution.py:955
  260.7 40.6 %all-to-all-start.6 = ((bf16[4,3,512,128]{3,2,1,0:T(8,128)(2,1)}), bf16[4,3,512,128]{3,2,1,0:T(8,128)(2,1)}, u32[]{:S(2)}, u32[]{:S(2)}) async-start(bf16[4,3,512,128]{3,2,1,0:T(8,128)(2,1)} %copy-done.9), calls=%async_computation.6 | async-start | bytes 3145728 | tf_op jit(solution)/shard_map/all_to_all | solution.py:925
  301.3 20.0 %all-to-all-start.5 = ((bf16[4,512,128]{2,1,0:T(8,128)(2,1)}), bf16[4,512,128]{2,1,0:T(8,128)(2,1)}, u32[]{:S(2)}, u32[]{:S(2)}) async-start(bf16[4,512,128]{2,1,0:T(8,128)(2,1)} %bitcast.356), calls=%async_computation.5 | async-start | bytes 1048576 | tf_op jit(solution)/shard_map/all_to_all | solution.py:925
  321.2 18.6 %all-to-all-start.7 = ((bf16[4,512,128]{2,1,0:T(8,128)(2,1)}), bf16[4,512,128]{2,1,0:T(8,128)(2,1)}, u32[]{:S(2)}, u32[]{:S(2)}) async-start(bf16[4,512,128]{2,1,0:T(8,128)(2,1)} %bitcast.355), calls=%async_computation.7 | async-start | bytes 1048576 | tf_op jit(solution)/shard_map/all_to_all | solution.py:925
  326.3 196.5 %reduce-scatter.11.cloned.1.call-start = ((), (), s32[]{:S(2)}) async-start(), calls=%async_computation.28 | async-start | bytes 4718592 | tf_op jit(solution)/shard_map/reduce_scatter | solution.py:1094
  369.6 153.2 %reduce-scatter.13.cloned.1.call-start = ((), (), s32[]{:S(2)}) async-start(), calls=%async_computation.29 | async-start | bytes 4718592 | tf_op jit(solution)/shard_map/reduce_scatter | solution.py:1094
  394.2 26.7 %all-to-all-start.10 = ((bf16[4,512,128]{2,1,0:T(8,128)(2,1)}), bf16[4,512,128]{2,1,0:T(8,128)(2,1)}, u32[]{:S(2)}, u32[]{:S(2)}) async-start(bf16[4,512,128]{2,1,0:T(8,128)(2,1)} %get-tuple-element.118), calls=%async_computation.10 | async-start | bytes 1048576 | tf_op jit(solution)/shard_map/all_to_all | solution.py:925
  420.9 40.6 %all-to-all-start.9 = ((bf16[4,3,512,128]{3,2,1,0:T(8,128)(2,1)}), bf16[4,3,512,128]{3,2,1,0:T(8,128)(2,1)}, u32[]{:S(2)}, u32[]{:S(2)}) async-start(bf16[4,3,512,128]{3,2,1,0:T(8,128)(2,1)} %shard_map.501), calls=%async_computation.9 | async-start | bytes 3145728 | tf_op jit(solution)/shard_map/all_to_all | solution.py:925
  461.5 40.9 %all-to-all-start.11 = ((bf16[4,3,512,128]{3,2,1,0:T(8,128)(2,1)}), bf16[4,3,512,128]{3,2,1,0:T(8,128)(2,1)}, u32[]{:S(2)}, u32[]{:S(2)}) async-start(bf16[4,3,512,128]{3,2,1,0:T(8,128)(2,1)} %shard_map.502), calls=%async_computation.11 | async-start | bytes 3145728 | tf_op jit(solution)/shard_map/all_to_all | solution.py:925
  465.9 176.7 %reduce-scatter.9.cloned.1.call-start = ((), (), s32[]{:S(2)}) async-start(), calls=%async_computation.27 | async-start | bytes 2359296 | tf_op jit(solution)/shard_map/reduce_scatter | solution.py:1094
  472.8 169.9 %reduce-scatter.7.cloned.1.call-start = ((), (), s32[]{:S(2)}) async-start(), calls=%async_computation.26 | async-start | bytes 7077888 | tf_op jit(solution)/shard_map/reduce_scatter | solution.py:1094
  474.7 39.6 %copy-start.147 = (f32[512,1]{0,1:T(1,128)S(1)}, f32[512,1]{0,1:T(1,128)}, u32[]{:S(2)}) copy-start(f32[512,1]{0,1:T(1,128)} %get-tuple-element.525) | copy-start | bytes 6148
  474.7 39.6 %copy-start.149 = (f32[512,1]{0,1:T(1,128)S(1)}, f32[512,1]{0,1:T(1,128)}, u32[]{:S(2)}) copy-start(f32[512,1]{0,1:T(1,128)} %get-tuple-element.526) | copy-start | bytes 6148
  525.7 28.7 %all-to-all-start.13 = ((bf16[4,512,256]{2,1,0:T(8,128)(2,1)}), bf16[4,512,256]{2,1,0:T(8,128)(2,1)S(1)}, u32[]{:S(2)}, u32[]{:S(2)}) async-start(bf16[4,512,256]{2,1,0:T(8,128)(2,1)} %bitcast.365), calls=%async_computation.17 | async-start | bytes 2097152 | tf_op jit(solution)/shard_map/all_to_all | solution.py:925
  555.3 39.5 %all-to-all-start.12 = ((bf16[4,128,1024]{2,1,0:T(8,128)(2,1)}), bf16[4,128,1024]{2,1,0:T(8,128)(2,1)S(1)}, u32[]{:S(2)}, u32[]{:S(2)}) async-start(bf16[4,128,1024]{2,1,0:T(8,128)(2,1)} %pad_maximum_fusion.2), calls=%async_computation.16 | async-start | bytes 2097152 | tf_op jit(solution)/shard_map/all_to_all | solution.py:925
  595.9 44.6 %all-to-all-start.14 = ((bf16[4,512,256]{2,1,0:T(8,128)(2,1)}), bf16[4,512,256]{2,1,0:T(8,128)(2,1)S(1)}, u32[]{:S(2)}, u32[]{:S(2)}) async-start(bf16[4,512,256]{2,1,0:T(8,128)(2,1)} %bitcast.366), calls=%async_computation.18 | async-start | bytes 2097152 | tf_op jit(solution)/shard_map/all_to_all | solution.py:925
  600.9 88.4 %reduce-scatter.17.cloned.1.call-start = ((), (), s32[]{:S(2)}) async-start(), calls=%async_computation.31 | async-start | bytes 2285568 | tf_op jit(solution)/shard_map/reduce_scatter | solution.py:1094
  646.0 29.4 %all-to-all-start.15 = ((bf16[4,128,1024]{2,1,0:T(8,128)(2,1)}), bf16[4,128,1024]{2,1,0:T(8,128)(2,1)}, u32[]{:S(2)}, u32[]{:S(2)}) async-start(bf16[4,128,1024]{2,1,0:T(8,128)(2,1)} %pad_maximum_fusion.3), calls=%async_computation.20 | async-start | bytes 2097152 | tf_op jit(solution)/shard_map/all_to_all | solution.py:925
  651.1 128.5 %reduce-scatter.15.cloned.1.call-start = ((), (), s32[]{:S(2)}) async-start(), calls=%async_computation.30 | async-start | bytes 1769472 | tf_op jit(solution)/shard_map/reduce_scatter | solution.py:1094
  663.3 126.9 %all-gather.16.cloned.1.call-start = ((), (), s32[]{:S(2)}) async-start(), calls=%async_computation.32 | async-start | bytes 2621440 | tf_op jit(solution)/shard_map/all_gather | solution.py:1152
  737.4 94.6 %all-gather.18.cloned.1.call-start = ((), (), s32[]{:S(2)}) async-start(), calls=%async_computation.33 | async-start | bytes 2621440 | tf_op jit(solution)/shard_map/all_gather | solution.py:1152
  (285 other events, 2357.8 us)
Sparse Core Ops, SparseCore 0:
  54.0 46.4 all-gather.7
  145.5 26.9 all-gather.9
  174.4 36.7 all-gather.11
  212.9 36.7 all-gather.13
  369.7 54.3 reduce-scatter.10
  427.7 51.3 reduce-scatter.12
  482.4 43.0 reduce-scatter.8
  529.8 61.7 reduce-scatter.6
  636.7 52.5 reduce-scatter.16
  693.0 39.5 reduce-scatter.14
  737.6 46.8 all-gather.15
  785.9 46.0 all-gather.17

commit v7 on v6

--- a/solution.py
+++ b/solution.py
@@ -128,9 +128,64 @@
     )(values)
 
 
-def last_kernel(dp, mp, n_all, n_mp, n_both, n_gather, *refs):
+def places(dp, mp, width, kind):
+    share = width // dp
+    if kind in ("dp", "both"):
+        return [(0, 0, share, 0, share, None)], 1
+    count = share // mp
+    found = []
+    for z in range(mp):
+        at = z * count
+        column = z * dp * count if kind == "crossed" else 0
+        found.append((at // LANES, at % LANES, count, column, count, z))
+    return found, -(-share // LANES)
+
+
+def pack_rows(dp, mp, pieces, sources, pack, z):
+    pack[...] = jnp.zeros_like(pack)
+    at = 0
+    for source, first, rows, width, kind, _, _ in pieces:
+        found, used = places(dp, mp, width, kind)
+        for row, lane, count, column, step, device in found:
+            for d in range(dp):
+                start = column + d * step
+                value = sources[source][first : first + rows, start : start + count]
+                if kind == "mine":
+                    value = jnp.where(z == device, value, 0.0)
+                to = slice(at + row, at + row + rows)
+                pack[d // 2, d % 2, to, lane : lane + count] = value
+        at += rows * used
+
+
+def unpack_rows(dp, mp, pieces, value, outs, z):
+    at = 0
+    for _, _, rows, width, kind, out, where in pieces:
+        found, used = places(dp, mp, width, kind)
+        if kind == "both":
+            count = width // dp // mp
+            found = [(0, device * count, count, 0, 0, device) for device in range(mp)]
+        total = None
+        for row, lane, count, _, _, device in found:
+            part = value[at + row : at + row + rows, lane : lane + count]
+            if device is not None:
+                part = jnp.where(z == device, part, 0.0)
+            total = part if total is None else total + part
+        lead, row = where
+        if lead is None:
+            outs[out][row : row + rows, :] = total
+        else:
+            outs[out][lead, row : row + rows, :] = total
+        at += rows * used
+
+
+def last_kernel(dp, mp, n_all, n_mp, n_both, n_gather, n_sources, n_small, pieces, *refs):
     n_in = n_all + n_mp + n_both + n_gather
-    ins, outs, rest = refs[:n_in], refs[n_in : 2 * n_in], list(refs[2 * n_in :])
+    ins, refs = list(refs[: n_in - 1]), refs[n_in - 1 :]
+    sources, refs = refs[:n_sources], refs[n_sources:]
+    outs, refs = list(refs[: n_in - 1]), refs[n_in - 1 :]
+    small_outs, rest = refs[:n_small], list(refs[n_small:])
+    ins.insert(n_all - 1, rest.pop(0))
+    outs.insert(n_all - 1, None)
 
     def take(count):
         return [rest.pop(0) for _ in range(count)]
@@ -196,6 +251,8 @@
 
     local = []
     for t in range(n_all):
+        if t == n_all - 1:
+            pack_rows(dp, mp, pieces, sources, ins[t], z)
         to_partner(t).start()
         copy = pltpu.make_async_copy(ins[t].at[:, core], own[t], own_sems.at[t])
         copy.start()
@@ -249,16 +306,20 @@
             copy = to_z(t, step, other_z[step])
             copy.wait_send()
             copy.wait_recv()
-        if t < n_in - n_gather:
+        if t == n_all - 1:
+            unpack_rows(dp, mp, pieces, total(slots[t], mp), small_outs, z)
+        elif t < n_in - n_gather:
             outs[t][...] = total(slots[t], mp)
         else:
             outs[t][...] = slots[t][...].astype(F32)
 
 
-def last_sums(over_all, small, over_mp, both, gathered):
+def last_sums(over_all, sources, pieces, small_shapes, over_mp, both, gathered):
     dp, mp = lax.axis_size("dp"), lax.axis_size("mp")
     chips = dp // 2
-    everywhere = [v.reshape((chips, 2) + v.shape[1:]) for v in list(over_all) + [small]]
+    rows = sum(p[2] * places(dp, mp, p[3], p[4])[1] for p in pieces)
+    packed = jax.ShapeDtypeStruct((chips, 2, -(-rows // 8) * 8, LANES), F32)
+    everywhere = [v.reshape((chips, 2) + v.shape[1:]) for v in over_all] + [packed]
     ins = everywhere + list(over_mp) + list(both) + list(gathered)
     n_all, n_mp, n_both, n_gather = len(everywhere), len(over_mp), len(both), len(gathered)
     halves = [pltpu.VMEM((chips,) + v.shape[2:], v.dtype) for v in everywhere]
@@ -276,11 +337,18 @@
         outs.append((mp,) + shape if t >= len(ins) - n_gather else shape)
     dma = pltpu.SemaphoreType.DMA
     return pl.pallas_call(
-        partial(last_kernel, dp, mp, n_all, n_mp, n_both, n_gather),
-        out_shape=[jax.ShapeDtypeStruct(shape, F32) for shape in outs],
-        in_specs=[pl.BlockSpec(memory_space=pl.ANY)] * len(ins),
-        out_specs=[pl.BlockSpec(memory_space=pltpu.VMEM)] * len(ins),
-        scratch_shapes=halves * 4
+        partial(
+            last_kernel, dp, mp, n_all, n_mp, n_both, n_gather, len(sources), len(small_shapes), pieces
+        ),
+        out_shape=[
+            jax.ShapeDtypeStruct(shape, F32)
+            for shape in outs[: n_all - 1] + outs[n_all:] + list(small_shapes)
+        ],
+        in_specs=[pl.BlockSpec(memory_space=pl.ANY)] * (len(ins) - 1)
+        + [pl.BlockSpec(memory_space=pltpu.VMEM)] * len(sources),
+        out_specs=[pl.BlockSpec(memory_space=pltpu.VMEM)] * (len(ins) - 1 + len(small_shapes)),
+        scratch_shapes=[pltpu.VMEM(packed.shape, F32)]
+        + halves * 4
         + middle
         + slots
         + [
@@ -295,7 +363,7 @@
         compiler_params=pltpu.CompilerParams(
             collective_id=3, has_side_effects=True, vmem_limit_bytes=56 << 20
         ),
-    )(*ins)
+    )(*ins[: n_all - 1], *ins[n_all:], *sources)
 
 
 def conv_norm(hidden, segment, conv, vec, gain):
@@ -361,7 +429,7 @@
     g_vec = g_vec.at[2].add(g_out)
     return (
         grad + grad_hidden,
-        (g_conv, g_vec, g_gain, g_up, jnp.stack([g_bias, g_scale, g_shift]), g_down),
+        (g_conv, g_vec, g_gain, g_up, (g_bias, g_scale, g_shift), g_down),
         extra,
         waiting,
     )
@@ -1073,10 +1141,9 @@
     o_parts = [exchange(a[0].reshape(shards, rows, LANES), "mp") for a in attended]
     grad = lax.dynamic_slice_in_dim(out_grad, first, rows)
     seg_own = lax.dynamic_slice_in_dim(segment, first, rows)[:, None]
-    out, n2, r, df, dh, da, dx2, g_ff_b1, sums, *do_parts = middle(
+    out, n2, r, df, dh, da, dx2, ff_sums, sums, *do_parts = middle(
         o_parts, x1, grad, seg_own, mod, out_full, out_b, w1_full, b1_full, w2_full, ff_b2
     )
-    g_ff_b1, g_ff_b2, g_out_b = g_ff_b1[0], sums[4 * clips], sums[4 * clips + 1]
     dmod_gate_f, dmod_shift_f, dmod_scale_f, dmod_gate_a = (
         sums[i * clips : (i + 1) * clips] for i in range(4)
     )
@@ -1147,10 +1214,9 @@
     dtext = jnp.pad(dot(dx0, emb_text, NT), ((HALO, HALO), (0, 0)))
     text_grads = [None] * blocks
     extra = dmod
-    at_got, out, dtext = lax.optimization_barrier((exchange(at_pair, "mp"), out, dtext))
-    result = [
-        lax.all_gather(half, "mp", tiled=True) for half in (out[:, : width // 2], out[:, width // 2 :])
-    ]
+    result = lax.all_gather(out[:, : width // 2], "mp", tiled=True)
+    at_got, result, out, dtext = lax.optimization_barrier((exchange(at_pair, "mp"), result, out, dtext))
+    result = [result, lax.all_gather(out[:, width // 2 :], "mp", tiled=True)]
     waiting = sent_conv
     for b in reversed(range(blocks)):
         dtext, text_grads[b], summed, waiting = text_behind(
@@ -1160,10 +1226,10 @@
             stamps = jnp.broadcast_to(t_index[0].astype(F32)[:, None], (clips, 128))
             dmod_all = lax.all_gather(jnp.concatenate([summed, stamps], axis=1), "dp", tiled=True)
             sent_emb, dtext = lax.optimization_barrier((sent_emb, dtext))
-            sent_conv, waiting = waiting, result[0]
+            sent_conv, waiting = waiting, at_got
             dmod_all, all_steps = dmod_all[:, : 6 * width], dmod_all[:, 6 * width]
         extra = None
-    result = [waiting, result[1]]
+    at_got = waiting
     result[1], dtext = lax.optimization_barrier((result[1], dtext))
     result = jnp.concatenate(result, axis=1).astype(F32)
     vocab = txt_table.shape[0]
@@ -1172,58 +1238,53 @@
     g_table = dot(dtext, chosen, TN)
     hidden_width = txt_up.shape[2]
 
-    def placed(values):
-        full = jnp.zeros((shards,) + values.shape, F32)
-        return lax.dynamic_update_slice_in_dim(full, values[None], rank, 0)
-
-    g_pos_bias = placed(jnp.stack([g_pos_a, g_pos_b])).transpose(1, 0, 2).reshape(2, width)
     g_qkv_b = jnp.concatenate([pair_merge(g_qkv_b[:, :2]), g_qkv_b[:, 2:]], axis=1)
     g_qkv_b = g_qkv_b.transpose(1, 0, 2).reshape(3, width)
-    small = [
-        (jnp.stack([g[0] for g in text_grads]), "both"),
-        (jnp.stack([g[1] for g in text_grads]), "both"),
-        (jnp.stack([g[2] for g in text_grads]), "both"),
-        (jnp.stack([g[4] for g in text_grads]), "both"),
-        (g_emb_bias, "dp"),
-        (g_pos_bias, "crossed"),
-        (g_qkv_b, "crossed"),
-        (g_out_b, "dp"),
-        (g_ff_b1, "crossed"),
-        (g_ff_b2, "dp"),
+    sources, pieces = [], []
+    everyone = groups * shards
+
+    def piece(value, kind, out, where, first=0, count=None):
+        value = value if value.ndim == 2 else value[None]
+        known = [i for i, have in enumerate(sources) if have is value]
+        if not known:
+            sources.append(value)
+        index = known[0] if known else len(sources) - 1
+        columns = value.shape[1] * (shards if kind == "mine" else 1)
+        pieces.append((index, first, count or value.shape[0], columns, kind, out, where))
+
+    for b, (g_conv_b, g_vec, g_gain, _, g_hid, _) in enumerate(text_grads):
+        piece(g_conv_b, "both", 0, (b, 0))
+        piece(g_vec, "both", 1, (b, 0))
+        piece(g_gain, "both", 2, (None, b))
+        for i, value in enumerate(g_hid):
+            piece(value, "both", 3, (b, i))
+    piece(g_emb_bias, "dp", 4, (None, 0))
+    piece(g_pos_a, "mine", 5, (None, 0))
+    piece(g_pos_b, "mine", 5, (None, 1))
+    piece(g_qkv_b, "crossed", 6, (None, 0))
+    piece(sums, "dp", 7, (None, 0), 4 * clips + 1, 1)
+    piece(ff_sums, "crossed", 8, (None, 0), 0, 1)
+    piece(sums, "dp", 9, (None, 0), 4 * clips, 1)
+    text_part, hid_part, part = text_width // everyone, hidden_width // everyone, width // everyone
+    small_shapes = [
+        (blocks, txt_conv.shape[1], text_part), (blocks, 3, text_part), (blocks, text_part),
+        (blocks, 3, hid_part), (1, width // groups), (2, part), (3, part), (1, width // groups),
+        (1, ff_sums.shape[1] // everyone), (1, width // groups),
     ]
-    packed = []
-    for value, kind in small:
-        lead = value.size // value.shape[-1]
-        if kind == "crossed":
-            value = value.reshape(lead, shards, groups, -1).transpose(2, 0, 1, 3)
-        else:
-            value = value.reshape(lead, groups, -1).transpose(1, 0, 2)
-        packed.append(value.reshape(groups, -1))
-    packed = jnp.concatenate(packed, axis=1)
-    length = packed.shape[1]
-    packed = jnp.pad(packed, ((0, 0), (0, -length % 1024))).reshape(groups, -1, 128)
-    table_sum, up0, up1, down0, down1, packed, g_emb, mel_grad = last_sums(
+    table_sum, up0, up1, down0, down1, g_emb, mel_grad, *unpacked = last_sums(
         [for_dp(g_table)]
         + [for_dp(text_grads[b][3]) for b in range(blocks)]
         + [for_dp(text_grads[b][5]) for b in range(blocks)],
-        packed,
+        sources,
+        pieces,
+        small_shapes,
         [],
         [sent_emb],
         [mel_grad],
     )
     mel_grad = mel_grad.reshape(total, -1)
-    packed = packed.reshape(-1)
-    unpacked, at = [], 0
-    for value, kind in small:
-        size = value.size // groups
-        piece = packed[at : at + size]
-        at += size
-        if kind == "dp":
-            unpacked.append(piece.reshape(value.shape[:-1] + (-1,)))
-        else:
-            piece = piece.reshape(value.size // value.shape[-1], shards, -1)
-            piece = lax.dynamic_slice_in_dim(piece, rank, 1, 1)
-            unpacked.append(piece.reshape(value.shape[:-1] + (-1,)))
+    for i in (4, 7, 8, 9):
+        unpacked[i] = unpacked[i].reshape(-1)
     o_table = table_sum[:, :vocab].T
     o_up = jnp.stack([up0.T, up1.T])
     o_down = jnp.stack([down0.T, down1.T])

time: 945 us -> 939 us (level)
  blocking collectives: 69.7 us -> 111 us
  waiting for transfers between devices: 156 us -> 115 us
    all_to_all x2 -> x3, blocking collectives: 57.7 us -> 99.4 us  [exchange(): return lax.all_to_all(values, axis, 0, 0)]
    all_to_all x12 -> x11, waiting for transfers between devices: 124 us -> 103 us  [exchange(): return lax.all_to_all(values, axis, 0, 0)]
    all_gather x2, waiting for transfers between devices: 16.6 us -> 0.02 us  [the longest x1 0.02 us: local(): result = lax.all_gather(out[:, :width // 2], 'mp', tiled=True)]
    all_to_all x12 -> x11, starting transfers between devices: 53.7 us -> 48.7 us  [exchange(): return lax.all_to_all(values, axis, 0, 0)]
    unnamed x611 -> x625, local copies, waits for them, and re-layouts: 54.3 us -> 56.5 us
  transfers between devices with their start and end apart: 26 -> 25, of which waited for: 11 -> 10; matrix products, arithmetic and copies ran while one was open for 29% -> 29% of each run, Pallas kernels for 19% -> 19%
where the time goes in v7:
time: 939 us; the launch traced here: 927 us
  Pallas kernels  270 us (29%)
  matrix products  124 us (13%)
  waiting for transfers between devices  115 us (12%)
  local copies, waits for them, and re-layouts  114 us (12%)
  blocking collectives  111 us (12%)
  other arithmetic  109 us (12%)
  starting transfers between devices  60.8 us (6%)
  between operations  22.6 us (2%)
    all_to_all x11, waiting for transfers between devices, exchange(): return lax.all_to_all(values, axis, 0, 0)  103 us
    all_to_all x3, blocking collectives, exchange(): return lax.all_to_all(values, axis, 0, 0)  99.4 us
    dot_general x22, matrix products, dot(): lax.dot_general(left.astype(BF), right.astype(BF), dims, preferred_elemen...  68.3 us
    pallas_call x1, Pallas kernels, last_sums(): pl.pallas_call(partial(last_kernel, dp, mp, n_all, n_mp, n_both, n_gather...  67.5 us
    unnamed x625, local copies, waits for them, and re-layouts  56.5 us
    all_to_all x11, starting transfers between devices, exchange(): return lax.all_to_all(values, axis, 0, 0)  48.7 us
    pallas_call x4, Pallas kernels, apply_conv(): pl.pallas_call(partial(conv_kernel, taps, turned), out_shape=jax.ShapeDty...  39.2 us
    pallas_call x2, Pallas kernels, attend_back(): pl.pallas_call(attend_back_kernel, out_shape=jax.ShapeDtypeStruct((shards...  35.6 us
  transfers between devices with their start and end apart: 25, of which 10 were waited for; matrix products, arithmetic and copies ran while one was open for 29% of the time, Pallas kernels for 19%

profile of v7, /device:TPU:0, one launch (start us, length us, event | category | flops | bytes accessed | tf_op | source)
XLA Modules:
  0.0 926.6 jit_solution(10685702976912893430)
XLA Ops:
  53.4 8.2 multiply_multiply_fusion.12
  114.3 9.8 %shard_map.495 = f32[2112,256]{1,0:T(8,128)S(1)} custom-call(f32[2144,256]{1,0:T(8,128)S(1)} %pad_add_fusion.1.x_ref, bf16[31,64,256]{2,1,0:T(8,128)(2,1)S(1)} %get-tuple-element.444.w_ref), custom_call_target="tpu_custom_call" | custom-call | flops 8581545984 | bytes 8388608 | tf_op jit(solution)/shard_map/pallas_call | solution.py:509
  127.0 9.8 %shard_map.496 = f32[2112,256]{1,0:T(8,128)S(1)} custom-call(f32[2144,256]{1,0:T(8,128)S(1)} %pad_convert_fusion.x_ref, bf16[31,64,256]{2,1,0:T(8,128)(2,1)S(1)} %copy-done.18), custom_call_target="tpu_custom_call" | custom-call | flops 8581545984 | bytes 8388608 | tf_op jit(solution)/shard_map/pallas_call | solution.py:509
  156.2 7.2 fusion.139
  176.0 22.3 %all-to-all-done.2 = bf16[4,512,256]{2,1,0:T(8,128)(2,1)} async-done(((bf16[4,512,256]{2,1,0:T(8,128)(2,1)}), bf16[4,512,256]{2,1,0:T(8,128)(2,1)}, u32[]{:S(2)}, u32[]{:S(2)}) %all-to-all-start.2) | async-done | bytes 1048608 | tf_op jit(solution)/shard_map/all_to_all | solution.py:993
  219.7 39.6 %all_to_all.80.q_ref.k_ref.v_ref = bf16[4,3,512,128]{3,2,1,0:T(8,128)(2,1)} all-to-all(bf16[4,3,512,128]{3,2,1,0:T(8,128)(2,1)S(1)} %get-tuple-element.118), channel_id=1, replica_groups=mesh['dp'=8,'mp'=4] {'mp'}, dimensions={0} | all-to-all | bytes 3145728 | tf_op jit(solution)/shard_map/all_to_all | solution.py:993
  269.7 11.6 %shard_map.498 = (bf16[2048,128]{1,0:T(8,128)(2,1)S(1)}, f32[128,2048]{1,0:T(8,128)S(1)}, f32[8,2048]{1,0:T(8,128)S(1)}) custom-call(s32[4,2]{1,0:T(4,128)S(1)} %pad_add_fusion.18.bounds, bf16[4,3,512,128]{3,2,1,0:T(8,128)(2,1)S(1)} %copy-done.8, bf16[4,3,512,128]{3,2,1,0:T(8,128)(2,1)S(1)} %copy-done.8, bf16[4,3,512,128]{3,2,1,0:T(8,128)(2,1)S(1)} %copy-done.8, ...), custom_call_target="tpu_custom_call" | custom-call | flops 2147483648 | bytes 8388608 | tf_op jit(solution)/shard_map/pallas_call | solution.py:741
  283.1 16.8 %all-to-all-done.6.q_ref.k_ref.v_ref = bf16[4,3,512,128]{3,2,1,0:T(8,128)(2,1)} async-done(((bf16[4,3,512,128]{3,2,1,0:T(8,128)(2,1)}), bf16[4,3,512,128]{3,2,1,0:T(8,128)(2,1)}, u32[]{:S(2)}, u32[]{:S(2)}) %all-to-all-start.6) | async-done | bytes 1572896 | tf_op jit(solution)/shard_map/all_to_all | solution.py:993
  305.2 12.8 %shard_map.499 = (bf16[2048,128]{1,0:T(8,128)(2,1)S(1)}, f32[128,2048]{1,0:T(8,128)S(1)}, f32[8,2048]{1,0:T(8,128)S(1)}) custom-call(s32[4,2]{1,0:T(4,128)S(1)} %pad_add_fusion.18.bounds, bf16[4,3,512,128]{3,2,1,0:T(8,128)(2,1)} %all-to-all-done.6.q_ref.k_ref.v_ref, bf16[4,3,512,128]{3,2,1,0:T(8,128)(2,1)} %all-to-all-done.6.q_ref.k_ref.v_ref, ...), custom_call_target="tpu_custom_call" | custom-call | flops 2147483648 | bytes 8388608 | tf_op jit(solution)/shard_map/pallas_call | solution.py:741
  329.1 10.7 %all-to-all-done.7.refs_1_ = bf16[4,512,128]{2,1,0:T(8,128)(2,1)} async-done(((bf16[4,512,128]{2,1,0:T(8,128)(2,1)}), bf16[4,512,128]{2,1,0:T(8,128)(2,1)}, u32[]{:S(2)}, u32[]{:S(2)}) %all-to-all-start.7) | async-done | bytes 524320 | tf_op jit(solution)/shard_map/all_to_all | solution.py:993
  339.8 23.4 %shard_map.500 = (bf16[512,1024]{1,0:T(8,128)(2,1)}, bf16[512,1024]{1,0:T(8,128)(2,1)}, bf16[512,2048]{1,0:T(8,128)(2,1)}, bf16[512,1024]{1,0:T(8,128)(2,1)}, bf...) custom-call(bf16[4,512,128]{2,1,0:T(8,128)(2,1)} %all-to-all-done.5., ...), custom_call_target="tpu_custom_call" | custom-call | flops 10737418240 | bytes 20971520 | tf_op jit(solution)/shard_map/pallas_call | solution.py:967
  376.1 20.1 %all_to_all.81 = bf16[4,512,128]{2,1,0:T(8,128)(2,1)} all-to-all(bf16[4,512,128]{2,1,0:T(8,128)(2,1)} %get-tuple-element.125), channel_id=1, replica_groups=mesh['dp'=8,'mp'=4] {'mp'}, dimensions={0} | all-to-all | bytes 1048576 | tf_op jit(solution)/shard_map/all_to_all | solution.py:993
  405.1 17.7 %shard_map.501 = bf16[4,3,512,128]{3,2,1,0:T(8,128)(2,1)} custom-call(s32[4,2]{1,0:T(4,128)S(1)} %pad_add_fusion.18.bounds, bf16[4,3,512,128]{3,2,1,0:T(8,128)(2,1)} %all_to_all.80.q_ref.k_ref.v_ref, bf16[4,3,512,128]{3,2,1,0:T(8,128)(2,1)} %all_to_all.80.q_ref.k_ref.v_ref, bf16[4,3,512,128]{3,2,1,0:T(8,128)(2,1)} %all_to_all.80.q_ref.k_ref.v_ref, ...), custom_call_target="tpu_custom_call" | custom-call | flops 5368709120 | bytes 16777216 | tf_op jit(solution)/shard_map/pallas_call | solution.py:847
  440.7 17.8 %shard_map.502 = bf16[4,3,512,128]{3,2,1,0:T(8,128)(2,1)} custom-call(s32[4,2]{1,0:T(4,128)S(1)} %pad_add_fusion.18.bounds, bf16[4,3,512,128]{3,2,1,0:T(8,128)(2,1)} %all-to-all-done.6.q_ref.k_ref.v_ref, bf16[4,3,512,128]{3,2,1,0:T(8,128)(2,1)} %all-to-all-done.6.q_ref.k_ref.v_ref, bf16[4,3,512,128]{3,2,1,0:T(8,128)(2,1)} %all-to-all-done.6.q_ref.k_ref.v_ref, ...), custom_call_target="tpu_custom_call" | custom-call | flops 5368709120 | bytes 16777216 | tf_op jit(solution)/shard_map/pallas_call | solution.py:847
  465.4 39.7 %all_to_all.82.refs_1_ = bf16[4,3,512,128]{3,2,1,0:T(8,128)(2,1)S(1)} all-to-all(bf16[4,3,512,128]{3,2,1,0:T(8,128)(2,1)} %shard_map.502), channel_id=1, replica_groups=mesh['dp'=8,'mp'=4] {'mp'}, dimensions={0} | all-to-all | bytes 3145728 | tf_op jit(solution)/shard_map/all_to_all | solution.py:993
  505.1 11.6 %shard_map.503 = (f32[512,1024]{1,0:T(8,128)}, bf16[1024,3072]{1,0:T(8,128)(2,1)}, f32[4,3,256]{2,1,0:T(4,128)S(1)}) custom-call(bf16[4,3,512,128]{3,2,1,0:T(8,128)(2,1)} %all-to-all-done.9.refs_0_, bf16[4,3,512,128]{3,2,1,0:T(8,128)(2,1)S(1)} %all_to_all.82.refs_1_, bf16[512,1024]{1,0:T(8,128)(2,1)S(1)} %copy-done.11, ...), custom_call_target="tpu_custom_call" | custom-call | flops 6442450944 | bytes 20971520 | tf_op jit(solution)/shard_map/pallas_call | solution.py:636
  541.4 15.6 %all-to-all-done.13 = bf16[4,512,256]{2,1,0:T(8,128)(2,1)S(1)} async-done(((bf16[4,512,256]{2,1,0:T(8,128)(2,1)}), bf16[4,512,256]{2,1,0:T(8,128)(2,1)S(1)}, u32[]{:S(2)}, u32[]{:S(2)}) %all-to-all-start.13) | async-done | bytes 1048608 | tf_op jit(solution)/shard_map/all_to_all | solution.py:993
  570.5 9.8 %shard_map.504 = f32[2112,256]{1,0:T(8,128)S(1)} custom-call(f32[2144,256]{1,0:T(8,128)S(1)} %pad_add_fusion.x_ref, bf16[31,64,256]{2,1,0:T(8,128)(2,1)S(1)} %copy-done.19), custom_call_target="tpu_custom_call" | custom-call | flops 8581545984 | bytes 8388608 | tf_op jit(solution)/shard_map/pallas_call | solution.py:509
  585.9 9.8 %shard_map.505 = f32[2112,256]{1,0:T(8,128)S(1)} custom-call(f32[2144,256]{1,0:T(8,128)S(1)} %pad.195.x_ref, bf16[31,64,256]{2,1,0:T(8,128)(2,1)S(1)} %copy-done.17), custom_call_target="tpu_custom_call" | custom-call | flops 8581545984 | bytes 8388608 | tf_op jit(solution)/shard_map/pallas_call | solution.py:509
  606.4 15.7 %shard_map.507 = f32[256,1984]{1,0:T(8,128)S(1)} custom-call(f32[2144,256]{1,0:T(8,128)} %copy-done.3, f32[2112,256]{1,0:T(8,128)S(1)} %copy-done.4), custom_call_target="tpu_custom_call" | custom-call | flops 8581545984 | bytes 8388608 | tf_op jit(solution)/shard_map/pallas_call | solution.py:548
  622.2 15.7 %shard_map.506 = f32[256,1984]{1,0:T(8,128)S(1)} custom-call(f32[2144,256]{1,0:T(8,128)} %copy-done.2, f32[2112,256]{1,0:T(8,128)S(1)} %convert_element_type.342.g_ref), custom_call_target="tpu_custom_call" | custom-call | flops 8581545984 | bytes 8388608 | tf_op jit(solution)/shard_map/pallas_call | solution.py:548
  642.9 13.8 %all-to-all-done.14 = bf16[4,512,256]{2,1,0:T(8,128)(2,1)S(1)} async-done(((bf16[4,512,256]{2,1,0:T(8,128)(2,1)}), bf16[4,512,256]{2,1,0:T(8,128)(2,1)S(1)}, u32[]{:S(2)}, u32[]{:S(2)}) %all-to-all-start.14) | async-done | bytes 1048608 | tf_op jit(solution)/shard_map/all_to_all | solution.py:993
  679.0 13.4 %all-to-all-done.15 = bf16[4,128,1024]{2,1,0:T(8,128)(2,1)} async-done(((bf16[4,128,1024]{2,1,0:T(8,128)(2,1)}), bf16[4,128,1024]{2,1,0:T(8,128)(2,1)}, u32[]{:S(2)}, u32[]{:S(2)}) %all-to-all-start.15) | async-done | bytes 1048608 | tf_op jit(solution)/shard_map/all_to_all | solution.py:993
  695.8 7.3 reduce-scatter.17.cloned.1.call-done
  703.1 11.9 %shard_map.508 = f32[4,7168]{1,0:T(4,128)S(1)} custom-call(f32[4,7168]{1,0:T(4,128)S(1)} %pad_maximum_fusion.10.x_ref), custom_call_target="tpu_custom_call" | custom-call | tf_op jit(solution)/shard_map/pallas_call | solution.py:115
  715.1 11.8 %all-gather = f32[8,4,6272]{2,1,0:T(4,128)} all-gather(f32[1,4,6272]{2,1,0:T(4,128)S(1)} %maximum_bitcast_fusion.1), channel_id=1, replica_groups=mesh['dp'=8,'mp'=4] {'dp'}, dimensions={0}, use_global_device_ids=true | all-gather | bytes 903168 | tf_op jit(solution)/shard_map/all_gather | solution.py:1227
  731.5 7.0 fusion.282
  747.9 8.7 fusion.47
  795.1 8.3 shard_map.509
  805.4 7.5 fusion.281
  831.0 67.5 %shard_map.510 = (f32[16,2560]{1,0:T(8,128)}, f32[32,512]{1,0:T(8,128)}, f32[32,512]{1,0:T(8,128)}, f32[16,1024]{1,0:T(8,128)}, f32[16,1024]{1,0:T(8,128)}, /*in...) custom-call(bf16[4,2,64,2560]{3,2,1,0:T(8,128)(2,1)} %bitcast.328, ...), custom_call_target="tpu_custom_call" | custom-call | tf_op jit(solution)/shard_map/pallas_call | solution.py:339
  907.4 6.9 maximum_convert_fusion
  (946 shorter events, 394.3 us)
Async XLA Ops:
  13.1 38.1 %all-to-all-start.3 = ((bf16[4,400,256]{2,1,0:T(8,128)(2,1)}), bf16[4,400,256]{2,1,0:T(8,128)(2,1)}, u32[]{:S(2)}, u32[]{:S(2)}) async-start(bf16[4,400,256]{2,1,0:T(8,128)(2,1)} %broadcast_in_dim.324), calls=%async_computation.3 | async-start | bytes 1638400 | tf_op jit(solution)/shard_map/all_to_all | solution.py:1020
  19.4 191.0 %all-gather.8.cloned.1.call-start = ((), (), s32[]{:S(2)}) async-start(), calls=%async_computation.22 | async-start | bytes 7077888 | tf_op jit(solution)/shard_map/all_gather | solution.py:1023
  22.7 49.2 %copy-start.138 = (f32[1,1,1024]{2,0,1:T(1,128)}, f32[1,1,1024]{2,0,1:T(1,128)S(1)}, u32[]{:S(2)}) copy-start(f32[1,1,1024]{2,0,1:T(1,128)S(1)} %get-tuple-element.507) | copy-start | bytes 12292
  78.9 27.5 %all-to-all-start = ((bf16[4,512,256]{2,1,0:T(8,128)(2,1)}), bf16[4,512,256]{2,1,0:T(8,128)(2,1)S(1)}, u32[]{:S(2)}, u32[]{:S(2)}) async-start(bf16[4,512,256]{2,1,0:T(8,128)(2,1)} %bitcast.302), calls=%async_computation | async-start | bytes 2097152 | tf_op jit(solution)/shard_map/all_to_all | solution.py:993
  95.1 70.8 %copy-start.158 = (pred[2048]{0:T(1024)(128)(4,1)}, pred[2048]{0:T(1024)(128)(4,1)S(1)}, u32[]{:S(2)}) copy-start(pred[2048]{0:T(1024)(128)(4,1)S(1)} %get-tuple-element.594) | copy-start | bytes 6148
  96.4 69.5 %copy-start.160 = (pred[2048]{0:T(1024)(128)(4,1)}, pred[2048]{0:T(1024)(128)(4,1)S(1)}, u32[]{:S(2)}) copy-start(pred[2048]{0:T(1024)(128)(4,1)S(1)} %get-tuple-element.596) | copy-start | bytes 6148
  97.7 68.1 %copy-start.162 = (pred[2048]{0:T(1024)(128)(4,1)}, pred[2048]{0:T(1024)(128)(4,1)S(1)}, u32[]{:S(2)}) copy-start(pred[2048]{0:T(1024)(128)(4,1)S(1)} %get-tuple-element.598) | copy-start | bytes 6148
  107.6 34.7 %all-to-all-start.1 = ((bf16[4,160,1024]{2,1,0:T(8,128)(2,1)}), bf16[4,160,1024]{2,1,0:T(8,128)(2,1)}, u32[]{:S(2)}, u32[]{:S(2)}) async-start(bf16[4,160,1024]{2,1,0:T(8,128)(2,1)} %broadcast_in_dim.321), calls=%async_computation.1 | async-start | bytes 2621440 | tf_op jit(solution)/shard_map/all_to_all | solution.py:1020
  111.9 217.2 %all-gather.10.cloned.1.call-start = ((), (), s32[]{:S(2)}) async-start(), calls=%async_computation.23 | async-start | bytes 2359296 | tf_op jit(solution)/shard_map/all_gather | solution.py:1023
  144.0 185.1 %all-gather.12.cloned.1.call-start = ((), (), s32[]{:S(2)}) async-start(), calls=%async_computation.24 | async-start | bytes 4718592 | tf_op jit(solution)/shard_map/all_gather | solution.py:1023
  154.4 48.6 %copy-start.147 = (f32[512,1]{0,1:T(1,128)}, f32[512,1]{0,1:T(1,128)S(1)}, u32[]{:S(2)}) copy-start(f32[512,1]{0,1:T(1,128)S(1)} %get-tuple-element.533) | copy-start | bytes 6148
  154.4 48.6 %copy-start.149 = (f32[512,1]{0,1:T(1,128)}, f32[512,1]{0,1:T(1,128)S(1)}, u32[]{:S(2)}) copy-start(f32[512,1]{0,1:T(1,128)S(1)} %get-tuple-element.534) | copy-start | bytes 6148
  168.6 29.7 %all-to-all-start.2 = ((bf16[4,512,256]{2,1,0:T(8,128)(2,1)}), bf16[4,512,256]{2,1,0:T(8,128)(2,1)}, u32[]{:S(2)}, u32[]{:S(2)}) async-start(bf16[4,512,256]{2,1,0:T(8,128)(2,1)} %bitcast.323), calls=%async_computation.2 | async-start | bytes 2097152 | tf_op jit(solution)/shard_map/all_to_all | solution.py:993
  173.0 156.1 %all-gather.14.cloned.1.call-start = ((), (), s32[]{:S(2)}) async-start(), calls=%async_computation.25 | async-start | bytes 4718592 | tf_op jit(solution)/shard_map/all_gather | solution.py:1023
  259.3 40.6 %all-to-all-start.6 = ((bf16[4,3,512,128]{3,2,1,0:T(8,128)(2,1)}), bf16[4,3,512,128]{3,2,1,0:T(8,128)(2,1)}, u32[]{:S(2)}, u32[]{:S(2)}) async-start(bf16[4,3,512,128]{3,2,1,0:T(8,128)(2,1)} %copy-done.9), calls=%async_computation.6 | async-start | bytes 3145728 | tf_op jit(solution)/shard_map/all_to_all | solution.py:993
  299.8 20.0 %all-to-all-start.5 = ((bf16[4,512,128]{2,1,0:T(8,128)(2,1)}), bf16[4,512,128]{2,1,0:T(8,128)(2,1)}, u32[]{:S(2)}, u32[]{:S(2)}) async-start(bf16[4,512,128]{2,1,0:T(8,128)(2,1)} %bitcast.312), calls=%async_computation.5 | async-start | bytes 1048576 | tf_op jit(solution)/shard_map/all_to_all | solution.py:993
  319.8 20.0 %all-to-all-start.7 = ((bf16[4,512,128]{2,1,0:T(8,128)(2,1)}), bf16[4,512,128]{2,1,0:T(8,128)(2,1)}, u32[]{:S(2)}, u32[]{:S(2)}) async-start(bf16[4,512,128]{2,1,0:T(8,128)(2,1)} %bitcast.311), calls=%async_computation.7 | async-start | bytes 1048576 | tf_op jit(solution)/shard_map/all_to_all | solution.py:993
  324.9 199.6 %reduce-scatter.11.cloned.1.call-start = ((), (), s32[]{:S(2)}) async-start(), calls=%async_computation.28 | async-start | bytes 4718592 | tf_op jit(solution)/shard_map/reduce_scatter | solution.py:1161
  369.6 154.9 %reduce-scatter.13.cloned.1.call-start = ((), (), s32[]{:S(2)}) async-start(), calls=%async_computation.29 | async-start | bytes 4718592 | tf_op jit(solution)/shard_map/reduce_scatter | solution.py:1161
  396.2 26.7 %all-to-all-start.10 = ((bf16[4,512,128]{2,1,0:T(8,128)(2,1)}), bf16[4,512,128]{2,1,0:T(8,128)(2,1)}, u32[]{:S(2)}, u32[]{:S(2)}) async-start(bf16[4,512,128]{2,1,0:T(8,128)(2,1)} %get-tuple-element.128), calls=%async_computation.10 | async-start | bytes 1048576 | tf_op jit(solution)/shard_map/all_to_all | solution.py:993
  422.9 42.5 %all-to-all-start.9 = ((bf16[4,3,512,128]{3,2,1,0:T(8,128)(2,1)}), bf16[4,3,512,128]{3,2,1,0:T(8,128)(2,1)}, u32[]{:S(2)}, u32[]{:S(2)}) async-start(bf16[4,3,512,128]{3,2,1,0:T(8,128)(2,1)} %shard_map.501), calls=%async_computation.9 | async-start | bytes 3145728 | tf_op jit(solution)/shard_map/all_to_all | solution.py:993
  427.9 230.9 %reduce-scatter.9.cloned.1.call-start = ((), (), s32[]{:S(2)}) async-start(), calls=%async_computation.27 | async-start | bytes 2359296 | tf_op jit(solution)/shard_map/reduce_scatter | solution.py:1161
  436.7 222.2 %reduce-scatter.7.cloned.1.call-start = ((), (), s32[]{:S(2)}) async-start(), calls=%async_computation.26 | async-start | bytes 7077888 | tf_op jit(solution)/shard_map/reduce_scatter | solution.py:1161
  458.5 46.6 %copy-start.11 = (bf16[512,1024]{1,0:T(8,128)(2,1)S(1)}, bf16[512,1024]{1,0:T(8,128)(2,1)}, u32[]{:S(2)}) copy-start(bf16[512,1024]{1,0:T(8,128)(2,1)} %add_convert_fusion.2.x_ref.refs_2_) | copy-start | bytes 3145732
  527.3 29.6 %all-to-all-start.13 = ((bf16[4,512,256]{2,1,0:T(8,128)(2,1)}), bf16[4,512,256]{2,1,0:T(8,128)(2,1)S(1)}, u32[]{:S(2)}, u32[]{:S(2)}) async-start(bf16[4,512,256]{2,1,0:T(8,128)(2,1)} %bitcast.321), calls=%async_computation.17 | async-start | bytes 2097152 | tf_op jit(solution)/shard_map/all_to_all | solution.py:993
  530.8 148.2 %all-gather.16.cloned.1.call-start = ((), (), s32[]{:S(2)}) async-start(), calls=%async_computation.30 | async-start | bytes 2621440 | tf_op jit(solution)/shard_map/all_gather | solution.py:1217
  557.9 40.6 %all-to-all-start.12 = ((bf16[4,128,1024]{2,1,0:T(8,128)(2,1)}), bf16[4,128,1024]{2,1,0:T(8,128)(2,1)S(1)}, u32[]{:S(2)}, u32[]{:S(2)}) async-start(bf16[4,128,1024]{2,1,0:T(8,128)(2,1)} %pad_maximum_fusion.2), calls=%async_computation.16 | async-start | bytes 2097152 | tf_op jit(solution)/shard_map/all_to_all | solution.py:993
  599.5 57.2 %all-to-all-start.14 = ((bf16[4,512,256]{2,1,0:T(8,128)(2,1)}), bf16[4,512,256]{2,1,0:T(8,128)(2,1)S(1)}, u32[]{:S(2)}, u32[]{:S(2)}) async-start(bf16[4,512,256]{2,1,0:T(8,128)(2,1)} %bitcast.322), calls=%async_computation.18 | async-start | bytes 2097152 | tf_op jit(solution)/shard_map/all_to_all | solution.py:993
  604.6 98.5 %reduce-scatter.17.cloned.1.call-start = ((), (), s32[]{:S(2)}) async-start(), calls=%async_computation.33 | async-start | bytes 2285568 | tf_op jit(solution)/shard_map/reduce_scatter | solution.py:1161
  662.2 30.2 %all-to-all-start.15 = ((bf16[4,128,1024]{2,1,0:T(8,128)(2,1)}), bf16[4,128,1024]{2,1,0:T(8,128)(2,1)}, u32[]{:S(2)}, u32[]{:S(2)}) async-start(bf16[4,128,1024]{2,1,0:T(8,128)(2,1)} %pad_maximum_fusion.3), calls=%async_computation.19 | async-start | bytes 2097152 | tf_op jit(solution)/shard_map/all_to_all | solution.py:993
  666.5 117.5 %reduce-scatter.15.cloned.1.call-start = ((), (), s32[]{:S(2)}) async-start(), calls=%async_computation.32 | async-start | bytes 1769472 | tf_op jit(solution)/shard_map/reduce_scatter | solution.py:1161
  678.9 148.1 %all-gather.18.cloned.1.call-start = ((), (), s32[]{:S(2)}) async-start(), calls=%async_computation.31 | async-start | bytes 2621440 | tf_op jit(solution)/shard_map/all_gather | solution.py:1219
  (293 other events, 2171.9 us)
Sparse Core Ops, SparseCore 0:
  53.5 46.4 all-gather.7
  144.1 27.0 all-gather.9
  173.1 36.6 all-gather.11
  211.6 36.7 all-gather.13
  369.7 53.8 reduce-scatter.10
  427.2 51.2 reduce-scatter.12
  481.8 41.2 reduce-scatter.8
  527.4 61.7 reduce-scatter.6
  591.4 68.1 all-gather.15
  663.3 39.7 reduce-scatter.16
  707.0 38.4 reduce-scatter.14
  774.6 48.6 all-gather.17

commit v8 on v7

--- a/solution.py
+++ b/solution.py
@@ -1073,7 +1073,6 @@
         time_vec = precise(act_one, time_w2) + time_bias[1]
         return sinusoid, pre_one, act_one, time_vec, jax.nn.silu(time_vec)
 
-    mod = precise(time_path(t_index[0])[4], ada_w) + ada_b
 
     hidden = jnp.take(txt_table, ids, axis=0).astype(F32)
     kept = []
@@ -1111,7 +1110,10 @@
     w1_piece = received[:, cut[1] :].reshape((shards,) + w1_shape).transpose(1, 0, 2)
     w1_full = gather(w1_piece.reshape(w1_shape[0], -1), 0)
     w2_full = gather(received[:, cut[0] : cut[1]], 1).reshape(-1, width)
-    c_pos = to_rows(gather_back(mish(pre_b).astype(BF), starts, ends))
+    conv_out = gather_back(mish(pre_b).astype(BF), starts, ends)
+    conv_out, steps, position = lax.optimization_barrier((conv_out, t_index[0], position))
+    mod = precise(time_path(steps)[4], ada_w) + ada_b
+    c_pos = to_rows(conv_out)
     x1 = x0 + c_pos.astype(F32)
 
     def modulate(state, mod_in, shift_part, scale_part):

time: 939 us -> 926 us (0.986)
  waiting for transfers between devices: 115 us -> 104 us
    all_to_all x11, waiting for transfers between devices: 103 us -> 80.6 us  [exchange(): return lax.all_to_all(values, axis, 0, 0)]
    reduce_scatter x6, waiting for transfers between devices: 7.36 us -> 19 us  [scatter_dp(): lax.psum_scatter(matrix.astype(BF), 'dp', scatter_dimension=0, tiled=True)]
  transfers between devices with their start and end apart: 25 -> 25, of which waited for: 10 -> 10; matrix products, arithmetic and copies ran while one was open for 29% -> 29% of each run, Pallas kernels for 19% -> 20%
where the time goes in v8:
time: 926 us; the launch traced here: 915 us
  Pallas kernels  270 us (29%)
  matrix products  122 us (13%)
  local copies, waits for them, and re-layouts  115 us (12%)
  other arithmetic  111 us (12%)
  blocking collectives  109 us (12%)
  waiting for transfers between devices  104 us (11%)
  starting transfers between devices  60.6 us (7%)
  between operations  22.4 us (2%)
    all_to_all x3, blocking collectives, exchange(): return lax.all_to_all(values, axis, 0, 0)  97.9 us
    all_to_all x11, waiting for transfers between devices, exchange(): return lax.all_to_all(values, axis, 0, 0)  80.6 us
    dot_general x22, matrix products, dot(): lax.dot_general(left.astype(BF), right.astype(BF), dims, preferred_elemen...  68.2 us
    pallas_call x1, Pallas kernels, last_sums(): pl.pallas_call(partial(last_kernel, dp, mp, n_all, n_mp, n_both, n_gather...  67.7 us
    unnamed x625, local copies, waits for them, and re-layouts  58 us
    all_to_all x11, starting transfers between devices, exchange(): return lax.all_to_all(values, axis, 0, 0)  48.4 us
    pallas_call x4, Pallas kernels, apply_conv(): pl.pallas_call(partial(conv_kernel, taps, turned), out_shape=jax.ShapeDty...  39.2 us
    pallas_call x2, Pallas kernels, attend_back(): pl.pallas_call(attend_back_kernel, out_shape=jax.ShapeDtypeStruct((shards...  35.7 us
  transfers between devices with their start and end apart: 25, of which 10 were waited for; matrix products, arithmetic and copies ran while one was open for 29% of the time, Pallas kernels for 20%

profile of v8, /device:TPU:0, one launch (start us, length us, event | category | flops | bytes accessed | tf_op | source)
XLA Modules:
  0.0 914.9 jit_solution(11363914024551940868)
XLA Ops:
  53.9 8.2 multiply_multiply_fusion.12
  115.3 9.8 %shard_map.495 = f32[2112,256]{1,0:T(8,128)S(1)} custom-call(f32[2144,256]{1,0:T(8,128)S(1)} %pad_add_fusion.1.x_ref, bf16[31,64,256]{2,1,0:T(8,128)(2,1)S(1)} %get-tuple-element.450.w_ref), custom_call_target="tpu_custom_call" | custom-call | flops 8581545984 | bytes 8388608 | tf_op jit(solution)/shard_map/pallas_call | solution.py:509
  128.1 9.8 %shard_map.496 = f32[2112,256]{1,0:T(8,128)S(1)} custom-call(f32[2144,256]{1,0:T(8,128)S(1)} %pad_convert_fusion.x_ref, bf16[31,64,256]{2,1,0:T(8,128)(2,1)S(1)} %copy-done.18), custom_call_target="tpu_custom_call" | custom-call | flops 8581545984 | bytes 8388608 | tf_op jit(solution)/shard_map/pallas_call | solution.py:509
  176.7 10.2 %all-to-all-done.2 = bf16[4,512,256]{2,1,0:T(8,128)(2,1)} async-done(((bf16[4,512,256]{2,1,0:T(8,128)(2,1)}), bf16[4,512,256]{2,1,0:T(8,128)(2,1)}, u32[]{:S(2)}, u32[]{:S(2)}) %all-to-all-start.2) | async-done | bytes 1048608 | tf_op jit(solution)/shard_map/all_to_all | solution.py:993
  192.1 6.9 add_convert_fusion.2.x_ref.refs_2_
  208.3 39.6 %all_to_all.80.q_ref.k_ref.v_ref = bf16[4,3,512,128]{3,2,1,0:T(8,128)(2,1)} all-to-all(bf16[4,3,512,128]{3,2,1,0:T(8,128)(2,1)S(1)} %get-tuple-element.124), channel_id=1, replica_groups=mesh['dp'=8,'mp'=4] {'mp'}, dimensions={0} | all-to-all | bytes 3145728 | tf_op jit(solution)/shard_map/all_to_all | solution.py:993
  258.4 11.6 %shard_map.498 = (bf16[2048,128]{1,0:T(8,128)(2,1)S(1)}, f32[128,2048]{1,0:T(8,128)S(1)}, f32[8,2048]{1,0:T(8,128)S(1)}) custom-call(s32[4,2]{1,0:T(4,128)S(1)} %pad_add_fusion.18.bounds, bf16[4,3,512,128]{3,2,1,0:T(8,128)(2,1)S(1)} %copy-done.8, bf16[4,3,512,128]{3,2,1,0:T(8,128)(2,1)S(1)} %copy-done.8, bf16[4,3,512,128]{3,2,1,0:T(8,128)(2,1)S(1)} %copy-done.8, ...), custom_call_target="tpu_custom_call" | custom-call | flops 2147483648 | bytes 8388608 | tf_op jit(solution)/shard_map/pallas_call | solution.py:741
  271.8 16.8 %all-to-all-done.6.q_ref.k_ref.v_ref = bf16[4,3,512,128]{3,2,1,0:T(8,128)(2,1)} async-done(((bf16[4,3,512,128]{3,2,1,0:T(8,128)(2,1)}), bf16[4,3,512,128]{3,2,1,0:T(8,128)(2,1)}, u32[]{:S(2)}, u32[]{:S(2)}) %all-to-all-start.6) | async-done | bytes 1572896 | tf_op jit(solution)/shard_map/all_to_all | solution.py:993
  293.9 12.8 %shard_map.499 = (bf16[2048,128]{1,0:T(8,128)(2,1)S(1)}, f32[128,2048]{1,0:T(8,128)S(1)}, f32[8,2048]{1,0:T(8,128)S(1)}) custom-call(s32[4,2]{1,0:T(4,128)S(1)} %pad_add_fusion.18.bounds, bf16[4,3,512,128]{3,2,1,0:T(8,128)(2,1)} %all-to-all-done.6.q_ref.k_ref.v_ref, bf16[4,3,512,128]{3,2,1,0:T(8,128)(2,1)} %all-to-all-done.6.q_ref.k_ref.v_ref, ...), custom_call_target="tpu_custom_call" | custom-call | flops 2147483648 | bytes 8388608 | tf_op jit(solution)/shard_map/pallas_call | solution.py:741
  317.6 9.5 %all-to-all-done.7.refs_1_ = bf16[4,512,128]{2,1,0:T(8,128)(2,1)} async-done(((bf16[4,512,128]{2,1,0:T(8,128)(2,1)}), bf16[4,512,128]{2,1,0:T(8,128)(2,1)}, u32[]{:S(2)}, u32[]{:S(2)}) %all-to-all-start.7) | async-done | bytes 524320 | tf_op jit(solution)/shard_map/all_to_all | solution.py:993
  327.1 23.4 %shard_map.500 = (bf16[512,1024]{1,0:T(8,128)(2,1)}, bf16[512,1024]{1,0:T(8,128)(2,1)}, bf16[512,2048]{1,0:T(8,128)(2,1)}, bf16[512,1024]{1,0:T(8,128)(2,1)}, bf...) custom-call(bf16[4,512,128]{2,1,0:T(8,128)(2,1)} %all-to-all-done.5., ...), custom_call_target="tpu_custom_call" | custom-call | flops 10737418240 | bytes 20971520 | tf_op jit(solution)/shard_map/pallas_call | solution.py:967
  363.6 18.1 %all_to_all.81 = bf16[4,512,128]{2,1,0:T(8,128)(2,1)} all-to-all(bf16[4,512,128]{2,1,0:T(8,128)(2,1)} %get-tuple-element.131), channel_id=1, replica_groups=mesh['dp'=8,'mp'=4] {'mp'}, dimensions={0} | all-to-all | bytes 1048576 | tf_op jit(solution)/shard_map/all_to_all | solution.py:993
  390.6 17.7 %shard_map.501 = bf16[4,3,512,128]{3,2,1,0:T(8,128)(2,1)} custom-call(s32[4,2]{1,0:T(4,128)S(1)} %pad_add_fusion.18.bounds, bf16[4,3,512,128]{3,2,1,0:T(8,128)(2,1)} %all_to_all.80.q_ref.k_ref.v_ref, bf16[4,3,512,128]{3,2,1,0:T(8,128)(2,1)} %all_to_all.80.q_ref.k_ref.v_ref, bf16[4,3,512,128]{3,2,1,0:T(8,128)(2,1)} %all_to_all.80.q_ref.k_ref.v_ref, ...), custom_call_target="tpu_custom_call" | custom-call | flops 5368709120 | bytes 16777216 | tf_op jit(solution)/shard_map/pallas_call | solution.py:847
  426.2 17.9 %shard_map.502 = bf16[4,3,512,128]{3,2,1,0:T(8,128)(2,1)} custom-call(s32[4,2]{1,0:T(4,128)S(1)} %pad_add_fusion.18.bounds, bf16[4,3,512,128]{3,2,1,0:T(8,128)(2,1)} %all-to-all-done.6.q_ref.k_ref.v_ref, bf16[4,3,512,128]{3,2,1,0:T(8,128)(2,1)} %all-to-all-done.6.q_ref.k_ref.v_ref, bf16[4,3,512,128]{3,2,1,0:T(8,128)(2,1)} %all-to-all-done.6.q_ref.k_ref.v_ref, ...), custom_call_target="tpu_custom_call" | custom-call | flops 5368709120 | bytes 16777216 | tf_op jit(solution)/shard_map/pallas_call | solution.py:847
  449.0 40.2 %all_to_all.82.refs_1_ = bf16[4,3,512,128]{3,2,1,0:T(8,128)(2,1)S(1)} all-to-all(bf16[4,3,512,128]{3,2,1,0:T(8,128)(2,1)} %shard_map.502), channel_id=1, replica_groups=mesh['dp'=8,'mp'=4] {'mp'}, dimensions={0} | all-to-all | bytes 3145728 | tf_op jit(solution)/shard_map/all_to_all | solution.py:993
  489.1 11.6 %shard_map.503 = (f32[512,1024]{1,0:T(8,128)}, bf16[1024,3072]{1,0:T(8,128)(2,1)}, f32[4,3,256]{2,1,0:T(4,128)S(1)}) custom-call(bf16[4,3,512,128]{3,2,1,0:T(8,128)(2,1)} %all-to-all-done.9.refs_0_, bf16[4,3,512,128]{3,2,1,0:T(8,128)(2,1)S(1)} %all_to_all.82.refs_1_, bf16[512,1024]{1,0:T(8,128)(2,1)S(1)} %copy-done.11, ...), custom_call_target="tpu_custom_call" | custom-call | flops 6442450944 | bytes 20971520 | tf_op jit(solution)/shard_map/pallas_call | solution.py:636
  525.8 14.2 %all-to-all-done.13 = bf16[4,512,256]{2,1,0:T(8,128)(2,1)S(1)} async-done(((bf16[4,512,256]{2,1,0:T(8,128)(2,1)}), bf16[4,512,256]{2,1,0:T(8,128)(2,1)S(1)}, u32[]{:S(2)}, u32[]{:S(2)}) %all-to-all-start.13) | async-done | bytes 1048608 | tf_op jit(solution)/shard_map/all_to_all | solution.py:993
  553.4 9.9 %shard_map.504 = f32[2112,256]{1,0:T(8,128)S(1)} custom-call(f32[2144,256]{1,0:T(8,128)S(1)} %pad_add_fusion.x_ref, bf16[31,64,256]{2,1,0:T(8,128)(2,1)S(1)} %copy-done.19), custom_call_target="tpu_custom_call" | custom-call | flops 8581545984 | bytes 8388608 | tf_op jit(solution)/shard_map/pallas_call | solution.py:509
  568.8 9.8 %shard_map.505 = f32[2112,256]{1,0:T(8,128)S(1)} custom-call(f32[2144,256]{1,0:T(8,128)S(1)} %pad.195.x_ref, bf16[31,64,256]{2,1,0:T(8,128)(2,1)S(1)} %copy-done.17), custom_call_target="tpu_custom_call" | custom-call | flops 8581545984 | bytes 8388608 | tf_op jit(solution)/shard_map/pallas_call | solution.py:509
  589.7 15.7 %shard_map.507 = f32[256,1984]{1,0:T(8,128)S(1)} custom-call(f32[2144,256]{1,0:T(8,128)} %copy-done.3, f32[2112,256]{1,0:T(8,128)S(1)} %copy-done.4), custom_call_target="tpu_custom_call" | custom-call | flops 8581545984 | bytes 8388608 | tf_op jit(solution)/shard_map/pallas_call | solution.py:548
  605.5 15.7 %shard_map.506 = f32[256,1984]{1,0:T(8,128)S(1)} custom-call(f32[2144,256]{1,0:T(8,128)} %copy-done.2, f32[2112,256]{1,0:T(8,128)S(1)} %convert_element_type.336.g_ref), custom_call_target="tpu_custom_call" | custom-call | flops 8581545984 | bytes 8388608 | tf_op jit(solution)/shard_map/pallas_call | solution.py:548
  626.2 11.8 %all-to-all-done.14 = bf16[4,512,256]{2,1,0:T(8,128)(2,1)S(1)} async-done(((bf16[4,512,256]{2,1,0:T(8,128)(2,1)}), bf16[4,512,256]{2,1,0:T(8,128)(2,1)S(1)}, u32[]{:S(2)}, u32[]{:S(2)}) %all-to-all-start.14) | async-done | bytes 1048608 | tf_op jit(solution)/shard_map/all_to_all | solution.py:993
  660.0 9.2 %all-to-all-done.15 = bf16[4,128,1024]{2,1,0:T(8,128)(2,1)} async-done(((bf16[4,128,1024]{2,1,0:T(8,128)(2,1)}), bf16[4,128,1024]{2,1,0:T(8,128)(2,1)}, u32[]{:S(2)}, u32[]{:S(2)}) %all-to-all-start.15) | async-done | bytes 1048608 | tf_op jit(solution)/shard_map/all_to_all | solution.py:993
  672.7 18.9 %reduce-scatter.17.cloned.1.call-done = bf16[32,3968]{1,0:T(8,128)(2,1)} async-done(((bf16[256,3968]{1,0:T(8,128)(2,1)}), bf16[32,3968]{1,0:T(8,128)(2,1)}) %reduce-scatter.17.cloned.1.call-update) | async-done | bytes 253968 | tf_op jit(solution)/shard_map/reduce_scatter | solution.py:1163
  691.6 11.9 %shard_map.508 = f32[4,7168]{1,0:T(4,128)S(1)} custom-call(f32[4,7168]{1,0:T(4,128)S(1)} %pad_maximum_fusion.10.x_ref), custom_call_target="tpu_custom_call" | custom-call | tf_op jit(solution)/shard_map/pallas_call | solution.py:115
  703.6 11.5 %all-gather = f32[8,4,6272]{2,1,0:T(4,128)} all-gather(f32[1,4,6272]{2,1,0:T(4,128)S(1)} %maximum_bitcast_fusion.1), channel_id=1, replica_groups=mesh['dp'=8,'mp'=4] {'dp'}, dimensions={0}, use_global_device_ids=true | all-gather | bytes 903168 | tf_op jit(solution)/shard_map/all_gather | solution.py:1229
  719.9 7.0 fusion.282
  736.3 8.7 fusion.47
  783.5 8.3 shard_map.509
  793.8 7.5 fusion.281
  819.3 67.7 %shard_map.510 = (f32[16,2560]{1,0:T(8,128)}, f32[32,512]{1,0:T(8,128)}, f32[32,512]{1,0:T(8,128)}, f32[16,1024]{1,0:T(8,128)}, f32[16,1024]{1,0:T(8,128)}, /*in...) custom-call(bf16[4,2,64,2560]{3,2,1,0:T(8,128)(2,1)} %bitcast.328, ...), custom_call_target="tpu_custom_call" | custom-call | tf_op jit(solution)/shard_map/pallas_call | solution.py:339
  895.9 6.9 maximum_convert_fusion
  (949 shorter events, 393.9 us)
Async XLA Ops:
  13.1 38.6 %all-to-all-start.3 = ((bf16[4,400,256]{2,1,0:T(8,128)(2,1)}), bf16[4,400,256]{2,1,0:T(8,128)(2,1)}, u32[]{:S(2)}, u32[]{:S(2)}) async-start(bf16[4,400,256]{2,1,0:T(8,128)(2,1)} %broadcast_in_dim.326), calls=%async_computation.3 | async-start | bytes 1638400 | tf_op jit(solution)/shard_map/all_to_all | solution.py:1020
  19.4 179.6 %all-gather.8.cloned.1.call-start = ((), (), s32[]{:S(2)}) async-start(), calls=%async_computation.22 | async-start | bytes 7077888 | tf_op jit(solution)/shard_map/all_gather | solution.py:1023
  22.7 50.3 %copy-start.138 = (f32[1,1,1024]{2,0,1:T(1,128)}, f32[1,1,1024]{2,0,1:T(1,128)S(1)}, u32[]{:S(2)}) copy-start(f32[1,1,1024]{2,0,1:T(1,128)S(1)} %get-tuple-element.513) | copy-start | bytes 12292
  80.0 27.5 %all-to-all-start = ((bf16[4,512,256]{2,1,0:T(8,128)(2,1)}), bf16[4,512,256]{2,1,0:T(8,128)(2,1)S(1)}, u32[]{:S(2)}, u32[]{:S(2)}) async-start(bf16[4,512,256]{2,1,0:T(8,128)(2,1)} %bitcast.302), calls=%async_computation | async-start | bytes 2097152 | tf_op jit(solution)/shard_map/all_to_all | solution.py:993
  96.1 58.5 %copy-start.158 = (pred[2048]{0:T(1024)(128)(4,1)}, pred[2048]{0:T(1024)(128)(4,1)S(1)}, u32[]{:S(2)}) copy-start(pred[2048]{0:T(1024)(128)(4,1)S(1)} %get-tuple-element.598) | copy-start | bytes 6148
  97.5 57.1 %copy-start.160 = (pred[2048]{0:T(1024)(128)(4,1)}, pred[2048]{0:T(1024)(128)(4,1)S(1)}, u32[]{:S(2)}) copy-start(pred[2048]{0:T(1024)(128)(4,1)S(1)} %get-tuple-element.600) | copy-start | bytes 6148
  98.8 55.8 %copy-start.162 = (pred[2048]{0:T(1024)(128)(4,1)}, pred[2048]{0:T(1024)(128)(4,1)S(1)}, u32[]{:S(2)}) copy-start(pred[2048]{0:T(1024)(128)(4,1)S(1)} %get-tuple-element.602) | copy-start | bytes 6148
  108.7 34.7 %all-to-all-start.1 = ((bf16[4,160,1024]{2,1,0:T(8,128)(2,1)}), bf16[4,160,1024]{2,1,0:T(8,128)(2,1)}, u32[]{:S(2)}, u32[]{:S(2)}) async-start(bf16[4,160,1024]{2,1,0:T(8,128)(2,1)} %broadcast_in_dim.323), calls=%async_computation.1 | async-start | bytes 2621440 | tf_op jit(solution)/shard_map/all_to_all | solution.py:1020
  113.0 204.6 %all-gather.10.cloned.1.call-start = ((), (), s32[]{:S(2)}) async-start(), calls=%async_computation.23 | async-start | bytes 2359296 | tf_op jit(solution)/shard_map/all_gather | solution.py:1023
  145.1 172.6 %all-gather.12.cloned.1.call-start = ((), (), s32[]{:S(2)}) async-start(), calls=%async_computation.24 | async-start | bytes 4718592 | tf_op jit(solution)/shard_map/all_gather | solution.py:1023
  149.6 42.0 %copy-start.147 = (f32[512,1]{0,1:T(1,128)}, f32[512,1]{0,1:T(1,128)S(1)}, u32[]{:S(2)}) copy-start(f32[512,1]{0,1:T(1,128)S(1)} %get-tuple-element.539) | copy-start | bytes 6148
  157.3 29.6 %all-to-all-start.2 = ((bf16[4,512,256]{2,1,0:T(8,128)(2,1)}), bf16[4,512,256]{2,1,0:T(8,128)(2,1)}, u32[]{:S(2)}, u32[]{:S(2)}) async-start(bf16[4,512,256]{2,1,0:T(8,128)(2,1)} %bitcast.322), calls=%async_computation.2 | async-start | bytes 2097152 | tf_op jit(solution)/shard_map/all_to_all | solution.py:993
  161.7 155.9 %all-gather.14.cloned.1.call-start = ((), (), s32[]{:S(2)}) async-start(), calls=%async_computation.25 | async-start | bytes 4718592 | tf_op jit(solution)/shard_map/all_gather | solution.py:1023
  208.3 39.6 %copy-start.9 = (bf16[4,3,512,128]{3,2,1,0:T(8,128)(2,1)}, bf16[4,3,512,128]{3,2,1,0:T(8,128)(2,1)S(1)}, u32[]{:S(2)}) copy-start(bf16[4,3,512,128]{3,2,1,0:T(8,128)(2,1)S(1)} %get-tuple-element.128) | copy-start | bytes 4718596
  248.0 40.6 %all-to-all-start.6 = ((bf16[4,3,512,128]{3,2,1,0:T(8,128)(2,1)}), bf16[4,3,512,128]{3,2,1,0:T(8,128)(2,1)}, u32[]{:S(2)}, u32[]{:S(2)}) async-start(bf16[4,3,512,128]{3,2,1,0:T(8,128)(2,1)} %copy-done.9), calls=%async_computation.6 | async-start | bytes 3145728 | tf_op jit(solution)/shard_map/all_to_all | solution.py:993
  288.5 20.0 %all-to-all-start.5 = ((bf16[4,512,128]{2,1,0:T(8,128)(2,1)}), bf16[4,512,128]{2,1,0:T(8,128)(2,1)}, u32[]{:S(2)}, u32[]{:S(2)}) async-start(bf16[4,512,128]{2,1,0:T(8,128)(2,1)} %bitcast.312), calls=%async_computation.5 | async-start | bytes 1048576 | tf_op jit(solution)/shard_map/all_to_all | solution.py:993
  308.5 18.6 %all-to-all-start.7 = ((bf16[4,512,128]{2,1,0:T(8,128)(2,1)}), bf16[4,512,128]{2,1,0:T(8,128)(2,1)}, u32[]{:S(2)}, u32[]{:S(2)}) async-start(bf16[4,512,128]{2,1,0:T(8,128)(2,1)} %bitcast.311), calls=%async_computation.7 | async-start | bytes 1048576 | tf_op jit(solution)/shard_map/all_to_all | solution.py:993
  313.6 195.4 %reduce-scatter.11.cloned.1.call-start = ((), (), s32[]{:S(2)}) async-start(), calls=%async_computation.28 | async-start | bytes 4718592 | tf_op jit(solution)/shard_map/reduce_scatter | solution.py:1163
  356.9 152.1 %reduce-scatter.13.cloned.1.call-start = ((), (), s32[]{:S(2)}) async-start(), calls=%async_computation.29 | async-start | bytes 4718592 | tf_op jit(solution)/shard_map/reduce_scatter | solution.py:1163
  381.7 26.6 %all-to-all-start.10 = ((bf16[4,512,128]{2,1,0:T(8,128)(2,1)}), bf16[4,512,128]{2,1,0:T(8,128)(2,1)}, u32[]{:S(2)}, u32[]{:S(2)}) async-start(bf16[4,512,128]{2,1,0:T(8,128)(2,1)} %get-tuple-element.134), calls=%async_computation.10 | async-start | bytes 1048576 | tf_op jit(solution)/shard_map/all_to_all | solution.py:993
  408.4 40.6 %all-to-all-start.9 = ((bf16[4,3,512,128]{3,2,1,0:T(8,128)(2,1)}), bf16[4,3,512,128]{3,2,1,0:T(8,128)(2,1)}, u32[]{:S(2)}, u32[]{:S(2)}) async-start(bf16[4,3,512,128]{3,2,1,0:T(8,128)(2,1)} %shard_map.501), calls=%async_computation.9 | async-start | bytes 3145728 | tf_op jit(solution)/shard_map/all_to_all | solution.py:993
  413.4 226.7 %reduce-scatter.9.cloned.1.call-start = ((), (), s32[]{:S(2)}) async-start(), calls=%async_computation.27 | async-start | bytes 2359296 | tf_op jit(solution)/shard_map/reduce_scatter | solution.py:1163
  422.2 218.0 %reduce-scatter.7.cloned.1.call-start = ((), (), s32[]{:S(2)}) async-start(), calls=%async_computation.26 | async-start | bytes 7077888 | tf_op jit(solution)/shard_map/reduce_scatter | solution.py:1163
  444.2 45.0 %copy-start.11 = (bf16[512,1024]{1,0:T(8,128)(2,1)S(1)}, bf16[512,1024]{1,0:T(8,128)(2,1)}, u32[]{:S(2)}) copy-start(bf16[512,1024]{1,0:T(8,128)(2,1)} %add_convert_fusion.2.x_ref.refs_2_) | copy-start | bytes 3145732
  511.8 28.2 %all-to-all-start.13 = ((bf16[4,512,256]{2,1,0:T(8,128)(2,1)}), bf16[4,512,256]{2,1,0:T(8,128)(2,1)S(1)}, u32[]{:S(2)}, u32[]{:S(2)}) async-start(bf16[4,512,256]{2,1,0:T(8,128)(2,1)} %bitcast.321), calls=%async_computation.17 | async-start | bytes 2097152 | tf_op jit(solution)/shard_map/all_to_all | solution.py:993
  515.4 144.7 %all-gather.16.cloned.1.call-start = ((), (), s32[]{:S(2)}) async-start(), calls=%async_computation.30 | async-start | bytes 2621440 | tf_op jit(solution)/shard_map/all_gather | solution.py:1219
  541.0 40.5 %all-to-all-start.12 = ((bf16[4,128,1024]{2,1,0:T(8,128)(2,1)}), bf16[4,128,1024]{2,1,0:T(8,128)(2,1)S(1)}, u32[]{:S(2)}, u32[]{:S(2)}) async-start(bf16[4,128,1024]{2,1,0:T(8,128)(2,1)} %pad_maximum_fusion.2), calls=%async_computation.16 | async-start | bytes 2097152 | tf_op jit(solution)/shard_map/all_to_all | solution.py:993
  582.5 55.5 %all-to-all-start.14 = ((bf16[4,512,256]{2,1,0:T(8,128)(2,1)}), bf16[4,512,256]{2,1,0:T(8,128)(2,1)S(1)}, u32[]{:S(2)}, u32[]{:S(2)}) async-start(bf16[4,512,256]{2,1,0:T(8,128)(2,1)} %bitcast.323), calls=%async_computation.18 | async-start | bytes 2097152 | tf_op jit(solution)/shard_map/all_to_all | solution.py:993
  587.5 104.1 %reduce-scatter.17.cloned.1.call-start = ((), (), s32[]{:S(2)}) async-start(), calls=%async_computation.33 | async-start | bytes 2285568 | tf_op jit(solution)/shard_map/reduce_scatter | solution.py:1163
  643.5 25.8 %all-to-all-start.15 = ((bf16[4,128,1024]{2,1,0:T(8,128)(2,1)}), bf16[4,128,1024]{2,1,0:T(8,128)(2,1)}, u32[]{:S(2)}, u32[]{:S(2)}) async-start(bf16[4,128,1024]{2,1,0:T(8,128)(2,1)} %pad_maximum_fusion.3), calls=%async_computation.19 | async-start | bytes 2097152 | tf_op jit(solution)/shard_map/all_to_all | solution.py:993
  647.8 124.6 %reduce-scatter.15.cloned.1.call-start = ((), (), s32[]{:S(2)}) async-start(), calls=%async_computation.32 | async-start | bytes 1769472 | tf_op jit(solution)/shard_map/reduce_scatter | solution.py:1163
  659.9 155.4 %all-gather.18.cloned.1.call-start = ((), (), s32[]{:S(2)}) async-start(), calls=%async_computation.31 | async-start | bytes 2621440 | tf_op jit(solution)/shard_map/all_gather | solution.py:1221
  (293 other events, 2108.9 us)
Sparse Core Ops, SparseCore 0:
  54.0 46.4 all-gather.7
  145.2 26.9 all-gather.9
  174.1 36.7 all-gather.11
  212.6 36.7 all-gather.13
  357.0 55.2 reduce-scatter.10
  415.9 51.3 reduce-scatter.12
  470.5 41.1 reduce-scatter.8
  516.1 61.7 reduce-scatter.6
  580.0 66.3 all-gather.15
  650.2 41.3 reduce-scatter.16
  695.5 38.4 reduce-scatter.14
  763.0 48.7 all-gather.17
